TPU v7x, 256 devices: a whole 4x4x8 slice. The times are simulated.
256 devices in a mesh: row: 16 (over z, core), col: 8 (over y_lo, x), gz: 2 (over y_hi).
Axes of the slice: x: 4, y: 4 (y_hi: 2, y_lo: 2; y = y_hi * 2 + y_lo), z: 8, core: 2. Of those that a mesh axis runs over, the one named last changes fastest.
Arguments:
- initial_field: float32 [8, 64, 128, 256], P(None, 'row', 'col', 'gz'), may hold values from -6 to 6
- source_term: float32 [8, 64, 128, 256], P(None, 'row', 'col', 'gz'), may hold values from -6 to 6
- cell_class: int32 [64, 128, 256], P('row', 'col', 'gz'), may hold values from 0 to 15
- class_shift: float32 [16], replicated, may hold values from 0.05 to 4
- surface_cell: int32 [32768], P(('row', 'col', 'gz')), may hold values from 0 to 8191
- live_count: int32 [256], P(('row', 'col', 'gz')), may hold values from 1 to 128, 20480 in all
- panel_geometry: float32 [4, 32768], P(None, ('row', 'col', 'gz')), may hold values from 0.5 to 2
Outputs:
- final_field: float32 [8, 64, 128, 256], P(None, 'row', 'col', 'gz')
- boundary_potential: float32 [8, 32768], P(None, ('row', 'col', 'gz'))
Inputs may be any that keep to these rules, and one draw needn't show every extreme that they name: Slots 0 to live_count[b] - 1 of brick b are in use; the counts sum to 20480. `surface_cell`: A cell index inside the panel's own brick, x * 16 * 128 + y * 128 + z.
All inputs are finite; a program needn't handle non-finite values. No bound on the sum of `live_count` on one device may be relied on, other than what follows from the above.
Results may differ from a plain program's by a relative error of at most 0.004.
Values may be sent and summed in bfloat16 or wider, within the bound.
No kernel may reach another device: no remote copies, remote signals or barrier semaphores. Data moves between devices by JAX's collectives and lax.ppermute only.
A program may use at most 128 MiB of HBM per device.

v0:
```python
import math

import jax
import jax.numpy as jnp
from jax import lax
from jax.sharding import PartitionSpec as P

SWEEPS = 3
ROUNDS = 2


relax_weight = 0.8
wave_number = 25.0
soften = 0.05
coupling = 0.5


def in_order(blocks, dim):
    blocks = jnp.moveaxis(blocks, 0, dim)
    shape = blocks.shape
    return blocks.reshape(*shape[:dim], shape[dim] * shape[dim + 1], *shape[dim + 2 :])


def from_everyone(x, axis):
    copies = jnp.broadcast_to(x, (lax.axis_size(axis), *x.shape))
    return lax.all_to_all(copies, axis, split_axis=0, concat_axis=0, tiled=True)


def collect(x, axis, dim):
    return in_order(from_everyone(x, axis), dim)


def padded_2(x, sides, width):
    edges = {}
    for axis, dim in sides:
        devices, length = (lax.axis_size(axis), x.shape[dim])
        up = [(i, (i + 1) % devices) for i in range(devices - 1)]
        last = lax.slice_in_dim(x, length - width, length, axis=dim)
        initial = lax.slice_in_dim(x, 0, width, axis=dim)
        edges[dim] = (
            lax.ppermute(last, axis, up),
            lax.ppermute(initial, axis, [(b, a) for a, b in up]),
        )
    done = []
    for _, dim in sides:
        low, high = edges[dim]
        around = [(width, width) if d in done else (0, 0) for d in range(x.ndim)]
        x = jnp.concatenate([jnp.pad(low, around), x, jnp.pad(high, around)], axis=dim)
        done.append(dim)
    return x


def in_blocks(x, dim, devices):
    before, after = (x.shape[:dim], x.shape[dim + 1 :])
    return jnp.moveaxis(x.reshape(*before, devices, -1, *after), dim, 0)


def sent_and_summed(x, axis, dim):
    devices = lax.axis_size(axis)
    blocks = lax.all_to_all(in_blocks(x, dim, devices), axis, 0, 0, tiled=True)
    return jnp.sum(blocks, axis=0)


def neighbours(padded):
    total = padded[:, 2:, 1:-1, 1:-1] + padded[:, :-2, 1:-1, 1:-1]
    total = total + padded[:, 1:-1, 2:, 1:-1] + padded[:, 1:-1, :-2, 1:-1]
    total = total + padded[:, 1:-1, 1:-1, 2:] + padded[:, 1:-1, 1:-1, :-2]
    return total


def relax(state, padded, forcing, shift_field):
    diagonal = 6.0 + shift_field
    residual = forcing - (diagonal * state - neighbours(padded))
    return state + relax_weight * residual / diagonal


def kernel_tile(sources, targets, factor):
    delta_x = targets[0][None, :] - sources[0][:, None]
    delta_y = targets[1][None, :] - sources[1][:, None]
    delta_z = targets[2][None, :] - sources[2][:, None]
    distance = jnp.sqrt(delta_x * delta_x + delta_y * delta_y + delta_z * delta_z)
    values = sources[3][:, None] * jnp.cos(wave_number * distance) / (distance + soften)
    return (values * factor).astype(jnp.bfloat16)


def shift_lookup(cell_class, class_shift):
    shift_field = jnp.zeros(cell_class.shape, jnp.float32)
    for level in range(class_shift.shape[0]):
        shift_field = shift_field + jnp.where(cell_class == level, class_shift[level], 0.0)
    return shift_field


def local(
    initial_field, source_term, cell_class, class_shift, surface_cell, live_count, panel_geometry
):
    channels, size_x, size_y, size_z = initial_field.shape
    slots = surface_cell.shape[0]
    panels = slots * lax.axis_size("row") * lax.axis_size("col") * lax.axis_size("gz")
    factor = 1.0 / math.sqrt(panels)
    shift_field = shift_lookup(cell_class, class_shift)
    live = (jnp.arange(slots, dtype=jnp.int32) < live_count[0]).astype(jnp.float32)
    source_geo = collect(panel_geometry, ("row", "gz"), 1)
    target_geo = collect(panel_geometry, "col", 1)
    state = initial_field
    load = jnp.zeros_like(source_term)
    potential = jnp.zeros((channels, slots), jnp.float32)
    for round_index in range(ROUNDS):
        forcing = source_term + load
        for sweep_index in range(SWEEPS):
            padded = padded_2(state, (("row", 1), ("col", 2), ("gz", 3)), 1)
            state = relax(state, padded, forcing, shift_field)
        density = (jnp.take(state.reshape(channels, -1), surface_cell, axis=1) * live).astype(
            jnp.bfloat16
        )
        initial = jnp.zeros((channels, target_geo.shape[1]), jnp.float32)
        piece = collect(density, ("row", "gz"), 1)
        count = piece.shape[1]
        width = math.gcd(count, 512)

        def add_block(block_index, carry):
            offset = block_index * width
            values = lax.dynamic_slice_in_dim(piece, offset, width, 1)
            sources = lax.dynamic_slice_in_dim(source_geo, offset, width, 1)
            tile = kernel_tile(sources, target_geo, factor)
            return carry + jnp.dot(values, tile, preferred_element_type=jnp.float32)

        partial_value = lax.fori_loop(0, count // width, add_block, initial)
        summed = sent_and_summed(partial_value, "col", 1)
        potential = summed * live
        if round_index + 1 < ROUNDS:
            spread = (
                jnp.zeros((channels, size_x * size_y * size_z), jnp.float32)
                .at[:, surface_cell]
                .add(coupling * potential)
            )
            load = spread.reshape(source_term.shape)
    return (state, potential)


def solution(mesh):
    placed = (
        P(None, "row", "col", "gz"),
        P(None, "row", "col", "gz"),
        P("row", "col", "gz"),
        P(),
        P(("row", "col", "gz")),
        P(("row", "col", "gz")),
        P(None, ("row", "col", "gz")),
    )
    return jax.shard_map(
        local,
        mesh=mesh,
        in_specs=placed,
        out_specs=(P(None, "row", "col", "gz"), P(None, ("row", "col", "gz"))),
        check_vma=False,
    )
```

profile of v0, /device:TPU:1, one launch (start us, length us, event | category | flops | bytes accessed | tf_op | source)
XLA Modules:
  0.0 396.3 jit_solution(11003822734046080696)
XLA Ops:
  18.5 5.9 %all-to-all-start.2 = ((f32[8,4,128]{2,1,0:T(4,128)}), f32[8,4,128]{2,1,0:T(4,128)S(1)}, u32[]{:S(2)}, u32[]{:S(2)}) async-start(f32[8,4,128]{2,1,0:T(4,128)} %broadcast_in_dim.132), calls=%async_computation.2 | async-start | bytes 32768 | tf_op jit(solution)/shard_map/all_to_all | solution.py:26
  27.0 10.9 %add_add_fusion = f32[4,16,128]{2,1,0:T(8,128)S(1)} fusion(s32[4,16,128]{2,1,0:T(8,128)} %param.15, f32[]{:T(128)} %bitcast.15, f32[]{:T(128)} %bitcast.14, f32[]{:T(128)} %bitcast.13, f32[]{:T(128)} %bitcast.12, f32[]{:T(128)} %bitcast.11, f32[]{:T(128)} %bitcast.10, f32[]{:T(128)} %bitcast.9, f32[]{:T(128)} %bitcast.8, f32[]{:T(128)} %bitcast.7, ...), kind=kLoop, calls=%fused_computation.213 | loop fusion | flops 393216 | bytes 65600 | tf_op jit(solution)/shard_map/add | solution.py:72
  52.6 5.5 %collective-permute-start.11 = (f32[8,4,16,1]{3,2,1,0:T(8,128)S(1)}, f32[8,4,16,1]{3,2,1,0:T(8,128)S(1)}, u32[]{:S(2)}, u32[]{:S(2)}) collective-permute-start(f32[8,4,16,1]{3,2,1,0:T(8,128)S(1)} %get-tuple-element.294), channel_id=1, source_target_pairs={{0,1},{2,3},{4,5},{6,7},{8,9},{10,11},{12,13},{14,15},{16,17},{18,... | collective-permute-start | bytes 6152 | tf_op jit(solution)/shard_map/ppermute | solution.py:41
  73.5 5.5 %collective-permute-start.17 = (f32[8,4,16,1]{3,2,1,0:T(8,128)S(1)}, f32[8,4,16,1]{3,2,1,0:T(8,128)S(1)}, u32[]{:S(2)}, u32[]{:S(2)}) collective-permute-start(f32[8,4,16,1]{3,2,1,0:T(8,128)S(1)} %get-tuple-element.288), channel_id=1, source_target_pairs={{0,1},{2,3},{4,5},{6,7},{8,9},{10,11},{12,13},{14,15},{16,17},{18,... | collective-permute-start | bytes 6152 | tf_op jit(solution)/shard_map/ppermute | solution.py:41
  102.5 9.5 %all-to-all-start.1 = ((f32[32,4,128]{2,1,0:T(4,128)}), f32[32,4,128]{2,1,0:T(4,128)S(1)}, u32[]{:S(2)}, u32[]{:S(2)}) async-start(f32[32,4,128]{2,1,0:T(4,128)} %broadcast_in_dim.131), calls=%async_computation.1 | async-start | bytes 131072 | tf_op jit(solution)/shard_map/all_to_all | solution.py:26
  111.9 9.6 %all-to-all-done.1 = f32[32,4,128]{2,1,0:T(4,128)S(1)} async-done(((f32[32,4,128]{2,1,0:T(4,128)}), f32[32,4,128]{2,1,0:T(4,128)S(1)}, u32[]{:S(2)}, u32[]{:S(2)}) %all-to-all-start.1) | async-done | bytes 65568 | tf_op jit(solution)/shard_map/all_to_all | solution.py:26
  126.7 9.6 %all-to-all-done = bf16[32,8,128]{2,1,0:T(8,128)(2,1)S(1)} async-done(((bf16[32,8,128]{2,1,0:T(8,128)(2,1)}), bf16[32,8,128]{2,1,0:T(8,128)(2,1)S(1)}, u32[]{:S(2)}, u32[]{:S(2)}) %all-to-all-start) | async-done | bytes 65568 | tf_op jit(solution)/shard_map/all_to_all | solution.py:26
  136.3 77.5 %while.28 = (s32[]{:T(128)}, f32[8,1024]{1,0:T(8,128)}, bf16[8,4096]{1,0:T(8,128)(2,1)S(1)}, f32[4,4096]{1,0:T(4,128)S(1)}, f32[4,1024]{1,0:T(4,128)S(1)}, /*ind...) while((s32[]{:T(128)}, f32[8,1024]{1,0:T(8,128)}, ...), condition=%wide.region_1.3_spmd.clone, body=%wide.region_0.2_spmd.clone.sunk | while | flops 15745034 | bytes 135397 | solution.py:127
  136.4 8.9 %convolution_add_fusion.4 = f32[8,1024]{1,0:T(8,128)} fusion(f32[512]{0:T(512)S(1)} %bitcast.107, f32[1024]{0:T(1024)S(1)} %bitcast.97, f32[512]{0:T(512)S(1)} %bitcast.105, f32[1024]{0:T(1024)S(1)} %bitcast.98, f32[512]{0:T(512)S(1)} %bitcast.106, f32[1024]{0:T(1024)S(1)} %bitcast.96, f32[512]{0:T(512)S(1)} %bitcast.104, ...), kind=kOutput, calls=%fused_computation.4.clone.1 | convolution fusion | flops 15745024 | bytes 94213 | tf_op jit(solution)/shard_map/while/body/eval_jaxpr/dot_general | solution.py:125
  145.4 9.7 %convolution_add_fusion.4 = f32[8,1024]{1,0:T(8,128)} fusion(f32[512]{0:T(512)S(1)} %bitcast.107, f32[1024]{0:T(1024)S(1)} %bitcast.97, f32[512]{0:T(512)S(1)} %bitcast.105, f32[1024]{0:T(1024)S(1)} %bitcast.98, f32[512]{0:T(512)S(1)} %bitcast.106, f32[1024]{0:T(1024)S(1)} %bitcast.96, f32[512]{0:T(512)S(1)} %bitcast.104, ...), kind=kOutput, calls=%fused_computation.4.clone.1 | convolution fusion | flops 15745024 | bytes 94213 | tf_op jit(solution)/shard_map/while/body/eval_jaxpr/dot_general | solution.py:125
  155.2 9.7 %convolution_add_fusion.4 = f32[8,1024]{1,0:T(8,128)} fusion(f32[512]{0:T(512)S(1)} %bitcast.107, f32[1024]{0:T(1024)S(1)} %bitcast.97, f32[512]{0:T(512)S(1)} %bitcast.105, f32[1024]{0:T(1024)S(1)} %bitcast.98, f32[512]{0:T(512)S(1)} %bitcast.106, f32[1024]{0:T(1024)S(1)} %bitcast.96, f32[512]{0:T(512)S(1)} %bitcast.104, ...), kind=kOutput, calls=%fused_computation.4.clone.1 | convolution fusion | flops 15745024 | bytes 94213 | tf_op jit(solution)/shard_map/while/body/eval_jaxpr/dot_general | solution.py:125
  165.0 9.7 %convolution_add_fusion.4 = f32[8,1024]{1,0:T(8,128)} fusion(f32[512]{0:T(512)S(1)} %bitcast.107, f32[1024]{0:T(1024)S(1)} %bitcast.97, f32[512]{0:T(512)S(1)} %bitcast.105, f32[1024]{0:T(1024)S(1)} %bitcast.98, f32[512]{0:T(512)S(1)} %bitcast.106, f32[1024]{0:T(1024)S(1)} %bitcast.96, f32[512]{0:T(512)S(1)} %bitcast.104, ...), kind=kOutput, calls=%fused_computation.4.clone.1 | convolution fusion | flops 15745024 | bytes 94213 | tf_op jit(solution)/shard_map/while/body/eval_jaxpr/dot_general | solution.py:125
  174.8 9.7 %convolution_add_fusion.4 = f32[8,1024]{1,0:T(8,128)} fusion(f32[512]{0:T(512)S(1)} %bitcast.107, f32[1024]{0:T(1024)S(1)} %bitcast.97, f32[512]{0:T(512)S(1)} %bitcast.105, f32[1024]{0:T(1024)S(1)} %bitcast.98, f32[512]{0:T(512)S(1)} %bitcast.106, f32[1024]{0:T(1024)S(1)} %bitcast.96, f32[512]{0:T(512)S(1)} %bitcast.104, ...), kind=kOutput, calls=%fused_computation.4.clone.1 | convolution fusion | flops 15745024 | bytes 94213 | tf_op jit(solution)/shard_map/while/body/eval_jaxpr/dot_general | solution.py:125
  184.6 9.7 %convolution_add_fusion.4 = f32[8,1024]{1,0:T(8,128)} fusion(f32[512]{0:T(512)S(1)} %bitcast.107, f32[1024]{0:T(1024)S(1)} %bitcast.97, f32[512]{0:T(512)S(1)} %bitcast.105, f32[1024]{0:T(1024)S(1)} %bitcast.98, f32[512]{0:T(512)S(1)} %bitcast.106, f32[1024]{0:T(1024)S(1)} %bitcast.96, f32[512]{0:T(512)S(1)} %bitcast.104, ...), kind=kOutput, calls=%fused_computation.4.clone.1 | convolution fusion | flops 15745024 | bytes 94213 | tf_op jit(solution)/shard_map/while/body/eval_jaxpr/dot_general | solution.py:125
  194.3 9.7 %convolution_add_fusion.4 = f32[8,1024]{1,0:T(8,128)} fusion(f32[512]{0:T(512)S(1)} %bitcast.107, f32[1024]{0:T(1024)S(1)} %bitcast.97, f32[512]{0:T(512)S(1)} %bitcast.105, f32[1024]{0:T(1024)S(1)} %bitcast.98, f32[512]{0:T(512)S(1)} %bitcast.106, f32[1024]{0:T(1024)S(1)} %bitcast.96, f32[512]{0:T(512)S(1)} %bitcast.104, ...), kind=kOutput, calls=%fused_computation.4.clone.1 | convolution fusion | flops 15745024 | bytes 94213 | tf_op jit(solution)/shard_map/while/body/eval_jaxpr/dot_general | solution.py:125
  204.1 9.7 %convolution_add_fusion.4 = f32[8,1024]{1,0:T(8,128)} fusion(f32[512]{0:T(512)S(1)} %bitcast.107, f32[1024]{0:T(1024)S(1)} %bitcast.97, f32[512]{0:T(512)S(1)} %bitcast.105, f32[1024]{0:T(1024)S(1)} %bitcast.98, f32[512]{0:T(512)S(1)} %bitcast.106, f32[1024]{0:T(1024)S(1)} %bitcast.96, f32[512]{0:T(512)S(1)} %bitcast.104, ...), kind=kOutput, calls=%fused_computation.4.clone.1 | convolution fusion | flops 15745024 | bytes 94213 | tf_op jit(solution)/shard_map/while/body/eval_jaxpr/dot_general | solution.py:125
  213.8 10.5 %all-to-all-start.3 = ((f32[8,8,128]{2,1,0:T(8,128)}), f32[8,8,128]{2,1,0:T(8,128)S(1)}, u32[]{:S(2)}, u32[]{:S(2)}) async-start(f32[8,8,128]{2,1,0:T(8,128)} %bitcast.26), calls=%async_computation.3 | async-start | bytes 65536 | tf_op jit(solution)/shard_map/all_to_all | solution.py:60
  225.7 5.5 %collective-permute-start.23 = (f32[8,4,16,1]{3,2,1,0:T(8,128)S(1)}, f32[8,4,16,1]{3,2,1,0:T(8,128)S(1)}, u32[]{:S(2)}, u32[]{:S(2)}) collective-permute-start(f32[8,4,16,1]{3,2,1,0:T(8,128)S(1)} %get-tuple-element.282), channel_id=1, source_target_pairs={{0,1},{2,3},{4,5},{6,7},{8,9},{10,11},{12,13},{14,15},{16,17},{18,... | collective-permute-start | bytes 6152 | tf_op jit(solution)/shard_map/ppermute | solution.py:41
  256.4 5.7 %collective-permute-start.29 = (f32[8,4,16,1]{3,2,1,0:T(8,128)S(1)}, f32[8,4,16,1]{3,2,1,0:T(8,128)S(1)}, u32[]{:S(2)}, u32[]{:S(2)}) collective-permute-start(f32[8,4,16,1]{3,2,1,0:T(8,128)S(1)} %get-tuple-element.276), channel_id=1, source_target_pairs={{0,1},{2,3},{4,5},{6,7},{8,9},{10,11},{12,13},{14,15},{16,17},{18,... | collective-permute-start | bytes 6152 | tf_op jit(solution)/shard_map/ppermute | solution.py:41
  280.7 5.5 %collective-permute-start.35 = (f32[8,4,16,1]{3,2,1,0:T(8,128)S(1)}, f32[8,4,16,1]{3,2,1,0:T(8,128)S(1)}, u32[]{:S(2)}, u32[]{:S(2)}) collective-permute-start(f32[8,4,16,1]{3,2,1,0:T(8,128)S(1)} %get-tuple-element.270), channel_id=1, source_target_pairs={{0,1},{2,3},{4,5},{6,7},{8,9},{10,11},{12,13},{14,15},{16,17},{18,... | collective-permute-start | bytes 6152 | tf_op jit(solution)/shard_map/ppermute | solution.py:41
  298.6 7.0 %all-to-all-start.4 = ((bf16[32,8,128]{2,1,0:T(8,128)(2,1)}), bf16[32,8,128]{2,1,0:T(8,128)(2,1)S(1)}, u32[]{:S(2)}, u32[]{:S(2)}) async-start(bf16[32,8,128]{2,1,0:T(8,128)(2,1)} %broadcast_in_dim.133), calls=%async_computation.4 | async-start | bytes 131072 | tf_op jit(solution)/shard_map/all_to_all | solution.py:26
  305.7 9.6 %all-to-all-done.4 = bf16[32,8,128]{2,1,0:T(8,128)(2,1)S(1)} async-done(((bf16[32,8,128]{2,1,0:T(8,128)(2,1)}), bf16[32,8,128]{2,1,0:T(8,128)(2,1)S(1)}, u32[]{:S(2)}, u32[]{:S(2)}) %all-to-all-start.4) | async-done | bytes 65568 | tf_op jit(solution)/shard_map/all_to_all | solution.py:26
  315.3 67.4 %while.29 = (s32[]{:T(128)}, f32[8,1024]{1,0:T(8,128)S(1)}, bf16[8,4096]{1,0:T(8,128)(2,1)S(1)}, f32[4,4096]{1,0:T(4,128)S(1)}, f32[4,1024]{1,0:T(4,128)S(1)}, /...) while((s32[]{:T(128)}, f32[8,1024]{1,0:T(8,128)S(1)}, ...), condition=%wide.region_5.7_spmd.clone, body=%wide.region_4.6_spmd.clone.sunk | while | flops 15745034 | bytes 135397 | solution.py:127
  315.4 8.3 %convolution_add_fusion.5 = f32[8,1024]{1,0:T(8,128)S(1)} fusion(f32[512]{0:T(512)S(1)} %bitcast.111, f32[1024]{0:T(1024)S(1)} %bitcast.100, f32[512]{0:T(512)S(1)} %bitcast.109, f32[1024]{0:T(1024)S(1)} %bitcast.101, f32[512]{0:T(512)S(1)} %bitcast.110, f32[1024]{0:T(1024)S(1)} %bitcast.99, f32[512]{0:T(512)S(1)} %bitcast.108, ...), kind=kOutput, calls=%fused_computation.21.clone.1 | convolution fusion | flops 15745024 | bytes 94213 | tf_op jit(solution)/shard_map/while/body/eval_jaxpr/dot_general | solution.py:125
  323.8 8.3 %convolution_add_fusion.5 = f32[8,1024]{1,0:T(8,128)S(1)} fusion(f32[512]{0:T(512)S(1)} %bitcast.111, f32[1024]{0:T(1024)S(1)} %bitcast.100, f32[512]{0:T(512)S(1)} %bitcast.109, f32[1024]{0:T(1024)S(1)} %bitcast.101, f32[512]{0:T(512)S(1)} %bitcast.110, f32[1024]{0:T(1024)S(1)} %bitcast.99, f32[512]{0:T(512)S(1)} %bitcast.108, ...), kind=kOutput, calls=%fused_computation.21.clone.1 | convolution fusion | flops 15745024 | bytes 94213 | tf_op jit(solution)/shard_map/while/body/eval_jaxpr/dot_general | solution.py:125
  332.2 8.3 %convolution_add_fusion.5 = f32[8,1024]{1,0:T(8,128)S(1)} fusion(f32[512]{0:T(512)S(1)} %bitcast.111, f32[1024]{0:T(1024)S(1)} %bitcast.100, f32[512]{0:T(512)S(1)} %bitcast.109, f32[1024]{0:T(1024)S(1)} %bitcast.101, f32[512]{0:T(512)S(1)} %bitcast.110, f32[1024]{0:T(1024)S(1)} %bitcast.99, f32[512]{0:T(512)S(1)} %bitcast.108, ...), kind=kOutput, calls=%fused_computation.21.clone.1 | convolution fusion | flops 15745024 | bytes 94213 | tf_op jit(solution)/shard_map/while/body/eval_jaxpr/dot_general | solution.py:125
  340.7 8.3 %convolution_add_fusion.5 = f32[8,1024]{1,0:T(8,128)S(1)} fusion(f32[512]{0:T(512)S(1)} %bitcast.111, f32[1024]{0:T(1024)S(1)} %bitcast.100, f32[512]{0:T(512)S(1)} %bitcast.109, f32[1024]{0:T(1024)S(1)} %bitcast.101, f32[512]{0:T(512)S(1)} %bitcast.110, f32[1024]{0:T(1024)S(1)} %bitcast.99, f32[512]{0:T(512)S(1)} %bitcast.108, ...), kind=kOutput, calls=%fused_computation.21.clone.1 | convolution fusion | flops 15745024 | bytes 94213 | tf_op jit(solution)/shard_map/while/body/eval_jaxpr/dot_general | solution.py:125
  349.1 8.3 %convolution_add_fusion.5 = f32[8,1024]{1,0:T(8,128)S(1)} fusion(f32[512]{0:T(512)S(1)} %bitcast.111, f32[1024]{0:T(1024)S(1)} %bitcast.100, f32[512]{0:T(512)S(1)} %bitcast.109, f32[1024]{0:T(1024)S(1)} %bitcast.101, f32[512]{0:T(512)S(1)} %bitcast.110, f32[1024]{0:T(1024)S(1)} %bitcast.99, f32[512]{0:T(512)S(1)} %bitcast.108, ...), kind=kOutput, calls=%fused_computation.21.clone.1 | convolution fusion | flops 15745024 | bytes 94213 | tf_op jit(solution)/shard_map/while/body/eval_jaxpr/dot_general | solution.py:125
  357.5 8.3 %convolution_add_fusion.5 = f32[8,1024]{1,0:T(8,128)S(1)} fusion(f32[512]{0:T(512)S(1)} %bitcast.111, f32[1024]{0:T(1024)S(1)} %bitcast.100, f32[512]{0:T(512)S(1)} %bitcast.109, f32[1024]{0:T(1024)S(1)} %bitcast.101, f32[512]{0:T(512)S(1)} %bitcast.110, f32[1024]{0:T(1024)S(1)} %bitcast.99, f32[512]{0:T(512)S(1)} %bitcast.108, ...), kind=kOutput, calls=%fused_computation.21.clone.1 | convolution fusion | flops 15745024 | bytes 94213 | tf_op jit(solution)/shard_map/while/body/eval_jaxpr/dot_general | solution.py:125
  365.9 8.3 %convolution_add_fusion.5 = f32[8,1024]{1,0:T(8,128)S(1)} fusion(f32[512]{0:T(512)S(1)} %bitcast.111, f32[1024]{0:T(1024)S(1)} %bitcast.100, f32[512]{0:T(512)S(1)} %bitcast.109, f32[1024]{0:T(1024)S(1)} %bitcast.101, f32[512]{0:T(512)S(1)} %bitcast.110, f32[1024]{0:T(1024)S(1)} %bitcast.99, f32[512]{0:T(512)S(1)} %bitcast.108, ...), kind=kOutput, calls=%fused_computation.21.clone.1 | convolution fusion | flops 15745024 | bytes 94213 | tf_op jit(solution)/shard_map/while/body/eval_jaxpr/dot_general | solution.py:125
  374.4 8.3 %convolution_add_fusion.5 = f32[8,1024]{1,0:T(8,128)S(1)} fusion(f32[512]{0:T(512)S(1)} %bitcast.111, f32[1024]{0:T(1024)S(1)} %bitcast.100, f32[512]{0:T(512)S(1)} %bitcast.109, f32[1024]{0:T(1024)S(1)} %bitcast.101, f32[512]{0:T(512)S(1)} %bitcast.110, f32[1024]{0:T(1024)S(1)} %bitcast.99, f32[512]{0:T(512)S(1)} %bitcast.108, ...), kind=kOutput, calls=%fused_computation.21.clone.1 | convolution fusion | flops 15745024 | bytes 94213 | tf_op jit(solution)/shard_map/while/body/eval_jaxpr/dot_general | solution.py:125
  382.7 13.0 %all_to_all.30 = f32[8,8,128]{2,1,0:T(8,128)S(1)} all-to-all(f32[8,8,128]{2,1,0:T(8,128)S(1)} %bitcast.112), channel_id=1, replica_groups=mesh['row'=16,'col'=8,'gz'=2] {'col'}, dimensions={0} | all-to-all | bytes 65536 | tf_op jit(solution)/shard_map/all_to_all | solution.py:60
  (175 shorter events, 137.4 us)
Async XLA Ops:
  1.6 42.5 %collective-permute-start.1 = (f32[8,1,16,128]{3,2,1,0:T(8,128)S(1)}, f32[8,1,16,128]{3,2,1,0:T(8,128)S(1)}, u32[]{:S(2)}, u32[]{:S(2)}) collective-permute-start(f32[8,1,16,128]{3,2,1,0:T(8,128)S(1)} %get-tuple-element.304), channel_id=1, source_target_pairs={{0,16},{16,32},{32,48},{48,64},{64,80},{80,96},{96,112},{112,128},... | collective-permute-start | bytes 196616 | tf_op jit(solution)/shard_map/ppermute | solution.py:41
  6.5 38.6 %collective-permute-start = (f32[8,1,16,128]{3,2,1,0:T(8,128)S(1)}, f32[8,1,16,128]{3,2,1,0:T(8,128)S(1)}, u32[]{:S(2)}, u32[]{:S(2)}) collective-permute-start(f32[8,1,16,128]{3,2,1,0:T(8,128)S(1)} %get-tuple-element.303), channel_id=1, source_target_pairs={{16,0},{32,16},{48,32},{64,48},{80,64},{96,80},{112,96},{128,112},... | collective-permute-start | bytes 196616 | tf_op jit(solution)/shard_map/ppermute | solution.py:42
  9.6 35.5 %collective-permute-start.4 = (f32[8,4,16,1]{3,2,1,0:T(8,128)S(1)}, f32[8,4,16,1]{3,2,1,0:T(8,128)S(1)}, u32[]{:S(2)}, u32[]{:S(2)}) collective-permute-start(f32[8,4,16,1]{3,2,1,0:T(8,128)S(1)} %get-tuple-element.299), channel_id=1, source_target_pairs={{1,0},{3,2},{5,4},{7,6},{9,8},{11,10},{13,12},{15,14},{17,16},{19,... | collective-permute-start | bytes 6152 | tf_op jit(solution)/shard_map/ppermute | solution.py:42
  11.9 26.6 %collective-permute-start.2 = (f32[8,4,1,128]{3,2,1,0:T(1,128)S(1)}, f32[8,4,1,128]{3,2,1,0:T(1,128)S(1)}, u32[]{:S(2)}, u32[]{:S(2)}) collective-permute-start(f32[8,4,1,128]{3,2,1,0:T(1,128)S(1)} %get-tuple-element.302), channel_id=1, source_target_pairs={{2,0},{4,2},{6,4},{8,6},{10,8},{12,10},{14,12},{3,1},{5,3},{7,5},{... | collective-permute-start | bytes 49160 | tf_op jit(solution)/shard_map/ppermute | solution.py:42
  13.2 30.9 %collective-permute-start.3 = (f32[8,4,1,128]{3,2,1,0:T(1,128)S(1)}, f32[8,4,1,128]{3,2,1,0:T(1,128)S(1)}, u32[]{:S(2)}, u32[]{:S(2)}) collective-permute-start(f32[8,4,1,128]{3,2,1,0:T(1,128)S(1)} %get-tuple-element.301), channel_id=1, source_target_pairs={{0,2},{2,4},{4,6},{6,8},{8,10},{10,12},{12,14},{1,3},{3,5},{5,7},{... | collective-permute-start | bytes 49160 | tf_op jit(solution)/shard_map/ppermute | solution.py:41
  18.5 83.3 %all-to-all-start.2 = ((f32[8,4,128]{2,1,0:T(4,128)}), f32[8,4,128]{2,1,0:T(4,128)S(1)}, u32[]{:S(2)}, u32[]{:S(2)}) async-start(f32[8,4,128]{2,1,0:T(4,128)} %broadcast_in_dim.132), calls=%async_computation.2 | async-start | bytes 32768 | tf_op jit(solution)/shard_map/all_to_all | solution.py:26
  50.0 15.2 %collective-permute-start.8 = (f32[8,4,1,128]{3,2,1,0:T(1,128)S(1)}, f32[8,4,1,128]{3,2,1,0:T(1,128)S(1)}, u32[]{:S(2)}, u32[]{:S(2)}) collective-permute-start(f32[8,4,1,128]{3,2,1,0:T(1,128)S(1)} %get-tuple-element.298), channel_id=1, source_target_pairs={{2,0},{4,2},{6,4},{8,6},{10,8},{12,10},{14,12},{3,1},{5,3},{7,5},{... | collective-permute-start | bytes 49160 | tf_op jit(solution)/shard_map/ppermute | solution.py:42
  51.3 19.0 %collective-permute-start.10 = (f32[8,4,16,1]{3,2,1,0:T(8,128)S(1)}, f32[8,4,16,1]{3,2,1,0:T(8,128)S(1)}, u32[]{:S(2)}, u32[]{:S(2)}) collective-permute-start(f32[8,4,16,1]{3,2,1,0:T(8,128)S(1)} %get-tuple-element.293), channel_id=1, source_target_pairs={{1,0},{3,2},{5,4},{7,6},{9,8},{11,10},{13,12},{15,14},{17,16},{19,... | collective-permute-start | bytes 6152 | tf_op jit(solution)/shard_map/ppermute | solution.py:42
  52.6 17.8 %collective-permute-start.11 = (f32[8,4,16,1]{3,2,1,0:T(8,128)S(1)}, f32[8,4,16,1]{3,2,1,0:T(8,128)S(1)}, u32[]{:S(2)}, u32[]{:S(2)}) collective-permute-start(f32[8,4,16,1]{3,2,1,0:T(8,128)S(1)} %get-tuple-element.294), channel_id=1, source_target_pairs={{0,1},{2,3},{4,5},{6,7},{8,9},{10,11},{12,13},{14,15},{16,17},{18,... | collective-permute-start | bytes 6152 | tf_op jit(solution)/shard_map/ppermute | solution.py:41
  58.1 12.2 %collective-permute-start.6 = (f32[8,1,16,128]{3,2,1,0:T(8,128)S(1)}, f32[8,1,16,128]{3,2,1,0:T(8,128)S(1)}, u32[]{:S(2)}, u32[]{:S(2)}) collective-permute-start(f32[8,1,16,128]{3,2,1,0:T(8,128)S(1)} %get-tuple-element.296), channel_id=1, source_target_pairs={{16,0},{32,16},{48,32},{64,48},{80,64},{96,80},{112,96},{128,112},... | collective-permute-start | bytes 196616 | tf_op jit(solution)/shard_map/ppermute | solution.py:42
  70.9 13.9 %collective-permute-start.14 = (f32[8,4,1,128]{3,2,1,0:T(1,128)S(1)}, f32[8,4,1,128]{3,2,1,0:T(1,128)S(1)}, u32[]{:S(2)}, u32[]{:S(2)}) collective-permute-start(f32[8,4,1,128]{3,2,1,0:T(1,128)S(1)} %get-tuple-element.292), channel_id=1, source_target_pairs={{2,0},{4,2},{6,4},{8,6},{10,8},{12,10},{14,12},{3,1},{5,3},{7,5},{... | collective-permute-start | bytes 49160 | tf_op jit(solution)/shard_map/ppermute | solution.py:42
  72.2 18.0 %collective-permute-start.16 = (f32[8,4,16,1]{3,2,1,0:T(8,128)S(1)}, f32[8,4,16,1]{3,2,1,0:T(8,128)S(1)}, u32[]{:S(2)}, u32[]{:S(2)}) collective-permute-start(f32[8,4,16,1]{3,2,1,0:T(8,128)S(1)} %get-tuple-element.287), channel_id=1, source_target_pairs={{1,0},{3,2},{5,4},{7,6},{9,8},{11,10},{13,12},{15,14},{17,16},{19,... | collective-permute-start | bytes 6152 | tf_op jit(solution)/shard_map/ppermute | solution.py:42
  73.5 16.8 %collective-permute-start.17 = (f32[8,4,16,1]{3,2,1,0:T(8,128)S(1)}, f32[8,4,16,1]{3,2,1,0:T(8,128)S(1)}, u32[]{:S(2)}, u32[]{:S(2)}) collective-permute-start(f32[8,4,16,1]{3,2,1,0:T(8,128)S(1)} %get-tuple-element.288), channel_id=1, source_target_pairs={{0,1},{2,3},{4,5},{6,7},{8,9},{10,11},{12,13},{14,15},{16,17},{18,... | collective-permute-start | bytes 6152 | tf_op jit(solution)/shard_map/ppermute | solution.py:41
  79.0 11.2 %collective-permute-start.12 = (f32[8,1,16,128]{3,2,1,0:T(8,128)S(1)}, f32[8,1,16,128]{3,2,1,0:T(8,128)S(1)}, u32[]{:S(2)}, u32[]{:S(2)}) collective-permute-start(f32[8,1,16,128]{3,2,1,0:T(8,128)S(1)} %get-tuple-element.290), channel_id=1, source_target_pairs={{16,0},{32,16},{48,32},{64,48},{80,64},{96,80},{112,96},{128,112},... | collective-permute-start | bytes 196616 | tf_op jit(solution)/shard_map/ppermute | solution.py:42
  96.2 138.6 %collective-permute-start.20 = (f32[8,4,1,128]{3,2,1,0:T(1,128)S(1)}, f32[8,4,1,128]{3,2,1,0:T(1,128)S(1)}, u32[]{:S(2)}, u32[]{:S(2)}) collective-permute-start(f32[8,4,1,128]{3,2,1,0:T(1,128)S(1)} %get-tuple-element.286), channel_id=1, source_target_pairs={{2,0},{4,2},{6,4},{8,6},{10,8},{12,10},{14,12},{3,1},{5,3},{7,5},{... | collective-permute-start | bytes 49160 | tf_op jit(solution)/shard_map/ppermute | solution.py:42
  97.5 139.6 %collective-permute-start.21 = (f32[8,4,1,128]{3,2,1,0:T(1,128)S(1)}, f32[8,4,1,128]{3,2,1,0:T(1,128)S(1)}, u32[]{:S(2)}, u32[]{:S(2)}) collective-permute-start(f32[8,4,1,128]{3,2,1,0:T(1,128)S(1)} %get-tuple-element.285), channel_id=1, source_target_pairs={{0,2},{2,4},{4,6},{6,8},{8,10},{10,12},{12,14},{1,3},{3,5},{5,7},{... | collective-permute-start | bytes 49160 | tf_op jit(solution)/shard_map/ppermute | solution.py:41
  102.5 19.1 %all-to-all-start.1 = ((f32[32,4,128]{2,1,0:T(4,128)}), f32[32,4,128]{2,1,0:T(4,128)S(1)}, u32[]{:S(2)}, u32[]{:S(2)}) async-start(f32[32,4,128]{2,1,0:T(4,128)} %broadcast_in_dim.131), calls=%async_computation.1 | async-start | bytes 131072 | tf_op jit(solution)/shard_map/all_to_all | solution.py:26
  122.2 14.1 %all-to-all-start = ((bf16[32,8,128]{2,1,0:T(8,128)(2,1)}), bf16[32,8,128]{2,1,0:T(8,128)(2,1)S(1)}, u32[]{:S(2)}, u32[]{:S(2)}) async-start(bf16[32,8,128]{2,1,0:T(8,128)(2,1)} %broadcast_in_dim.130), calls=%async_computation | async-start | bytes 131072 | tf_op jit(solution)/shard_map/all_to_all | solution.py:26
  213.8 23.3 %all-to-all-start.3 = ((f32[8,8,128]{2,1,0:T(8,128)}), f32[8,8,128]{2,1,0:T(8,128)S(1)}, u32[]{:S(2)}, u32[]{:S(2)}) async-start(f32[8,8,128]{2,1,0:T(8,128)} %bitcast.26), calls=%async_computation.3 | async-start | bytes 65536 | tf_op jit(solution)/shard_map/all_to_all | solution.py:60
  224.4 18.9 %collective-permute-start.22 = (f32[8,4,16,1]{3,2,1,0:T(8,128)S(1)}, f32[8,4,16,1]{3,2,1,0:T(8,128)S(1)}, u32[]{:S(2)}, u32[]{:S(2)}) collective-permute-start(f32[8,4,16,1]{3,2,1,0:T(8,128)S(1)} %get-tuple-element.281), channel_id=1, source_target_pairs={{1,0},{3,2},{5,4},{7,6},{9,8},{11,10},{13,12},{15,14},{17,16},{19,... | collective-permute-start | bytes 6152 | tf_op jit(solution)/shard_map/ppermute | solution.py:42
  225.7 17.6 %collective-permute-start.23 = (f32[8,4,16,1]{3,2,1,0:T(8,128)S(1)}, f32[8,4,16,1]{3,2,1,0:T(8,128)S(1)}, u32[]{:S(2)}, u32[]{:S(2)}) collective-permute-start(f32[8,4,16,1]{3,2,1,0:T(8,128)S(1)} %get-tuple-element.282), channel_id=1, source_target_pairs={{0,1},{2,3},{4,5},{6,7},{8,9},{10,11},{12,13},{14,15},{16,17},{18,... | collective-permute-start | bytes 6152 | tf_op jit(solution)/shard_map/ppermute | solution.py:41
  231.2 12.1 %collective-permute-start.18 = (f32[8,1,16,128]{3,2,1,0:T(8,128)S(1)}, f32[8,1,16,128]{3,2,1,0:T(8,128)S(1)}, u32[]{:S(2)}, u32[]{:S(2)}) collective-permute-start(f32[8,1,16,128]{3,2,1,0:T(8,128)S(1)} %get-tuple-element.284), channel_id=1, source_target_pairs={{16,0},{32,16},{48,32},{64,48},{80,64},{96,80},{112,96},{128,112},... | collective-permute-start | bytes 196616 | tf_op jit(solution)/shard_map/ppermute | solution.py:42
  243.8 24.2 %collective-permute-start.24 = (f32[8,1,16,128]{3,2,1,0:T(8,128)S(1)}, f32[8,1,16,128]{3,2,1,0:T(8,128)S(1)}, u32[]{:S(2)}, u32[]{:S(2)}) collective-permute-start(f32[8,1,16,128]{3,2,1,0:T(8,128)S(1)} %get-tuple-element.278), channel_id=1, source_target_pairs={{16,0},{32,16},{48,32},{64,48},{80,64},{96,80},{112,96},{128,112},... | collective-permute-start | bytes 196616 | tf_op jit(solution)/shard_map/ppermute | solution.py:42
  245.8 22.2 %collective-permute-start.25 = (f32[8,1,16,128]{3,2,1,0:T(8,128)S(1)}, f32[8,1,16,128]{3,2,1,0:T(8,128)S(1)}, u32[]{:S(2)}, u32[]{:S(2)}) collective-permute-start(f32[8,1,16,128]{3,2,1,0:T(8,128)S(1)} %get-tuple-element.277), channel_id=1, source_target_pairs={{0,16},{16,32},{32,48},{48,64},{64,80},{80,96},{96,112},{112,128},... | collective-permute-start | bytes 196616 | tf_op jit(solution)/shard_map/ppermute | solution.py:41
  250.6 11.5 %collective-permute-start.27 = (f32[8,4,1,128]{3,2,1,0:T(1,128)S(1)}, f32[8,4,1,128]{3,2,1,0:T(1,128)S(1)}, u32[]{:S(2)}, u32[]{:S(2)}) collective-permute-start(f32[8,4,1,128]{3,2,1,0:T(1,128)S(1)} %get-tuple-element.279), channel_id=1, source_target_pairs={{0,2},{2,4},{4,6},{6,8},{8,10},{10,12},{12,14},{1,3},{3,5},{5,7},{... | collective-permute-start | bytes 49160 | tf_op jit(solution)/shard_map/ppermute | solution.py:41
  255.1 11.1 %collective-permute-start.28 = (f32[8,4,16,1]{3,2,1,0:T(8,128)S(1)}, f32[8,4,16,1]{3,2,1,0:T(8,128)S(1)}, u32[]{:S(2)}, u32[]{:S(2)}) collective-permute-start(f32[8,4,16,1]{3,2,1,0:T(8,128)S(1)} %get-tuple-element.275), channel_id=1, source_target_pairs={{1,0},{3,2},{5,4},{7,6},{9,8},{11,10},{13,12},{15,14},{17,16},{19,... | collective-permute-start | bytes 6152 | tf_op jit(solution)/shard_map/ppermute | solution.py:42
  256.4 11.6 %collective-permute-start.29 = (f32[8,4,16,1]{3,2,1,0:T(8,128)S(1)}, f32[8,4,16,1]{3,2,1,0:T(8,128)S(1)}, u32[]{:S(2)}, u32[]{:S(2)}) collective-permute-start(f32[8,4,16,1]{3,2,1,0:T(8,128)S(1)} %get-tuple-element.276), channel_id=1, source_target_pairs={{0,1},{2,3},{4,5},{6,7},{8,9},{10,11},{12,13},{14,15},{16,17},{18,... | collective-permute-start | bytes 6152 | tf_op jit(solution)/shard_map/ppermute | solution.py:41
  268.4 23.6 %collective-permute-start.30 = (f32[8,1,16,128]{3,2,1,0:T(8,128)S(1)}, f32[8,1,16,128]{3,2,1,0:T(8,128)S(1)}, u32[]{:S(2)}, u32[]{:S(2)}) collective-permute-start(f32[8,1,16,128]{3,2,1,0:T(8,128)S(1)} %get-tuple-element.272), channel_id=1, source_target_pairs={{16,0},{32,16},{48,32},{64,48},{80,64},{96,80},{112,96},{128,112},... | collective-permute-start | bytes 196616 | tf_op jit(solution)/shard_map/ppermute | solution.py:42
  270.6 21.4 %collective-permute-start.31 = (f32[8,1,16,128]{3,2,1,0:T(8,128)S(1)}, f32[8,1,16,128]{3,2,1,0:T(8,128)S(1)}, u32[]{:S(2)}, u32[]{:S(2)}) collective-permute-start(f32[8,1,16,128]{3,2,1,0:T(8,128)S(1)} %get-tuple-element.271), channel_id=1, source_target_pairs={{0,16},{16,32},{32,48},{48,64},{64,80},{80,96},{96,112},{112,128},... | collective-permute-start | bytes 196616 | tf_op jit(solution)/shard_map/ppermute | solution.py:41
  279.4 12.0 %collective-permute-start.34 = (f32[8,4,16,1]{3,2,1,0:T(8,128)S(1)}, f32[8,4,16,1]{3,2,1,0:T(8,128)S(1)}, u32[]{:S(2)}, u32[]{:S(2)}) collective-permute-start(f32[8,4,16,1]{3,2,1,0:T(8,128)S(1)} %get-tuple-element.269), channel_id=1, source_target_pairs={{1,0},{3,2},{5,4},{7,6},{9,8},{11,10},{13,12},{15,14},{17,16},{19,... | collective-permute-start | bytes 6152 | tf_op jit(solution)/shard_map/ppermute | solution.py:42
  280.7 11.3 %collective-permute-start.35 = (f32[8,4,16,1]{3,2,1,0:T(8,128)S(1)}, f32[8,4,16,1]{3,2,1,0:T(8,128)S(1)}, u32[]{:S(2)}, u32[]{:S(2)}) collective-permute-start(f32[8,4,16,1]{3,2,1,0:T(8,128)S(1)} %get-tuple-element.270), channel_id=1, source_target_pairs={{0,1},{2,3},{4,5},{6,7},{8,9},{10,11},{12,13},{14,15},{16,17},{18,... | collective-permute-start | bytes 6152 | tf_op jit(solution)/shard_map/ppermute | solution.py:41
  298.6 16.6 %all-to-all-start.4 = ((bf16[32,8,128]{2,1,0:T(8,128)(2,1)}), bf16[32,8,128]{2,1,0:T(8,128)(2,1)S(1)}, u32[]{:S(2)}, u32[]{:S(2)}) async-start(bf16[32,8,128]{2,1,0:T(8,128)(2,1)} %broadcast_in_dim.133), calls=%async_computation.4 | async-start | bytes 131072 | tf_op jit(solution)/shard_map/all_to_all | solution.py:26
  (13 other events, 185.5 us)
where the time goes:
time: 399 us; the launch traced here: 396 us
  starting transfers between devices  148 us (37%)
  matrix products  143 us (36%)
  waiting for transfers between devices  45.7 us (11%)
  local copies, waits for them, and re-layouts  25.9 us (6%)
  other arithmetic  18.2 us (5%)
  blocking collectives  13 us (3%)
    dot_general x16, matrix products, add_block(): return carry + jnp.dot(values, tile, preferred_element_type=jnp.float32)  143 us
    ppermute x18, starting transfers between devices, padded_2(): lax.ppermute(last, axis, up)  81.5 us
    ppermute x18, starting transfers between devices, padded_2(): lax.ppermute(initial, axis, [(b, a) for a, b in up])  29.3 us
    all_to_all x4, waiting for transfers between devices, from_everyone(): return lax.all_to_all(copies, axis, split_axis=0, concat_axis=0, tiled=True)  28.8 us
    all_to_all x4, starting transfers between devices, from_everyone(): return lax.all_to_all(copies, axis, split_axis=0, concat_axis=0, tiled=True)  26.6 us
    all_to_all x1, blocking collectives, sent_and_summed(): blocks = lax.all_to_all(in_blocks(x, dim, devices), axis, 0, 0, tiled=True)  13 us
    add x1, other arithmetic, relax(): diagonal = 6.0 + shift_field  10.9 us
    all_to_all x1, starting transfers between devices, sent_and_summed(): blocks = lax.all_to_all(in_blocks(x, dim, devices), axis, 0, 0, tiled=True)  10.5 us
  transfers between devices with their start and end apart: 41, of which 10 were waited for; matrix products, arithmetic and copies ran while one was open for 28% of the time, Pallas kernels for 0%

commit v1 on v0

v1 whole, which is shorter than its diff:
```python
import math

import jax
import jax.numpy as jnp
from jax import lax
from jax.experimental import pallas as pl
from jax.experimental.pallas import tpu as pltpu
from jax.sharding import PartitionSpec as P

SWEEPS = 3
ROUNDS = 2

relax_weight = 0.8
wave_number = 25.0
soften = 0.05
coupling = 0.5

SINE = (6.2831851600894435, -41.34165503141112, 81.60100407296788, -76.54978228730859, 39.53670602126459)
TURNS = wave_number / (2.0 * math.pi)
ROUNDER = 12582912.0


def tile_kernel(source_ref, target_ref, out_ref, columns):
    bricks, slots = target_ref.shape[0], target_ref.shape[2]
    live = jnp.max(source_ref[0, 4:5, :]).astype(jnp.int32)
    columns[...] = jnp.transpose(source_ref[0])
    steps = (live + 15) // 16

    def fill(step, carry):
        rows = pl.ds(pl.multiple_of(step * 16, 16), 16)
        here = columns[rows, :]
        spread = [jnp.broadcast_to(here[:, d : d + 1], (16, slots)) for d in range(4)]
        for brick in range(bricks):
            square = 1e-30
            for d in range(3):
                delta = target_ref[brick, d : d + 1, :] - spread[d]
                square = square + delta * delta
            turns = square * lax.rsqrt(square)
            whole = (turns + ROUNDER) - ROUNDER
            angle = 0.25 - jnp.abs(turns - whole)
            angle2 = angle * angle
            wave = SINE[4]
            for c in SINE[3::-1]:
                wave = wave * angle2 + c
            below = turns + soften * TURNS
            guess = pl.reciprocal(below, approx=True)
            value = (angle * spread[3]) * (guess * (2.0 - below * guess)) * wave
            out_ref[rows, brick * slots : (brick + 1) * slots] = value.astype(jnp.bfloat16)
        return carry

    lax.fori_loop(0, steps, fill, 0)

    def clear(step, carry):
        rows = pl.ds(pl.multiple_of(step * 16, 16), 16)
        out_ref[rows, :] = jnp.zeros((16, out_ref.shape[1]), jnp.bfloat16)
        return carry

    lax.fori_loop(steps, slots // 16, clear, 0)


def make_tile(sources, targets):
    bricks, rows, slots = sources.shape
    width = targets.shape[0] * slots
    return pl.pallas_call(
        tile_kernel,
        grid=(bricks,),
        in_specs=[
            pl.BlockSpec((1, rows, slots), lambda b: (b, 0, 0)),
            pl.BlockSpec(targets.shape, lambda b: (0, 0, 0)),
        ],
        out_specs=pl.BlockSpec((slots, width), lambda b: (b, 0)),
        out_shape=jax.ShapeDtypeStruct((bricks * slots, width), jnp.bfloat16),
        scratch_shapes=[pltpu.VMEM((slots, rows), jnp.float32)],
        name="tile",
    )(sources, targets)


def product_kernel(density_ref, tile_ref, out_ref, total):
    step = pl.program_id(0)

    @pl.when(step == 0)
    def _():
        total[...] = jnp.zeros_like(total)

    values = jnp.concatenate([density_ref[0], density_ref[1]], axis=1)
    total[...] += jnp.dot(values, tile_ref[...], preferred_element_type=jnp.float32)

    @pl.when(step == pl.num_programs(0) - 1)
    def _():
        slots = out_ref.shape[2]
        for brick in range(out_ref.shape[0]):
            out_ref[brick] = total[:, brick * slots : (brick + 1) * slots]


def products(densities, tile):
    bricks, channels, slots = densities.shape
    width = tile.shape[1]
    return pl.pallas_call(
        product_kernel,
        grid=(bricks // 2,),
        in_specs=[
            pl.BlockSpec((2, channels, slots), lambda b: (b, 0, 0)),
            pl.BlockSpec((2 * slots, width), lambda b: (b, 0)),
        ],
        out_specs=pl.BlockSpec((width // slots, channels, slots), lambda b: (0, 0, 0)),
        out_shape=jax.ShapeDtypeStruct((width // slots, channels, slots), jnp.float32),
        scratch_shapes=[pltpu.VMEM((channels, width), jnp.float32)],
        name="product",
    )(densities, tile)


def from_everyone(x, axis):
    copies = jnp.broadcast_to(x, (lax.axis_size(axis), *x.shape))
    return lax.all_to_all(copies, axis, split_axis=0, concat_axis=0, tiled=True)


def padded_2(x, sides, width):
    edges = {}
    for axis, dim in sides:
        devices, length = (lax.axis_size(axis), x.shape[dim])
        up = [(i, (i + 1) % devices) for i in range(devices - 1)]
        last = lax.slice_in_dim(x, length - width, length, axis=dim)
        initial = lax.slice_in_dim(x, 0, width, axis=dim)
        edges[dim] = (
            lax.ppermute(last, axis, up),
            lax.ppermute(initial, axis, [(b, a) for a, b in up]),
        )
    done = []
    for _, dim in sides:
        low, high = edges[dim]
        around = [(width, width) if d in done else (0, 0) for d in range(x.ndim)]
        x = jnp.concatenate([jnp.pad(low, around), x, jnp.pad(high, around)], axis=dim)
        done.append(dim)
    return x


def neighbours(padded):
    total = padded[:, 2:, 1:-1, 1:-1] + padded[:, :-2, 1:-1, 1:-1]
    total = total + padded[:, 1:-1, 2:, 1:-1] + padded[:, 1:-1, :-2, 1:-1]
    total = total + padded[:, 1:-1, 1:-1, 2:] + padded[:, 1:-1, 1:-1, :-2]
    return total


def relax(state, padded, forcing, shift_field):
    diagonal = 6.0 + shift_field
    residual = forcing - (diagonal * state - neighbours(padded))
    return state + relax_weight * residual / diagonal


def shift_lookup(cell_class, class_shift):
    shift_field = jnp.zeros(cell_class.shape, jnp.float32)
    for level in range(class_shift.shape[0]):
        shift_field = shift_field + jnp.where(cell_class == level, class_shift[level], 0.0)
    return shift_field


def local(
    initial_field, source_term, cell_class, class_shift, surface_cell, live_count, panel_geometry
):
    channels, size_x, size_y, size_z = initial_field.shape
    slots = surface_cell.shape[0]
    panels = slots * lax.axis_size("row") * lax.axis_size("col") * lax.axis_size("gz")
    factor = 1.0 / math.sqrt(panels)
    live_row = jnp.broadcast_to(live_count.astype(jnp.float32)[:, None], (1, slots))
    message = jnp.concatenate(
        [panel_geometry[:3] * TURNS, panel_geometry[3:] * (factor * TURNS), live_row, jnp.zeros((3, slots), jnp.float32)]
    )
    sources = from_everyone(message, "row")
    targets = from_everyone(message, ("col", "gz"))
    tile = make_tile(sources, targets)
    shift_field = shift_lookup(cell_class, class_shift)
    live = (jnp.arange(slots, dtype=jnp.int32) < live_count[0]).astype(jnp.float32)
    state = initial_field
    load = jnp.zeros_like(source_term)
    for round_index in range(ROUNDS):
        forcing = source_term + load
        for sweep_index in range(SWEEPS):
            padded = padded_2(state, (("row", 1), ("col", 2), ("gz", 3)), 1)
            state = relax(state, padded, forcing, shift_field)
        density = (jnp.take(state.reshape(channels, -1), surface_cell, axis=1) * live).astype(
            jnp.bfloat16
        )
        shares = products(from_everyone(density, "row"), tile)
        parts = lax.all_to_all(shares, ("col", "gz"), 0, 0, tiled=True)
        potential = jnp.sum(parts, axis=0) * live
        if round_index + 1 < ROUNDS:
            spread = (
                jnp.zeros((channels, size_x * size_y * size_z), jnp.float32)
                .at[:, surface_cell]
                .add(coupling * potential)
            )
            load = spread.reshape(source_term.shape)
    return (state, potential)


def solution(mesh):
    placed = (
        P(None, "row", "col", "gz"),
        P(None, "row", "col", "gz"),
        P("row", "col", "gz"),
        P(),
        P(("row", "col", "gz")),
        P(("row", "col", "gz")),
        P(None, ("row", "col", "gz")),
    )
    return jax.shard_map(
        local,
        mesh=mesh,
        in_specs=placed,
        out_specs=(P(None, "row", "col", "gz"), P(None, ("row", "col", "gz"))),
        check_vma=False,
    )
```

time: 399 us -> 282 us (0.71)
  matrix products: 143 us -> 0 us
  Pallas kernels: 0 us -> 38.9 us
  waiting for transfers between devices: 45.7 us -> 19.2 us
  blocking collectives: 13 us -> 31.7 us
  starting transfers between devices: 148 us -> 142 us
    dot_general x16 -> x0, matrix products: 143 us -> none  [add_block(): return carry + jnp.dot(values, tile, preferred_element_type=jnp.float32)]
    pallas_call x0 -> x3, Pallas kernels: none -> 38.9 us  [the longest x1 24.7 us: make_tile(): pl.pallas_call(tile_kernel, grid=(bricks,), in_specs=[pl.BlockSpec((1, ro...]
    all_to_all x4 -> x3, waiting for transfers between devices: 28.8 us -> 2.05 us  [from_everyone(): return lax.all_to_all(copies, axis, split_axis=0, concat_axis=0, tiled=True)]
    all_to_all x1 -> x2, blocking collectives: 13 us -> 31.7 us  [the longest x1 18.2 us: local(): parts = lax.all_to_all(shares, ('col', 'gz'), 0, 0, tiled=True)]
    all_to_all x4 -> x3, starting transfers between devices: 26.6 us -> 24.6 us  [from_everyone(): return lax.all_to_all(copies, axis, split_axis=0, concat_axis=0, tiled=True)]
  transfers between devices with their start and end apart: 41 -> 40, of which waited for: 10 -> 7; matrix products, arithmetic and copies ran while one was open for 28% -> 10% of each run, Pallas kernels for 0% -> 11%
where the time goes in v1:
time: 282 us; the launch traced here: 279 us
  starting transfers between devices  142 us (50%)
  Pallas kernels  38.9 us (14%)
  blocking collectives  31.7 us (11%)
  local copies, waits for them, and re-layouts  23.9 us (8%)
  other arithmetic  20.9 us (7%)
  waiting for transfers between devices  19.2 us (7%)
    ppermute x18, starting transfers between devices, padded_2(): lax.ppermute(last, axis, up)  79.4 us
    ppermute x18, starting transfers between devices, padded_2(): lax.ppermute(initial, axis, [(b, a) for a, b in up])  29.8 us
    pallas_call x1, Pallas kernels, make_tile(): pl.pallas_call(tile_kernel, grid=(bricks,), in_specs=[pl.BlockSpec((1, ro...  24.7 us
    all_to_all x3, starting transfers between devices, from_everyone(): return lax.all_to_all(copies, axis, split_axis=0, concat_axis=0, tiled=True)  24.6 us
    all_to_all x1, blocking collectives, local(): parts = lax.all_to_all(shares, ('col', 'gz'), 0, 0, tiled=True)  18.2 us
    pallas_call x2, Pallas kernels, products(): pl.pallas_call(product_kernel, grid=(bricks // 2,), in_specs=[pl.BlockSpe...  14.2 us
    all_to_all x1, blocking collectives, from_everyone(): return lax.all_to_all(copies, axis, split_axis=0, concat_axis=0, tiled=True)  13.6 us
    add x1, other arithmetic, relax(): diagonal = 6.0 + shift_field  10.8 us
  transfers between devices with their start and end apart: 40, of which 7 were waited for; matrix products, arithmetic and copies ran while one was open for 10% of the time, Pallas kernels for 11%

profile of v1, /device:TPU:1, one launch (start us, length us, event | category | flops | bytes accessed | tf_op | source)
XLA Modules:
  0.0 278.9 jit_solution(5347396609739507393)
XLA Ops:
  1.6 4.9 %collective-permute-start.1 = (f32[8,1,16,128]{3,2,1,0:T(8,128)S(1)}, f32[8,1,16,128]{3,2,1,0:T(8,128)S(1)}, u32[]{:S(2)}, u32[]{:S(2)}) collective-permute-start(f32[8,1,16,128]{3,2,1,0:T(8,128)S(1)} %get-tuple-element.44), channel_id=1, source_target_pairs={{0,16},{16,32},{32,48},{48,64},{64,80},{80,96},{96,112},{112,128},... | collective-permute-start | bytes 196616 | tf_op jit(solution)/shard_map/ppermute | solution.py:125
  13.2 4.0 %collective-permute-start.3 = (f32[8,4,1,128]{3,2,1,0:T(1,128)S(1)}, f32[8,4,1,128]{3,2,1,0:T(1,128)S(1)}, u32[]{:S(2)}, u32[]{:S(2)}) collective-permute-start(f32[8,4,1,128]{3,2,1,0:T(1,128)S(1)} %get-tuple-element.41), channel_id=1, source_target_pairs={{0,2},{2,4},{4,6},{6,8},{8,10},{10,12},{12,14},{1,3},{3,5},{5,7},{... | collective-permute-start | bytes 49160 | tf_op jit(solution)/shard_map/ppermute | solution.py:125
  20.1 9.3 %all-to-all-start.2 = ((f32[16,8,128]{2,1,0:T(8,128)}), f32[16,8,128]{2,1,0:T(8,128)S(1)}, u32[]{:S(2)}, u32[]{:S(2)}) async-start(f32[16,8,128]{2,1,0:T(8,128)} %broadcast_in_dim.143), calls=%async_computation.2 | async-start | bytes 131072 | tf_op jit(solution)/shard_map/all_to_all | solution.py:114
  32.0 10.8 %add_add_fusion = f32[4,16,128]{2,1,0:T(8,128)S(1)} fusion(s32[4,16,128]{2,1,0:T(8,128)} %param.11, f32[]{:T(128)} %bitcast.15, f32[]{:T(128)} %bitcast.14, f32[]{:T(128)} %bitcast.13, f32[]{:T(128)} %bitcast.12, f32[]{:T(128)} %bitcast.11, f32[]{:T(128)} %bitcast.10, f32[]{:T(128)} %bitcast.9, f32[]{:T(128)} %bitcast.8, f32[]{:T(128)} %bitcast.7, ...), kind=kLoop, calls=%fused_computation.179 | loop fusion | flops 393216 | bytes 65600 | tf_op jit(solution)/shard_map/add | solution.py:145
  43.4 4.8 %collective-permute-start.5 = (f32[8,4,16,1]{3,2,1,0:T(8,128)S(1)}, f32[8,4,16,1]{3,2,1,0:T(8,128)S(1)}, u32[]{:S(2)}, u32[]{:S(2)}) collective-permute-start(f32[8,4,16,1]{3,2,1,0:T(8,128)S(1)} %get-tuple-element.40), channel_id=1, source_target_pairs={{0,1},{2,3},{4,5},{6,7},{8,9},{10,11},{12,13},{14,15},{16,17},{18,... | collective-permute-start | bytes 6152 | tf_op jit(solution)/shard_map/ppermute | solution.py:125
  49.3 4.5 %collective-permute-done.5 = f32[8,4,16,1]{3,2,1,0:T(8,128)S(1)} collective-permute-done((f32[8,4,16,1]{3,2,1,0:T(8,128)S(1)}, f32[8,4,16,1]{3,2,1,0:T(8,128)S(1)}, u32[]{:S(2)}, u32[]{:S(2)}) %collective-permute-start.5) | collective-permute-done | bytes 2080 | tf_op jit(solution)/shard_map/ppermute | solution.py:125
  58.2 5.5 %collective-permute-start.11 = (f32[8,4,16,1]{3,2,1,0:T(8,128)S(1)}, f32[8,4,16,1]{3,2,1,0:T(8,128)S(1)}, u32[]{:S(2)}, u32[]{:S(2)}) collective-permute-start(f32[8,4,16,1]{3,2,1,0:T(8,128)S(1)} %get-tuple-element.34), channel_id=1, source_target_pairs={{0,1},{2,3},{4,5},{6,7},{8,9},{10,11},{12,13},{14,15},{16,17},{18,... | collective-permute-start | bytes 6152 | tf_op jit(solution)/shard_map/ppermute | solution.py:125
  66.2 4.3 %collective-permute-start.7 = (f32[8,1,16,128]{3,2,1,0:T(8,128)S(1)}, f32[8,1,16,128]{3,2,1,0:T(8,128)S(1)}, u32[]{:S(2)}, u32[]{:S(2)}) collective-permute-start(f32[8,1,16,128]{3,2,1,0:T(8,128)S(1)} %get-tuple-element.35), channel_id=1, source_target_pairs={{0,16},{16,32},{32,48},{48,64},{64,80},{80,96},{96,112},{112,128},... | collective-permute-start | bytes 196616 | tf_op jit(solution)/shard_map/ppermute | solution.py:125
  70.5 4.3 %collective-permute-start.9 = (f32[8,4,1,128]{3,2,1,0:T(1,128)S(1)}, f32[8,4,1,128]{3,2,1,0:T(1,128)S(1)}, u32[]{:S(2)}, u32[]{:S(2)}) collective-permute-start(f32[8,4,1,128]{3,2,1,0:T(1,128)S(1)} %get-tuple-element.37), channel_id=1, source_target_pairs={{0,2},{2,4},{4,6},{6,8},{8,10},{10,12},{12,14},{1,3},{3,5},{5,7},{... | collective-permute-start | bytes 49160 | tf_op jit(solution)/shard_map/ppermute | solution.py:125
  77.6 8.8 %all-to-all-start.1 = ((f32[16,8,128]{2,1,0:T(8,128)}), f32[16,8,128]{2,1,0:T(8,128)S(1)}, u32[]{:S(2)}, u32[]{:S(2)}) async-start(f32[16,8,128]{2,1,0:T(8,128)} %broadcast_in_dim.143), calls=%async_computation.1 | async-start | bytes 131072 | tf_op jit(solution)/shard_map/all_to_all | solution.py:114
  87.7 5.5 %collective-permute-start.17 = (f32[8,4,16,1]{3,2,1,0:T(8,128)S(1)}, f32[8,4,16,1]{3,2,1,0:T(8,128)S(1)}, u32[]{:S(2)}, u32[]{:S(2)}) collective-permute-start(f32[8,4,16,1]{3,2,1,0:T(8,128)S(1)} %get-tuple-element.28), channel_id=1, source_target_pairs={{0,1},{2,3},{4,5},{6,7},{8,9},{10,11},{12,13},{14,15},{16,17},{18,... | collective-permute-start | bytes 6152 | tf_op jit(solution)/shard_map/ppermute | solution.py:125
  95.8 3.4 %collective-permute-start.13 = (f32[8,1,16,128]{3,2,1,0:T(8,128)S(1)}, f32[8,1,16,128]{3,2,1,0:T(8,128)S(1)}, u32[]{:S(2)}, u32[]{:S(2)}) collective-permute-start(f32[8,1,16,128]{3,2,1,0:T(8,128)S(1)} %get-tuple-element.29), channel_id=1, source_target_pairs={{0,16},{16,32},{32,48},{48,64},{64,80},{80,96},{96,112},{112,128},... | collective-permute-start | bytes 196616 | tf_op jit(solution)/shard_map/ppermute | solution.py:125
  99.3 4.5 %collective-permute-start.15 = (f32[8,4,1,128]{3,2,1,0:T(1,128)S(1)}, f32[8,4,1,128]{3,2,1,0:T(1,128)S(1)}, u32[]{:S(2)}, u32[]{:S(2)}) collective-permute-start(f32[8,4,1,128]{3,2,1,0:T(1,128)S(1)} %get-tuple-element.31), channel_id=1, source_target_pairs={{0,2},{2,4},{4,6},{6,8},{8,10},{10,12},{12,14},{1,3},{3,5},{5,7},{... | collective-permute-start | bytes 49160 | tf_op jit(solution)/shard_map/ppermute | solution.py:125
  104.5 24.7 %tile.1.tile_ref = bf16[2048,2048]{1,0:T(8,128)(2,1)} custom-call(f32[16,8,128]{2,1,0:T(8,128)} %copy-done.3, f32[16,8,128]{2,1,0:T(8,128)} %copy-done.2), custom_call_target="tpu_custom_call" | custom-call | tf_op jit(solution)/shard_map/tile/pallas_call | solution.py:64
  136.0 6.5 %all-to-all-start = ((bf16[16,8,128]{2,1,0:T(8,128)(2,1)}), bf16[16,8,128]{2,1,0:T(8,128)(2,1)S(1)}, u32[]{:S(2)}, u32[]{:S(2)}) async-start(bf16[16,8,128]{2,1,0:T(8,128)(2,1)} %broadcast_in_dim.139), calls=%async_computation | async-start | bytes 65536 | tf_op jit(solution)/shard_map/all_to_all | solution.py:114
  143.9 4.0 %collective-permute-start.21 = (f32[8,4,1,128]{3,2,1,0:T(1,128)S(1)}, f32[8,4,1,128]{3,2,1,0:T(1,128)S(1)}, u32[]{:S(2)}, u32[]{:S(2)}) collective-permute-start(f32[8,4,1,128]{3,2,1,0:T(1,128)S(1)} %get-tuple-element.25), channel_id=1, source_target_pairs={{0,2},{2,4},{4,6},{6,8},{8,10},{10,12},{12,14},{1,3},{3,5},{5,7},{... | collective-permute-start | bytes 49160 | tf_op jit(solution)/shard_map/ppermute | solution.py:125
  150.6 7.1 %product.2 = f32[16,8,128]{2,1,0:T(8,128)} custom-call(bf16[16,8,128]{2,1,0:T(8,128)(2,1)} %copy-done.4, bf16[2048,2048]{1,0:T(8,128)(2,1)} %tile.1.tile_ref), custom_call_target="tpu_custom_call" | custom-call | tf_op jit(solution)/shard_map/product/pallas_call | solution.py:98
  157.7 8.3 %all-to-all-start.3 = ((f32[16,8,128]{2,1,0:T(8,128)}), f32[16,8,128]{2,1,0:T(8,128)S(1)}, u32[]{:S(2)}, u32[]{:S(2)}) async-start(f32[16,8,128]{2,1,0:T(8,128)} %product.2), calls=%async_computation.3 | async-start | bytes 131072 | tf_op jit(solution)/shard_map/all_to_all | solution.py:184
  167.3 5.5 %collective-permute-start.23 = (f32[8,4,16,1]{3,2,1,0:T(8,128)S(1)}, f32[8,4,16,1]{3,2,1,0:T(8,128)S(1)}, u32[]{:S(2)}, u32[]{:S(2)}) collective-permute-start(f32[8,4,16,1]{3,2,1,0:T(8,128)S(1)} %get-tuple-element.22), channel_id=1, source_target_pairs={{0,1},{2,3},{4,5},{6,7},{8,9},{10,11},{12,13},{14,15},{16,17},{18,... | collective-permute-start | bytes 6152 | tf_op jit(solution)/shard_map/ppermute | solution.py:125
  172.8 3.1 %collective-permute-start.18 = (f32[8,1,16,128]{3,2,1,0:T(8,128)S(1)}, f32[8,1,16,128]{3,2,1,0:T(8,128)S(1)}, u32[]{:S(2)}, u32[]{:S(2)}) collective-permute-start(f32[8,1,16,128]{3,2,1,0:T(8,128)S(1)} %get-tuple-element.24), channel_id=1, source_target_pairs={{16,0},{32,16},{48,32},{64,48},{80,64},{96,80},{112,96},{128,112},... | collective-permute-start | bytes 196616 | tf_op jit(solution)/shard_map/ppermute | solution.py:126
  178.6 3.3 %scatter_custom_fusion = f32[8,8192]{0,1:T(8,128)} fusion(s32[128]{0:T(128)S(1)} %compare_select_fusion, f32[128,8]{1,0:T(8,128)S(1)} %copy.27, f32[]{:T(128)} %constant.32.clone.1), kind=kCustom, calls=%fused_computation.3 | custom fusion | flops 1024 | bytes 262148 | tf_op jit(solution)/shard_map/scatter-add | solution.py:190
  187.1 3.6 %collective-permute-start.25 = (f32[8,1,16,128]{3,2,1,0:T(8,128)S(1)}, f32[8,1,16,128]{3,2,1,0:T(8,128)S(1)}, u32[]{:S(2)}, u32[]{:S(2)}) collective-permute-start(f32[8,1,16,128]{3,2,1,0:T(8,128)S(1)} %get-tuple-element.17), channel_id=1, source_target_pairs={{0,16},{16,32},{32,48},{48,64},{64,80},{80,96},{96,112},{112,128},... | collective-permute-start | bytes 196616 | tf_op jit(solution)/shard_map/ppermute | solution.py:125
  192.1 4.1 %collective-permute-start.27 = (f32[8,4,1,128]{3,2,1,0:T(1,128)S(1)}, f32[8,4,1,128]{3,2,1,0:T(1,128)S(1)}, u32[]{:S(2)}, u32[]{:S(2)}) collective-permute-start(f32[8,4,1,128]{3,2,1,0:T(1,128)S(1)} %get-tuple-element.19), channel_id=1, source_target_pairs={{0,2},{2,4},{4,6},{6,8},{8,10},{10,12},{12,14},{1,3},{3,5},{5,7},{... | collective-permute-start | bytes 49160 | tf_op jit(solution)/shard_map/ppermute | solution.py:125
  197.6 5.5 %collective-permute-start.29 = (f32[8,4,16,1]{3,2,1,0:T(8,128)S(1)}, f32[8,4,16,1]{3,2,1,0:T(8,128)S(1)}, u32[]{:S(2)}, u32[]{:S(2)}) collective-permute-start(f32[8,4,16,1]{3,2,1,0:T(8,128)S(1)} %get-tuple-element.16), channel_id=1, source_target_pairs={{0,1},{2,3},{4,5},{6,7},{8,9},{10,11},{12,13},{14,15},{16,17},{18,... | collective-permute-start | bytes 6152 | tf_op jit(solution)/shard_map/ppermute | solution.py:125
  203.2 4.2 %collective-permute-done.28 = f32[8,4,16,1]{3,2,1,0:T(8,128)S(1)} collective-permute-done((f32[8,4,16,1]{3,2,1,0:T(8,128)S(1)}, f32[8,4,16,1]{3,2,1,0:T(8,128)S(1)}, u32[]{:S(2)}, u32[]{:S(2)}) %collective-permute-start.28) | collective-permute-done | bytes 2080 | tf_op jit(solution)/shard_map/ppermute | solution.py:126
  211.9 3.3 %collective-permute-start.31 = (f32[8,1,16,128]{3,2,1,0:T(8,128)S(1)}, f32[8,1,16,128]{3,2,1,0:T(8,128)S(1)}, u32[]{:S(2)}, u32[]{:S(2)}) collective-permute-start(f32[8,1,16,128]{3,2,1,0:T(8,128)S(1)} %get-tuple-element.11), channel_id=1, source_target_pairs={{0,16},{16,32},{32,48},{48,64},{64,80},{80,96},{96,112},{112,128},... | collective-permute-start | bytes 196616 | tf_op jit(solution)/shard_map/ppermute | solution.py:125
  216.5 4.0 %collective-permute-start.33 = (f32[8,4,1,128]{3,2,1,0:T(1,128)S(1)}, f32[8,4,1,128]{3,2,1,0:T(1,128)S(1)}, u32[]{:S(2)}, u32[]{:S(2)}) collective-permute-start(f32[8,4,1,128]{3,2,1,0:T(1,128)S(1)} %get-tuple-element.13), channel_id=1, source_target_pairs={{0,2},{2,4},{4,6},{6,8},{8,10},{10,12},{12,14},{1,3},{3,5},{5,7},{... | collective-permute-start | bytes 49160 | tf_op jit(solution)/shard_map/ppermute | solution.py:125
  222.0 5.6 %collective-permute-start.35 = (f32[8,4,16,1]{3,2,1,0:T(8,128)S(1)}, f32[8,4,16,1]{3,2,1,0:T(8,128)S(1)}, u32[]{:S(2)}, u32[]{:S(2)}) collective-permute-start(f32[8,4,16,1]{3,2,1,0:T(8,128)S(1)} %get-tuple-element.10), channel_id=1, source_target_pairs={{0,1},{2,3},{4,5},{6,7},{8,9},{10,11},{12,13},{14,15},{16,17},{18,... | collective-permute-start | bytes 6152 | tf_op jit(solution)/shard_map/ppermute | solution.py:125
  227.7 5.1 %collective-permute-done.34 = f32[8,4,16,1]{3,2,1,0:T(8,128)S(1)} collective-permute-done((f32[8,4,16,1]{3,2,1,0:T(8,128)S(1)}, f32[8,4,16,1]{3,2,1,0:T(8,128)S(1)}, u32[]{:S(2)}, u32[]{:S(2)}) %collective-permute-start.34) | collective-permute-done | bytes 2080 | tf_op jit(solution)/shard_map/ppermute | solution.py:126
  239.4 13.6 %all_to_all.30.density_ref = bf16[16,8,128]{2,1,0:T(8,128)(2,1)} all-to-all(bf16[16,8,128]{2,1,0:T(8,128)(2,1)S(1)} %broadcast_in_dim.144), channel_id=1, replica_groups=mesh['row'=16,'col'=8,'gz'=2] {'row'}, dimensions={0} | all-to-all | bytes 65536 | tf_op jit(solution)/shard_map/all_to_all | solution.py:114
  253.0 7.1 %product.3 = f32[16,8,128]{2,1,0:T(8,128)} custom-call(bf16[16,8,128]{2,1,0:T(8,128)(2,1)} %all_to_all.30.density_ref, bf16[2048,2048]{1,0:T(8,128)(2,1)} %tile.1.tile_ref), custom_call_target="tpu_custom_call" | custom-call | tf_op jit(solution)/shard_map/product/pallas_call | solution.py:98
  260.1 18.2 %all_to_all.31 = f32[16,8,128]{2,1,0:T(8,128)S(1)} all-to-all(f32[16,8,128]{2,1,0:T(8,128)} %product.3), channel_id=1, replica_groups=mesh['row'=16,'col'=8,'gz'=2] {'col','gz'}, dimensions={0} | all-to-all | bytes 131072 | tf_op jit(solution)/shard_map/all_to_all | solution.py:184
  (132 shorter events, 65.1 us)
Async XLA Ops:
  1.6 46.7 %collective-permute-start.1 = (f32[8,1,16,128]{3,2,1,0:T(8,128)S(1)}, f32[8,1,16,128]{3,2,1,0:T(8,128)S(1)}, u32[]{:S(2)}, u32[]{:S(2)}) collective-permute-start(f32[8,1,16,128]{3,2,1,0:T(8,128)S(1)} %get-tuple-element.44), channel_id=1, source_target_pairs={{0,16},{16,32},{32,48},{48,64},{64,80},{80,96},{96,112},{112,128},... | collective-permute-start | bytes 196616 | tf_op jit(solution)/shard_map/ppermute | solution.py:125
  6.5 42.7 %collective-permute-start = (f32[8,1,16,128]{3,2,1,0:T(8,128)S(1)}, f32[8,1,16,128]{3,2,1,0:T(8,128)S(1)}, u32[]{:S(2)}, u32[]{:S(2)}) collective-permute-start(f32[8,1,16,128]{3,2,1,0:T(8,128)S(1)} %get-tuple-element.43), channel_id=1, source_target_pairs={{16,0},{32,16},{48,32},{64,48},{80,64},{96,80},{112,96},{128,112},... | collective-permute-start | bytes 196616 | tf_op jit(solution)/shard_map/ppermute | solution.py:126
  9.6 39.7 %collective-permute-start.4 = (f32[8,4,16,1]{3,2,1,0:T(8,128)S(1)}, f32[8,4,16,1]{3,2,1,0:T(8,128)S(1)}, u32[]{:S(2)}, u32[]{:S(2)}) collective-permute-start(f32[8,4,16,1]{3,2,1,0:T(8,128)S(1)} %get-tuple-element.39), channel_id=1, source_target_pairs={{1,0},{3,2},{5,4},{7,6},{9,8},{11,10},{13,12},{15,14},{17,16},{19,... | collective-permute-start | bytes 6152 | tf_op jit(solution)/shard_map/ppermute | solution.py:126
  11.9 31.5 %collective-permute-start.2 = (f32[8,4,1,128]{3,2,1,0:T(1,128)S(1)}, f32[8,4,1,128]{3,2,1,0:T(1,128)S(1)}, u32[]{:S(2)}, u32[]{:S(2)}) collective-permute-start(f32[8,4,1,128]{3,2,1,0:T(1,128)S(1)} %get-tuple-element.42), channel_id=1, source_target_pairs={{2,0},{4,2},{6,4},{8,6},{10,8},{12,10},{14,12},{3,1},{5,3},{7,5},{... | collective-permute-start | bytes 49160 | tf_op jit(solution)/shard_map/ppermute | solution.py:126
  13.2 35.0 %collective-permute-start.3 = (f32[8,4,1,128]{3,2,1,0:T(1,128)S(1)}, f32[8,4,1,128]{3,2,1,0:T(1,128)S(1)}, u32[]{:S(2)}, u32[]{:S(2)}) collective-permute-start(f32[8,4,1,128]{3,2,1,0:T(1,128)S(1)} %get-tuple-element.41), channel_id=1, source_target_pairs={{0,2},{2,4},{4,6},{6,8},{8,10},{10,12},{12,14},{1,3},{3,5},{5,7},{... | collective-permute-start | bytes 49160 | tf_op jit(solution)/shard_map/ppermute | solution.py:125
  20.1 57.5 %all-to-all-start.2 = ((f32[16,8,128]{2,1,0:T(8,128)}), f32[16,8,128]{2,1,0:T(8,128)S(1)}, u32[]{:S(2)}, u32[]{:S(2)}) async-start(f32[16,8,128]{2,1,0:T(8,128)} %broadcast_in_dim.143), calls=%async_computation.2 | async-start | bytes 131072 | tf_op jit(solution)/shard_map/all_to_all | solution.py:114
  55.6 14.9 %collective-permute-start.8 = (f32[8,4,1,128]{3,2,1,0:T(1,128)S(1)}, f32[8,4,1,128]{3,2,1,0:T(1,128)S(1)}, u32[]{:S(2)}, u32[]{:S(2)}) collective-permute-start(f32[8,4,1,128]{3,2,1,0:T(1,128)S(1)} %get-tuple-element.38), channel_id=1, source_target_pairs={{2,0},{4,2},{6,4},{8,6},{10,8},{12,10},{14,12},{3,1},{5,3},{7,5},{... | collective-permute-start | bytes 49160 | tf_op jit(solution)/shard_map/ppermute | solution.py:126
  56.9 18.8 %collective-permute-start.10 = (f32[8,4,16,1]{3,2,1,0:T(8,128)S(1)}, f32[8,4,16,1]{3,2,1,0:T(8,128)S(1)}, u32[]{:S(2)}, u32[]{:S(2)}) collective-permute-start(f32[8,4,16,1]{3,2,1,0:T(8,128)S(1)} %get-tuple-element.33), channel_id=1, source_target_pairs={{1,0},{3,2},{5,4},{7,6},{9,8},{11,10},{13,12},{15,14},{17,16},{19,... | collective-permute-start | bytes 6152 | tf_op jit(solution)/shard_map/ppermute | solution.py:126
  58.2 17.5 %collective-permute-start.11 = (f32[8,4,16,1]{3,2,1,0:T(8,128)S(1)}, f32[8,4,16,1]{3,2,1,0:T(8,128)S(1)}, u32[]{:S(2)}, u32[]{:S(2)}) collective-permute-start(f32[8,4,16,1]{3,2,1,0:T(8,128)S(1)} %get-tuple-element.34), channel_id=1, source_target_pairs={{0,1},{2,3},{4,5},{6,7},{8,9},{10,11},{12,13},{14,15},{16,17},{18,... | collective-permute-start | bytes 6152 | tf_op jit(solution)/shard_map/ppermute | solution.py:125
  63.7 12.0 %collective-permute-start.6 = (f32[8,1,16,128]{3,2,1,0:T(8,128)S(1)}, f32[8,1,16,128]{3,2,1,0:T(8,128)S(1)}, u32[]{:S(2)}, u32[]{:S(2)}) collective-permute-start(f32[8,1,16,128]{3,2,1,0:T(8,128)S(1)} %get-tuple-element.36), channel_id=1, source_target_pairs={{16,0},{32,16},{48,32},{64,48},{80,64},{96,80},{112,96},{128,112},... | collective-permute-start | bytes 196616 | tf_op jit(solution)/shard_map/ppermute | solution.py:126
  76.3 23.0 %collective-permute-start.14 = (f32[8,4,1,128]{3,2,1,0:T(1,128)S(1)}, f32[8,4,1,128]{3,2,1,0:T(1,128)S(1)}, u32[]{:S(2)}, u32[]{:S(2)}) collective-permute-start(f32[8,4,1,128]{3,2,1,0:T(1,128)S(1)} %get-tuple-element.32), channel_id=1, source_target_pairs={{2,0},{4,2},{6,4},{8,6},{10,8},{12,10},{14,12},{3,1},{5,3},{7,5},{... | collective-permute-start | bytes 49160 | tf_op jit(solution)/shard_map/ppermute | solution.py:126
  77.6 26.2 %all-to-all-start.1 = ((f32[16,8,128]{2,1,0:T(8,128)}), f32[16,8,128]{2,1,0:T(8,128)S(1)}, u32[]{:S(2)}, u32[]{:S(2)}) async-start(f32[16,8,128]{2,1,0:T(8,128)} %broadcast_in_dim.143), calls=%async_computation.1 | async-start | bytes 131072 | tf_op jit(solution)/shard_map/all_to_all | solution.py:114
  86.4 42.8 %collective-permute-start.16 = (f32[8,4,16,1]{3,2,1,0:T(8,128)S(1)}, f32[8,4,16,1]{3,2,1,0:T(8,128)S(1)}, u32[]{:S(2)}, u32[]{:S(2)}) collective-permute-start(f32[8,4,16,1]{3,2,1,0:T(8,128)S(1)} %get-tuple-element.27), channel_id=1, source_target_pairs={{1,0},{3,2},{5,4},{7,6},{9,8},{11,10},{13,12},{15,14},{17,16},{19,... | collective-permute-start | bytes 6152 | tf_op jit(solution)/shard_map/ppermute | solution.py:126
  87.7 41.5 %collective-permute-start.17 = (f32[8,4,16,1]{3,2,1,0:T(8,128)S(1)}, f32[8,4,16,1]{3,2,1,0:T(8,128)S(1)}, u32[]{:S(2)}, u32[]{:S(2)}) collective-permute-start(f32[8,4,16,1]{3,2,1,0:T(8,128)S(1)} %get-tuple-element.28), channel_id=1, source_target_pairs={{0,1},{2,3},{4,5},{6,7},{8,9},{10,11},{12,13},{14,15},{16,17},{18,... | collective-permute-start | bytes 6152 | tf_op jit(solution)/shard_map/ppermute | solution.py:125
  93.2 36.0 %collective-permute-start.12 = (f32[8,1,16,128]{3,2,1,0:T(8,128)S(1)}, f32[8,1,16,128]{3,2,1,0:T(8,128)S(1)}, u32[]{:S(2)}, u32[]{:S(2)}) collective-permute-start(f32[8,1,16,128]{3,2,1,0:T(8,128)S(1)} %get-tuple-element.30), channel_id=1, source_target_pairs={{16,0},{32,16},{48,32},{64,48},{80,64},{96,80},{112,96},{128,112},... | collective-permute-start | bytes 196616 | tf_op jit(solution)/shard_map/ppermute | solution.py:126
  95.8 33.5 %collective-permute-start.13 = (f32[8,1,16,128]{3,2,1,0:T(8,128)S(1)}, f32[8,1,16,128]{3,2,1,0:T(8,128)S(1)}, u32[]{:S(2)}, u32[]{:S(2)}) collective-permute-start(f32[8,1,16,128]{3,2,1,0:T(8,128)S(1)} %get-tuple-element.29), channel_id=1, source_target_pairs={{0,16},{16,32},{32,48},{48,64},{64,80},{80,96},{96,112},{112,128},... | collective-permute-start | bytes 196616 | tf_op jit(solution)/shard_map/ppermute | solution.py:125
  99.3 29.9 %collective-permute-start.15 = (f32[8,4,1,128]{3,2,1,0:T(1,128)S(1)}, f32[8,4,1,128]{3,2,1,0:T(1,128)S(1)}, u32[]{:S(2)}, u32[]{:S(2)}) collective-permute-start(f32[8,4,1,128]{3,2,1,0:T(1,128)S(1)} %get-tuple-element.31), channel_id=1, source_target_pairs={{0,2},{2,4},{4,6},{6,8},{8,10},{10,12},{12,14},{1,3},{3,5},{5,7},{... | collective-permute-start | bytes 49160 | tf_op jit(solution)/shard_map/ppermute | solution.py:125
  136.0 13.9 %all-to-all-start = ((bf16[16,8,128]{2,1,0:T(8,128)(2,1)}), bf16[16,8,128]{2,1,0:T(8,128)(2,1)S(1)}, u32[]{:S(2)}, u32[]{:S(2)}) async-start(bf16[16,8,128]{2,1,0:T(8,128)(2,1)} %broadcast_in_dim.139), calls=%async_computation | async-start | bytes 65536 | tf_op jit(solution)/shard_map/all_to_all | solution.py:114
  142.6 33.4 %collective-permute-start.20 = (f32[8,4,1,128]{3,2,1,0:T(1,128)S(1)}, f32[8,4,1,128]{3,2,1,0:T(1,128)S(1)}, u32[]{:S(2)}, u32[]{:S(2)}) collective-permute-start(f32[8,4,1,128]{3,2,1,0:T(1,128)S(1)} %get-tuple-element.26), channel_id=1, source_target_pairs={{2,0},{4,2},{6,4},{8,6},{10,8},{12,10},{14,12},{3,1},{5,3},{7,5},{... | collective-permute-start | bytes 49160 | tf_op jit(solution)/shard_map/ppermute | solution.py:126
  143.9 34.6 %collective-permute-start.21 = (f32[8,4,1,128]{3,2,1,0:T(1,128)S(1)}, f32[8,4,1,128]{3,2,1,0:T(1,128)S(1)}, u32[]{:S(2)}, u32[]{:S(2)}) collective-permute-start(f32[8,4,1,128]{3,2,1,0:T(1,128)S(1)} %get-tuple-element.25), channel_id=1, source_target_pairs={{0,2},{2,4},{4,6},{6,8},{8,10},{10,12},{12,14},{1,3},{3,5},{5,7},{... | collective-permute-start | bytes 49160 | tf_op jit(solution)/shard_map/ppermute | solution.py:125
  157.7 20.8 %all-to-all-start.3 = ((f32[16,8,128]{2,1,0:T(8,128)}), f32[16,8,128]{2,1,0:T(8,128)S(1)}, u32[]{:S(2)}, u32[]{:S(2)}) async-start(f32[16,8,128]{2,1,0:T(8,128)} %product.2), calls=%async_computation.3 | async-start | bytes 131072 | tf_op jit(solution)/shard_map/all_to_all | solution.py:184
  166.0 18.7 %collective-permute-start.22 = (f32[8,4,16,1]{3,2,1,0:T(8,128)S(1)}, f32[8,4,16,1]{3,2,1,0:T(8,128)S(1)}, u32[]{:S(2)}, u32[]{:S(2)}) collective-permute-start(f32[8,4,16,1]{3,2,1,0:T(8,128)S(1)} %get-tuple-element.21), channel_id=1, source_target_pairs={{1,0},{3,2},{5,4},{7,6},{9,8},{11,10},{13,12},{15,14},{17,16},{19,... | collective-permute-start | bytes 6152 | tf_op jit(solution)/shard_map/ppermute | solution.py:126
  167.3 17.4 %collective-permute-start.23 = (f32[8,4,16,1]{3,2,1,0:T(8,128)S(1)}, f32[8,4,16,1]{3,2,1,0:T(8,128)S(1)}, u32[]{:S(2)}, u32[]{:S(2)}) collective-permute-start(f32[8,4,16,1]{3,2,1,0:T(8,128)S(1)} %get-tuple-element.22), channel_id=1, source_target_pairs={{0,1},{2,3},{4,5},{6,7},{8,9},{10,11},{12,13},{14,15},{16,17},{18,... | collective-permute-start | bytes 6152 | tf_op jit(solution)/shard_map/ppermute | solution.py:125
  172.8 11.9 %collective-permute-start.18 = (f32[8,1,16,128]{3,2,1,0:T(8,128)S(1)}, f32[8,1,16,128]{3,2,1,0:T(8,128)S(1)}, u32[]{:S(2)}, u32[]{:S(2)}) collective-permute-start(f32[8,1,16,128]{3,2,1,0:T(8,128)S(1)} %get-tuple-element.24), channel_id=1, source_target_pairs={{16,0},{32,16},{48,32},{64,48},{80,64},{96,80},{112,96},{128,112},... | collective-permute-start | bytes 196616 | tf_op jit(solution)/shard_map/ppermute | solution.py:126
  185.2 24.0 %collective-permute-start.24 = (f32[8,1,16,128]{3,2,1,0:T(8,128)S(1)}, f32[8,1,16,128]{3,2,1,0:T(8,128)S(1)}, u32[]{:S(2)}, u32[]{:S(2)}) collective-permute-start(f32[8,1,16,128]{3,2,1,0:T(8,128)S(1)} %get-tuple-element.18), channel_id=1, source_target_pairs={{16,0},{32,16},{48,32},{64,48},{80,64},{96,80},{112,96},{128,112},... | collective-permute-start | bytes 196616 | tf_op jit(solution)/shard_map/ppermute | solution.py:126
  187.1 22.1 %collective-permute-start.25 = (f32[8,1,16,128]{3,2,1,0:T(8,128)S(1)}, f32[8,1,16,128]{3,2,1,0:T(8,128)S(1)}, u32[]{:S(2)}, u32[]{:S(2)}) collective-permute-start(f32[8,1,16,128]{3,2,1,0:T(8,128)S(1)} %get-tuple-element.17), channel_id=1, source_target_pairs={{0,16},{16,32},{32,48},{48,64},{64,80},{80,96},{96,112},{112,128},... | collective-permute-start | bytes 196616 | tf_op jit(solution)/shard_map/ppermute | solution.py:125
  196.3 11.1 %collective-permute-start.28 = (f32[8,4,16,1]{3,2,1,0:T(8,128)S(1)}, f32[8,4,16,1]{3,2,1,0:T(8,128)S(1)}, u32[]{:S(2)}, u32[]{:S(2)}) collective-permute-start(f32[8,4,16,1]{3,2,1,0:T(8,128)S(1)} %get-tuple-element.15), channel_id=1, source_target_pairs={{1,0},{3,2},{5,4},{7,6},{9,8},{11,10},{13,12},{15,14},{17,16},{19,... | collective-permute-start | bytes 6152 | tf_op jit(solution)/shard_map/ppermute | solution.py:126
  197.6 11.6 %collective-permute-start.29 = (f32[8,4,16,1]{3,2,1,0:T(8,128)S(1)}, f32[8,4,16,1]{3,2,1,0:T(8,128)S(1)}, u32[]{:S(2)}, u32[]{:S(2)}) collective-permute-start(f32[8,4,16,1]{3,2,1,0:T(8,128)S(1)} %get-tuple-element.16), channel_id=1, source_target_pairs={{0,1},{2,3},{4,5},{6,7},{8,9},{10,11},{12,13},{14,15},{16,17},{18,... | collective-permute-start | bytes 6152 | tf_op jit(solution)/shard_map/ppermute | solution.py:125
  209.7 23.7 %collective-permute-start.30 = (f32[8,1,16,128]{3,2,1,0:T(8,128)S(1)}, f32[8,1,16,128]{3,2,1,0:T(8,128)S(1)}, u32[]{:S(2)}, u32[]{:S(2)}) collective-permute-start(f32[8,1,16,128]{3,2,1,0:T(8,128)S(1)} %get-tuple-element.12), channel_id=1, source_target_pairs={{16,0},{32,16},{48,32},{64,48},{80,64},{96,80},{112,96},{128,112},... | collective-permute-start | bytes 196616 | tf_op jit(solution)/shard_map/ppermute | solution.py:126
  211.9 21.4 %collective-permute-start.31 = (f32[8,1,16,128]{3,2,1,0:T(8,128)S(1)}, f32[8,1,16,128]{3,2,1,0:T(8,128)S(1)}, u32[]{:S(2)}, u32[]{:S(2)}) collective-permute-start(f32[8,1,16,128]{3,2,1,0:T(8,128)S(1)} %get-tuple-element.11), channel_id=1, source_target_pairs={{0,16},{16,32},{32,48},{48,64},{64,80},{80,96},{96,112},{112,128},... | collective-permute-start | bytes 196616 | tf_op jit(solution)/shard_map/ppermute | solution.py:125
  220.7 12.1 %collective-permute-start.34 = (f32[8,4,16,1]{3,2,1,0:T(8,128)S(1)}, f32[8,4,16,1]{3,2,1,0:T(8,128)S(1)}, u32[]{:S(2)}, u32[]{:S(2)}) collective-permute-start(f32[8,4,16,1]{3,2,1,0:T(8,128)S(1)} %get-tuple-element.9), channel_id=1, source_target_pairs={{1,0},{3,2},{5,4},{7,6},{9,8},{11,10},{13,12},{15,14},{17,16},{19,... | collective-permute-start | bytes 6152 | tf_op jit(solution)/shard_map/ppermute | solution.py:126
  222.0 11.4 %collective-permute-start.35 = (f32[8,4,16,1]{3,2,1,0:T(8,128)S(1)}, f32[8,4,16,1]{3,2,1,0:T(8,128)S(1)}, u32[]{:S(2)}, u32[]{:S(2)}) collective-permute-start(f32[8,4,16,1]{3,2,1,0:T(8,128)S(1)} %get-tuple-element.10), channel_id=1, source_target_pairs={{0,1},{2,3},{4,5},{6,7},{8,9},{10,11},{12,13},{14,15},{16,17},{18,... | collective-permute-start | bytes 6152 | tf_op jit(solution)/shard_map/ppermute | solution.py:125
  (13 other events, 198.5 us)

commit v2 on v1

v2 whole, which is shorter than its diff:
```python
import functools
import math

import jax
import jax.numpy as jnp
from jax import lax
from jax.experimental import pallas as pl
from jax.experimental.pallas import tpu as pltpu
from jax.sharding import PartitionSpec as P

SIZE_Y = 16

relax_weight = 0.8
wave_number = 25.0
soften = 0.05
coupling = 0.5

SINE = (6.2831851600894435, -41.34165503141112, 81.60100407296788, -76.54978228730859, 39.53670602126459)
TURNS = wave_number / (2.0 * math.pi)
ROUNDER = 12582912.0


def tile_kernel(source_ref, target_ref, out_ref, columns):
    bricks, slots = target_ref.shape[0], target_ref.shape[2]
    live = jnp.max(source_ref[0, 4:5, :]).astype(jnp.int32)
    columns[...] = jnp.transpose(source_ref[0])
    steps = (live + 15) // 16

    def fill(step, carry):
        rows = pl.ds(pl.multiple_of(step * 16, 16), 16)
        here = columns[rows, :]
        spread = [jnp.broadcast_to(here[:, d : d + 1], (16, slots)) for d in range(4)]
        for brick in range(bricks):
            square = 1e-30
            for d in range(3):
                delta = target_ref[brick, d : d + 1, :] - spread[d]
                square = square + delta * delta
            turns = square * lax.rsqrt(square)
            whole = (turns + ROUNDER) - ROUNDER
            angle = 0.25 - jnp.abs(turns - whole)
            angle2 = angle * angle
            wave = SINE[4]
            for c in SINE[3::-1]:
                wave = wave * angle2 + c
            below = turns + soften * TURNS
            guess = pl.reciprocal(below, approx=True)
            value = (angle * spread[3]) * (guess * (2.0 - below * guess)) * wave
            out_ref[rows, brick * slots : (brick + 1) * slots] = value.astype(jnp.bfloat16)
        return carry

    lax.fori_loop(0, steps, fill, 0)

    def clear(step, carry):
        rows = pl.ds(pl.multiple_of(step * 16, 16), 16)
        out_ref[rows, :] = jnp.zeros((16, out_ref.shape[1]), jnp.bfloat16)
        return carry

    lax.fori_loop(steps, slots // 16, clear, 0)


def make_tile(sources, targets):
    bricks, rows, slots = sources.shape
    width = targets.shape[0] * slots
    return pl.pallas_call(
        tile_kernel,
        grid=(bricks,),
        in_specs=[
            pl.BlockSpec((1, rows, slots), lambda b: (b, 0, 0)),
            pl.BlockSpec(targets.shape, lambda b: (0, 0, 0)),
        ],
        out_specs=pl.BlockSpec((slots, width), lambda b: (b, 0)),
        out_shape=jax.ShapeDtypeStruct((bricks * slots, width), jnp.bfloat16),
        scratch_shapes=[pltpu.VMEM((slots, rows), jnp.float32)],
        name="tile",
    )(sources, targets)


def product_kernel(near, density_ref, tile_ref, out_ref, total):
    step = pl.program_id(0)

    @pl.when(step == 0)
    def _():
        total[...] = jnp.zeros_like(total)

    values = jnp.concatenate([density_ref[0], density_ref[1]], axis=1)
    total[...] += jnp.dot(values, tile_ref[...], preferred_element_type=jnp.float32)

    @pl.when(step == pl.num_programs(0) - 1)
    def _():
        bricks, slots = out_ref.shape[0], out_ref.shape[-1]
        for brick in range(bricks):
            if not near:
                out_ref[brick] = total[:, brick * slots : (brick + 1) * slots]
                continue
            for n in range(6):
                side, half = brick // 2 + n % 3 - 1, (brick + n // 3) % 2
                other = side * 2 + half
                if 0 <= side < bricks // 2:
                    out_ref[brick, n] = total[:, other * slots : (other + 1) * slots]
                else:
                    out_ref[brick, n] = jnp.zeros((total.shape[0], slots), jnp.float32)


def products(densities, tile, near):
    bricks, channels, slots = densities.shape
    width = tile.shape[1]
    shape = (width // slots, 6, channels, slots) if near else (width // slots, channels, slots)
    return pl.pallas_call(
        functools.partial(product_kernel, near),
        grid=(bricks // 2,),
        in_specs=[
            pl.BlockSpec((2, channels, slots), lambda b: (b, 0, 0)),
            pl.BlockSpec((2 * slots, width), lambda b: (b, 0)),
        ],
        out_specs=pl.BlockSpec(shape, lambda b: (0,) * len(shape)),
        out_shape=jax.ShapeDtypeStruct(shape, jnp.float32),
        scratch_shapes=[pltpu.VMEM((channels, width), jnp.float32)],
        name="product",
    )(densities, tile)


def from_everyone(x, axis):
    copies = jnp.broadcast_to(x, (lax.axis_size(axis), *x.shape))
    return lax.all_to_all(copies, axis, split_axis=0, concat_axis=0, tiled=True)


REACH = 3
XO, YO = 3, 4
SEND = 5


def lanes(shape):
    return lax.broadcasted_iota(jnp.int32, shape, len(shape) - 1)


def turned(x, shift):
    return pltpu.roll(x, shift % x.shape[-1], x.ndim - 1)


def params(megabytes=24):
    return pltpu.CompilerParams(vmem_limit_bytes=megabytes << 20)


def whole_call(kernel, out_shape, scratch, name, scalars, *operands):
    smem = pl.BlockSpec(memory_space=pltpu.SMEM)
    vmem = pl.BlockSpec(memory_space=pltpu.VMEM)
    return pl.pallas_call(
        kernel,
        in_specs=[smem] * len(scalars) + [vmem] * len(operands),
        out_specs=jax.tree.map(lambda _: vmem, out_shape),
        out_shape=out_shape,
        scratch_shapes=scratch,
        compiler_params=params(),
        name=name,
    )(*scalars, *operands)


def f32(*shape):
    return jax.ShapeDtypeStruct(shape, jnp.float32)


def bf16(*shape):
    return jax.ShapeDtypeStruct(shape, jnp.bfloat16)


def put_planes(up_ref, down_ref, base, field_ref, depth, offset=0):
    size_x, size_y = field_ref.shape[-3], field_ref.shape[-2]
    for e in range(field_ref.shape[0]):
        for i in range(depth):
            rows = pl.ds(base + (e * depth + i) * size_y, size_y)
            high = field_ref[e, size_x - depth + i] + offset
            low = field_ref[e, i] + offset
            up_ref[rows, :] = high.astype(jnp.bfloat16)
            down_ref[rows, :] = low.astype(jnp.bfloat16)
    return base + field_ref.shape[0] * depth * size_y


def planes_kernel(state_ref, source_ref, class_ref, up_ref, down_ref):
    base = put_planes(up_ref, down_ref, 0, state_ref, 3)
    base = put_planes(up_ref, down_ref, base, source_ref, 2)
    put_planes(up_ref, down_ref, base, class_ref, 2, 1.0)


def framed(frame_ref, field_ref, low_ref, high_ref, base, depth, offset=0):
    channels, size_x, size_y = field_ref.shape[:3]
    planes, rows = size_x + 2 * XO, size_y + 2 * YO
    frame_ref[...] = jnp.zeros_like(frame_ref)
    for e in range(channels):
        for x in range(size_x):
            at = (e * planes + XO + x) * rows + YO
            frame_ref[at : at + size_y, :] = field_ref[e, x].astype(jnp.float32) + offset
        for i in range(depth):
            here = pl.ds(base + (e * depth + i) * size_y, size_y)
            at = (e * planes + XO - depth + i) * rows + YO
            frame_ref[at : at + size_y, :] = low_ref[here, :].astype(jnp.float32)
            at = (e * planes + XO + size_x + i) * rows + YO
            frame_ref[at : at + size_y, :] = high_ref[here, :].astype(jnp.float32)
    return base + channels * depth * size_y


def depth_rows(frames, gz, x, size_y, rows, planes, channels):
    lane = lanes((size_y, 128))
    out = jnp.zeros((size_y, 128), jnp.float32)
    for e in range(channels):
        for index, frame_ref in enumerate(frames):
            own = frame_ref.shape[0] == planes * rows
            at = ((0 if own else e) * planes + x) * rows + YO
            start = e * 16 + index * SEND + 1
            moved = turned(frame_ref[at : at + size_y, :], start + 3 - 3 * gz)
            out = jnp.where((lane >= start) & (lane < start + 3), moved, out)
    return out


def frame_kernel(full, place_ref, *refs):
    if full:
        state_ref, source_ref, class_ref, low_ref, high_ref, frame_ref, forcing_ref, code_ref, depth_ref = refs
    else:
        state_ref, low_ref, high_ref, frame_ref, depth_ref = refs
    channels, size_x, size_y = state_ref.shape[:3]
    planes, rows = size_x + 2 * XO, size_y + 2 * YO
    base = framed(frame_ref, state_ref, low_ref, high_ref, 0, 3)
    frames = [frame_ref]
    if full:
        base = framed(forcing_ref, source_ref, low_ref, high_ref, base, 2)
        framed(code_ref, class_ref, low_ref, high_ref, base, 2, 1.0)
        frames = [frame_ref, forcing_ref, code_ref]
    gz = place_ref[1]
    for x in range(planes):
        out = depth_rows(frames, gz, x, size_y, rows, planes, channels)
        depth_ref[x * size_y : (x + 1) * size_y, :] = out.astype(jnp.bfloat16)


def edge_kernel(full, *refs):
    if full:
        frame_ref, forcing_ref, code_ref, other_ref, depth_ref, up_ref, down_ref = refs
    else:
        frame_ref, other_ref, depth_ref, up_ref, down_ref = refs
    rows = SIZE_Y + 2 * YO
    planes = depth_ref.shape[0] // rows
    depth_ref[...] = jnp.zeros_like(depth_ref)
    for x in range(planes):
        here = other_ref[x * SIZE_Y : (x + 1) * SIZE_Y, :].astype(jnp.float32)
        depth_ref[x * rows + YO : x * rows + YO + SIZE_Y, :] = here

    def put(base, ref, depth, step):
        count = ref.shape[0] // rows
        for j in range(depth):
            high = ref[pl.ds(YO + SIZE_Y - depth + j, count, stride=rows), :]
            low = ref[pl.ds(YO + j, count, stride=rows), :]
            up_ref[base + j * step : base + j * step + count, :] = high.astype(jnp.bfloat16)
            down_ref[base + j * step : base + j * step + count, :] = low.astype(jnp.bfloat16)
        return base + depth * step

    if full:
        up_ref[edge_tail(full) :, :] = jnp.zeros((80, 128), jnp.bfloat16)
        down_ref[edge_tail(full) :, :] = jnp.zeros((80, 128), jnp.bfloat16)
    else:
        up_ref[edge_tail(full) :, :] = jnp.zeros((48, 128), jnp.bfloat16)
        down_ref[edge_tail(full) :, :] = jnp.zeros((48, 128), jnp.bfloat16)
    base = put(0, frame_ref, 3, 80)
    if full:
        base = put(base, forcing_ref, 2, 80)
        base = put(base, code_ref, 2, 16)
    put(base, depth_ref, 3, 16)


def edge_tail(full):
    return 400 if full else 240


def take_edges(frame_ref, low_ref, high_ref, base, depth, step):
    rows = SIZE_Y + 2 * YO
    count = frame_ref.shape[0] // rows
    for j in range(depth):
        low = low_ref[base + j * step : base + j * step + count, :].astype(jnp.float32)
        high = high_ref[base + j * step : base + j * step + count, :].astype(jnp.float32)
        frame_ref[pl.ds(YO - depth + j, count, stride=rows), :] = low
        frame_ref[pl.ds(YO + SIZE_Y + j, count, stride=rows), :] = high
    return base + depth * step


def faces(get, e_range, gz, shape):
    lane = lanes(shape)
    out = jnp.zeros(shape, jnp.float32)
    for e in e_range:
        out = jnp.where(lane == e * 16 + 4 * gz, turned(get(e), e * 16 + 1 + 3 * gz), out)
    return out


def sweep(src, dst, zsrc, zdst, forcing, coef, zforcing, zcoef, gz, x_low, x_high, channels, planes, finish=None):
    rows = SIZE_Y + 2 * YO
    shape = (rows, 128)
    lane = lanes(shape)
    keep = 1.0 - relax_weight
    inner_low = (lane > 0).astype(jnp.float32)
    inner_high = (lane < 127).astype(jnp.float32)
    border = (lane == 127 - 127 * gz).astype(jnp.float32)
    face_lane = (lane & 15) == 4 * gz

    def one_plane(x, carry):
        at = pl.multiple_of(x * rows, 8)
        other = zsrc[pl.ds(at, rows), :]
        weight = coef[pl.ds(at, rows), :]
        fresh = []
        for e in range(channels):
            row = pl.multiple_of((e * planes + x) * rows, 8)
            own = src[pl.ds(row, rows), :]
            total = src[pl.ds(row + rows, rows), :] + src[pl.ds(row - rows, rows), :]
            total = total + pltpu.roll(own, rows - 1, 0) + pltpu.roll(own, 1, 0)
            total = total + pltpu.roll(own, 127, 1) * inner_high + pltpu.roll(own, 1, 1) * inner_low
            total = total + turned(other, 126 - gz - 16 * e + 256) * border
            new = keep * own + weight * (forcing[pl.ds(row, rows), :] + total)
            if finish is None:
                dst[pl.ds(row, rows), :] = new
            else:
                finish(e, x, new)
            fresh.append(new)
        if finish is None:
            total = zsrc[pl.ds(at + rows, rows), :] + zsrc[pl.ds(at - rows, rows), :]
            total = total + pltpu.roll(other, rows - 1, 0) + pltpu.roll(other, 1, 0)
            total = total + pltpu.roll(other, 127, 1) + pltpu.roll(other, 1, 1)
            new = keep * other + zcoef[pl.ds(at, rows), :] * (zforcing[pl.ds(at, rows), :] + total)
            face = faces(lambda e: fresh[e], range(channels), gz, shape)
            zdst[pl.ds(at, rows), :] = jnp.where(face_lane, face, new)
        return carry

    lax.fori_loop(x_low, x_high, one_plane, 0)


def sweeps(frame, second, zframe, zsecond, forcing, coef, zforcing, zcoef, gz, out_ref, planes):
    channels = out_ref.shape[0]
    rows = SIZE_Y + 2 * YO
    face_lane = (lanes((rows, 128)) & 15) == 4 * gz
    for x in range(planes):
        face = faces(lambda e: frame[(e * planes + x) * rows : (e * planes + x + 1) * rows, :], range(channels), gz, (rows, 128))
        here = zframe[x * rows : (x + 1) * rows, :]
        zframe[x * rows : (x + 1) * rows, :] = jnp.where(face_lane, face, here)
    sweep(frame, second, zframe, zsecond, forcing, coef, zforcing, zcoef, gz, 1, planes - 1, channels, planes)
    sweep(second, frame, zsecond, zframe, forcing, coef, zforcing, zcoef, gz, 2, planes - 2, channels, planes)

    def finish(e, x, new):
        out_ref[e, x - XO] = new[YO : YO + SIZE_Y, :]

    sweep(frame, None, zframe, None, forcing, coef, zforcing, zcoef, gz, XO, planes - XO, channels, planes, finish)


def put_density(out_ref, density_ref, cell_ref, live):
    channels, size_x, size_y, size_z = out_ref.shape
    slots = cell_ref.shape[1]
    cell = cell_ref[...]
    pick = (lax.broadcasted_iota(jnp.int32, (size_z, slots), 0) == (cell & (size_z - 1))).astype(jnp.bfloat16)
    count = size_x * size_y
    layers = out_ref[...].reshape(channels * count, size_z).astype(jnp.bfloat16)
    lines = jnp.dot(layers, pick, preferred_element_type=jnp.float32)
    used = lanes((count, slots)) < live
    mask = used & (lax.broadcasted_iota(jnp.int32, (count, slots), 0) == (cell >> 7))
    found = [
        jnp.sum(jnp.where(mask, lines[e * count : (e + 1) * count, :], 0.0), axis=0, keepdims=True)
        for e in range(channels)
    ]
    density = jnp.concatenate(found, axis=0).astype(jnp.bfloat16)
    for brick in range(density_ref.shape[0]):
        density_ref[brick] = density


def first_kernel(
    place_ref, coef_table_ref, frame_ref, forcing_ref, code_ref, depth_ref, low_ref, high_ref, cell_ref,
    out_ref, forcing_out, coef_out, zforcing_out, zcoef_out, density_ref, up_ref, down_ref,
    first, second, zfirst, zsecond, code, zcode,
):
    gz = place_ref[1]
    rows = SIZE_Y + 2 * YO
    planes = code_ref.shape[0] // rows
    first[...] = frame_ref[...]
    forcing_out[...] = forcing_ref[...]
    code[...] = code_ref[...]
    zcode[...] = depth_ref[...]
    base = take_edges(first, low_ref, high_ref, 0, 3, 80)
    base = take_edges(forcing_out, low_ref, high_ref, base, 2, 80)
    base = take_edges(code, low_ref, high_ref, base, 2, 16)
    take_edges(zcode, low_ref, high_ref, base, 3, 16)
    lane = lanes((rows, 128)) & 15
    outer = (lane >= 1) & (lane <= 3)
    for x in range(planes):
        here = pl.ds(x * rows, rows)
        packed = zcode[here, :]
        zfirst[here, :] = jnp.where(outer, packed, 0.0)
        zforcing_out[here, :] = jnp.where(outer, turned(packed, 128 - SEND), 0.0)
        level = jnp.where(outer, turned(packed, 128 - 2 * SEND), 0.0)
        own_level = code[here, :]
        zweight = jnp.zeros((rows, 128), jnp.float32)
        weight = jnp.zeros((rows, 128), jnp.float32)
        for index in range(coef_table_ref.shape[0]):
            value = coef_table_ref[index]
            zweight = jnp.where(level == index + 1.0, value, zweight)
            weight = jnp.where(own_level == index + 1.0, value, weight)
        zcoef_out[here, :] = zweight
        coef_out[here, :] = weight
    sweeps(first, second, zfirst, zsecond, forcing_out, coef_out, zforcing_out, zcoef_out, gz, out_ref, planes)
    put_density(out_ref, density_ref, cell_ref, place_ref[2])
    put_planes(up_ref, down_ref, 0, out_ref, 3)


def split(x):
    high = x.astype(jnp.bfloat16)
    return high, (x - high.astype(jnp.float32)).astype(jnp.bfloat16)


def across(a, b):
    return lax.dot_general(a, b, (((1,), (1,)), ((), ())), preferred_element_type=jnp.float32)


def add_load(forcing, zforcing, near_ref, side, gz, channels, planes):
    rows = SIZE_Y + 2 * YO
    size_x = planes - 2 * XO
    cells = near_ref[6].astype(jnp.int32)
    slots = cells.shape[1]
    wide = 3 * slots

    def row_of(first):
        cell = jnp.concatenate([cells[first + n : first + n + 1, :] for n in range(3)], axis=1)
        shift = jnp.concatenate([jnp.full((1, slots), YO + SIZE_Y * (n - 1), jnp.int32) for n in range(3)], axis=1)
        value = coupling * jnp.concatenate([near_ref[first + n] for n in range(3)], axis=1)
        return cell & 127, ((cell >> 7) & (SIZE_Y - 1)) + shift, cell >> 11, value

    span = {-1: range(size_x - 2, size_x), 0: range(size_x), 1: range(2)}[side]
    level = lax.broadcasted_iota(jnp.int32, (rows, wide), 0)
    z, y, x, value = row_of(0)
    pick = (lax.broadcasted_iota(jnp.int32, (128, wide), 0) == z).astype(jnp.bfloat16)
    for plane in span:
        mask = (level == y) & (x == plane)
        spread = jnp.concatenate([jnp.where(mask, value[e : e + 1, :], 0.0) for e in range(channels)], axis=0)
        high, low = split(spread)
        load = across(high, pick) + across(low, pick)
        at = plane + XO + size_x * side
        for e in range(channels):
            row = (e * planes + at) * rows
            forcing[row : row + rows, :] += load[e * rows : (e + 1) * rows, :]
    z, y, x, value = row_of(3)
    lane = z - 125 * gz + 1
    step = lax.broadcasted_iota(jnp.int32, (16, wide), 0)
    ok = (step == lane) & (step >= 1) & (step <= 3)
    spread = jnp.concatenate([jnp.where(ok, value[e : e + 1, :], 0.0) for e in range(channels)], axis=0)
    high, low = split(spread)
    for plane in span:
        mask = ((level == y) & (x == plane)).astype(jnp.bfloat16)
        row = (plane + XO + size_x * side) * rows
        zforcing[row : row + rows, :] += across(mask, high) + across(mask, low)


def second_kernel(
    place_ref, frame_ref, forcing_ref, coef_ref, zforcing_ref, zcoef_ref, depth_ref, low_ref, high_ref, cell_ref,
    near_low, near_own, near_high, out_ref, density_ref, first, second, zfirst, zsecond, forcing, zforcing,
):
    gz = place_ref[1]
    rows = SIZE_Y + 2 * YO
    planes = coef_ref.shape[0] // rows
    channels = out_ref.shape[0]
    first[...] = frame_ref[...]
    zfirst[...] = depth_ref[...]
    forcing[...] = forcing_ref[...]
    zforcing[...] = zforcing_ref[...]
    base = take_edges(first, low_ref, high_ref, 0, 3, 80)
    take_edges(zfirst, low_ref, high_ref, base, 3, 16)
    for side, near in ((-1, near_low), (0, near_own), (1, near_high)):
        add_load(forcing, zforcing, near, side, gz, channels, planes)
    sweeps(first, second, zfirst, zsecond, forcing, coef_ref, zforcing, zcoef_ref, gz, out_ref, planes)
    put_density(out_ref, density_ref, cell_ref, place_ref[2])


def near_kernel(place_ref, parts_ref, targets_ref, near_ref, own_ref):
    col, gz = place_ref[0], place_ref[1]
    cols = targets_ref.shape[0] // 2
    slots = targets_ref.shape[2]
    lane = lanes((8, slots))
    near_ref[6] = jnp.zeros((8, slots), jnp.float32)
    for n in range(6):
        side = jnp.clip(col + n % 3 - 1, 0, cols - 1)
        half = gz if n < 3 else 1 - gz
        about = targets_ref[side * 2 + half]
        total = parts_ref[0, n]
        for sender in range(1, parts_ref.shape[0]):
            total = total + parts_ref[sender, n]
        total = jnp.where(lane < about[4:5, :].astype(jnp.int32), total, 0.0)
        near_ref[n] = total
        near_ref[6, n : n + 1, :] = about[5:6, :]
        if n == 1:
            own_ref[...] = total


def last_kernel(place_ref, parts_ref, own_ref):
    total = parts_ref[0]
    for sender in range(1, parts_ref.shape[0]):
        total = total + parts_ref[sender]
    own_ref[...] = jnp.where(lanes(total.shape) < place_ref[2], total, 0.0)


def both_ways(up, down, axis):
    devices = lax.axis_size(axis)
    pairs = [(i, i + 1) for i in range(devices - 1)]
    return lax.ppermute(up, axis, pairs), lax.ppermute(down, axis, [(b, a) for a, b in pairs])


def local(
    initial_field, source_term, cell_class, class_shift, surface_cell, live_count, panel_geometry
):
    channels, size_x, size_y, size_z = initial_field.shape
    slots = surface_cell.shape[0]
    bricks = lax.axis_size("row")
    panels = slots * lax.axis_size("row") * lax.axis_size("col") * lax.axis_size("gz")
    factor = 1.0 / math.sqrt(panels)
    planes, rows = size_x + 2 * XO, size_y + 2 * YO
    frame, flat = (channels * planes * rows, 128), (planes * rows, 128)
    place = jnp.stack([lax.axis_index("col"), lax.axis_index("gz"), live_count[0]]).astype(jnp.int32)
    coefs = relax_weight / (6.0 + class_shift)
    classes = cell_class[None]
    cells = surface_cell[None]

    send_x = channels * 5 * size_y + 2 * size_y
    up, down = whole_call(
        planes_kernel, (bf16(send_x, 128), bf16(send_x, 128)), [], "planes", (),
        initial_field, source_term, classes,
    )
    low, high = both_ways(up, down, "row")
    start, forcing, code, depth = whole_call(
        functools.partial(frame_kernel, True),
        (f32(*frame), f32(*frame), f32(*flat), bf16(planes * size_y, 128)), [], "frame", (place,),
        initial_field, source_term, classes, low, high,
    )
    other = lax.ppermute(depth, "gz", [(0, 1), (1, 0)])

    live_row = jnp.broadcast_to(live_count.astype(jnp.float32)[:, None], (1, slots))
    message = jnp.concatenate(
        [panel_geometry[:3] * TURNS, panel_geometry[3:] * (factor * TURNS), live_row,
         cells.astype(jnp.float32), jnp.zeros((2, slots), jnp.float32)]
    )
    sources = from_everyone(message, "row")
    targets = from_everyone(message, ("col", "gz"))
    tile = make_tile(sources, targets)

    zframe, up, down = whole_call(
        functools.partial(edge_kernel, True), (f32(*flat), bf16(480, 128), bf16(480, 128)), [], "edges", (),
        start, forcing, code, other,
    )
    low, high = both_ways(up, down, "col")
    vm = lambda shape: pltpu.VMEM(shape, jnp.float32)
    state, forcing, coef, zforcing, zcoef, density, up, down = whole_call(
        first_kernel,
        (f32(*initial_field.shape), f32(*frame), f32(*flat), f32(*flat), f32(*flat), bf16(bricks, channels, slots),
         bf16(channels * 3 * size_y, 128), bf16(channels * 3 * size_y, 128)),
        [vm(frame), vm(frame), vm(flat), vm(flat), vm(flat), vm(flat)], "first", (place, coefs),
        start, forcing, code, zframe, low, high, cells,
    )
    densities = lax.all_to_all(density, "row", 0, 0, tiled=True)
    shares = products(densities, tile, True)
    parts = lax.all_to_all(shares, ("col", "gz"), 0, 0, tiled=True)
    near, _ = whole_call(near_kernel, (f32(7, channels, slots), f32(channels, slots)), [], "near", (place,), parts, targets)
    near_low, near_high = both_ways(near, near, "row")

    low, high = both_ways(up, down, "row")
    start, depth = whole_call(
        functools.partial(frame_kernel, False), (f32(*frame), bf16(planes * size_y, 128)), [], "frame", (place,),
        state, low, high,
    )
    other = lax.ppermute(depth, "gz", [(0, 1), (1, 0)])
    zframe, up, down = whole_call(
        functools.partial(edge_kernel, False), (f32(*flat), bf16(288, 128), bf16(288, 128)), [], "edges", (),
        start, other,
    )
    low, high = both_ways(up, down, "col")
    state, density = whole_call(
        second_kernel, (f32(*initial_field.shape), bf16(bricks, channels, slots)),
        [vm(frame), vm(frame), vm(flat), vm(flat), vm(frame), vm(flat)], "second", (place,),
        start, forcing, coef, zforcing, zcoef, zframe, low, high, cells, near_low, near, near_high,
    )
    densities = lax.all_to_all(density, "row", 0, 0, tiled=True)
    shares = products(densities, tile, False)
    parts = lax.all_to_all(shares, ("col", "gz"), 0, 0, tiled=True)
    potential = whole_call(last_kernel, f32(channels, slots), [], "last", (place,), parts)
    return (state, potential)


def solution(mesh):
    placed = (
        P(None, "row", "col", "gz"),
        P(None, "row", "col", "gz"),
        P("row", "col", "gz"),
        P(),
        P(("row", "col", "gz")),
        P(("row", "col", "gz")),
        P(None, ("row", "col", "gz")),
    )
    return jax.shard_map(
        local,
        mesh=mesh,
        in_specs=placed,
        out_specs=(P(None, "row", "col", "gz"), P(None, ("row", "col", "gz"))),
        check_vma=False,
    )
```

time: 282 us -> 185 us (0.66)
  starting transfers between devices: 142 us -> 70.5 us
  other arithmetic: 20.9 us -> 2.76 us
  Pallas kernels: 38.9 us -> 54 us
  local copies, waits for them, and re-layouts: 23.9 us -> 14.5 us
  waiting for transfers between devices: 19.2 us -> 10.6 us
    ppermute x36 -> x12, starting transfers between devices: 109 us -> 32.7 us  [the longest x5 18.5 us: both_ways(): lax.ppermute(up, axis, pairs)]
    pallas_call x2 -> x11, Pallas kernels: 14.2 us -> 30.8 us  [the longest x9 16.4 us: whole_call(): pl.pallas_call(kernel, in_specs=[smem] * len(scalars) + [vmem] * len(oper...]
    add x7 -> x0, other arithmetic: 14.1 us -> none  [the longest x1 10.8 us: relax(): diagonal = 6.0 + shift_field]
    unnamed x12 -> x50, local copies, waits for them, and re-layouts: 2.23 us -> 13.8 us
    all_to_all x0 -> x1, starting transfers between devices: none -> 7.23 us  [local(): densities = lax.all_to_all(density, 'row', 0, 0, tiled=True)]
    ppermute x36 -> x12, waiting for transfers between devices: 17.2 us -> 10.5 us  [the longest x5 7.53 us: both_ways(): lax.ppermute(down, axis, [(b, a) for a, b in pairs])]
    all_to_all x3 -> x2, starting transfers between devices: 24.6 us -> 18.7 us  [from_everyone(): return lax.all_to_all(copies, axis, split_axis=0, concat_axis=0, tiled=True)]
    slice x19 -> x0, local copies, waits for them, and re-layouts: 5.86 us -> none  [the longest x7 2.74 us: padded_2(): initial = lax.slice_in_dim(x, 0, width, axis=dim)]
  transfers between devices with their start and end apart: 40 -> 16, of which waited for: 7 -> 4; matrix products, arithmetic and copies ran while one was open for 10% -> 2% of each run, Pallas kernels for 11% -> 17%
where the time goes in v2:
time: 185 us; the launch traced here: 184 us
  starting transfers between devices  70.5 us (38%)
  Pallas kernels  54 us (29%)
  blocking collectives  30 us (16%)
  local copies, waits for them, and re-layouts  14.5 us (8%)
  waiting for transfers between devices  10.6 us (6%)
  other arithmetic  2.76 us (1%)
    pallas_call x1, Pallas kernels, make_tile(): pl.pallas_call(tile_kernel, grid=(bricks,), in_specs=[pl.BlockSpec((1, ro...  23.2 us
    all_to_all x2, starting transfers between devices, from_everyone(): return lax.all_to_all(copies, axis, split_axis=0, concat_axis=0, tiled=True)  18.7 us
    ppermute x5, starting transfers between devices, both_ways(): lax.ppermute(up, axis, pairs)  18.5 us
    pallas_call x9, Pallas kernels, whole_call(): pl.pallas_call(kernel, in_specs=[smem] * len(scalars) + [vmem] * len(oper...  16.4 us
    all_to_all x1, blocking collectives, local(): densities = lax.all_to_all(density, 'row', 0, 0, tiled=True)  15.6 us
    all_to_all x1, blocking collectives, local(): parts = lax.all_to_all(shares, ('col', 'gz'), 0, 0, tiled=True)  14.4 us
    pallas_call x2, Pallas kernels, products(): pl.pallas_call(functools.partial(product_kernel, near), grid=(bricks // 2...  14.4 us
    unnamed x50, local copies, waits for them, and re-layouts  13.8 us
  transfers between devices with their start and end apart: 16, of which 4 were waited for; matrix products, arithmetic and copies ran while one was open for 2% of the time, Pallas kernels for 17%

profile of v2, /device:TPU:1, one launch (start us, length us, event | category | flops | bytes accessed | tf_op | source)
XLA Modules:
  0.0 183.8 jit_solution(8251729784720622380)
XLA Ops:
  1.6 0.9 copy-done.2
  3.3 4.9 %collective-permute-start = (bf16[672,128]{1,0:T(8,128)(2,1)S(1)}, bf16[672,128]{1,0:T(8,128)(2,1)S(1)}, u32[]{:S(2)}, u32[]{:S(2)}) collective-permute-start(bf16[672,128]{1,0:T(8,128)(2,1)S(1)} %get-tuple-element.27), channel_id=1, source_target_pairs={{0,16},{16,32},{32,48},{48,64},{64,80},{80,96},{96,112},{112,128},... | collective-permute-start | bytes 516104 | tf_op jit(solution)/shard_map/ppermute | solution.py:501
  8.3 1.9 %collective-permute-start.1 = (bf16[672,128]{1,0:T(8,128)(2,1)S(1)}, bf16[672,128]{1,0:T(8,128)(2,1)S(1)}, u32[]{:S(2)}, u32[]{:S(2)}) collective-permute-start(bf16[672,128]{1,0:T(8,128)(2,1)S(1)} %get-tuple-element.28), channel_id=1, source_target_pairs={{16,0},{32,16},{48,32},{64,48},{80,64},{96,80},{112,96},{128,112},... | collective-permute-start | bytes 516104 | tf_op jit(solution)/shard_map/ppermute | solution.py:501
  13.6 6.8 %all-to-all-start.2 = ((f32[16,8,128]{2,1,0:T(8,128)}), f32[16,8,128]{2,1,0:T(8,128)S(1)}, u32[]{:S(2)}, u32[]{:S(2)}) async-start(f32[16,8,128]{2,1,0:T(8,128)} %broadcast_in_dim.26), calls=%async_computation.2 | async-start | bytes 131072 | tf_op jit(solution)/shard_map/all_to_all | solution.py:124
  21.4 0.9 copy-done.3
  23.1 1.0 frame.2
  24.1 2.9 %collective-permute-start.2 = (bf16[160,128]{1,0:T(8,128)(2,1)S(1)}, bf16[160,128]{1,0:T(8,128)(2,1)S(1)}, u32[]{:S(2)}, u32[]{:S(2)}) collective-permute-start(bf16[160,128]{1,0:T(8,128)(2,1)S(1)} %get-tuple-element.32), channel_id=1, source_target_pairs={{0,1},{1,0},{2,3},{3,2},{4,5},{5,4},{6,7},{7,6},{8,9},{9,8},{10,11... | collective-permute-start | bytes 122888 | tf_op jit(solution)/shard_map/ppermute | solution.py:530
  27.1 1.5 collective-permute-done.2.refs_3_
  29.3 3.3 %collective-permute-start.3 = (bf16[480,128]{1,0:T(8,128)(2,1)S(1)}, bf16[480,128]{1,0:T(8,128)(2,1)S(1)}, u32[]{:S(2)}, u32[]{:S(2)}) collective-permute-start(bf16[480,128]{1,0:T(8,128)(2,1)S(1)} %get-tuple-element.34), channel_id=1, source_target_pairs={{0,2},{2,4},{4,6},{6,8},{8,10},{10,12},{12,14},{1,3},{3,5},{5,7},{... | collective-permute-start | bytes 368648 | tf_op jit(solution)/shard_map/ppermute | solution.py:501
  32.6 1.3 collective-permute-start.4
  33.9 11.9 %all-to-all-start.1 = ((f32[16,8,128]{2,1,0:T(8,128)}), f32[16,8,128]{2,1,0:T(8,128)}, u32[]{:S(2)}, u32[]{:S(2)}) async-start(f32[16,8,128]{2,1,0:T(8,128)} %broadcast_in_dim.26), calls=%async_computation.1 | async-start | bytes 131072 | tf_op jit(solution)/shard_map/all_to_all | solution.py:124
  51.1 5.6 %first.1 = (f32[8,4,16,128]{3,2,1,0:T(8,128)S(1)}, f32[1920,128]{1,0:T(8,128)S(1)}, f32[240,128]{1,0:T(8,128)S(1)}, f32[240,128]{1,0:T(8,128)S(1)}, f32[240,128]...) custom-call(s32[3]{0:T(128)S(1)} %pad_add_fusion.place_ref, ...), custom_call_target="tpu_custom_call" | custom-call | tf_op jit(solution)/shard_map/first/pallas_call | solution.py:147
  59.4 7.2 %all-to-all-start = ((bf16[16,8,128]{2,1,0:T(8,128)(2,1)}), bf16[16,8,128]{2,1,0:T(8,128)(2,1)S(1)}, u32[]{:S(2)}, u32[]{:S(2)}) async-start(bf16[16,8,128]{2,1,0:T(8,128)(2,1)} %get-tuple-element.48), calls=%async_computation | async-start | bytes 65536 | tf_op jit(solution)/shard_map/all_to_all | solution.py:554
  66.6 23.2 %tile.1.tile_ref = bf16[2048,2048]{1,0:T(8,128)(2,1)} custom-call(f32[16,8,128]{2,1,0:T(8,128)} %all-to-all-done.1.source_ref, f32[16,8,128]{2,1,0:T(8,128)} %copy-done.4), custom_call_target="tpu_custom_call" | custom-call | tf_op jit(solution)/shard_map/tile/pallas_call | solution.py:64
  90.4 7.3 %product.2 = f32[16,6,8,128]{3,2,1,0:T(8,128)} custom-call(bf16[16,8,128]{2,1,0:T(8,128)(2,1)} %copy-done.24, bf16[2048,2048]{1,0:T(8,128)(2,1)} %tile.1.tile_ref), custom_call_target="tpu_custom_call" | custom-call | tf_op jit(solution)/shard_map/product/pallas_call | solution.py:108
  97.7 11.9 %all-to-all-start.3 = ((f32[16,6,8,128]{3,2,1,0:T(8,128)}), f32[16,6,8,128]{3,2,1,0:T(8,128)S(1)}, u32[]{:S(2)}, u32[]{:S(2)}) async-start(f32[16,6,8,128]{3,2,1,0:T(8,128)} %product.2), calls=%async_computation.3 | async-start | bytes 786432 | tf_op jit(solution)/shard_map/all_to_all | solution.py:556
  109.6 3.8 %collective-permute-start.5 = (bf16[384,128]{1,0:T(8,128)(2,1)S(1)}, bf16[384,128]{1,0:T(8,128)(2,1)S(1)}, u32[]{:S(2)}, u32[]{:S(2)}) collective-permute-start(bf16[384,128]{1,0:T(8,128)(2,1)S(1)} %copy-done.23), channel_id=1, source_target_pairs={{0,16},{16,32},{32,48},{48,64},{64,80},{80,96},{96,112},{112,128},... | collective-permute-start | bytes 294920 | tf_op jit(solution)/shard_map/ppermute | solution.py:501
  113.4 1.9 %collective-permute-start.6 = (bf16[384,128]{1,0:T(8,128)(2,1)S(1)}, bf16[384,128]{1,0:T(8,128)(2,1)S(1)}, u32[]{:S(2)}, u32[]{:S(2)}) collective-permute-start(bf16[384,128]{1,0:T(8,128)(2,1)S(1)} %copy-done.21), channel_id=1, source_target_pairs={{16,0},{32,16},{48,32},{64,48},{80,64},{96,80},{112,96},{128,112},... | collective-permute-start | bytes 294920 | tf_op jit(solution)/shard_map/ppermute | solution.py:501
  115.3 4.3 %collective-permute-done.6.refs_2_ = bf16[384,128]{1,0:T(8,128)(2,1)S(1)} collective-permute-done((bf16[384,128]{1,0:T(8,128)(2,1)S(1)}, bf16[384,128]{1,0:T(8,128)(2,1)S(1)}, u32[]{:S(2)}, u32[]{:S(2)}) %collective-permute-start.6) | collective-permute-done | bytes 98336 | tf_op jit(solution)/shard_map/ppermute | solution.py:501
  120.4 2.9 %collective-permute-start.7 = (bf16[160,128]{1,0:T(8,128)(2,1)S(1)}, bf16[160,128]{1,0:T(8,128)(2,1)S(1)}, u32[]{:S(2)}, u32[]{:S(2)}) collective-permute-start(bf16[160,128]{1,0:T(8,128)(2,1)S(1)} %get-tuple-element.44), channel_id=1, source_target_pairs={{0,1},{1,0},{2,3},{3,2},{4,5},{5,4},{6,7},{7,6},{8,9},{9,8},{10,11... | collective-permute-start | bytes 122888 | tf_op jit(solution)/shard_map/ppermute | solution.py:565
  123.4 1.5 collective-permute-done.7.refs_1_
  124.9 3.3 %collective-permute-start.8 = (bf16[288,128]{1,0:T(8,128)(2,1)S(1)}, bf16[288,128]{1,0:T(8,128)(2,1)S(1)}, u32[]{:S(2)}, u32[]{:S(2)}) collective-permute-start(bf16[288,128]{1,0:T(8,128)(2,1)S(1)} %get-tuple-element.46), channel_id=1, source_target_pairs={{0,2},{2,4},{4,6},{6,8},{8,10},{10,12},{12,14},{1,3},{3,5},{5,7},{... | collective-permute-start | bytes 221192 | tf_op jit(solution)/shard_map/ppermute | solution.py:501
  128.2 1.3 collective-permute-start.9
  129.5 1.2 near.1
  130.7 3.2 %collective-permute-start.10 = (f32[7,8,128]{2,1,0:T(8,128)S(1)}, f32[7,8,128]{2,1,0:T(8,128)S(1)}, u32[]{:S(2)}, u32[]{:S(2)}) collective-permute-start(f32[7,8,128]{2,1,0:T(8,128)S(1)} %get-tuple-element.49.near_own), channel_id=1, source_target_pairs={{0,16},{16,32},{32,48},{48,64},{64,80},{80,96},{96,112},{112,128},... | collective-permute-start | bytes 86024 | tf_op jit(solution)/shard_map/ppermute | solution.py:501
  133.9 1.9 %collective-permute-start.11 = (f32[7,8,128]{2,1,0:T(8,128)S(1)}, f32[7,8,128]{2,1,0:T(8,128)S(1)}, u32[]{:S(2)}, u32[]{:S(2)}) collective-permute-start(f32[7,8,128]{2,1,0:T(8,128)S(1)} %get-tuple-element.49.near_own), channel_id=1, source_target_pairs={{16,0},{32,16},{48,32},{64,48},{80,64},{96,80},{112,96},{128,112},... | collective-permute-start | bytes 86024 | tf_op jit(solution)/shard_map/ppermute | solution.py:501
  135.9 3.2 %collective-permute-done.11.near_high = f32[7,8,128]{2,1,0:T(8,128)S(1)} collective-permute-done((f32[7,8,128]{2,1,0:T(8,128)S(1)}, f32[7,8,128]{2,1,0:T(8,128)S(1)}, u32[]{:S(2)}, u32[]{:S(2)}) %collective-permute-start.11) | collective-permute-done | bytes 28704 | tf_op jit(solution)/shard_map/ppermute | solution.py:501
  139.1 6.5 %second.1 = (f32[8,4,16,128]{3,2,1,0:T(8,128)}, bf16[16,8,128]{2,1,0:T(8,128)(2,1)S(1)}) custom-call(s32[3]{0:T(128)S(1)} %pad_add_fusion.place_ref, f32[1920,128]{1,0:T(8,128)S(1)} %get-tuple-element.39.refs_0_.frame_ref, f32[1920,128]{1,0:T(8,128)S(1)} %get-tuple-element.40.forcing_ref, f32[240,128]{1,0:T(8,128)S(1)} %get-tuple-element.41.coef_ref, ...), custom_call_target="tpu_custom_call" | custom-call | tf_op jit(solution)/shard_map/second/pallas_call | solution.py:147
  145.6 15.6 %all_to_all.30.density_ref = bf16[16,8,128]{2,1,0:T(8,128)(2,1)} all-to-all(bf16[16,8,128]{2,1,0:T(8,128)(2,1)S(1)} %get-tuple-element.51), channel_id=1, replica_groups=mesh['row'=16,'col'=8,'gz'=2] {'row'}, dimensions={0} | all-to-all | bytes 65536 | tf_op jit(solution)/shard_map/all_to_all | solution.py:576
  161.2 7.1 %product.3 = f32[16,8,128]{2,1,0:T(8,128)} custom-call(bf16[16,8,128]{2,1,0:T(8,128)(2,1)} %all_to_all.30.density_ref, bf16[2048,2048]{1,0:T(8,128)(2,1)} %tile.1.tile_ref), custom_call_target="tpu_custom_call" | custom-call | tf_op jit(solution)/shard_map/product/pallas_call | solution.py:108
  168.3 14.4 %all_to_all.31.parts_ref = f32[16,8,128]{2,1,0:T(8,128)S(1)} all-to-all(f32[16,8,128]{2,1,0:T(8,128)} %product.3), channel_id=1, replica_groups=mesh['row'=16,'col'=8,'gz'=2] {'col','gz'}, dimensions={0} | all-to-all | bytes 131072 | tf_op jit(solution)/shard_map/all_to_all | solution.py:578
  182.7 1.1 last.1
  (73 shorter events, 16.4 us)
Async XLA Ops:
  0.6 1.0 copy-start
  1.6 0.9 copy-start.2
  2.5 0.8 copy-start.6
  3.3 17.1 %collective-permute-start = (bf16[672,128]{1,0:T(8,128)(2,1)S(1)}, bf16[672,128]{1,0:T(8,128)(2,1)S(1)}, u32[]{:S(2)}, u32[]{:S(2)}) collective-permute-start(bf16[672,128]{1,0:T(8,128)(2,1)S(1)} %get-tuple-element.27), channel_id=1, source_target_pairs={{0,16},{16,32},{32,48},{48,64},{64,80},{80,96},{96,112},{112,128},... | collective-permute-start | bytes 516104 | tf_op jit(solution)/shard_map/ppermute | solution.py:501
  8.3 12.1 %collective-permute-start.1 = (bf16[672,128]{1,0:T(8,128)(2,1)S(1)}, bf16[672,128]{1,0:T(8,128)(2,1)S(1)}, u32[]{:S(2)}, u32[]{:S(2)}) collective-permute-start(bf16[672,128]{1,0:T(8,128)(2,1)S(1)} %get-tuple-element.28), channel_id=1, source_target_pairs={{16,0},{32,16},{48,32},{64,48},{80,64},{96,80},{112,96},{128,112},... | collective-permute-start | bytes 516104 | tf_op jit(solution)/shard_map/ppermute | solution.py:501
  13.6 20.3 %all-to-all-start.2 = ((f32[16,8,128]{2,1,0:T(8,128)}), f32[16,8,128]{2,1,0:T(8,128)S(1)}, u32[]{:S(2)}, u32[]{:S(2)}) async-start(f32[16,8,128]{2,1,0:T(8,128)} %broadcast_in_dim.26), calls=%async_computation.2 | async-start | bytes 131072 | tf_op jit(solution)/shard_map/all_to_all | solution.py:124
  20.4 1.0 copy-start.1
  21.4 0.9 copy-start.3
  22.3 0.8 copy-start.7
  24.1 4.4 %collective-permute-start.2 = (bf16[160,128]{1,0:T(8,128)(2,1)S(1)}, bf16[160,128]{1,0:T(8,128)(2,1)S(1)}, u32[]{:S(2)}, u32[]{:S(2)}) collective-permute-start(bf16[160,128]{1,0:T(8,128)(2,1)S(1)} %get-tuple-element.32), channel_id=1, source_target_pairs={{0,1},{1,0},{2,3},{3,2},{4,5},{5,4},{6,7},{7,6},{8,9},{9,8},{10,11... | collective-permute-start | bytes 122888 | tf_op jit(solution)/shard_map/ppermute | solution.py:530
  29.3 17.1 %collective-permute-start.3 = (bf16[480,128]{1,0:T(8,128)(2,1)S(1)}, bf16[480,128]{1,0:T(8,128)(2,1)S(1)}, u32[]{:S(2)}, u32[]{:S(2)}) collective-permute-start(bf16[480,128]{1,0:T(8,128)(2,1)S(1)} %get-tuple-element.34), channel_id=1, source_target_pairs={{0,2},{2,4},{4,6},{6,8},{8,10},{10,12},{12,14},{1,3},{3,5},{5,7},{... | collective-permute-start | bytes 368648 | tf_op jit(solution)/shard_map/ppermute | solution.py:501
  32.6 14.5 %collective-permute-start.4 = (bf16[480,128]{1,0:T(8,128)(2,1)S(1)}, bf16[480,128]{1,0:T(8,128)(2,1)S(1)}, u32[]{:S(2)}, u32[]{:S(2)}) collective-permute-start(bf16[480,128]{1,0:T(8,128)(2,1)S(1)} %get-tuple-element.35), channel_id=1, source_target_pairs={{2,0},{4,2},{6,4},{8,6},{10,8},{12,10},{14,12},{3,1},{5,3},{7,5},{... | collective-permute-start | bytes 368648 | tf_op jit(solution)/shard_map/ppermute | solution.py:501
  33.9 32.7 %copy-start.4 = (f32[16,8,128]{2,1,0:T(8,128)}, f32[16,8,128]{2,1,0:T(8,128)S(1)}, u32[]{:S(2)}) copy-start(f32[16,8,128]{2,1,0:T(8,128)S(1)} %all-to-all-done.2.target_ref.targets_ref) | copy-start | bytes 196612
  33.9 25.5 %all-to-all-start.1 = ((f32[16,8,128]{2,1,0:T(8,128)}), f32[16,8,128]{2,1,0:T(8,128)}, u32[]{:S(2)}, u32[]{:S(2)}) async-start(f32[16,8,128]{2,1,0:T(8,128)} %broadcast_in_dim.26), calls=%async_computation.1 | async-start | bytes 131072 | tf_op jit(solution)/shard_map/all_to_all | solution.py:124
  47.8 0.9 copy-start.13
  48.7 0.9 copy-start.15
  49.6 0.9 copy-start.17
  59.4 30.5 %all-to-all-start = ((bf16[16,8,128]{2,1,0:T(8,128)(2,1)}), bf16[16,8,128]{2,1,0:T(8,128)(2,1)S(1)}, u32[]{:S(2)}, u32[]{:S(2)}) async-start(bf16[16,8,128]{2,1,0:T(8,128)(2,1)} %get-tuple-element.48), calls=%async_computation | async-start | bytes 65536 | tf_op jit(solution)/shard_map/all_to_all | solution.py:554
  66.6 43.0 %copy-start.23 = (bf16[384,128]{1,0:T(8,128)(2,1)S(1)}, bf16[384,128]{1,0:T(8,128)(2,1)}, u32[]{:S(2)}) copy-start(bf16[384,128]{1,0:T(8,128)(2,1)} %copy-done.22) | copy-start | bytes 294916
  66.6 46.8 %copy-start.21 = (bf16[384,128]{1,0:T(8,128)(2,1)S(1)}, bf16[384,128]{1,0:T(8,128)(2,1)}, u32[]{:S(2)}) copy-start(bf16[384,128]{1,0:T(8,128)(2,1)} %copy-done.20) | copy-start | bytes 294916
  66.6 72.5 %copy-start.9 = (f32[240,128]{1,0:T(8,128)S(1)}, f32[240,128]{1,0:T(8,128)}, u32[]{:S(2)}) copy-start(f32[240,128]{1,0:T(8,128)} %copy-done.8) | copy-start | bytes 368644
  66.6 72.5 %copy-start.11 = (f32[240,128]{1,0:T(8,128)S(1)}, f32[240,128]{1,0:T(8,128)}, u32[]{:S(2)}) copy-start(f32[240,128]{1,0:T(8,128)} %copy-done.10) | copy-start | bytes 368644
  66.6 72.5 %copy-start.19 = (s32[128]{0:T(128)S(1)}, s32[128]{0:T(128)}, u32[]{:S(2)}) copy-start(s32[128]{0:T(128)} %param.11) | copy-start | bytes 1540
  89.8 39.7 %copy-start.5 = (f32[16,8,128]{2,1,0:T(8,128)S(1)}, f32[16,8,128]{2,1,0:T(8,128)}, u32[]{:S(2)}) copy-start(f32[16,8,128]{2,1,0:T(8,128)} %copy-done.4) | copy-start | bytes 196612
  97.7 31.8 %all-to-all-start.3 = ((f32[16,6,8,128]{3,2,1,0:T(8,128)}), f32[16,6,8,128]{3,2,1,0:T(8,128)S(1)}, u32[]{:S(2)}, u32[]{:S(2)}) async-start(f32[16,6,8,128]{3,2,1,0:T(8,128)} %product.2), calls=%async_computation.3 | async-start | bytes 786432 | tf_op jit(solution)/shard_map/all_to_all | solution.py:556
  109.6 5.7 %collective-permute-start.5 = (bf16[384,128]{1,0:T(8,128)(2,1)S(1)}, bf16[384,128]{1,0:T(8,128)(2,1)S(1)}, u32[]{:S(2)}, u32[]{:S(2)}) collective-permute-start(bf16[384,128]{1,0:T(8,128)(2,1)S(1)} %copy-done.23), channel_id=1, source_target_pairs={{0,16},{16,32},{32,48},{48,64},{64,80},{80,96},{96,112},{112,128},... | collective-permute-start | bytes 294920 | tf_op jit(solution)/shard_map/ppermute | solution.py:501
  113.4 6.2 %collective-permute-start.6 = (bf16[384,128]{1,0:T(8,128)(2,1)S(1)}, bf16[384,128]{1,0:T(8,128)(2,1)S(1)}, u32[]{:S(2)}, u32[]{:S(2)}) collective-permute-start(bf16[384,128]{1,0:T(8,128)(2,1)S(1)} %copy-done.21), channel_id=1, source_target_pairs={{16,0},{32,16},{48,32},{64,48},{80,64},{96,80},{112,96},{128,112},... | collective-permute-start | bytes 294920 | tf_op jit(solution)/shard_map/ppermute | solution.py:501
  120.4 4.4 %collective-permute-start.7 = (bf16[160,128]{1,0:T(8,128)(2,1)S(1)}, bf16[160,128]{1,0:T(8,128)(2,1)S(1)}, u32[]{:S(2)}, u32[]{:S(2)}) collective-permute-start(bf16[160,128]{1,0:T(8,128)(2,1)S(1)} %get-tuple-element.44), channel_id=1, source_target_pairs={{0,1},{1,0},{2,3},{3,2},{4,5},{5,4},{6,7},{7,6},{8,9},{9,8},{10,11... | collective-permute-start | bytes 122888 | tf_op jit(solution)/shard_map/ppermute | solution.py:565
  124.9 10.9 %collective-permute-start.8 = (bf16[288,128]{1,0:T(8,128)(2,1)S(1)}, bf16[288,128]{1,0:T(8,128)(2,1)S(1)}, u32[]{:S(2)}, u32[]{:S(2)}) collective-permute-start(bf16[288,128]{1,0:T(8,128)(2,1)S(1)} %get-tuple-element.46), channel_id=1, source_target_pairs={{0,2},{2,4},{4,6},{6,8},{8,10},{10,12},{12,14},{1,3},{3,5},{5,7},{... | collective-permute-start | bytes 221192 | tf_op jit(solution)/shard_map/ppermute | solution.py:501
  128.2 7.7 %collective-permute-start.9 = (bf16[288,128]{1,0:T(8,128)(2,1)S(1)}, bf16[288,128]{1,0:T(8,128)(2,1)S(1)}, u32[]{:S(2)}, u32[]{:S(2)}) collective-permute-start(bf16[288,128]{1,0:T(8,128)(2,1)S(1)} %get-tuple-element.47), channel_id=1, source_target_pairs={{2,0},{4,2},{6,4},{8,6},{10,8},{12,10},{14,12},{3,1},{5,3},{7,5},{... | collective-permute-start | bytes 221192 | tf_op jit(solution)/shard_map/ppermute | solution.py:501
  130.7 5.2 %collective-permute-start.10 = (f32[7,8,128]{2,1,0:T(8,128)S(1)}, f32[7,8,128]{2,1,0:T(8,128)S(1)}, u32[]{:S(2)}, u32[]{:S(2)}) collective-permute-start(f32[7,8,128]{2,1,0:T(8,128)S(1)} %get-tuple-element.49.near_own), channel_id=1, source_target_pairs={{0,16},{16,32},{32,48},{48,64},{64,80},{80,96},{96,112},{112,128},... | collective-permute-start | bytes 86024 | tf_op jit(solution)/shard_map/ppermute | solution.py:501
  133.9 5.2 %collective-permute-start.11 = (f32[7,8,128]{2,1,0:T(8,128)S(1)}, f32[7,8,128]{2,1,0:T(8,128)S(1)}, u32[]{:S(2)}, u32[]{:S(2)}) collective-permute-start(f32[7,8,128]{2,1,0:T(8,128)S(1)} %get-tuple-element.49.near_own), channel_id=1, source_target_pairs={{16,0},{32,16},{48,32},{64,48},{80,64},{96,80},{112,96},{128,112},... | collective-permute-start | bytes 86024 | tf_op jit(solution)/shard_map/ppermute | solution.py:501
  (9 other events, 5.8 us)

commit v3 on v2

--- a/solution.py
+++ b/solution.py
@@ -9,6 +9,7 @@
 from jax.sharding import PartitionSpec as P
 
 SIZE_Y = 16
+ROOM = 8
 
 relax_weight = 0.8
 wave_number = 25.0
@@ -20,105 +21,6 @@
 ROUNDER = 12582912.0
 
 
-def tile_kernel(source_ref, target_ref, out_ref, columns):
-    bricks, slots = target_ref.shape[0], target_ref.shape[2]
-    live = jnp.max(source_ref[0, 4:5, :]).astype(jnp.int32)
-    columns[...] = jnp.transpose(source_ref[0])
-    steps = (live + 15) // 16
-
-    def fill(step, carry):
-        rows = pl.ds(pl.multiple_of(step * 16, 16), 16)
-        here = columns[rows, :]
-        spread = [jnp.broadcast_to(here[:, d : d + 1], (16, slots)) for d in range(4)]
-        for brick in range(bricks):
-            square = 1e-30
-            for d in range(3):
-                delta = target_ref[brick, d : d + 1, :] - spread[d]
-                square = square + delta * delta
-            turns = square * lax.rsqrt(square)
-            whole = (turns + ROUNDER) - ROUNDER
-            angle = 0.25 - jnp.abs(turns - whole)
-            angle2 = angle * angle
-            wave = SINE[4]
-            for c in SINE[3::-1]:
-                wave = wave * angle2 + c
-            below = turns + soften * TURNS
-            guess = pl.reciprocal(below, approx=True)
-            value = (angle * spread[3]) * (guess * (2.0 - below * guess)) * wave
-            out_ref[rows, brick * slots : (brick + 1) * slots] = value.astype(jnp.bfloat16)
-        return carry
-
-    lax.fori_loop(0, steps, fill, 0)
-
-    def clear(step, carry):
-        rows = pl.ds(pl.multiple_of(step * 16, 16), 16)
-        out_ref[rows, :] = jnp.zeros((16, out_ref.shape[1]), jnp.bfloat16)
-        return carry
-
-    lax.fori_loop(steps, slots // 16, clear, 0)
-
-
-def make_tile(sources, targets):
-    bricks, rows, slots = sources.shape
-    width = targets.shape[0] * slots
-    return pl.pallas_call(
-        tile_kernel,
-        grid=(bricks,),
-        in_specs=[
-            pl.BlockSpec((1, rows, slots), lambda b: (b, 0, 0)),
-            pl.BlockSpec(targets.shape, lambda b: (0, 0, 0)),
-        ],
-        out_specs=pl.BlockSpec((slots, width), lambda b: (b, 0)),
-        out_shape=jax.ShapeDtypeStruct((bricks * slots, width), jnp.bfloat16),
-        scratch_shapes=[pltpu.VMEM((slots, rows), jnp.float32)],
-        name="tile",
-    )(sources, targets)
-
-
-def product_kernel(near, density_ref, tile_ref, out_ref, total):
-    step = pl.program_id(0)
-
-    @pl.when(step == 0)
-    def _():
-        total[...] = jnp.zeros_like(total)
-
-    values = jnp.concatenate([density_ref[0], density_ref[1]], axis=1)
-    total[...] += jnp.dot(values, tile_ref[...], preferred_element_type=jnp.float32)
-
-    @pl.when(step == pl.num_programs(0) - 1)
-    def _():
-        bricks, slots = out_ref.shape[0], out_ref.shape[-1]
-        for brick in range(bricks):
-            if not near:
-                out_ref[brick] = total[:, brick * slots : (brick + 1) * slots]
-                continue
-            for n in range(6):
-                side, half = brick // 2 + n % 3 - 1, (brick + n // 3) % 2
-                other = side * 2 + half
-                if 0 <= side < bricks // 2:
-                    out_ref[brick, n] = total[:, other * slots : (other + 1) * slots]
-                else:
-                    out_ref[brick, n] = jnp.zeros((total.shape[0], slots), jnp.float32)
-
-
-def products(densities, tile, near):
-    bricks, channels, slots = densities.shape
-    width = tile.shape[1]
-    shape = (width // slots, 6, channels, slots) if near else (width // slots, channels, slots)
-    return pl.pallas_call(
-        functools.partial(product_kernel, near),
-        grid=(bricks // 2,),
-        in_specs=[
-            pl.BlockSpec((2, channels, slots), lambda b: (b, 0, 0)),
-            pl.BlockSpec((2 * slots, width), lambda b: (b, 0)),
-        ],
-        out_specs=pl.BlockSpec(shape, lambda b: (0,) * len(shape)),
-        out_shape=jax.ShapeDtypeStruct(shape, jnp.float32),
-        scratch_shapes=[pltpu.VMEM((channels, width), jnp.float32)],
-        name="product",
-    )(densities, tile)
-
-
 def from_everyone(x, axis):
     copies = jnp.broadcast_to(x, (lax.axis_size(axis), *x.shape))
     return lax.all_to_all(copies, axis, split_axis=0, concat_axis=0, tiled=True)
@@ -137,20 +39,22 @@
     return pltpu.roll(x, shift % x.shape[-1], x.ndim - 1)
 
 
-def params(megabytes=24):
+def params(megabytes):
     return pltpu.CompilerParams(vmem_limit_bytes=megabytes << 20)
 
 
-def whole_call(kernel, out_shape, scratch, name, scalars, *operands):
+def whole_call(kernel, out_shape, scratch, name, scalars, *operands, megabytes=4, away=(), aliases={}):
     smem = pl.BlockSpec(memory_space=pltpu.SMEM)
     vmem = pl.BlockSpec(memory_space=pltpu.VMEM)
+    far = pl.BlockSpec(memory_space=pltpu.HBM)
     return pl.pallas_call(
         kernel,
-        in_specs=[smem] * len(scalars) + [vmem] * len(operands),
+        in_specs=[smem] * len(scalars) + [far if n in away else vmem for n in range(len(operands))],
         out_specs=jax.tree.map(lambda _: vmem, out_shape),
         out_shape=out_shape,
         scratch_shapes=scratch,
-        compiler_params=params(),
+        compiler_params=params(megabytes),
+        input_output_aliases={len(scalars) + k: v for k, v in aliases.items()},
         name=name,
     )(*scalars, *operands)
 
@@ -161,6 +65,207 @@
 
 def bf16(*shape):
     return jax.ShapeDtypeStruct(shape, jnp.bfloat16)
+
+
+def split(x):
+    high = x.astype(jnp.bfloat16)
+    return high, (x - high.astype(jnp.float32)).astype(jnp.bfloat16)
+
+
+def across(a, b):
+    return lax.dot_general(a, b, (((1,), (1,)), ((), ())), preferred_element_type=jnp.float32)
+
+
+def compact_kernel(message_ref, target_ref, source_out, target_out, table_ref, counts, table, arrived):
+    bricks, depth, slots = message_ref.shape
+    channels = depth // 2
+    lane = lanes((8, slots))
+    first = jnp.zeros((8, slots), jnp.float32)
+    for brick in range(bricks):
+        first = jnp.where(lane == brick, message_ref[brick, channels + 4 : channels + 5, :], first)
+        first = jnp.where(lane == bricks + brick, target_ref[brick, 4:5, :], first)
+    counts[...] = first.astype(jnp.int32)
+    copy = pltpu.make_async_copy(counts, table, arrived)
+    copy.start()
+    source_out[...] = jnp.zeros_like(source_out)
+    target_out[...] = jnp.zeros_like(target_out)
+    copy.wait()
+    begin = [jnp.int32(0), jnp.int32(0)]
+    for brick in range(bricks):
+        for which, ref, out in ((0, message_ref, source_out), (1, target_ref, target_out)):
+            count = table[0, which * bricks + brick]
+            append(out, ref[brick], begin[which], count)
+            table_ref[which, brick] = begin[which]
+            begin[which] = begin[which] + count
+    table_ref[0, bricks] = begin[0]
+    table_ref[1, bricks] = begin[1]
+
+
+def append(out, rows, begin, count):
+    group, shift = begin >> 7, begin & 127
+    lane = lanes(rows.shape)
+    moved = pltpu.roll(rows, shift, 1)
+    out[group] = jnp.where((lane >= shift) & (lane < shift + count), moved, out[group])
+    out[group + 1] = jnp.where(lane < shift + count - rows.shape[1], moved, out[group + 1])
+
+
+def tile_kernel(half, table_ref, source_ref, target_ref, *refs):
+    tile_ref, share_ref, columns, density = refs[-4:]
+    bricks, slots = source_ref.shape[0] - 1, source_ref.shape[2]
+    channels = share_ref.shape[1]
+    step = pl.program_id(0)
+    pairs = (table_ref[0, bricks] + (2 * slots - 1)) >> 8
+
+    @pl.when(step == 0)
+    def _():
+        for group in range(bricks):
+            density[:, group * slots : (group + 1) * slots] = source_ref[group, :channels].astype(jnp.bfloat16)
+
+    @pl.when((2 * step + half) * slots < table_ref[1, bricks])
+    def _():
+        columns[...] = jnp.transpose(target_ref[0])
+        spread = [jnp.broadcast_to(columns[:, d : d + 1], (slots, slots)) for d in range(3)]
+
+        def one_pair(pair, total):
+            both = []
+            for index in range(2):
+                here = source_ref.at[2 * pair + index]
+                square = 1e-30
+                for d in range(3):
+                    delta = spread[d] - here[channels + d : channels + d + 1, :]
+                    square = square + delta * delta
+                turns = square * lax.rsqrt(square)
+                whole = (turns + ROUNDER) - ROUNDER
+                angle = 0.25 - jnp.abs(turns - whole)
+                angle2 = angle * angle
+                wave = SINE[4]
+                for c in SINE[3::-1]:
+                    wave = wave * angle2 + c
+                weight = here[channels + 3 : channels + 4, :]
+                value = (angle * weight) * wave / (turns + soften * TURNS)
+                both.append(value.astype(jnp.bfloat16))
+            values = jnp.concatenate(both, axis=1)
+            at = pl.ds(pl.multiple_of(pair * 2 * slots, 2 * slots), 2 * slots)
+            tile_ref[:, at] = values
+            return total + across(density[:, at], values)
+
+        share_ref[0] = lax.fori_loop(0, pairs, one_pair, jnp.zeros((channels, slots), jnp.float32))
+
+        def clear(pair, carry):
+            at = pl.ds(pl.multiple_of(pair * 2 * slots, 2 * slots), 2 * slots)
+            tile_ref[:, at] = jnp.zeros((slots, 2 * slots), jnp.bfloat16)
+            return carry
+
+        lax.fori_loop(pairs, bricks // 2, clear, 0)
+
+
+def make_tile(half, table, sources, targets, channels, before=()):
+    bricks, slots = sources.shape[0] - 1, sources.shape[2]
+    far = pl.BlockSpec(memory_space=pl.ANY)
+    return pl.pallas_call(
+        functools.partial(tile_kernel, half),
+        grid=(bricks // 2,),
+        in_specs=[
+            pl.BlockSpec(memory_space=pltpu.SMEM),
+            pl.BlockSpec(sources.shape, lambda b: (0, 0, 0)),
+            pl.BlockSpec((1, targets.shape[1], slots), lambda b: (2 * b + half, 0, 0)),
+        ]
+        + [far] * len(before),
+        out_specs=[
+            pl.BlockSpec((slots, bricks * slots), lambda b: (2 * b + half, 0)),
+            pl.BlockSpec((1, channels, slots), lambda b: (2 * b + half, 0, 0)),
+        ],
+        out_shape=[
+            jax.ShapeDtypeStruct((ROOM * bricks * slots, bricks * slots), jnp.bfloat16),
+            jax.ShapeDtypeStruct((bricks, channels, slots), jnp.float32),
+        ],
+        scratch_shapes=[
+            pltpu.VMEM((slots, targets.shape[1]), jnp.float32),
+            pltpu.VMEM((channels, bricks * slots), jnp.bfloat16),
+        ],
+        input_output_aliases={3 + n: n for n in range(len(before))},
+        compiler_params=params(8),
+        name="tile",
+    )(table, sources, targets, *before)
+
+
+def taken(share_ref, table_ref, brick, bricks):
+    begin = table_ref[1, brick]
+    count = table_ref[1, brick + 1] - begin
+    group, shift = begin >> 7, begin & 127
+    lane = lanes(share_ref.shape[1:])
+    slots = share_ref.shape[2]
+    this = pltpu.roll(share_ref[group], (slots - shift) & 127, 1)
+    following = pltpu.roll(share_ref[jnp.minimum(group + 1, bricks - 1)], (slots - shift) & 127, 1)
+    return jnp.where(lane < count, jnp.where(lane < slots - shift, this, following), 0.0)
+
+
+def arrange_kernel(table_ref, share_ref, out_ref):
+    bricks = out_ref.shape[0]
+    for index in range(bricks):
+        value = taken(share_ref, table_ref, index, bricks)
+        for n in range(6):
+            side, other = index // 2 - (n % 3 - 1), (index + n // 3) % 2
+            if 0 <= side < bricks // 2:
+                out_ref[side * 2 + other, n] = value
+    for brick in range(bricks):
+        for n in range(6):
+            if not 0 <= brick // 2 + n % 3 - 1 < bricks // 2:
+                out_ref[brick, n] = jnp.zeros(out_ref.shape[2:], jnp.float32)
+
+
+def product_kernel(table_ref, density_ref, tile_ref, out_ref, sources, density, shares):
+    bricks, channels, slots = density_ref.shape
+    step = pl.program_id(0)
+    count = tile_ref.shape[0] // slots
+
+    @pl.when(step == 0)
+    def _():
+        sources[...] = jnp.zeros_like(sources)
+        for brick in range(bricks):
+            begin = table_ref[0, brick]
+            append(sources, density_ref[brick].astype(jnp.float32), begin, table_ref[0, brick + 1] - begin)
+        for group in range(bricks):
+            density[:, group * slots : (group + 1) * slots] = sources[group].astype(jnp.bfloat16)
+
+    @pl.when(step * count * slots < table_ref[1, bricks])
+    def _():
+        total = across(density[...], tile_ref[...])
+        for index in range(count):
+            shares[step * count + index] = total[:, index * slots : (index + 1) * slots]
+
+    @pl.when(step == pl.num_programs(0) - 1)
+    def _():
+        for brick in range(bricks):
+            out_ref[brick] = taken(shares, table_ref, brick, bricks)
+
+
+def products(table, density, tile, rows):
+    bricks, channels, slots = density.shape
+    width = tile.shape[1]
+    steps = bricks * slots // rows
+
+    def block(b, table_ref):
+        last = (table_ref[1, bricks] + rows - 1) // rows - 1
+        return jnp.minimum(b, last), 0
+
+    return pl.pallas_call(
+        product_kernel,
+        grid_spec=pltpu.PrefetchScalarGridSpec(
+            num_scalar_prefetch=1,
+            grid=(steps,),
+            in_specs=[pl.BlockSpec(density.shape, lambda b, t: (0, 0, 0)), pl.BlockSpec((rows, width), block)],
+            out_specs=pl.BlockSpec((bricks, channels, slots), lambda b, t: (0, 0, 0)),
+            scratch_shapes=[
+                pltpu.VMEM((bricks + 1, channels, slots), jnp.float32),
+                pltpu.VMEM((channels, width), jnp.bfloat16),
+                pltpu.VMEM((bricks, channels, slots), jnp.float32),
+            ],
+        ),
+        out_shape=jax.ShapeDtypeStruct((bricks, channels, slots), jnp.float32),
+        compiler_params=params(12),
+        name="product",
+    )(table, density, tile)
 
 
 def put_planes(up_ref, down_ref, base, field_ref, depth, offset=0):
@@ -175,13 +280,7 @@
     return base + field_ref.shape[0] * depth * size_y
 
 
-def planes_kernel(state_ref, source_ref, class_ref, up_ref, down_ref):
-    base = put_planes(up_ref, down_ref, 0, state_ref, 3)
-    base = put_planes(up_ref, down_ref, base, source_ref, 2)
-    put_planes(up_ref, down_ref, base, class_ref, 2, 1.0)
-
-
-def framed(frame_ref, field_ref, low_ref, high_ref, base, depth, offset=0):
+def own_cells(frame_ref, field_ref, offset=0):
     channels, size_x, size_y = field_ref.shape[:3]
     planes, rows = size_x + 2 * XO, size_y + 2 * YO
     frame_ref[...] = jnp.zeros_like(frame_ref)
@@ -189,13 +288,54 @@
         for x in range(size_x):
             at = (e * planes + XO + x) * rows + YO
             frame_ref[at : at + size_y, :] = field_ref[e, x].astype(jnp.float32) + offset
+
+
+def planes_kernel(
+    factor, live_ref, state_hbm, source_hbm, class_hbm, geometry_ref, cell_ref,
+    up_ref, down_ref, frame_ref, forcing_ref, code_ref, message_ref, state_ref, source_ref, class_ref, arrived,
+):
+    copies = [
+        pltpu.make_async_copy(state_hbm, state_ref, arrived.at[0]),
+        pltpu.make_async_copy(source_hbm, source_ref, arrived.at[1]),
+        pltpu.make_async_copy(class_hbm, class_ref, arrived.at[2]),
+    ]
+    for copy in copies:
+        copy.start()
+    slots = cell_ref.shape[1]
+    message = jnp.concatenate(
+        [
+            geometry_ref[:3] * TURNS,
+            geometry_ref[3:] * (factor * TURNS),
+            jnp.full((1, slots), live_ref[0], jnp.int32).astype(jnp.float32),
+            cell_ref[...].astype(jnp.float32),
+            jnp.zeros((2, slots), jnp.float32),
+        ],
+        axis=0,
+    )
+    for brick in range(message_ref.shape[0]):
+        message_ref[brick] = message
+    for copy in copies:
+        copy.wait()
+    base = put_planes(up_ref, down_ref, 0, state_ref, 3)
+    base = put_planes(up_ref, down_ref, base, source_ref, 2)
+    put_planes(up_ref, down_ref, base, class_ref, 2, 1.0)
+    own_cells(frame_ref, state_ref)
+    own_cells(forcing_ref, source_ref)
+    own_cells(code_ref, class_ref, 1.0)
+
+
+def beside(frame_ref, channels, low_ref, high_ref, base, depth):
+    rows = SIZE_Y + 2 * YO
+    planes = frame_ref.shape[0] // (channels * rows)
+    size_x = planes - 2 * XO
+    for e in range(channels):
         for i in range(depth):
-            here = pl.ds(base + (e * depth + i) * size_y, size_y)
+            here = pl.ds(base + (e * depth + i) * SIZE_Y, SIZE_Y)
             at = (e * planes + XO - depth + i) * rows + YO
-            frame_ref[at : at + size_y, :] = low_ref[here, :].astype(jnp.float32)
+            frame_ref[at : at + SIZE_Y, :] = low_ref[here, :].astype(jnp.float32)
             at = (e * planes + XO + size_x + i) * rows + YO
-            frame_ref[at : at + size_y, :] = high_ref[here, :].astype(jnp.float32)
-    return base + channels * depth * size_y
+            frame_ref[at : at + SIZE_Y, :] = high_ref[here, :].astype(jnp.float32)
+    return base + channels * depth * SIZE_Y
 
 
 def depth_rows(frames, gz, x, size_y, rows, planes, channels):
@@ -211,23 +351,24 @@
     return out
 
 
-def frame_kernel(full, place_ref, *refs):
+def frame_kernel(full, channels, place_ref, *refs):
     if full:
-        state_ref, source_ref, class_ref, low_ref, high_ref, frame_ref, forcing_ref, code_ref, depth_ref = refs
+        _, _, _, low_ref, high_ref, frame_ref, forcing_ref, code_ref, depth_ref = refs
     else:
         state_ref, low_ref, high_ref, frame_ref, depth_ref = refs
-    channels, size_x, size_y = state_ref.shape[:3]
-    planes, rows = size_x + 2 * XO, size_y + 2 * YO
-    base = framed(frame_ref, state_ref, low_ref, high_ref, 0, 3)
+        own_cells(frame_ref, state_ref)
+    rows = SIZE_Y + 2 * YO
+    planes = frame_ref.shape[0] // (channels * rows)
+    base = beside(frame_ref, channels, low_ref, high_ref, 0, 3)
     frames = [frame_ref]
     if full:
-        base = framed(forcing_ref, source_ref, low_ref, high_ref, base, 2)
-        framed(code_ref, class_ref, low_ref, high_ref, base, 2, 1.0)
+        base = beside(forcing_ref, channels, low_ref, high_ref, base, 2)
+        beside(code_ref, 1, low_ref, high_ref, base, 2)
         frames = [frame_ref, forcing_ref, code_ref]
     gz = place_ref[1]
     for x in range(planes):
-        out = depth_rows(frames, gz, x, size_y, rows, planes, channels)
-        depth_ref[x * size_y : (x + 1) * size_y, :] = out.astype(jnp.bfloat16)
+        out = depth_rows(frames, gz, x, SIZE_Y, rows, planes, channels)
+        depth_ref[x * SIZE_Y : (x + 1) * SIZE_Y, :] = out.astype(jnp.bfloat16)
 
 
 def edge_kernel(full, *refs):
@@ -344,7 +485,7 @@
     sweep(frame, None, zframe, None, forcing, coef, zforcing, zcoef, gz, XO, planes - XO, channels, planes, finish)
 
 
-def put_density(out_ref, density_ref, cell_ref, live):
+def put_density(out_ref, density_ref, cell_ref, live, message_ref=None):
     channels, size_x, size_y, size_z = out_ref.shape
     slots = cell_ref.shape[1]
     cell = cell_ref[...]
@@ -359,12 +500,17 @@
         for e in range(channels)
     ]
     density = jnp.concatenate(found, axis=0).astype(jnp.bfloat16)
-    for brick in range(density_ref.shape[0]):
-        density_ref[brick] = density
+    if message_ref is None:
+        for brick in range(density_ref.shape[0]):
+            density_ref[brick] = density
+    else:
+        message = jnp.concatenate([density.astype(jnp.float32), message_ref[0]], axis=0)
+        for brick in range(density_ref.shape[0]):
+            density_ref[brick] = message
 
 
 def first_kernel(
-    place_ref, coef_table_ref, frame_ref, forcing_ref, code_ref, depth_ref, low_ref, high_ref, cell_ref,
+    place_ref, shift_ref, frame_ref, forcing_ref, code_ref, depth_ref, low_ref, high_ref, cell_ref, message_ref,
     out_ref, forcing_out, coef_out, zforcing_out, zcoef_out, density_ref, up_ref, down_ref,
     first, second, zfirst, zsecond, code, zcode,
 ):
@@ -390,24 +536,15 @@
         own_level = code[here, :]
         zweight = jnp.zeros((rows, 128), jnp.float32)
         weight = jnp.zeros((rows, 128), jnp.float32)
-        for index in range(coef_table_ref.shape[0]):
-            value = coef_table_ref[index]
+        for index in range(shift_ref.shape[0]):
+            value = shift_ref[index]
             zweight = jnp.where(level == index + 1.0, value, zweight)
             weight = jnp.where(own_level == index + 1.0, value, weight)
-        zcoef_out[here, :] = zweight
-        coef_out[here, :] = weight
+        zcoef_out[here, :] = jnp.where(level > 0.0, relax_weight / (6.0 + zweight), 0.0)
+        coef_out[here, :] = jnp.where(own_level > 0.0, relax_weight / (6.0 + weight), 0.0)
     sweeps(first, second, zfirst, zsecond, forcing_out, coef_out, zforcing_out, zcoef_out, gz, out_ref, planes)
-    put_density(out_ref, density_ref, cell_ref, place_ref[2])
     put_planes(up_ref, down_ref, 0, out_ref, 3)
-
-
-def split(x):
-    high = x.astype(jnp.bfloat16)
-    return high, (x - high.astype(jnp.float32)).astype(jnp.bfloat16)
-
-
-def across(a, b):
-    return lax.dot_general(a, b, (((1,), (1,)), ((), ())), preferred_element_type=jnp.float32)
+    put_density(out_ref, density_ref, cell_ref, place_ref[2], message_ref)
 
 
 def add_load(forcing, zforcing, near_ref, side, gz, channels, planes):
@@ -512,69 +649,79 @@
     planes, rows = size_x + 2 * XO, size_y + 2 * YO
     frame, flat = (channels * planes * rows, 128), (planes * rows, 128)
     place = jnp.stack([lax.axis_index("col"), lax.axis_index("gz"), live_count[0]]).astype(jnp.int32)
-    coefs = relax_weight / (6.0 + class_shift)
-    classes = cell_class[None]
     cells = surface_cell[None]
+    vm = lambda shape, dtype=jnp.float32: pltpu.VMEM(shape, dtype)
 
     send_x = channels * 5 * size_y + 2 * size_y
-    up, down = whole_call(
-        planes_kernel, (bf16(send_x, 128), bf16(send_x, 128)), [], "planes", (),
-        initial_field, source_term, classes,
+    up, down, start, forcing, code, message = whole_call(
+        functools.partial(planes_kernel, factor),
+        (bf16(send_x, 128), bf16(send_x, 128), f32(*frame), f32(*frame), f32(*flat), f32(bricks, 8, slots)),
+        [vm(initial_field.shape), vm(initial_field.shape), vm((1, *cell_class.shape), jnp.int32),
+         pltpu.SemaphoreType.DMA((3,))],
+        "planes", (live_count,), initial_field, source_term, cell_class[None], panel_geometry, cells,
+        away=(0, 1, 2),
     )
     low, high = both_ways(up, down, "row")
+    targets = lax.all_to_all(message, ("col", "gz"), 0, 0, tiled=True)
+    low, high, targets = lax.optimization_barrier((low, high, targets))
     start, forcing, code, depth = whole_call(
-        functools.partial(frame_kernel, True),
+        functools.partial(frame_kernel, True, channels),
         (f32(*frame), f32(*frame), f32(*flat), bf16(planes * size_y, 128)), [], "frame", (place,),
-        initial_field, source_term, classes, low, high,
+        start, forcing, code, low, high, aliases={0: 0, 1: 1, 2: 2},
     )
     other = lax.ppermute(depth, "gz", [(0, 1), (1, 0)])
-
-    live_row = jnp.broadcast_to(live_count.astype(jnp.float32)[:, None], (1, slots))
-    message = jnp.concatenate(
-        [panel_geometry[:3] * TURNS, panel_geometry[3:] * (factor * TURNS), live_row,
-         cells.astype(jnp.float32), jnp.zeros((2, slots), jnp.float32)]
-    )
-    sources = from_everyone(message, "row")
-    targets = from_everyone(message, ("col", "gz"))
-    tile = make_tile(sources, targets)
-
     zframe, up, down = whole_call(
         functools.partial(edge_kernel, True), (f32(*flat), bf16(480, 128), bf16(480, 128)), [], "edges", (),
         start, forcing, code, other,
     )
     low, high = both_ways(up, down, "col")
-    vm = lambda shape: pltpu.VMEM(shape, jnp.float32)
     state, forcing, coef, zforcing, zcoef, density, up, down = whole_call(
         first_kernel,
-        (f32(*initial_field.shape), f32(*frame), f32(*flat), f32(*flat), f32(*flat), bf16(bricks, channels, slots),
+        (f32(*initial_field.shape), f32(*frame), f32(*flat), f32(*flat), f32(*flat), f32(bricks, 2 * channels, slots),
          bf16(channels * 3 * size_y, 128), bf16(channels * 3 * size_y, 128)),
-        [vm(frame), vm(frame), vm(flat), vm(flat), vm(flat), vm(flat)], "first", (place, coefs),
-        start, forcing, code, zframe, low, high, cells,
-    )
+        [vm(frame), vm(frame), vm(flat), vm(flat), vm(flat), vm(flat)], "first", (place, class_shift),
+        start, forcing, code, zframe, low, high, cells, message, megabytes=8,
+    )
+    low, high = both_ways(up, down, "row")
     densities = lax.all_to_all(density, "row", 0, 0, tiled=True)
-    shares = products(densities, tile, True)
+    start, depth = whole_call(
+        functools.partial(frame_kernel, False, channels), (f32(*frame), bf16(planes * size_y, 128)), [], "frame", (place,),
+        state, low, high,
+    )
+    other = lax.ppermute(depth, "gz", [(0, 1), (1, 0)])
+    densities, depth = lax.optimization_barrier((densities, depth))
+    smem = pl.BlockSpec(memory_space=pltpu.SMEM)
+    vmem = pl.BlockSpec(memory_space=pltpu.VMEM)
+    packed, aims, table = pl.pallas_call(
+        compact_kernel,
+        in_specs=[vmem, vmem],
+        out_specs=(vmem, vmem, smem),
+        out_shape=(f32(bricks + 1, 2 * channels, slots), f32(bricks + 1, 8, slots),
+                   jax.ShapeDtypeStruct((2, bricks + 1), jnp.int32)),
+        scratch_shapes=[vm((8, slots), jnp.int32), pltpu.SMEM((8, slots), jnp.int32), pltpu.SemaphoreType.DMA],
+        compiler_params=params(4),
+        name="compact",
+    )(densities, targets)
+    tile, shares = make_tile(0, table, packed, aims, channels)
+    other, shares = lax.optimization_barrier((other, shares))
+    zframe, up, down = whole_call(
+        functools.partial(edge_kernel, False), (f32(*flat), bf16(288, 128), bf16(288, 128)), [], "edges", (),
+        start, other,
+    )
+    low, high = both_ways(up, down, "col")
+    packed, up = lax.optimization_barrier((packed, up))
+    tile, shares = make_tile(1, table, packed, aims, channels, (tile, shares))
+    shares = whole_call(arrange_kernel, f32(bricks, 6, channels, slots), [], "arrange", (table,), shares)
     parts = lax.all_to_all(shares, ("col", "gz"), 0, 0, tiled=True)
     near, _ = whole_call(near_kernel, (f32(7, channels, slots), f32(channels, slots)), [], "near", (place,), parts, targets)
     near_low, near_high = both_ways(near, near, "row")
-
-    low, high = both_ways(up, down, "row")
-    start, depth = whole_call(
-        functools.partial(frame_kernel, False), (f32(*frame), bf16(planes * size_y, 128)), [], "frame", (place,),
-        state, low, high,
-    )
-    other = lax.ppermute(depth, "gz", [(0, 1), (1, 0)])
-    zframe, up, down = whole_call(
-        functools.partial(edge_kernel, False), (f32(*flat), bf16(288, 128), bf16(288, 128)), [], "edges", (),
-        start, other,
-    )
-    low, high = both_ways(up, down, "col")
     state, density = whole_call(
         second_kernel, (f32(*initial_field.shape), bf16(bricks, channels, slots)),
         [vm(frame), vm(frame), vm(flat), vm(flat), vm(frame), vm(flat)], "second", (place,),
-        start, forcing, coef, zforcing, zcoef, zframe, low, high, cells, near_low, near, near_high,
+        start, forcing, coef, zforcing, zcoef, zframe, low, high, cells, near_low, near, near_high, megabytes=8,
     )
     densities = lax.all_to_all(density, "row", 0, 0, tiled=True)
-    shares = products(densities, tile, False)
+    shares = products(table, densities, tile, 512)
     parts = lax.all_to_all(shares, ("col", "gz"), 0, 0, tiled=True)
     potential = whole_call(last_kernel, f32(channels, slots), [], "last", (place,), parts)
     return (state, potential)

time: 185 us -> 170 us (0.919)
  starting transfers between devices: 70.5 us -> 53.2 us
  waiting for transfers between devices: 10.6 us -> 24.2 us
  local copies, waits for them, and re-layouts: 14.5 us -> 7.88 us
  other arithmetic: 2.76 us -> 0.08 us
    all_to_all x2 -> x1, starting transfers between devices: 18.7 us -> 6.77 us  [local(): targets = lax.all_to_all(message, ('col', 'gz'), 0, 0, tiled=True)]
    all_to_all x1, starting transfers between devices: 11.9 us -> 4.84 us  [local(): parts = lax.all_to_all(shares, ('col', 'gz'), 0, 0, tiled=True)]
    all_to_all x2 -> x1, waiting for transfers between devices: 0.01 us -> 6.65 us  [local(): targets = lax.all_to_all(message, ('col', 'gz'), 0, 0, tiled=True)]
    all_to_all x1, starting transfers between devices: 7.23 us -> 13.5 us  [local(): densities = lax.all_to_all(density, 'row', 0, 0, tiled=True)]
    unnamed x50 -> x28, local copies, waits for them, and re-layouts: 13.8 us -> 7.88 us
    ppermute x2, starting transfers between devices: 5.89 us -> 1.44 us  [local(): other = lax.ppermute(depth, 'gz', [(0, 1), (1, 0)])]
    all_to_all x1, waiting for transfers between devices: 0.01 us -> 3.76 us  [local(): parts = lax.all_to_all(shares, ('col', 'gz'), 0, 0, tiled=True)]
    all_to_all x1, blocking collectives: 15.6 us -> 17.9 us  [local(): densities = lax.all_to_all(density, 'row', 0, 0, tiled=True)]
  transfers between devices with their start and end apart: 16 -> 15, of which waited for: 4 -> 8; matrix products, arithmetic and copies ran while one was open for 2% -> 0% of each run, Pallas kernels for 17% -> 10%
where the time goes in v3:
time: 170 us
  starting transfers between devices  53.2 us (31%)
  Pallas kernels  52.8 us (31%)
  blocking collectives  30 us (18%)
  waiting for transfers between devices  24.2 us (14%)
  local copies, waits for them, and re-layouts  7.88 us (5%)
    pallas_call x2, Pallas kernels, make_tile(): pl.pallas_call(functools.partial(tile_kernel, half), grid=(bricks // 2,),...  27.1 us
    pallas_call x10, Pallas kernels, whole_call(): pl.pallas_call(kernel, in_specs=[smem] * len(scalars) + [far if n in away...  19 us
    ppermute x5, starting transfers between devices, both_ways(): lax.ppermute(up, axis, pairs)  18.3 us
    all_to_all x1, blocking collectives, local(): densities = lax.all_to_all(density, 'row', 0, 0, tiled=True)  17.9 us
    all_to_all x1, starting transfers between devices, local(): densities = lax.all_to_all(density, 'row', 0, 0, tiled=True)  13.5 us
    all_to_all x1, blocking collectives, local(): parts = lax.all_to_all(shares, ('col', 'gz'), 0, 0, tiled=True)  12 us
    ppermute x5, starting transfers between devices, both_ways(): lax.ppermute(down, axis, [(b, a) for a, b in pairs])  8.33 us
    unnamed x28, local copies, waits for them, and re-layouts  7.88 us
  transfers between devices with their start and end apart: 15, of which 8 were waited for; matrix products, arithmetic and copies ran while one was open for 0% of the time, Pallas kernels for 10%

profile of v3, /device:TPU:1, one launch (start us, length us, event | category | flops | bytes accessed | tf_op | source)
XLA Modules:
  0.0 169.6 jit_solution(12275589117977418119)
XLA Ops:
  1.3 0.9 copy-done
  2.3 0.9 copy-done.1
  6.2 4.9 %collective-permute-start = (bf16[672,128]{1,0:T(8,128)(2,1)S(1)}, bf16[672,128]{1,0:T(8,128)(2,1)S(1)}, u32[]{:S(2)}, u32[]{:S(2)}) collective-permute-start(bf16[672,128]{1,0:T(8,128)(2,1)S(1)} %get-tuple-element.48), channel_id=1, source_target_pairs={{0,16},{16,32},{32,48},{48,64},{64,80},{80,96},{96,112},{112,128},... | collective-permute-start | bytes 516104 | tf_op jit(solution)/shard_map/ppermute | solution.py:638
  11.1 1.9 %collective-permute-start.1 = (bf16[672,128]{1,0:T(8,128)(2,1)S(1)}, bf16[672,128]{1,0:T(8,128)(2,1)S(1)}, u32[]{:S(2)}, u32[]{:S(2)}) collective-permute-start(bf16[672,128]{1,0:T(8,128)(2,1)S(1)} %get-tuple-element.49), channel_id=1, source_target_pairs={{16,0},{32,16},{48,32},{64,48},{80,64},{96,80},{112,96},{128,112},... | collective-permute-start | bytes 516104 | tf_op jit(solution)/shard_map/ppermute | solution.py:638
  13.1 6.8 %all-to-all-start = ((f32[16,8,128]{2,1,0:T(8,128)}), f32[16,8,128]{2,1,0:T(8,128)S(1)}, u32[]{:S(2)}, u32[]{:S(2)}) async-start(f32[16,8,128]{2,1,0:T(8,128)} %get-tuple-element.50.message_ref), calls=%async_computation | async-start | bytes 131072 | tf_op jit(solution)/shard_map/all_to_all | solution.py:665
  19.9 6.7 %all-to-all-done.target_ref.targets_ref = f32[16,8,128]{2,1,0:T(8,128)S(1)} async-done(((f32[16,8,128]{2,1,0:T(8,128)}), f32[16,8,128]{2,1,0:T(8,128)S(1)}, u32[]{:S(2)}, u32[]{:S(2)}) %all-to-all-start) | async-done | bytes 65568 | tf_op jit(solution)/shard_map/all_to_all | solution.py:665
  28.2 3.7 %collective-permute-done.2.refs_3_ = bf16[160,128]{1,0:T(8,128)(2,1)S(1)} collective-permute-done((bf16[160,128]{1,0:T(8,128)(2,1)S(1)}, bf16[160,128]{1,0:T(8,128)(2,1)S(1)}, u32[]{:S(2)}, u32[]{:S(2)}) %collective-permute-start.2) | collective-permute-done | bytes 40992 | tf_op jit(solution)/shard_map/ppermute | solution.py:672
  32.0 2.2 %collective-permute-start.3 = (bf16[480,128]{1,0:T(8,128)(2,1)S(1)}, bf16[480,128]{1,0:T(8,128)(2,1)S(1)}, u32[]{:S(2)}, u32[]{:S(2)}) collective-permute-start(bf16[480,128]{1,0:T(8,128)(2,1)S(1)} %get-tuple-element.58), channel_id=1, source_target_pairs={{0,2},{2,4},{4,6},{6,8},{8,10},{10,12},{12,14},{1,3},{3,5},{5,7},{... | collective-permute-start | bytes 368648 | tf_op jit(solution)/shard_map/ppermute | solution.py:638
  34.2 1.3 collective-permute-start.4
  35.5 1.0 collective-permute-done.3.low_ref
  36.6 3.8 %collective-permute-done.4.high_ref = bf16[480,128]{1,0:T(8,128)(2,1)S(1)} collective-permute-done((bf16[480,128]{1,0:T(8,128)(2,1)S(1)}, bf16[480,128]{1,0:T(8,128)(2,1)S(1)}, u32[]{:S(2)}, u32[]{:S(2)}) %collective-permute-start.4) | collective-permute-done | bytes 122912 | tf_op jit(solution)/shard_map/ppermute | solution.py:638
  41.7 6.0 %first.1 = (f32[8,4,16,128]{3,2,1,0:T(8,128)S(1)}, f32[1920,128]{1,0:T(8,128)S(1)}, f32[240,128]{1,0:T(8,128)S(1)}, f32[240,128]{1,0:T(8,128)S(1)}, f32[240,128]...) custom-call(s32[3]{0:T(128)S(1)} %pad_add_fusion.place_ref, ...), custom_call_target="tpu_custom_call" | custom-call | tf_op jit(solution)/shard_map/first/pallas_call | solution.py:50
  50.3 13.5 %all-to-all-start.1 = ((f32[16,16,128]{2,1,0:T(8,128)}), f32[16,16,128]{2,1,0:T(8,128)S(1)}, u32[]{:S(2)}, u32[]{:S(2)}) async-start(f32[16,16,128]{2,1,0:T(8,128)} %get-tuple-element.69), calls=%async_computation.1 | async-start | bytes 262144 | tf_op jit(solution)/shard_map/all_to_all | solution.py:686
  63.8 3.5 %collective-permute-start.5 = (bf16[384,128]{1,0:T(8,128)(2,1)}, bf16[384,128]{1,0:T(8,128)(2,1)S(1)}, u32[]{:S(2)}, u32[]{:S(2)}) collective-permute-start(bf16[384,128]{1,0:T(8,128)(2,1)} %copy-done.13), channel_id=1, source_target_pairs={{0,16},{16,32},{32,48},{48,64},{64,80},{80,96},{96,112},{112,128},... | collective-permute-start | bytes 294920 | tf_op jit(solution)/shard_map/ppermute | solution.py:638
  67.4 1.9 %collective-permute-start.6 = (bf16[384,128]{1,0:T(8,128)(2,1)}, bf16[384,128]{1,0:T(8,128)(2,1)S(1)}, u32[]{:S(2)}, u32[]{:S(2)}) collective-permute-start(bf16[384,128]{1,0:T(8,128)(2,1)} %copy-done.12), channel_id=1, source_target_pairs={{16,0},{32,16},{48,32},{64,48},{80,64},{96,80},{112,96},{128,112},... | collective-permute-start | bytes 294920 | tf_op jit(solution)/shard_map/ppermute | solution.py:638
  69.6 3.9 %collective-permute-done.6.refs_2_ = bf16[384,128]{1,0:T(8,128)(2,1)S(1)} collective-permute-done((bf16[384,128]{1,0:T(8,128)(2,1)}, bf16[384,128]{1,0:T(8,128)(2,1)S(1)}, u32[]{:S(2)}, u32[]{:S(2)}) %collective-permute-start.6) | collective-permute-done | bytes 98336 | tf_op jit(solution)/shard_map/ppermute | solution.py:638
  75.0 1.3 compact.1
  76.3 13.6 %tile.2 = (bf16[16384,2048]{1,0:T(8,128)(2,1)}, f32[16,8,128]{2,1,0:T(8,128)S(1)}) custom-call(s32[2,17]{1,0:T(2,128)S(1)} %get-tuple-element.72.table_ref, f32[17,16,128]{2,1,0:T(8,128)S(1)} %get-tuple-element.80.source_ref, f32[17,8,128]{2,1,0:T(8,128)S(1)} %get-tuple-element.74.target_ref), custom_call_target="tpu_custom_call" | custom-call | tf_op jit(solution)/shard_map/tile/pallas_call | solution.py:165
  90.0 13.6 %tile.3 = (bf16[16384,2048]{1,0:T(8,128)(2,1)}, f32[16,8,128]{2,1,0:T(8,128)S(1)}) custom-call(s32[2,17]{1,0:T(2,128)S(1)} %get-tuple-element.72.table_ref, f32[17,16,128]{2,1,0:T(8,128)S(1)} %get-tuple-element.80.source_ref, f32[17,8,128]{2,1,0:T(8,128)S(1)} %get-tuple-element.74.target_ref, ...), custom_call_target="tpu_custom_call", output_to_operand_aliasing={{0}: (3, {}), {1}: (4, {})} | custom-call | tf_op jit(solution)/shard_map/tile/pallas_call | solution.py:165
  103.6 1.5 arrange.1
  105.0 4.8 %all-to-all-start.2 = ((f32[16,6,8,128]{3,2,1,0:T(8,128)}), f32[16,6,8,128]{3,2,1,0:T(8,128)S(1)}, u32[]{:S(2)}, u32[]{:S(2)}) async-start(f32[16,6,8,128]{3,2,1,0:T(8,128)} %arrange.1), calls=%async_computation.2 | async-start | bytes 786432 | tf_op jit(solution)/shard_map/all_to_all | solution.py:715
  109.9 1.3 collective-permute-start.9
  111.2 4.0 %collective-permute-start.8 = (bf16[288,128]{1,0:T(8,128)(2,1)S(1)}, bf16[288,128]{1,0:T(8,128)(2,1)S(1)}, u32[]{:S(2)}, u32[]{:S(2)}) collective-permute-start(bf16[288,128]{1,0:T(8,128)(2,1)S(1)} %get-tuple-element.78), channel_id=1, source_target_pairs={{0,2},{2,4},{4,6},{6,8},{8,10},{10,12},{12,14},{1,3},{3,5},{5,7},{... | collective-permute-start | bytes 221192 | tf_op jit(solution)/shard_map/ppermute | solution.py:638
  115.2 3.8 %all-to-all-done.2.parts_ref = f32[16,6,8,128]{3,2,1,0:T(8,128)S(1)} async-done(((f32[16,6,8,128]{3,2,1,0:T(8,128)}), f32[16,6,8,128]{3,2,1,0:T(8,128)S(1)}, u32[]{:S(2)}, u32[]{:S(2)}) %all-to-all-start.2) | async-done | bytes 393248 | tf_op jit(solution)/shard_map/all_to_all | solution.py:715
  118.9 1.2 near.1
  120.1 1.9 %collective-permute-start.11 = (f32[7,8,128]{2,1,0:T(8,128)S(1)}, f32[7,8,128]{2,1,0:T(8,128)S(1)}, u32[]{:S(2)}, u32[]{:S(2)}) collective-permute-start(f32[7,8,128]{2,1,0:T(8,128)S(1)} %get-tuple-element.84.near_own), channel_id=1, source_target_pairs={{16,0},{32,16},{48,32},{64,48},{80,64},{96,80},{112,96},{128,112},... | collective-permute-start | bytes 86024 | tf_op jit(solution)/shard_map/ppermute | solution.py:638
  122.0 3.6 %collective-permute-start.10 = (f32[7,8,128]{2,1,0:T(8,128)S(1)}, f32[7,8,128]{2,1,0:T(8,128)S(1)}, u32[]{:S(2)}, u32[]{:S(2)}) collective-permute-start(f32[7,8,128]{2,1,0:T(8,128)S(1)} %get-tuple-element.84.near_own), channel_id=1, source_target_pairs={{0,16},{16,32},{32,48},{48,64},{64,80},{80,96},{96,112},{112,128},... | collective-permute-start | bytes 86024 | tf_op jit(solution)/shard_map/ppermute | solution.py:638
  126.6 6.5 %second.1 = (f32[8,4,16,128]{3,2,1,0:T(8,128)}, bf16[16,8,128]{2,1,0:T(8,128)(2,1)S(1)}) custom-call(s32[3]{0:T(128)S(1)} %pad_add_fusion.place_ref, f32[1920,128]{1,0:T(8,128)S(1)} %get-tuple-element.63.refs_0_.frame_ref, f32[1920,128]{1,0:T(8,128)S(1)} %get-tuple-element.64.forcing_ref, f32[240,128]{1,0:T(8,128)S(1)} %get-tuple-element.65.coef_ref, ...), custom_call_target="tpu_custom_call" | custom-call | tf_op jit(solution)/shard_map/second/pallas_call | solution.py:50
  133.1 17.9 %all_to_all.25.density_ref = bf16[16,8,128]{2,1,0:T(8,128)(2,1)S(1)} all-to-all(bf16[16,8,128]{2,1,0:T(8,128)(2,1)S(1)} %get-tuple-element.86), channel_id=1, replica_groups=mesh['row'=16,'col'=8,'gz'=2] {'row'}, dimensions={0} | all-to-all | bytes 65536 | tf_op jit(solution)/shard_map/all_to_all | solution.py:723
  151.0 5.4 %product.1 = f32[16,8,128]{2,1,0:T(8,128)S(1)} custom-call(s32[2,17]{1,0:T(2,128)S(1)} %get-tuple-element.72.table_ref, bf16[16,8,128]{2,1,0:T(8,128)(2,1)S(1)} %all_to_all.25.density_ref, bf16[16384,2048]{1,0:T(8,128)(2,1)} %get-tuple-element.87.tile_ref), custom_call_target="tpu_custom_call" | custom-call | tf_op jit(solution)/shard_map/product/pallas_call | solution.py:252
  156.4 12.0 %all_to_all.26.parts_ref = f32[16,8,128]{2,1,0:T(8,128)S(1)} all-to-all(f32[16,8,128]{2,1,0:T(8,128)S(1)} %product.1), channel_id=1, replica_groups=mesh['row'=16,'col'=8,'gz'=2] {'col','gz'}, dimensions={0} | all-to-all | bytes 131072 | tf_op jit(solution)/shard_map/all_to_all | solution.py:725
  168.4 1.1 last.1
  (43 shorter events, 11.5 us)
Async XLA Ops:
  0.6 126.0 %copy-start.9 = (s32[128]{0:T(128)S(1)}, s32[128]{0:T(128)}, u32[]{:S(2)}) copy-start(s32[128]{0:T(128)} %param.11) | copy-start | bytes 1540
  1.3 1.0 copy-start
  2.3 0.9 copy-start.1
  3.2 0.8 copy-start.6
  4.0 0.7 copy-start.7
  4.6 0.7 copy-start.10
  6.2 20.4 %collective-permute-start = (bf16[672,128]{1,0:T(8,128)(2,1)S(1)}, bf16[672,128]{1,0:T(8,128)(2,1)S(1)}, u32[]{:S(2)}, u32[]{:S(2)}) collective-permute-start(bf16[672,128]{1,0:T(8,128)(2,1)S(1)} %get-tuple-element.48), channel_id=1, source_target_pairs={{0,16},{16,32},{32,48},{48,64},{64,80},{80,96},{96,112},{112,128},... | collective-permute-start | bytes 516104 | tf_op jit(solution)/shard_map/ppermute | solution.py:638
  11.1 15.4 %collective-permute-start.1 = (bf16[672,128]{1,0:T(8,128)(2,1)S(1)}, bf16[672,128]{1,0:T(8,128)(2,1)S(1)}, u32[]{:S(2)}, u32[]{:S(2)}) collective-permute-start(bf16[672,128]{1,0:T(8,128)(2,1)S(1)} %get-tuple-element.49), channel_id=1, source_target_pairs={{16,0},{32,16},{48,32},{64,48},{80,64},{96,80},{112,96},{128,112},... | collective-permute-start | bytes 516104 | tf_op jit(solution)/shard_map/ppermute | solution.py:638
  13.1 13.5 %all-to-all-start = ((f32[16,8,128]{2,1,0:T(8,128)}), f32[16,8,128]{2,1,0:T(8,128)S(1)}, u32[]{:S(2)}, u32[]{:S(2)}) async-start(f32[16,8,128]{2,1,0:T(8,128)} %get-tuple-element.50.message_ref), calls=%async_computation | async-start | bytes 131072 | tf_op jit(solution)/shard_map/all_to_all | solution.py:665
  27.5 4.5 %collective-permute-start.2 = (bf16[160,128]{1,0:T(8,128)(2,1)S(1)}, bf16[160,128]{1,0:T(8,128)(2,1)S(1)}, u32[]{:S(2)}, u32[]{:S(2)}) collective-permute-start(bf16[160,128]{1,0:T(8,128)(2,1)S(1)} %get-tuple-element.56), channel_id=1, source_target_pairs={{0,1},{1,0},{2,3},{3,2},{4,5},{5,4},{6,7},{7,6},{8,9},{9,8},{10,11... | collective-permute-start | bytes 122888 | tf_op jit(solution)/shard_map/ppermute | solution.py:672
  32.0 4.5 %collective-permute-start.3 = (bf16[480,128]{1,0:T(8,128)(2,1)S(1)}, bf16[480,128]{1,0:T(8,128)(2,1)S(1)}, u32[]{:S(2)}, u32[]{:S(2)}) collective-permute-start(bf16[480,128]{1,0:T(8,128)(2,1)S(1)} %get-tuple-element.58), channel_id=1, source_target_pairs={{0,2},{2,4},{4,6},{6,8},{8,10},{10,12},{12,14},{1,3},{3,5},{5,7},{... | collective-permute-start | bytes 368648 | tf_op jit(solution)/shard_map/ppermute | solution.py:638
  34.2 6.1 %collective-permute-start.4 = (bf16[480,128]{1,0:T(8,128)(2,1)S(1)}, bf16[480,128]{1,0:T(8,128)(2,1)S(1)}, u32[]{:S(2)}, u32[]{:S(2)}) collective-permute-start(bf16[480,128]{1,0:T(8,128)(2,1)S(1)} %get-tuple-element.59), channel_id=1, source_target_pairs={{2,0},{4,2},{6,4},{8,6},{10,8},{12,10},{14,12},{3,1},{5,3},{7,5},{... | collective-permute-start | bytes 368648 | tf_op jit(solution)/shard_map/ppermute | solution.py:638
  40.4 0.7 copy-start.8
  41.0 0.7 copy-start.11
  47.7 0.7 copy-start.2
  48.4 0.6 copy-start.4
  49.0 0.6 copy-start.12
  49.7 0.6 copy-start.13
  50.3 76.3 %copy-start.3 = (f32[240,128]{1,0:T(8,128)S(1)}, f32[240,128]{1,0:T(8,128)}, u32[]{:S(2)}) copy-start(f32[240,128]{1,0:T(8,128)} %copy-done.2) | copy-start | bytes 368644
  50.3 76.3 %copy-start.5 = (f32[240,128]{1,0:T(8,128)S(1)}, f32[240,128]{1,0:T(8,128)}, u32[]{:S(2)}) copy-start(f32[240,128]{1,0:T(8,128)} %copy-done.4) | copy-start | bytes 368644
  50.3 24.7 %all-to-all-start.1 = ((f32[16,16,128]{2,1,0:T(8,128)}), f32[16,16,128]{2,1,0:T(8,128)S(1)}, u32[]{:S(2)}, u32[]{:S(2)}) async-start(f32[16,16,128]{2,1,0:T(8,128)} %get-tuple-element.69), calls=%async_computation.1 | async-start | bytes 262144 | tf_op jit(solution)/shard_map/all_to_all | solution.py:686
  63.8 5.8 %collective-permute-start.5 = (bf16[384,128]{1,0:T(8,128)(2,1)}, bf16[384,128]{1,0:T(8,128)(2,1)S(1)}, u32[]{:S(2)}, u32[]{:S(2)}) collective-permute-start(bf16[384,128]{1,0:T(8,128)(2,1)} %copy-done.13), channel_id=1, source_target_pairs={{0,16},{16,32},{32,48},{48,64},{64,80},{80,96},{96,112},{112,128},... | collective-permute-start | bytes 294920 | tf_op jit(solution)/shard_map/ppermute | solution.py:638
  67.4 6.1 %collective-permute-start.6 = (bf16[384,128]{1,0:T(8,128)(2,1)}, bf16[384,128]{1,0:T(8,128)(2,1)S(1)}, u32[]{:S(2)}, u32[]{:S(2)}) collective-permute-start(bf16[384,128]{1,0:T(8,128)(2,1)} %copy-done.12), channel_id=1, source_target_pairs={{16,0},{32,16},{48,32},{64,48},{80,64},{96,80},{112,96},{128,112},... | collective-permute-start | bytes 294920 | tf_op jit(solution)/shard_map/ppermute | solution.py:638
  74.3 15.6 %collective-permute-start.7 = (bf16[160,128]{1,0:T(8,128)(2,1)S(1)}, bf16[160,128]{1,0:T(8,128)(2,1)S(1)}, u32[]{:S(2)}, u32[]{:S(2)}) collective-permute-start(bf16[160,128]{1,0:T(8,128)(2,1)S(1)} %get-tuple-element.68), channel_id=1, source_target_pairs={{0,1},{1,0},{2,3},{3,2},{4,5},{5,4},{6,7},{7,6},{8,9},{9,8},{10,11... | collective-permute-start | bytes 122888 | tf_op jit(solution)/shard_map/ppermute | solution.py:691
  105.0 13.9 %all-to-all-start.2 = ((f32[16,6,8,128]{3,2,1,0:T(8,128)}), f32[16,6,8,128]{3,2,1,0:T(8,128)S(1)}, u32[]{:S(2)}, u32[]{:S(2)}) async-start(f32[16,6,8,128]{3,2,1,0:T(8,128)} %arrange.1), calls=%async_computation.2 | async-start | bytes 786432 | tf_op jit(solution)/shard_map/all_to_all | solution.py:715
  109.9 15.8 %collective-permute-start.9 = (bf16[288,128]{1,0:T(8,128)(2,1)S(1)}, bf16[288,128]{1,0:T(8,128)(2,1)S(1)}, u32[]{:S(2)}, u32[]{:S(2)}) collective-permute-start(bf16[288,128]{1,0:T(8,128)(2,1)S(1)} %get-tuple-element.79), channel_id=1, source_target_pairs={{2,0},{4,2},{6,4},{8,6},{10,8},{12,10},{14,12},{3,1},{5,3},{7,5},{... | collective-permute-start | bytes 221192 | tf_op jit(solution)/shard_map/ppermute | solution.py:638
  111.2 14.5 %collective-permute-start.8 = (bf16[288,128]{1,0:T(8,128)(2,1)S(1)}, bf16[288,128]{1,0:T(8,128)(2,1)S(1)}, u32[]{:S(2)}, u32[]{:S(2)}) collective-permute-start(bf16[288,128]{1,0:T(8,128)(2,1)S(1)} %get-tuple-element.78), channel_id=1, source_target_pairs={{0,2},{2,4},{4,6},{6,8},{8,10},{10,12},{12,14},{1,3},{3,5},{5,7},{... | collective-permute-start | bytes 221192 | tf_op jit(solution)/shard_map/ppermute | solution.py:638
  120.1 5.6 %collective-permute-start.11 = (f32[7,8,128]{2,1,0:T(8,128)S(1)}, f32[7,8,128]{2,1,0:T(8,128)S(1)}, u32[]{:S(2)}, u32[]{:S(2)}) collective-permute-start(f32[7,8,128]{2,1,0:T(8,128)S(1)} %get-tuple-element.84.near_own), channel_id=1, source_target_pairs={{16,0},{32,16},{48,32},{64,48},{80,64},{96,80},{112,96},{128,112},... | collective-permute-start | bytes 86024 | tf_op jit(solution)/shard_map/ppermute | solution.py:638
  122.0 4.6 %collective-permute-start.10 = (f32[7,8,128]{2,1,0:T(8,128)S(1)}, f32[7,8,128]{2,1,0:T(8,128)S(1)}, u32[]{:S(2)}, u32[]{:S(2)}) collective-permute-start(f32[7,8,128]{2,1,0:T(8,128)S(1)} %get-tuple-element.84.near_own), channel_id=1, source_target_pairs={{0,16},{16,32},{32,48},{48,64},{64,80},{80,96},{96,112},{112,128},... | collective-permute-start | bytes 86024 | tf_op jit(solution)/shard_map/ppermute | solution.py:638

commit v4 on v3

--- a/solution.py
+++ b/solution.py
@@ -9,6 +9,8 @@
 from jax.sharding import PartitionSpec as P
 
 SIZE_Y = 16
+CLASSES = 16
+KEPT = 11
 ROOM = 8
 
 relax_weight = 0.8
@@ -16,7 +18,7 @@
 soften = 0.05
 coupling = 0.5
 
-SINE = (6.2831851600894435, -41.34165503141112, 81.60100407296788, -76.54978228730859, 39.53670602126459)
+SINE = (6.283164044297846, -41.33714237050646, 81.34076886863805, -70.99343309793157)
 TURNS = wave_number / (2.0 * math.pi)
 ROUNDER = 12582912.0
 
@@ -76,29 +78,23 @@
     return lax.dot_general(a, b, (((1,), (1,)), ((), ())), preferred_element_type=jnp.float32)
 
 
-def compact_kernel(message_ref, target_ref, source_out, target_out, table_ref, counts, table, arrived):
-    bricks, depth, slots = message_ref.shape
-    channels = depth // 2
-    lane = lanes((8, slots))
-    first = jnp.zeros((8, slots), jnp.float32)
+def compact_kernel(target_ref, target_out, table_ref, counts, table, arrived):
+    bricks, depth, slots = target_ref.shape
+    lane = lanes((depth, slots))
+    first = jnp.zeros((depth, slots), jnp.float32)
     for brick in range(bricks):
-        first = jnp.where(lane == brick, message_ref[brick, channels + 4 : channels + 5, :], first)
-        first = jnp.where(lane == bricks + brick, target_ref[brick, 4:5, :], first)
+        first = jnp.where(lane == brick, target_ref[brick, 4:5, :], first)
     counts[...] = first.astype(jnp.int32)
     copy = pltpu.make_async_copy(counts, table, arrived)
     copy.start()
-    source_out[...] = jnp.zeros_like(source_out)
     target_out[...] = jnp.zeros_like(target_out)
     copy.wait()
-    begin = [jnp.int32(0), jnp.int32(0)]
+    begin = jnp.int32(0)
     for brick in range(bricks):
-        for which, ref, out in ((0, message_ref, source_out), (1, target_ref, target_out)):
-            count = table[0, which * bricks + brick]
-            append(out, ref[brick], begin[which], count)
-            table_ref[which, brick] = begin[which]
-            begin[which] = begin[which] + count
-    table_ref[0, bricks] = begin[0]
-    table_ref[1, bricks] = begin[1]
+        append(target_out, target_ref[brick], begin, table[0, brick])
+        table_ref[brick] = begin
+        begin = begin + table[0, brick]
+    table_ref[bricks] = begin
 
 
 def append(out, rows, begin, count):
@@ -111,56 +107,45 @@
 
 def tile_kernel(half, table_ref, source_ref, target_ref, *refs):
     tile_ref, share_ref, columns, density = refs[-4:]
-    bricks, slots = source_ref.shape[0] - 1, source_ref.shape[2]
+    bricks, slots = source_ref.shape[0], source_ref.shape[2]
     channels = share_ref.shape[1]
     step = pl.program_id(0)
-    pairs = (table_ref[0, bricks] + (2 * slots - 1)) >> 8
 
     @pl.when(step == 0)
     def _():
-        for group in range(bricks):
-            density[:, group * slots : (group + 1) * slots] = source_ref[group, :channels].astype(jnp.bfloat16)
-
-    @pl.when((2 * step + half) * slots < table_ref[1, bricks])
+        for brick in range(bricks):
+            density[:, brick * slots : (brick + 1) * slots] = source_ref[brick, :channels].astype(jnp.bfloat16)
+
+    @pl.when((2 * step + half) * slots < table_ref[bricks])
     def _():
         columns[...] = jnp.transpose(target_ref[0])
         spread = [jnp.broadcast_to(columns[:, d : d + 1], (slots, slots)) for d in range(3)]
-
-        def one_pair(pair, total):
+        total = jnp.zeros((channels, slots), jnp.float32)
+        for pair in range(0, bricks, 2):
             both = []
-            for index in range(2):
-                here = source_ref.at[2 * pair + index]
+            for brick in (pair, pair + 1):
                 square = 1e-30
                 for d in range(3):
-                    delta = spread[d] - here[channels + d : channels + d + 1, :]
+                    delta = spread[d] - source_ref[brick, channels + d : channels + d + 1, :]
                     square = square + delta * delta
                 turns = square * lax.rsqrt(square)
                 whole = (turns + ROUNDER) - ROUNDER
                 angle = 0.25 - jnp.abs(turns - whole)
                 angle2 = angle * angle
-                wave = SINE[4]
-                for c in SINE[3::-1]:
+                wave = SINE[-1]
+                for c in SINE[-2::-1]:
                     wave = wave * angle2 + c
-                weight = here[channels + 3 : channels + 4, :]
+                weight = source_ref[brick, channels + 3 : channels + 4, :]
                 value = (angle * weight) * wave / (turns + soften * TURNS)
                 both.append(value.astype(jnp.bfloat16))
-            values = jnp.concatenate(both, axis=1)
-            at = pl.ds(pl.multiple_of(pair * 2 * slots, 2 * slots), 2 * slots)
-            tile_ref[:, at] = values
-            return total + across(density[:, at], values)
-
-        share_ref[0] = lax.fori_loop(0, pairs, one_pair, jnp.zeros((channels, slots), jnp.float32))
-
-        def clear(pair, carry):
-            at = pl.ds(pl.multiple_of(pair * 2 * slots, 2 * slots), 2 * slots)
-            tile_ref[:, at] = jnp.zeros((slots, 2 * slots), jnp.bfloat16)
-            return carry
-
-        lax.fori_loop(pairs, bricks // 2, clear, 0)
+                tile_ref[:, brick * slots : (brick + 1) * slots] = both[-1]
+            at = slice(pair * slots, (pair + 2) * slots)
+            total = total + across(density[:, at], jnp.concatenate(both, axis=1))
+        share_ref[0] = total
 
 
 def make_tile(half, table, sources, targets, channels, before=()):
-    bricks, slots = sources.shape[0] - 1, sources.shape[2]
+    bricks, slots = sources.shape[0], sources.shape[2]
     far = pl.BlockSpec(memory_space=pl.ANY)
     return pl.pallas_call(
         functools.partial(tile_kernel, half),
@@ -190,8 +175,8 @@
 
 
 def taken(share_ref, table_ref, brick, bricks):
-    begin = table_ref[1, brick]
-    count = table_ref[1, brick + 1] - begin
+    begin = table_ref[brick]
+    count = table_ref[brick + 1] - begin
     group, shift = begin >> 7, begin & 127
     lane = lanes(share_ref.shape[1:])
     slots = share_ref.shape[2]
@@ -214,21 +199,17 @@
                 out_ref[brick, n] = jnp.zeros(out_ref.shape[2:], jnp.float32)
 
 
-def product_kernel(table_ref, density_ref, tile_ref, out_ref, sources, density, shares):
+def product_kernel(table_ref, density_ref, tile_ref, out_ref, density, shares):
     bricks, channels, slots = density_ref.shape
     step = pl.program_id(0)
     count = tile_ref.shape[0] // slots
 
     @pl.when(step == 0)
     def _():
-        sources[...] = jnp.zeros_like(sources)
         for brick in range(bricks):
-            begin = table_ref[0, brick]
-            append(sources, density_ref[brick].astype(jnp.float32), begin, table_ref[0, brick + 1] - begin)
-        for group in range(bricks):
-            density[:, group * slots : (group + 1) * slots] = sources[group].astype(jnp.bfloat16)
-
-    @pl.when(step * count * slots < table_ref[1, bricks])
+            density[:, brick * slots : (brick + 1) * slots] = density_ref[brick]
+
+    @pl.when(step * count * slots < table_ref[bricks])
     def _():
         total = across(density[...], tile_ref[...])
         for index in range(count):
@@ -246,7 +227,7 @@
     steps = bricks * slots // rows
 
     def block(b, table_ref):
-        last = (table_ref[1, bricks] + rows - 1) // rows - 1
+        last = (table_ref[bricks] + rows - 1) // rows - 1
         return jnp.minimum(b, last), 0
 
     return pl.pallas_call(
@@ -257,7 +238,6 @@
             in_specs=[pl.BlockSpec(density.shape, lambda b, t: (0, 0, 0)), pl.BlockSpec((rows, width), block)],
             out_specs=pl.BlockSpec((bricks, channels, slots), lambda b, t: (0, 0, 0)),
             scratch_shapes=[
-                pltpu.VMEM((bricks + 1, channels, slots), jnp.float32),
                 pltpu.VMEM((channels, width), jnp.bfloat16),
                 pltpu.VMEM((bricks, channels, slots), jnp.float32),
             ],
@@ -291,7 +271,7 @@
 
 
 def planes_kernel(
-    factor, live_ref, state_hbm, source_hbm, class_hbm, geometry_ref, cell_ref,
+    factor, live_ref, shift_ref, state_hbm, source_hbm, class_hbm, geometry_ref, cell_ref,
     up_ref, down_ref, frame_ref, forcing_ref, code_ref, message_ref, state_ref, source_ref, class_ref, arrived,
 ):
     copies = [
@@ -302,13 +282,17 @@
     for copy in copies:
         copy.start()
     slots = cell_ref.shape[1]
+    shifts = jnp.zeros((1, slots), jnp.float32)
+    for index in range(CLASSES):
+        shifts = jnp.where(lanes((1, slots)) == index, shift_ref[index], shifts)
     message = jnp.concatenate(
         [
             geometry_ref[:3] * TURNS,
             geometry_ref[3:] * (factor * TURNS),
             jnp.full((1, slots), live_ref[0], jnp.int32).astype(jnp.float32),
             cell_ref[...].astype(jnp.float32),
-            jnp.zeros((2, slots), jnp.float32),
+            shifts,
+            jnp.zeros((1, slots), jnp.float32),
         ],
         axis=0,
     )
@@ -465,7 +449,7 @@
             zdst[pl.ds(at, rows), :] = jnp.where(face_lane, face, new)
         return carry
 
-    lax.fori_loop(x_low, x_high, one_plane, 0)
+    lax.fori_loop(x_low, x_high, one_plane, 0, unroll=True)
 
 
 def sweeps(frame, second, zframe, zsecond, forcing, coef, zforcing, zcoef, gz, out_ref, planes):
@@ -485,10 +469,9 @@
     sweep(frame, None, zframe, None, forcing, coef, zforcing, zcoef, gz, XO, planes - XO, channels, planes, finish)
 
 
-def put_density(out_ref, density_ref, cell_ref, live, message_ref=None):
+def put_density(out_ref, density_ref, cell, live, message_ref=None):
     channels, size_x, size_y, size_z = out_ref.shape
-    slots = cell_ref.shape[1]
-    cell = cell_ref[...]
+    slots = cell.shape[1]
     pick = (lax.broadcasted_iota(jnp.int32, (size_z, slots), 0) == (cell & (size_z - 1))).astype(jnp.bfloat16)
     count = size_x * size_y
     layers = out_ref[...].reshape(channels * count, size_z).astype(jnp.bfloat16)
@@ -509,42 +492,49 @@
             density_ref[brick] = message
 
 
+def parted(kept_ref):
+    flat = SIZE_Y + 2 * YO
+    flat = flat * (kept_ref.shape[0] // flat // KEPT)
+    ends = [kept_ref.shape[0] - 3 * flat + n * flat for n in range(4)]
+    return [kept_ref.at[0 : ends[0]]] + [kept_ref.at[ends[n] : ends[n + 1]] for n in range(3)]
+
+
 def first_kernel(
-    place_ref, shift_ref, frame_ref, forcing_ref, code_ref, depth_ref, low_ref, high_ref, cell_ref, message_ref,
-    out_ref, forcing_out, coef_out, zforcing_out, zcoef_out, density_ref, up_ref, down_ref,
-    first, second, zfirst, zsecond, code, zcode,
+    place_ref, frame_ref, forcing_ref, code_ref, depth_ref, low_ref, high_ref, message_ref,
+    out_ref, kept_ref, density_ref, up_ref, down_ref, first, second, zfirst, zsecond, code, zcode,
 ):
     gz = place_ref[1]
     rows = SIZE_Y + 2 * YO
     planes = code_ref.shape[0] // rows
+    forcing, coef, zforcing, zcoef = parted(kept_ref)
     first[...] = frame_ref[...]
-    forcing_out[...] = forcing_ref[...]
+    forcing[...] = forcing_ref[...]
     code[...] = code_ref[...]
     zcode[...] = depth_ref[...]
     base = take_edges(first, low_ref, high_ref, 0, 3, 80)
-    base = take_edges(forcing_out, low_ref, high_ref, base, 2, 80)
+    base = take_edges(forcing, low_ref, high_ref, base, 2, 80)
     base = take_edges(code, low_ref, high_ref, base, 2, 16)
     take_edges(zcode, low_ref, high_ref, base, 3, 16)
     lane = lanes((rows, 128)) & 15
     outer = (lane >= 1) & (lane <= 3)
+    shifts = [jnp.broadcast_to(message_ref[0, 6:7, n : n + 1], (rows, 128)) for n in range(CLASSES)]
     for x in range(planes):
         here = pl.ds(x * rows, rows)
         packed = zcode[here, :]
         zfirst[here, :] = jnp.where(outer, packed, 0.0)
-        zforcing_out[here, :] = jnp.where(outer, turned(packed, 128 - SEND), 0.0)
+        zforcing[here, :] = jnp.where(outer, turned(packed, 128 - SEND), 0.0)
         level = jnp.where(outer, turned(packed, 128 - 2 * SEND), 0.0)
         own_level = code[here, :]
-        zweight = jnp.zeros((rows, 128), jnp.float32)
-        weight = jnp.zeros((rows, 128), jnp.float32)
-        for index in range(shift_ref.shape[0]):
-            value = shift_ref[index]
-            zweight = jnp.where(level == index + 1.0, value, zweight)
-            weight = jnp.where(own_level == index + 1.0, value, weight)
-        zcoef_out[here, :] = jnp.where(level > 0.0, relax_weight / (6.0 + zweight), 0.0)
-        coef_out[here, :] = jnp.where(own_level > 0.0, relax_weight / (6.0 + weight), 0.0)
-    sweeps(first, second, zfirst, zsecond, forcing_out, coef_out, zforcing_out, zcoef_out, gz, out_ref, planes)
+        zshift = jnp.zeros((rows, 128), jnp.float32)
+        shift = jnp.zeros((rows, 128), jnp.float32)
+        for index in range(CLASSES):
+            zshift = jnp.where(level == index + 1.0, shifts[index], zshift)
+            shift = jnp.where(own_level == index + 1.0, shifts[index], shift)
+        zcoef[here, :] = jnp.where(level > 0.0, relax_weight / (6.0 + zshift), 0.0)
+        coef[here, :] = jnp.where(own_level > 0.0, relax_weight / (6.0 + shift), 0.0)
+    sweeps(first, second, zfirst, zsecond, forcing, coef, zforcing, zcoef, gz, out_ref, planes)
     put_planes(up_ref, down_ref, 0, out_ref, 3)
-    put_density(out_ref, density_ref, cell_ref, place_ref[2], message_ref)
+    put_density(out_ref, density_ref, message_ref[0, 5:6, :].astype(jnp.int32), place_ref[2], message_ref)
 
 
 def add_load(forcing, zforcing, near_ref, side, gz, channels, planes):
@@ -586,23 +576,24 @@
 
 
 def second_kernel(
-    place_ref, frame_ref, forcing_ref, coef_ref, zforcing_ref, zcoef_ref, depth_ref, low_ref, high_ref, cell_ref,
-    near_low, near_own, near_high, out_ref, density_ref, first, second, zfirst, zsecond, forcing, zforcing,
+    place_ref, frame_ref, kept_ref, depth_ref, low_ref, high_ref, near_low, near_own, near_high,
+    out_ref, density_ref, first, second, zfirst, zsecond, forcing, zforcing,
 ):
     gz = place_ref[1]
     rows = SIZE_Y + 2 * YO
-    planes = coef_ref.shape[0] // rows
+    planes = depth_ref.shape[0] // rows
     channels = out_ref.shape[0]
+    old, coef, zold, zcoef = parted(kept_ref)
     first[...] = frame_ref[...]
     zfirst[...] = depth_ref[...]
-    forcing[...] = forcing_ref[...]
-    zforcing[...] = zforcing_ref[...]
+    forcing[...] = old[...]
+    zforcing[...] = zold[...]
     base = take_edges(first, low_ref, high_ref, 0, 3, 80)
     take_edges(zfirst, low_ref, high_ref, base, 3, 16)
     for side, near in ((-1, near_low), (0, near_own), (1, near_high)):
         add_load(forcing, zforcing, near, side, gz, channels, planes)
-    sweeps(first, second, zfirst, zsecond, forcing, coef_ref, zforcing, zcoef_ref, gz, out_ref, planes)
-    put_density(out_ref, density_ref, cell_ref, place_ref[2])
+    sweeps(first, second, zfirst, zsecond, forcing, coef, zforcing, zcoef, gz, out_ref, planes)
+    put_density(out_ref, density_ref, near_own[6, 1:2, :].astype(jnp.int32), place_ref[2])
 
 
 def near_kernel(place_ref, parts_ref, targets_ref, near_ref, own_ref):
@@ -658,29 +649,41 @@
         (bf16(send_x, 128), bf16(send_x, 128), f32(*frame), f32(*frame), f32(*flat), f32(bricks, 8, slots)),
         [vm(initial_field.shape), vm(initial_field.shape), vm((1, *cell_class.shape), jnp.int32),
          pltpu.SemaphoreType.DMA((3,))],
-        "planes", (live_count,), initial_field, source_term, cell_class[None], panel_geometry, cells,
+        "planes", (live_count, class_shift), initial_field, source_term, cell_class[None], panel_geometry, cells,
         away=(0, 1, 2),
     )
     low, high = both_ways(up, down, "row")
     targets = lax.all_to_all(message, ("col", "gz"), 0, 0, tiled=True)
-    low, high, targets = lax.optimization_barrier((low, high, targets))
     start, forcing, code, depth = whole_call(
         functools.partial(frame_kernel, True, channels),
         (f32(*frame), f32(*frame), f32(*flat), bf16(planes * size_y, 128)), [], "frame", (place,),
         start, forcing, code, low, high, aliases={0: 0, 1: 1, 2: 2},
     )
     other = lax.ppermute(depth, "gz", [(0, 1), (1, 0)])
+    other, targets = lax.optimization_barrier((other, targets))
     zframe, up, down = whole_call(
         functools.partial(edge_kernel, True), (f32(*flat), bf16(480, 128), bf16(480, 128)), [], "edges", (),
         start, forcing, code, other,
     )
     low, high = both_ways(up, down, "col")
-    state, forcing, coef, zforcing, zcoef, density, up, down = whole_call(
+    smem = pl.BlockSpec(memory_space=pltpu.SMEM)
+    vmem = pl.BlockSpec(memory_space=pltpu.VMEM)
+    aims, table = pl.pallas_call(
+        compact_kernel,
+        in_specs=[vmem],
+        out_specs=(vmem, smem),
+        out_shape=(f32(bricks + 1, 8, slots), jax.ShapeDtypeStruct((bricks + 1,), jnp.int32)),
+        scratch_shapes=[vm((8, slots), jnp.int32), pltpu.SMEM((8, slots), jnp.int32), pltpu.SemaphoreType.DMA],
+        compiler_params=params(4),
+        name="compact",
+    )(targets)
+    low, high, aims, table = lax.optimization_barrier((low, high, aims, table))
+    state, kept, density, up, down = whole_call(
         first_kernel,
-        (f32(*initial_field.shape), f32(*frame), f32(*flat), f32(*flat), f32(*flat), f32(bricks, 2 * channels, slots),
+        (f32(*initial_field.shape), f32(frame[0] + 3 * flat[0], 128), f32(bricks, 2 * channels, slots),
          bf16(channels * 3 * size_y, 128), bf16(channels * 3 * size_y, 128)),
-        [vm(frame), vm(frame), vm(flat), vm(flat), vm(flat), vm(flat)], "first", (place, class_shift),
-        start, forcing, code, zframe, low, high, cells, message, megabytes=8,
+        [vm(frame), vm(frame), vm(flat), vm(flat), vm(flat), vm(flat)], "first", (place,),
+        start, forcing, code, zframe, low, high, message, megabytes=8,
     )
     low, high = both_ways(up, down, "row")
     densities = lax.all_to_all(density, "row", 0, 0, tiled=True)
@@ -690,27 +693,15 @@
     )
     other = lax.ppermute(depth, "gz", [(0, 1), (1, 0)])
     densities, depth = lax.optimization_barrier((densities, depth))
-    smem = pl.BlockSpec(memory_space=pltpu.SMEM)
-    vmem = pl.BlockSpec(memory_space=pltpu.VMEM)
-    packed, aims, table = pl.pallas_call(
-        compact_kernel,
-        in_specs=[vmem, vmem],
-        out_specs=(vmem, vmem, smem),
-        out_shape=(f32(bricks + 1, 2 * channels, slots), f32(bricks + 1, 8, slots),
-                   jax.ShapeDtypeStruct((2, bricks + 1), jnp.int32)),
-        scratch_shapes=[vm((8, slots), jnp.int32), pltpu.SMEM((8, slots), jnp.int32), pltpu.SemaphoreType.DMA],
-        compiler_params=params(4),
-        name="compact",
-    )(densities, targets)
-    tile, shares = make_tile(0, table, packed, aims, channels)
+    tile, shares = make_tile(0, table, densities, aims, channels)
     other, shares = lax.optimization_barrier((other, shares))
     zframe, up, down = whole_call(
         functools.partial(edge_kernel, False), (f32(*flat), bf16(288, 128), bf16(288, 128)), [], "edges", (),
         start, other,
     )
     low, high = both_ways(up, down, "col")
-    packed, up = lax.optimization_barrier((packed, up))
-    tile, shares = make_tile(1, table, packed, aims, channels, (tile, shares))
+    densities, up = lax.optimization_barrier((densities, up))
+    tile, shares = make_tile(1, table, densities, aims, channels, (tile, shares))
     shares = whole_call(arrange_kernel, f32(bricks, 6, channels, slots), [], "arrange", (table,), shares)
     parts = lax.all_to_all(shares, ("col", "gz"), 0, 0, tiled=True)
     near, _ = whole_call(near_kernel, (f32(7, channels, slots), f32(channels, slots)), [], "near", (place,), parts, targets)
@@ -718,7 +709,7 @@
     state, density = whole_call(
         second_kernel, (f32(*initial_field.shape), bf16(bricks, channels, slots)),
         [vm(frame), vm(frame), vm(flat), vm(flat), vm(frame), vm(flat)], "second", (place,),
-        start, forcing, coef, zforcing, zcoef, zframe, low, high, cells, near_low, near, near_high, megabytes=8,
+        start, kept, zframe, low, high, near_low, near, near_high, megabytes=8,
     )
     densities = lax.all_to_all(density, "row", 0, 0, tiled=True)
     shares = products(table, densities, tile, 512)

time: 170 us -> 154 us (0.906); the launches traced: 170 us -> 152 us
  Pallas kernels: 52.8 us -> 39.1 us
  waiting for transfers between devices: 24.2 us -> 15 us
  starting transfers between devices: 53.2 us -> 56.7 us
  local copies, waits for them, and re-layouts: 7.88 us -> 9.7 us
    pallas_call x2, Pallas kernels: 27.1 us -> 17.9 us  [make_tile(): pl.pallas_call(functools.partial(tile_kernel, half), grid=(bricks // 2,),...]
    ppermute x2, starting transfers between devices: 1.44 us -> 5.64 us  [local(): other = lax.ppermute(depth, 'gz', [(0, 1), (1, 0)])]
    pallas_call x10, Pallas kernels: 19 us -> 14.8 us  [whole_call(): pl.pallas_call(kernel, in_specs=[smem] * len(scalars) + [far if n in away...]
    all_to_all x1, waiting for transfers between devices: 6.65 us -> 2.77 us  [local(): targets = lax.all_to_all(message, ('col', 'gz'), 0, 0, tiled=True)]
    ppermute x2, waiting for transfers between devices: 3.75 us -> 0.01 us  [local(): other = lax.ppermute(depth, 'gz', [(0, 1), (1, 0)])]
    all_to_all x1, starting transfers between devices: 13.5 us -> 11.5 us  [local(): densities = lax.all_to_all(density, 'row', 0, 0, tiled=True)]
    unnamed x28 -> x26, local copies, waits for them, and re-layouts: 7.88 us -> 9.7 us
  transfers between devices with their start and end apart: 15 -> 15, of which waited for: 8 -> 6; matrix products, arithmetic and copies ran while one was open for 0% -> 0% of each run, Pallas kernels for 10% -> 9%
where the time goes in v4:
time: 154 us; the launch traced here: 152 us
  starting transfers between devices  56.7 us (37%)
  Pallas kernels  39.1 us (25%)
  blocking collectives  29.6 us (19%)
  waiting for transfers between devices  15 us (10%)
  local copies, waits for them, and re-layouts  9.7 us (6%)
    all_to_all x1, blocking collectives, local(): densities = lax.all_to_all(density, 'row', 0, 0, tiled=True)  19 us
    ppermute x5, starting transfers between devices, both_ways(): lax.ppermute(up, axis, pairs)  18.5 us
    pallas_call x2, Pallas kernels, make_tile(): pl.pallas_call(functools.partial(tile_kernel, half), grid=(bricks // 2,),...  17.9 us
    pallas_call x10, Pallas kernels, whole_call(): pl.pallas_call(kernel, in_specs=[smem] * len(scalars) + [far if n in away...  14.8 us
    all_to_all x1, starting transfers between devices, local(): densities = lax.all_to_all(density, 'row', 0, 0, tiled=True)  11.5 us
    all_to_all x1, blocking collectives, local(): parts = lax.all_to_all(shares, ('col', 'gz'), 0, 0, tiled=True)  10.6 us
    unnamed x26, local copies, waits for them, and re-layouts  9.7 us
    ppermute x5, starting transfers between devices, both_ways(): lax.ppermute(down, axis, [(b, a) for a, b in pairs])  8.33 us
  transfers between devices with their start and end apart: 15, of which 6 were waited for; matrix products, arithmetic and copies ran while one was open for 0% of the time, Pallas kernels for 9%

profile of v4, /device:TPU:1, one launch (start us, length us, event | category | flops | bytes accessed | tf_op | source)
XLA Modules:
  0.0 151.8 jit_solution(730795872636755481)
XLA Ops:
  5.9 1.4 planes.1
  7.4 4.9 %collective-permute-start = (bf16[672,128]{1,0:T(8,128)(2,1)S(1)}, bf16[672,128]{1,0:T(8,128)(2,1)S(1)}, u32[]{:S(2)}, u32[]{:S(2)}) collective-permute-start(bf16[672,128]{1,0:T(8,128)(2,1)S(1)} %get-tuple-element.47), channel_id=1, source_target_pairs={{0,16},{16,32},{32,48},{48,64},{64,80},{80,96},{96,112},{112,128},... | collective-permute-start | bytes 516104 | tf_op jit(solution)/shard_map/ppermute | solution.py:629
  12.3 1.9 %collective-permute-start.1 = (bf16[672,128]{1,0:T(8,128)(2,1)S(1)}, bf16[672,128]{1,0:T(8,128)(2,1)S(1)}, u32[]{:S(2)}, u32[]{:S(2)}) collective-permute-start(bf16[672,128]{1,0:T(8,128)(2,1)S(1)} %get-tuple-element.48), channel_id=1, source_target_pairs={{16,0},{32,16},{48,32},{64,48},{80,64},{96,80},{112,96},{128,112},... | collective-permute-start | bytes 516104 | tf_op jit(solution)/shard_map/ppermute | solution.py:629
  14.2 6.8 %all-to-all-start = ((f32[16,8,128]{2,1,0:T(8,128)}), f32[16,8,128]{2,1,0:T(8,128)S(1)}, u32[]{:S(2)}, u32[]{:S(2)}) async-start(f32[16,8,128]{2,1,0:T(8,128)} %get-tuple-element.53.message_ref), calls=%async_computation | async-start | bytes 131072 | tf_op jit(solution)/shard_map/all_to_all | solution.py:656
  22.0 2.9 %collective-permute-start.2 = (bf16[160,128]{1,0:T(8,128)(2,1)S(1)}, bf16[160,128]{1,0:T(8,128)(2,1)S(1)}, u32[]{:S(2)}, u32[]{:S(2)}) collective-permute-start(bf16[160,128]{1,0:T(8,128)(2,1)S(1)} %get-tuple-element.52), channel_id=1, source_target_pairs={{0,1},{1,0},{2,3},{3,2},{4,5},{5,4},{6,7},{7,6},{8,9},{9,8},{10,11... | collective-permute-start | bytes 122888 | tf_op jit(solution)/shard_map/ppermute | solution.py:662
  25.0 2.8 %all-to-all-done.target_ref.targets_ref = f32[16,8,128]{2,1,0:T(8,128)S(1)} async-done(((f32[16,8,128]{2,1,0:T(8,128)}), f32[16,8,128]{2,1,0:T(8,128)S(1)}, u32[]{:S(2)}, u32[]{:S(2)}) %all-to-all-start) | async-done | bytes 65568 | tf_op jit(solution)/shard_map/all_to_all | solution.py:656
  27.8 2.2 %collective-permute-start.3 = (bf16[480,128]{1,0:T(8,128)(2,1)S(1)}, bf16[480,128]{1,0:T(8,128)(2,1)S(1)}, u32[]{:S(2)}, u32[]{:S(2)}) collective-permute-start(bf16[480,128]{1,0:T(8,128)(2,1)S(1)} %get-tuple-element.56), channel_id=1, source_target_pairs={{0,2},{2,4},{4,6},{6,8},{8,10},{10,12},{12,14},{1,3},{3,5},{5,7},{... | collective-permute-start | bytes 368648 | tf_op jit(solution)/shard_map/ppermute | solution.py:629
  30.1 1.3 collective-permute-start.4
  31.4 1.2 compact.1
  33.2 3.9 %collective-permute-done.4.high_ref = bf16[480,128]{1,0:T(8,128)(2,1)S(1)} collective-permute-done((bf16[480,128]{1,0:T(8,128)(2,1)S(1)}, bf16[480,128]{1,0:T(8,128)(2,1)S(1)}, u32[]{:S(2)}, u32[]{:S(2)}) %collective-permute-start.4) | collective-permute-done | bytes 122912 | tf_op jit(solution)/shard_map/ppermute | solution.py:629
  37.1 3.6 %first.1 = (f32[8,4,16,128]{3,2,1,0:T(8,128)S(1)}, f32[2640,128]{1,0:T(8,128)S(1)}, f32[16,16,128]{2,1,0:T(8,128)S(1)}, bf16[384,128]{1,0:T(8,128)(2,1)S(1)}, bf16[384,128]{1,0:T(8,128)(2,1)S(1)}) custom-call(s32[3]{0:T(128)S(1)} %pad_add_fusion.place_ref, f32[1920,128]{1,0:T(8,128)S(1)} %get-tuple-element.49.refs_0_.frame_ref, ...), custom_call_target="tpu_custom_call" | custom-call | tf_op jit(solution)/shard_map/first/pallas_call | solution.py:52
  43.3 11.5 %all-to-all-start.1 = ((f32[16,16,128]{2,1,0:T(8,128)}), f32[16,16,128]{2,1,0:T(8,128)S(1)}, u32[]{:S(2)}, u32[]{:S(2)}) async-start(f32[16,16,128]{2,1,0:T(8,128)} %copy-done.6), calls=%async_computation.1 | async-start | bytes 262144 | tf_op jit(solution)/shard_map/all_to_all | solution.py:689
  54.8 3.5 %collective-permute-start.5 = (bf16[384,128]{1,0:T(8,128)(2,1)}, bf16[384,128]{1,0:T(8,128)(2,1)S(1)}, u32[]{:S(2)}, u32[]{:S(2)}) collective-permute-start(bf16[384,128]{1,0:T(8,128)(2,1)} %copy-done.12), channel_id=1, source_target_pairs={{0,16},{16,32},{32,48},{48,64},{64,80},{80,96},{96,112},{112,128},... | collective-permute-start | bytes 294920 | tf_op jit(solution)/shard_map/ppermute | solution.py:629
  58.3 1.9 %collective-permute-start.6 = (bf16[384,128]{1,0:T(8,128)(2,1)}, bf16[384,128]{1,0:T(8,128)(2,1)S(1)}, u32[]{:S(2)}, u32[]{:S(2)}) collective-permute-start(bf16[384,128]{1,0:T(8,128)(2,1)} %copy-done.11), channel_id=1, source_target_pairs={{16,0},{32,16},{48,32},{64,48},{80,64},{96,80},{112,96},{128,112},... | collective-permute-start | bytes 294920 | tf_op jit(solution)/shard_map/ppermute | solution.py:629
  60.6 3.9 %collective-permute-done.6.refs_2_ = bf16[384,128]{1,0:T(8,128)(2,1)S(1)} collective-permute-done((bf16[384,128]{1,0:T(8,128)(2,1)}, bf16[384,128]{1,0:T(8,128)(2,1)S(1)}, u32[]{:S(2)}, u32[]{:S(2)}) %collective-permute-start.6) | collective-permute-done | bytes 98336 | tf_op jit(solution)/shard_map/ppermute | solution.py:629
  64.5 0.9 copy-done.5
  66.2 2.7 %collective-permute-start.7 = (bf16[160,128]{1,0:T(8,128)(2,1)S(1)}, bf16[160,128]{1,0:T(8,128)(2,1)S(1)}, u32[]{:S(2)}, u32[]{:S(2)}) collective-permute-start(bf16[160,128]{1,0:T(8,128)(2,1)S(1)} %get-tuple-element.68), channel_id=1, source_target_pairs={{0,1},{1,0},{2,3},{3,2},{4,5},{5,4},{6,7},{7,6},{8,9},{9,8},{10,11... | collective-permute-start | bytes 122888 | tf_op jit(solution)/shard_map/ppermute | solution.py:694
  69.8 8.9 %tile.2 = (bf16[16384,2048]{1,0:T(8,128)(2,1)}, f32[16,8,128]{2,1,0:T(8,128)S(1)}) custom-call(s32[17]{0:T(128)S(1)} %get-tuple-element.69.table_ref, f32[16,16,128]{2,1,0:T(8,128)S(1)} %all-to-all-done.1.source_ref, f32[17,8,128]{2,1,0:T(8,128)S(1)} %copy-done.1), custom_call_target="tpu_custom_call" | custom-call | tf_op jit(solution)/shard_map/tile/pallas_call | solution.py:150
  78.8 9.0 %tile.3 = (bf16[16384,2048]{1,0:T(8,128)(2,1)}, f32[16,8,128]{2,1,0:T(8,128)S(1)}) custom-call(s32[17]{0:T(128)S(1)} %get-tuple-element.69.table_ref, f32[16,16,128]{2,1,0:T(8,128)S(1)} %all-to-all-done.1.source_ref, f32[17,8,128]{2,1,0:T(8,128)S(1)} %copy-done.1, ...), custom_call_target="tpu_custom_call", output_to_operand_aliasing={{0}: (3, {}), {1}: (4, {})} | custom-call | tf_op jit(solution)/shard_map/tile/pallas_call | solution.py:150
  87.8 1.4 arrange.1
  89.2 6.0 %all-to-all-start.2 = ((f32[16,6,8,128]{3,2,1,0:T(8,128)}), f32[16,6,8,128]{3,2,1,0:T(8,128)S(1)}, u32[]{:S(2)}, u32[]{:S(2)}) async-start(f32[16,6,8,128]{3,2,1,0:T(8,128)} %arrange.1), calls=%async_computation.2 | async-start | bytes 786432 | tf_op jit(solution)/shard_map/all_to_all | solution.py:706
  95.2 1.3 collective-permute-start.9
  96.5 4.0 %collective-permute-start.8 = (bf16[288,128]{1,0:T(8,128)(2,1)S(1)}, bf16[288,128]{1,0:T(8,128)(2,1)S(1)}, u32[]{:S(2)}, u32[]{:S(2)}) collective-permute-start(bf16[288,128]{1,0:T(8,128)(2,1)S(1)} %get-tuple-element.76), channel_id=1, source_target_pairs={{0,2},{2,4},{4,6},{6,8},{8,10},{10,12},{12,14},{1,3},{3,5},{5,7},{... | collective-permute-start | bytes 221192 | tf_op jit(solution)/shard_map/ppermute | solution.py:629
  100.5 3.4 %all-to-all-done.2.parts_ref = f32[16,6,8,128]{3,2,1,0:T(8,128)S(1)} async-done(((f32[16,6,8,128]{3,2,1,0:T(8,128)}), f32[16,6,8,128]{3,2,1,0:T(8,128)S(1)}, u32[]{:S(2)}, u32[]{:S(2)}) %all-to-all-start.2) | async-done | bytes 393248 | tf_op jit(solution)/shard_map/all_to_all | solution.py:706
  103.9 1.2 near.1
  105.0 1.9 %collective-permute-start.11 = (f32[7,8,128]{2,1,0:T(8,128)S(1)}, f32[7,8,128]{2,1,0:T(8,128)S(1)}, u32[]{:S(2)}, u32[]{:S(2)}) collective-permute-start(f32[7,8,128]{2,1,0:T(8,128)S(1)} %get-tuple-element.82.near_own), channel_id=1, source_target_pairs={{16,0},{32,16},{48,32},{64,48},{80,64},{96,80},{112,96},{128,112},... | collective-permute-start | bytes 86024 | tf_op jit(solution)/shard_map/ppermute | solution.py:629
  107.0 3.8 %collective-permute-start.10 = (f32[7,8,128]{2,1,0:T(8,128)S(1)}, f32[7,8,128]{2,1,0:T(8,128)S(1)}, u32[]{:S(2)}, u32[]{:S(2)}) collective-permute-start(f32[7,8,128]{2,1,0:T(8,128)S(1)} %get-tuple-element.82.near_own), channel_id=1, source_target_pairs={{0,16},{16,32},{32,48},{48,64},{64,80},{80,96},{96,112},{112,128},... | collective-permute-start | bytes 86024 | tf_op jit(solution)/shard_map/ppermute | solution.py:629
  111.6 4.2 %second.1 = (f32[8,4,16,128]{3,2,1,0:T(8,128)}, bf16[16,8,128]{2,1,0:T(8,128)(2,1)S(1)}) custom-call(s32[3]{0:T(128)S(1)} %pad_add_fusion.place_ref, f32[1920,128]{1,0:T(8,128)S(1)} %get-tuple-element.66.refs_0_.frame_ref, f32[2640,128]{1,0:T(8,128)S(1)} %get-tuple-element.67.kept_ref, f32[240,128]{1,0:T(8,128)S(1)} %get-tuple-element.75.depth_ref, ...), custom_call_target="tpu_custom_call" | custom-call | tf_op jit(solution)/shard_map/second/pallas_call | solution.py:52
  115.8 19.0 %all_to_all.25.density_ref = bf16[16,8,128]{2,1,0:T(8,128)(2,1)S(1)} all-to-all(bf16[16,8,128]{2,1,0:T(8,128)(2,1)S(1)} %get-tuple-element.84), channel_id=1, replica_groups=mesh['row'=16,'col'=8,'gz'=2] {'row'}, dimensions={0} | all-to-all | bytes 65536 | tf_op jit(solution)/shard_map/all_to_all | solution.py:714
  134.8 5.2 %product.1 = f32[16,8,128]{2,1,0:T(8,128)S(1)} custom-call(s32[17]{0:T(128)S(1)} %get-tuple-element.69.table_ref, bf16[16,8,128]{2,1,0:T(8,128)(2,1)S(1)} %all_to_all.25.density_ref, bf16[16384,2048]{1,0:T(8,128)(2,1)} %get-tuple-element.85.tile_ref), custom_call_target="tpu_custom_call" | custom-call | tf_op jit(solution)/shard_map/product/pallas_call | solution.py:233
  140.0 10.6 %all_to_all.26.parts_ref = f32[16,8,128]{2,1,0:T(8,128)S(1)} all-to-all(f32[16,8,128]{2,1,0:T(8,128)S(1)} %product.1), channel_id=1, replica_groups=mesh['row'=16,'col'=8,'gz'=2] {'col','gz'}, dimensions={0} | all-to-all | bytes 131072 | tf_op jit(solution)/shard_map/all_to_all | solution.py:716
  150.6 1.1 last.1
  (41 shorter events, 11.8 us)
Async XLA Ops:
  1.3 1.0 copy-start.2
  2.2 0.9 copy-start.3
  3.2 0.8 copy-start.7
  3.9 0.7 copy-start.8
  4.6 0.7 copy-start.9
  5.3 0.7 copy-start.10
  7.4 13.7 %collective-permute-start = (bf16[672,128]{1,0:T(8,128)(2,1)S(1)}, bf16[672,128]{1,0:T(8,128)(2,1)S(1)}, u32[]{:S(2)}, u32[]{:S(2)}) collective-permute-start(bf16[672,128]{1,0:T(8,128)(2,1)S(1)} %get-tuple-element.47), channel_id=1, source_target_pairs={{0,16},{16,32},{32,48},{48,64},{64,80},{80,96},{96,112},{112,128},... | collective-permute-start | bytes 516104 | tf_op jit(solution)/shard_map/ppermute | solution.py:629
  12.3 8.8 %collective-permute-start.1 = (bf16[672,128]{1,0:T(8,128)(2,1)S(1)}, bf16[672,128]{1,0:T(8,128)(2,1)S(1)}, u32[]{:S(2)}, u32[]{:S(2)}) collective-permute-start(bf16[672,128]{1,0:T(8,128)(2,1)S(1)} %get-tuple-element.48), channel_id=1, source_target_pairs={{16,0},{32,16},{48,32},{64,48},{80,64},{96,80},{112,96},{128,112},... | collective-permute-start | bytes 516104 | tf_op jit(solution)/shard_map/ppermute | solution.py:629
  14.2 13.5 %all-to-all-start = ((f32[16,8,128]{2,1,0:T(8,128)}), f32[16,8,128]{2,1,0:T(8,128)S(1)}, u32[]{:S(2)}, u32[]{:S(2)}) async-start(f32[16,8,128]{2,1,0:T(8,128)} %get-tuple-element.53.message_ref), calls=%async_computation | async-start | bytes 131072 | tf_op jit(solution)/shard_map/all_to_all | solution.py:656
  22.0 5.7 %collective-permute-start.2 = (bf16[160,128]{1,0:T(8,128)(2,1)S(1)}, bf16[160,128]{1,0:T(8,128)(2,1)S(1)}, u32[]{:S(2)}, u32[]{:S(2)}) collective-permute-start(bf16[160,128]{1,0:T(8,128)(2,1)S(1)} %get-tuple-element.52), channel_id=1, source_target_pairs={{0,1},{1,0},{2,3},{3,2},{4,5},{5,4},{6,7},{7,6},{8,9},{9,8},{10,11... | collective-permute-start | bytes 122888 | tf_op jit(solution)/shard_map/ppermute | solution.py:662
  27.8 5.4 %collective-permute-start.3 = (bf16[480,128]{1,0:T(8,128)(2,1)S(1)}, bf16[480,128]{1,0:T(8,128)(2,1)S(1)}, u32[]{:S(2)}, u32[]{:S(2)}) collective-permute-start(bf16[480,128]{1,0:T(8,128)(2,1)S(1)} %get-tuple-element.56), channel_id=1, source_target_pairs={{0,2},{2,4},{4,6},{6,8},{8,10},{10,12},{12,14},{1,3},{3,5},{5,7},{... | collective-permute-start | bytes 368648 | tf_op jit(solution)/shard_map/ppermute | solution.py:629
  30.1 7.0 %collective-permute-start.4 = (bf16[480,128]{1,0:T(8,128)(2,1)S(1)}, bf16[480,128]{1,0:T(8,128)(2,1)S(1)}, u32[]{:S(2)}, u32[]{:S(2)}) collective-permute-start(bf16[480,128]{1,0:T(8,128)(2,1)S(1)} %get-tuple-element.57), channel_id=1, source_target_pairs={{2,0},{4,2},{6,4},{8,6},{10,8},{12,10},{14,12},{3,1},{5,3},{7,5},{... | collective-permute-start | bytes 368648 | tf_op jit(solution)/shard_map/ppermute | solution.py:629
  32.6 0.6 copy-start
  40.7 0.7 copy-start.4
  41.4 0.6 copy-start.6
  42.0 0.6 copy-start.11
  42.6 0.6 copy-start.12
  43.3 25.6 %all-to-all-start.1 = ((f32[16,16,128]{2,1,0:T(8,128)}), f32[16,16,128]{2,1,0:T(8,128)S(1)}, u32[]{:S(2)}, u32[]{:S(2)}) async-start(f32[16,16,128]{2,1,0:T(8,128)} %copy-done.6), calls=%async_computation.1 | async-start | bytes 262144 | tf_op jit(solution)/shard_map/all_to_all | solution.py:689
  54.8 5.8 %collective-permute-start.5 = (bf16[384,128]{1,0:T(8,128)(2,1)}, bf16[384,128]{1,0:T(8,128)(2,1)S(1)}, u32[]{:S(2)}, u32[]{:S(2)}) collective-permute-start(bf16[384,128]{1,0:T(8,128)(2,1)} %copy-done.12), channel_id=1, source_target_pairs={{0,16},{16,32},{32,48},{48,64},{64,80},{80,96},{96,112},{112,128},... | collective-permute-start | bytes 294920 | tf_op jit(solution)/shard_map/ppermute | solution.py:629
  58.3 6.1 %collective-permute-start.6 = (bf16[384,128]{1,0:T(8,128)(2,1)}, bf16[384,128]{1,0:T(8,128)(2,1)S(1)}, u32[]{:S(2)}, u32[]{:S(2)}) collective-permute-start(bf16[384,128]{1,0:T(8,128)(2,1)} %copy-done.11), channel_id=1, source_target_pairs={{16,0},{32,16},{48,32},{64,48},{80,64},{96,80},{112,96},{128,112},... | collective-permute-start | bytes 294920 | tf_op jit(solution)/shard_map/ppermute | solution.py:629
  64.5 1.0 copy-start.5
  66.2 12.5 %collective-permute-start.7 = (bf16[160,128]{1,0:T(8,128)(2,1)S(1)}, bf16[160,128]{1,0:T(8,128)(2,1)S(1)}, u32[]{:S(2)}, u32[]{:S(2)}) collective-permute-start(bf16[160,128]{1,0:T(8,128)(2,1)S(1)} %get-tuple-element.68), channel_id=1, source_target_pairs={{0,1},{1,0},{2,3},{3,2},{4,5},{5,4},{6,7},{7,6},{8,9},{9,8},{10,11... | collective-permute-start | bytes 122888 | tf_op jit(solution)/shard_map/ppermute | solution.py:694
  68.9 0.9 copy-start.1
  89.2 14.7 %all-to-all-start.2 = ((f32[16,6,8,128]{3,2,1,0:T(8,128)}), f32[16,6,8,128]{3,2,1,0:T(8,128)S(1)}, u32[]{:S(2)}, u32[]{:S(2)}) async-start(f32[16,6,8,128]{3,2,1,0:T(8,128)} %arrange.1), calls=%async_computation.2 | async-start | bytes 786432 | tf_op jit(solution)/shard_map/all_to_all | solution.py:706
  95.2 15.6 %collective-permute-start.9 = (bf16[288,128]{1,0:T(8,128)(2,1)S(1)}, bf16[288,128]{1,0:T(8,128)(2,1)S(1)}, u32[]{:S(2)}, u32[]{:S(2)}) collective-permute-start(bf16[288,128]{1,0:T(8,128)(2,1)S(1)} %get-tuple-element.77), channel_id=1, source_target_pairs={{2,0},{4,2},{6,4},{8,6},{10,8},{12,10},{14,12},{3,1},{5,3},{7,5},{... | collective-permute-start | bytes 221192 | tf_op jit(solution)/shard_map/ppermute | solution.py:629
  96.5 14.3 %collective-permute-start.8 = (bf16[288,128]{1,0:T(8,128)(2,1)S(1)}, bf16[288,128]{1,0:T(8,128)(2,1)S(1)}, u32[]{:S(2)}, u32[]{:S(2)}) collective-permute-start(bf16[288,128]{1,0:T(8,128)(2,1)S(1)} %get-tuple-element.76), channel_id=1, source_target_pairs={{0,2},{2,4},{4,6},{6,8},{8,10},{10,12},{12,14},{1,3},{3,5},{5,7},{... | collective-permute-start | bytes 221192 | tf_op jit(solution)/shard_map/ppermute | solution.py:629
  105.0 5.8 %collective-permute-start.11 = (f32[7,8,128]{2,1,0:T(8,128)S(1)}, f32[7,8,128]{2,1,0:T(8,128)S(1)}, u32[]{:S(2)}, u32[]{:S(2)}) collective-permute-start(f32[7,8,128]{2,1,0:T(8,128)S(1)} %get-tuple-element.82.near_own), channel_id=1, source_target_pairs={{16,0},{32,16},{48,32},{64,48},{80,64},{96,80},{112,96},{128,112},... | collective-permute-start | bytes 86024 | tf_op jit(solution)/shard_map/ppermute | solution.py:629
  107.0 4.6 %collective-permute-start.10 = (f32[7,8,128]{2,1,0:T(8,128)S(1)}, f32[7,8,128]{2,1,0:T(8,128)S(1)}, u32[]{:S(2)}, u32[]{:S(2)}) collective-permute-start(f32[7,8,128]{2,1,0:T(8,128)S(1)} %get-tuple-element.82.near_own), channel_id=1, source_target_pairs={{0,16},{16,32},{32,48},{48,64},{64,80},{80,96},{96,112},{112,128},... | collective-permute-start | bytes 86024 | tf_op jit(solution)/shard_map/ppermute | solution.py:629

commit v5 on v4

--- a/solution.py
+++ b/solution.py
@@ -10,7 +10,8 @@
 
 SIZE_Y = 16
 CLASSES = 16
-KEPT = 11
+KEPT = 19
+TILES = 3
 ROOM = 8
 
 relax_weight = 0.8
@@ -20,7 +21,6 @@
 
 SINE = (6.283164044297846, -41.33714237050646, 81.34076886863805, -70.99343309793157)
 TURNS = wave_number / (2.0 * math.pi)
-ROUNDER = 12582912.0
 
 
 def from_everyone(x, axis):
@@ -78,7 +78,7 @@
     return lax.dot_general(a, b, (((1,), (1,)), ((), ())), preferred_element_type=jnp.float32)
 
 
-def compact_kernel(target_ref, target_out, table_ref, counts, table, arrived):
+def compact_kernel(place_ref, target_ref, target_out, note_ref, table_ref, counts, table, arrived):
     bricks, depth, slots = target_ref.shape
     lane = lanes((depth, slots))
     first = jnp.zeros((depth, slots), jnp.float32)
@@ -88,6 +88,7 @@
     copy = pltpu.make_async_copy(counts, table, arrived)
     copy.start()
     target_out[...] = jnp.zeros_like(target_out)
+    note_ref[...] = target_ref[place_ref[0] * 2 + place_ref[1]]
     copy.wait()
     begin = jnp.int32(0)
     for brick in range(bricks):
@@ -105,7 +106,7 @@
     out[group + 1] = jnp.where(lane < shift + count - rows.shape[1], moved, out[group + 1])
 
 
-def tile_kernel(half, table_ref, source_ref, target_ref, *refs):
+def tile_kernel(part, table_ref, source_ref, target_ref, *refs):
     tile_ref, share_ref, columns, density = refs[-4:]
     bricks, slots = source_ref.shape[0], source_ref.shape[2]
     channels = share_ref.shape[1]
@@ -116,7 +117,7 @@
         for brick in range(bricks):
             density[:, brick * slots : (brick + 1) * slots] = source_ref[brick, :channels].astype(jnp.bfloat16)
 
-    @pl.when((2 * step + half) * slots < table_ref[bricks])
+    @pl.when((TILES * step + part) * slots < table_ref[bricks])
     def _():
         columns[...] = jnp.transpose(target_ref[0])
         spread = [jnp.broadcast_to(columns[:, d : d + 1], (slots, slots)) for d in range(3)]
@@ -124,13 +125,10 @@
         for pair in range(0, bricks, 2):
             both = []
             for brick in (pair, pair + 1):
-                square = 1e-30
-                for d in range(3):
-                    delta = spread[d] - source_ref[brick, channels + d : channels + d + 1, :]
-                    square = square + delta * delta
+                delta = [spread[d] - source_ref[brick, channels + d : channels + d + 1, :] for d in range(3)]
+                square = delta[0] * delta[0] + (delta[1] * delta[1] + (delta[2] * delta[2] + 1e-30))
                 turns = square * lax.rsqrt(square)
-                whole = (turns + ROUNDER) - ROUNDER
-                angle = 0.25 - jnp.abs(turns - whole)
+                angle = 0.25 - jnp.abs(turns - jnp.round(turns))
                 angle2 = angle * angle
                 wave = SINE[-1]
                 for c in SINE[-2::-1]:
@@ -144,25 +142,25 @@
         share_ref[0] = total
 
 
-def make_tile(half, table, sources, targets, channels, before=()):
+def make_tile(part, table, sources, targets, channels, before=()):
     bricks, slots = sources.shape[0], sources.shape[2]
     far = pl.BlockSpec(memory_space=pl.ANY)
     return pl.pallas_call(
-        functools.partial(tile_kernel, half),
-        grid=(bricks // 2,),
+        functools.partial(tile_kernel, part),
+        grid=(-(-bricks // TILES),),
         in_specs=[
             pl.BlockSpec(memory_space=pltpu.SMEM),
             pl.BlockSpec(sources.shape, lambda b: (0, 0, 0)),
-            pl.BlockSpec((1, targets.shape[1], slots), lambda b: (2 * b + half, 0, 0)),
+            pl.BlockSpec((1, targets.shape[1], slots), lambda b: (TILES * b + part, 0, 0)),
         ]
         + [far] * len(before),
         out_specs=[
-            pl.BlockSpec((slots, bricks * slots), lambda b: (2 * b + half, 0)),
-            pl.BlockSpec((1, channels, slots), lambda b: (2 * b + half, 0, 0)),
+            pl.BlockSpec((slots, bricks * slots), lambda b: (TILES * b + part, 0)),
+            pl.BlockSpec((1, channels, slots), lambda b: (TILES * b + part, 0, 0)),
         ],
         out_shape=[
             jax.ShapeDtypeStruct((ROOM * bricks * slots, bricks * slots), jnp.bfloat16),
-            jax.ShapeDtypeStruct((bricks, channels, slots), jnp.float32),
+            jax.ShapeDtypeStruct((bricks + 2, channels, slots), jnp.float32),
         ],
         scratch_shapes=[
             pltpu.VMEM((slots, targets.shape[1]), jnp.float32),
@@ -270,21 +268,35 @@
             frame_ref[at : at + size_y, :] = field_ref[e, x].astype(jnp.float32) + offset
 
 
+def put_framed_planes(up_ref, down_ref, frame_ref, channels, depth):
+    rows = SIZE_Y + 2 * YO
+    planes = frame_ref.shape[0] // (channels * rows)
+    for e in range(channels):
+        for i in range(depth):
+            here = pl.ds((e * depth + i) * SIZE_Y, SIZE_Y)
+            high = (e * planes + planes - XO - depth + i) * rows + YO
+            low = (e * planes + XO + i) * rows + YO
+            up_ref[here, :] = frame_ref[high : high + SIZE_Y, :].astype(jnp.bfloat16)
+            down_ref[here, :] = frame_ref[low : low + SIZE_Y, :].astype(jnp.bfloat16)
+
+
 def planes_kernel(
-    factor, live_ref, shift_ref, state_hbm, source_hbm, class_hbm, geometry_ref, cell_ref,
-    up_ref, down_ref, frame_ref, forcing_ref, code_ref, message_ref, state_ref, source_ref, class_ref, arrived,
+    factor, live_ref, shift_ref, state_hbm, source_hbm, class_hbm, geometry_hbm, cell_hbm,
+    up_ref, down_ref, message_ref, state_ref, source_ref, class_ref, geometry_ref, cell_ref, arrived,
 ):
-    copies = [
-        pltpu.make_async_copy(state_hbm, state_ref, arrived.at[0]),
-        pltpu.make_async_copy(source_hbm, source_ref, arrived.at[1]),
-        pltpu.make_async_copy(class_hbm, class_ref, arrived.at[2]),
-    ]
+    pairs = (
+        (geometry_hbm, geometry_ref), (cell_hbm, cell_ref),
+        (state_hbm, state_ref), (source_hbm, source_ref), (class_hbm, class_ref),
+    )
+    copies = [pltpu.make_async_copy(a, b, arrived.at[n]) for n, (a, b) in enumerate(pairs)]
     for copy in copies:
         copy.start()
     slots = cell_ref.shape[1]
     shifts = jnp.zeros((1, slots), jnp.float32)
     for index in range(CLASSES):
         shifts = jnp.where(lanes((1, slots)) == index, shift_ref[index], shifts)
+    copies[0].wait()
+    copies[1].wait()
     message = jnp.concatenate(
         [
             geometry_ref[:3] * TURNS,
@@ -298,11 +310,15 @@
     )
     for brick in range(message_ref.shape[0]):
         message_ref[brick] = message
-    for copy in copies:
+    for copy in copies[2:]:
         copy.wait()
     base = put_planes(up_ref, down_ref, 0, state_ref, 3)
     base = put_planes(up_ref, down_ref, base, source_ref, 2)
     put_planes(up_ref, down_ref, base, class_ref, 2, 1.0)
+
+
+def own_kernel(state_ref, source_ref, class_ref, kept_ref):
+    frame_ref, forcing_ref, code_ref, _, _ = parted(kept_ref)
     own_cells(frame_ref, state_ref)
     own_cells(forcing_ref, source_ref)
     own_cells(code_ref, class_ref, 1.0)
@@ -335,12 +351,8 @@
     return out
 
 
-def frame_kernel(full, channels, place_ref, *refs):
-    if full:
-        _, _, _, low_ref, high_ref, frame_ref, forcing_ref, code_ref, depth_ref = refs
-    else:
-        state_ref, low_ref, high_ref, frame_ref, depth_ref = refs
-        own_cells(frame_ref, state_ref)
+def frame_kernel(full, channels, place_ref, _, low_ref, high_ref, kept_ref, depth_ref):
+    frame_ref, forcing_ref, code_ref, _, _ = parted(kept_ref)
     rows = SIZE_Y + 2 * YO
     planes = frame_ref.shape[0] // (channels * rows)
     base = beside(frame_ref, channels, low_ref, high_ref, 0, 3)
@@ -355,11 +367,8 @@
         depth_ref[x * SIZE_Y : (x + 1) * SIZE_Y, :] = out.astype(jnp.bfloat16)
 
 
-def edge_kernel(full, *refs):
-    if full:
-        frame_ref, forcing_ref, code_ref, other_ref, depth_ref, up_ref, down_ref = refs
-    else:
-        frame_ref, other_ref, depth_ref, up_ref, down_ref = refs
+def edge_kernel(full, kept_ref, other_ref, depth_ref, up_ref, down_ref):
+    frame_ref, forcing_ref, code_ref, _, _ = parted(kept_ref)
     rows = SIZE_Y + 2 * YO
     planes = depth_ref.shape[0] // rows
     depth_ref[...] = jnp.zeros_like(depth_ref)
@@ -452,8 +461,7 @@
     lax.fori_loop(x_low, x_high, one_plane, 0, unroll=True)
 
 
-def sweeps(frame, second, zframe, zsecond, forcing, coef, zforcing, zcoef, gz, out_ref, planes):
-    channels = out_ref.shape[0]
+def sweeps(frame, second, zframe, zsecond, forcing, coef, zforcing, zcoef, gz, channels, planes, finish):
     rows = SIZE_Y + 2 * YO
     face_lane = (lanes((rows, 128)) & 15) == 4 * gz
     for x in range(planes):
@@ -463,53 +471,41 @@
     sweep(frame, second, zframe, zsecond, forcing, coef, zforcing, zcoef, gz, 1, planes - 1, channels, planes)
     sweep(second, frame, zsecond, zframe, forcing, coef, zforcing, zcoef, gz, 2, planes - 2, channels, planes)
 
-    def finish(e, x, new):
-        out_ref[e, x - XO] = new[YO : YO + SIZE_Y, :]
-
     sweep(frame, None, zframe, None, forcing, coef, zforcing, zcoef, gz, XO, planes - XO, channels, planes, finish)
 
 
-def put_density(out_ref, density_ref, cell, live, message_ref=None):
-    channels, size_x, size_y, size_z = out_ref.shape
-    slots = cell.shape[1]
+def density_of(layers, cell, live, channels):
+    slots, size_z = cell.shape[1], layers.shape[1]
     pick = (lax.broadcasted_iota(jnp.int32, (size_z, slots), 0) == (cell & (size_z - 1))).astype(jnp.bfloat16)
-    count = size_x * size_y
-    layers = out_ref[...].reshape(channels * count, size_z).astype(jnp.bfloat16)
-    lines = jnp.dot(layers, pick, preferred_element_type=jnp.float32)
+    count = layers.shape[0] // channels
+    lines = jnp.dot(layers.astype(jnp.bfloat16), pick, preferred_element_type=jnp.float32)
     used = lanes((count, slots)) < live
     mask = used & (lax.broadcasted_iota(jnp.int32, (count, slots), 0) == (cell >> 7))
     found = [
         jnp.sum(jnp.where(mask, lines[e * count : (e + 1) * count, :], 0.0), axis=0, keepdims=True)
         for e in range(channels)
     ]
-    density = jnp.concatenate(found, axis=0).astype(jnp.bfloat16)
-    if message_ref is None:
-        for brick in range(density_ref.shape[0]):
-            density_ref[brick] = density
-    else:
-        message = jnp.concatenate([density.astype(jnp.float32), message_ref[0]], axis=0)
-        for brick in range(density_ref.shape[0]):
-            density_ref[brick] = message
+    return jnp.concatenate(found, axis=0).astype(jnp.bfloat16)
 
 
 def parted(kept_ref):
-    flat = SIZE_Y + 2 * YO
-    flat = flat * (kept_ref.shape[0] // flat // KEPT)
-    ends = [kept_ref.shape[0] - 3 * flat + n * flat for n in range(4)]
-    return [kept_ref.at[0 : ends[0]]] + [kept_ref.at[ends[n] : ends[n + 1]] for n in range(3)]
+    rows = kept_ref.shape[0] // KEPT
+    frame = (KEPT - 3) // 2 * rows
+    ends = [0, frame, 2 * frame] + [2 * frame + n * rows for n in range(1, 4)]
+    return [kept_ref.at[ends[n] : ends[n + 1]] for n in range(5)]
 
 
 def first_kernel(
-    place_ref, frame_ref, forcing_ref, code_ref, depth_ref, low_ref, high_ref, message_ref,
-    out_ref, kept_ref, density_ref, up_ref, down_ref, first, second, zfirst, zsecond, code, zcode,
+    place_ref, _, depth_ref, low_ref, high_ref, note_ref,
+    kept_ref, up_ref, down_ref, first, second, zfirst, zsecond, code, zcode,
 ):
     gz = place_ref[1]
     rows = SIZE_Y + 2 * YO
-    planes = code_ref.shape[0] // rows
-    forcing, coef, zforcing, zcoef = parted(kept_ref)
-    first[...] = frame_ref[...]
-    forcing[...] = forcing_ref[...]
-    code[...] = code_ref[...]
+    planes = depth_ref.shape[0] // rows
+    state, forcing, coef, zforcing, zcoef = parted(kept_ref)
+    channels = first.shape[0] // (planes * rows)
+    first[...] = state[...]
+    code[...] = coef[...]
     zcode[...] = depth_ref[...]
     base = take_edges(first, low_ref, high_ref, 0, 3, 80)
     base = take_edges(forcing, low_ref, high_ref, base, 2, 80)
@@ -517,7 +513,7 @@
     take_edges(zcode, low_ref, high_ref, base, 3, 16)
     lane = lanes((rows, 128)) & 15
     outer = (lane >= 1) & (lane <= 3)
-    shifts = [jnp.broadcast_to(message_ref[0, 6:7, n : n + 1], (rows, 128)) for n in range(CLASSES)]
+    shifts = [jnp.broadcast_to(note_ref[6:7, n : n + 1], (rows, 128)) for n in range(CLASSES)]
     for x in range(planes):
         here = pl.ds(x * rows, rows)
         packed = zcode[here, :]
@@ -532,9 +528,27 @@
             shift = jnp.where(own_level == index + 1.0, shifts[index], shift)
         zcoef[here, :] = jnp.where(level > 0.0, relax_weight / (6.0 + zshift), 0.0)
         coef[here, :] = jnp.where(own_level > 0.0, relax_weight / (6.0 + shift), 0.0)
-    sweeps(first, second, zfirst, zsecond, forcing, coef, zforcing, zcoef, gz, out_ref, planes)
-    put_planes(up_ref, down_ref, 0, out_ref, 3)
-    put_density(out_ref, density_ref, message_ref[0, 5:6, :].astype(jnp.int32), place_ref[2], message_ref)
+
+    def finish(e, x, new):
+        state[pl.ds((e * planes + x) * rows + YO, SIZE_Y), :] = new[YO : YO + SIZE_Y, :]
+
+    sweeps(first, second, zfirst, zsecond, forcing, coef, zforcing, zcoef, gz, channels, planes, finish)
+    put_framed_planes(up_ref, down_ref, state, channels, 3)
+
+
+def density_kernel(channels, place_ref, kept_ref, note_ref, density_ref, layers):
+    state = parted(kept_ref)[0]
+    rows = SIZE_Y + 2 * YO
+    planes = state.shape[0] // (channels * rows)
+    inner = planes - 2 * XO
+    for e in range(channels):
+        for x in range(inner):
+            at = (e * planes + XO + x) * rows + YO
+            layers[(e * inner + x) * SIZE_Y : (e * inner + x + 1) * SIZE_Y, :] = state[at : at + SIZE_Y, :]
+    density = density_of(layers[...], note_ref[5:6, :].astype(jnp.int32), place_ref[2], channels)
+    message = jnp.concatenate([density.astype(jnp.float32), note_ref[...]], axis=0)
+    for brick in range(density_ref.shape[0]):
+        density_ref[brick] = message
 
 
 def add_load(forcing, zforcing, near_ref, side, gz, channels, planes):
@@ -576,15 +590,15 @@
 
 
 def second_kernel(
-    place_ref, frame_ref, kept_ref, depth_ref, low_ref, high_ref, near_low, near_own, near_high,
+    place_ref, kept_ref, depth_ref, low_ref, high_ref, near_low, near_own, near_high,
     out_ref, density_ref, first, second, zfirst, zsecond, forcing, zforcing,
 ):
     gz = place_ref[1]
     rows = SIZE_Y + 2 * YO
     planes = depth_ref.shape[0] // rows
     channels = out_ref.shape[0]
-    old, coef, zold, zcoef = parted(kept_ref)
-    first[...] = frame_ref[...]
+    state, old, coef, zold, zcoef = parted(kept_ref)
+    first[...] = state[...]
     zfirst[...] = depth_ref[...]
     forcing[...] = old[...]
     zforcing[...] = zold[...]
@@ -592,8 +606,15 @@
     take_edges(zfirst, low_ref, high_ref, base, 3, 16)
     for side, near in ((-1, near_low), (0, near_own), (1, near_high)):
         add_load(forcing, zforcing, near, side, gz, channels, planes)
-    sweeps(first, second, zfirst, zsecond, forcing, coef, zforcing, zcoef, gz, out_ref, planes)
-    put_density(out_ref, density_ref, near_own[6, 1:2, :].astype(jnp.int32), place_ref[2])
+
+    def finish(e, x, new):
+        out_ref[e, x - XO] = new[YO : YO + SIZE_Y, :]
+
+    sweeps(first, second, zfirst, zsecond, forcing, coef, zforcing, zcoef, gz, channels, planes, finish)
+    layers = out_ref[...].reshape(-1, out_ref.shape[3])
+    density = density_of(layers, near_own[6, 1:2, :].astype(jnp.int32), place_ref[2], channels)
+    for brick in range(density_ref.shape[0]):
+        density_ref[brick] = density
 
 
 def near_kernel(place_ref, parts_ref, targets_ref, near_ref, own_ref):
@@ -644,64 +665,74 @@
     vm = lambda shape, dtype=jnp.float32: pltpu.VMEM(shape, dtype)
 
     send_x = channels * 5 * size_y + 2 * size_y
-    up, down, start, forcing, code, message = whole_call(
+    up, down, message = whole_call(
         functools.partial(planes_kernel, factor),
-        (bf16(send_x, 128), bf16(send_x, 128), f32(*frame), f32(*frame), f32(*flat), f32(bricks, 8, slots)),
+        (bf16(send_x, 128), bf16(send_x, 128), f32(bricks, 8, slots)),
         [vm(initial_field.shape), vm(initial_field.shape), vm((1, *cell_class.shape), jnp.int32),
-         pltpu.SemaphoreType.DMA((3,))],
+         vm(panel_geometry.shape), vm(cells.shape, jnp.int32), pltpu.SemaphoreType.DMA((5,))],
         "planes", (live_count, class_shift), initial_field, source_term, cell_class[None], panel_geometry, cells,
-        away=(0, 1, 2),
+        away=(0, 1, 2, 3, 4), megabytes=62,
+    )
+    kept = whole_call(
+        own_kernel, f32(2 * frame[0] + 3 * flat[0], 128), [], "own", (),
+        initial_field, source_term, cell_class[None],
     )
     low, high = both_ways(up, down, "row")
+    kept, depth = whole_call(
+        functools.partial(frame_kernel, True, channels),
+        (f32(*kept.shape), bf16(planes * size_y, 128)), [], "frame", (place,),
+        kept, low, high, aliases={0: 0},
+    )
+    other = lax.ppermute(depth, "gz", [(0, 1), (1, 0)])
     targets = lax.all_to_all(message, ("col", "gz"), 0, 0, tiled=True)
-    start, forcing, code, depth = whole_call(
-        functools.partial(frame_kernel, True, channels),
-        (f32(*frame), f32(*frame), f32(*flat), bf16(planes * size_y, 128)), [], "frame", (place,),
-        start, forcing, code, low, high, aliases={0: 0, 1: 1, 2: 2},
-    )
-    other = lax.ppermute(depth, "gz", [(0, 1), (1, 0)])
     other, targets = lax.optimization_barrier((other, targets))
     zframe, up, down = whole_call(
         functools.partial(edge_kernel, True), (f32(*flat), bf16(480, 128), bf16(480, 128)), [], "edges", (),
-        start, forcing, code, other,
+        kept, other,
     )
     low, high = both_ways(up, down, "col")
     smem = pl.BlockSpec(memory_space=pltpu.SMEM)
     vmem = pl.BlockSpec(memory_space=pltpu.VMEM)
-    aims, table = pl.pallas_call(
+    aims, note, table = pl.pallas_call(
         compact_kernel,
-        in_specs=[vmem],
-        out_specs=(vmem, smem),
-        out_shape=(f32(bricks + 1, 8, slots), jax.ShapeDtypeStruct((bricks + 1,), jnp.int32)),
+        in_specs=[smem, vmem],
+        out_specs=(vmem, vmem, smem),
+        out_shape=(f32(bricks + 2, 8, slots), f32(8, slots), jax.ShapeDtypeStruct((bricks + 1,), jnp.int32)),
         scratch_shapes=[vm((8, slots), jnp.int32), pltpu.SMEM((8, slots), jnp.int32), pltpu.SemaphoreType.DMA],
         compiler_params=params(4),
         name="compact",
-    )(targets)
+    )(place, targets)
     low, high, aims, table = lax.optimization_barrier((low, high, aims, table))
-    state, kept, density, up, down = whole_call(
+    kept, up, down = whole_call(
         first_kernel,
-        (f32(*initial_field.shape), f32(frame[0] + 3 * flat[0], 128), f32(bricks, 2 * channels, slots),
-         bf16(channels * 3 * size_y, 128), bf16(channels * 3 * size_y, 128)),
+        (f32(*kept.shape), bf16(channels * 3 * size_y, 128), bf16(channels * 3 * size_y, 128)),
         [vm(frame), vm(frame), vm(flat), vm(flat), vm(flat), vm(flat)], "first", (place,),
-        start, forcing, code, zframe, low, high, message, megabytes=8,
+        kept, zframe, low, high, note, aliases={0: 0}, megabytes=8,
+    )
+    density = whole_call(
+        functools.partial(density_kernel, channels), f32(bricks, 2 * channels, slots),
+        [vm((channels * size_x * size_y, size_z))], "density", (place,), kept, note,
     )
     low, high = both_ways(up, down, "row")
     densities = lax.all_to_all(density, "row", 0, 0, tiled=True)
-    start, depth = whole_call(
-        functools.partial(frame_kernel, False, channels), (f32(*frame), bf16(planes * size_y, 128)), [], "frame", (place,),
-        state, low, high,
+    done = make_tile(0, table, densities, aims, channels)
+    low, high, done = lax.optimization_barrier((low, high, done))
+    kept, depth = whole_call(
+        functools.partial(frame_kernel, False, channels),
+        (f32(*kept.shape), bf16(planes * size_y, 128)), [], "frame", (place,),
+        kept, low, high, aliases={0: 0},
     )
     other = lax.ppermute(depth, "gz", [(0, 1), (1, 0)])
     densities, depth = lax.optimization_barrier((densities, depth))
-    tile, shares = make_tile(0, table, densities, aims, channels)
-    other, shares = lax.optimization_barrier((other, shares))
+    done = make_tile(1, table, densities, aims, channels, done)
+    other, done = lax.optimization_barrier((other, done))
     zframe, up, down = whole_call(
         functools.partial(edge_kernel, False), (f32(*flat), bf16(288, 128), bf16(288, 128)), [], "edges", (),
-        start, other,
+        kept, other,
     )
     low, high = both_ways(up, down, "col")
     densities, up = lax.optimization_barrier((densities, up))
-    tile, shares = make_tile(1, table, densities, aims, channels, (tile, shares))
+    tile, shares = make_tile(2, table, densities, aims, channels, done)
     shares = whole_call(arrange_kernel, f32(bricks, 6, channels, slots), [], "arrange", (table,), shares)
     parts = lax.all_to_all(shares, ("col", "gz"), 0, 0, tiled=True)
     near, _ = whole_call(near_kernel, (f32(7, channels, slots), f32(channels, slots)), [], "near", (place,), parts, targets)
@@ -709,7 +740,7 @@
     state, density = whole_call(
         second_kernel, (f32(*initial_field.shape), bf16(bricks, channels, slots)),
         [vm(frame), vm(frame), vm(flat), vm(flat), vm(frame), vm(flat)], "second", (place,),
-        start, kept, zframe, low, high, near_low, near, near_high, megabytes=8,
+        kept, zframe, low, high, near_low, near, near_high, megabytes=8,
     )
     densities = lax.all_to_all(density, "row", 0, 0, tiled=True)
     shares = products(table, densities, tile, 512)

time: 154 us -> 149 us (0.968)
  local copies, waits for them, and re-layouts: 9.7 us -> 2.66 us
  Pallas kernels: 39.1 us -> 45.9 us
  blocking collectives: 29.6 us -> 27.2 us
  waiting for transfers between devices: 15 us -> 13 us
    unnamed x26 -> x6, local copies, waits for them, and re-layouts: 9.7 us -> 2.66 us
    pallas_call x3 -> x4, Pallas kernels: 19.1 us -> 23.7 us  [the longest x3 21.9 us: make_tile(): pl.pallas_call(functools.partial(tile_kernel, part), grid=(-(-bricks // T...]
    all_to_all x1, waiting for transfers between devices: 0.01 us -> 3.76 us  [local(): densities = lax.all_to_all(density, 'row', 0, 0, tiled=True)]
    ppermute x5, waiting for transfers between devices: 7.74 us -> 4 us  [both_ways(): lax.ppermute(down, axis, [(b, a) for a, b in pairs])]
    all_to_all x1, blocking collectives: 19 us -> 15.5 us  [local(): densities = lax.all_to_all(density, 'row', 0, 0, tiled=True)]
    all_to_all x1, waiting for transfers between devices: 2.77 us -> 0.01 us  [local(): targets = lax.all_to_all(message, ('col', 'gz'), 0, 0, tiled=True)]
    pallas_call x10 -> x12, Pallas kernels: 14.8 us -> 17 us  [whole_call(): pl.pallas_call(kernel, in_specs=[smem] * len(scalars) + [far if n in away...]
  transfers between devices with their start and end apart: 15 -> 15, of which waited for: 6 -> 5; matrix products, arithmetic and copies ran while one was open for 0% -> 0% of each run, Pallas kernels for 9% -> 13%
where the time goes in v5:
time: 149 us; the launch traced here: 148 us
  starting transfers between devices  57.8 us (39%)
  Pallas kernels  45.9 us (31%)
  blocking collectives  27.2 us (18%)
  waiting for transfers between devices  13 us (9%)
  local copies, waits for them, and re-layouts  2.66 us (2%)
  between operations  1.49 us (1%)
    pallas_call x3, Pallas kernels, make_tile(): pl.pallas_call(functools.partial(tile_kernel, part), grid=(-(-bricks // T...  21.9 us
    ppermute x5, starting transfers between devices, both_ways(): lax.ppermute(up, axis, pairs)  19.5 us
    pallas_call x12, Pallas kernels, whole_call(): pl.pallas_call(kernel, in_specs=[smem] * len(scalars) + [far if n in away...  17 us
    all_to_all x1, blocking collectives, local(): densities = lax.all_to_all(density, 'row', 0, 0, tiled=True)  15.5 us
    all_to_all x1, blocking collectives, local(): parts = lax.all_to_all(shares, ('col', 'gz'), 0, 0, tiled=True)  11.7 us
    all_to_all x1, starting transfers between devices, local(): densities = lax.all_to_all(density, 'row', 0, 0, tiled=True)  11.6 us
    ppermute x5, starting transfers between devices, both_ways(): lax.ppermute(down, axis, [(b, a) for a, b in pairs])  8.33 us
    all_to_all x1, starting transfers between devices, local(): targets = lax.all_to_all(message, ('col', 'gz'), 0, 0, tiled=True)  6.77 us
  transfers between devices with their start and end apart: 15, of which 5 were waited for; matrix products, arithmetic and copies ran while one was open for 0% of the time, Pallas kernels for 13%

profile of v5, /device:TPU:1, one launch (start us, length us, event | category | flops | bytes accessed | tf_op | source)
XLA Modules:
  0.0 148.1 jit_solution(13026779055406268903)
XLA Ops:
  1.3 2.5 %planes.1 = (bf16[672,128]{1,0:T(8,128)(2,1)}, bf16[672,128]{1,0:T(8,128)(2,1)}, f32[16,8,128]{2,1,0:T(8,128)}) custom-call(s32[1]{0:T(128)S(6)} %copy.23.live_ref, f32[16]{0:T(128)} %shift_ref.1, f32[8,4,16,128]{3,2,1,0:T(8,128)} %state_hbm.1, f32[8,4,16,128]{3,2,1,0:T(8,128)} %source_hbm.1, s32[1,4,16,128]{3,2,1,0:T(8,128)} %bitcast.4, ...), custom_call_target="tpu_custom_call" | custom-call | tf_op jit(solution)/shard_map/planes/pallas_call | solution.py:52
  3.8 4.9 %collective-permute-start = (bf16[672,128]{1,0:T(8,128)(2,1)}, bf16[672,128]{1,0:T(8,128)(2,1)S(1)}, u32[]{:S(2)}, u32[]{:S(2)}) collective-permute-start(bf16[672,128]{1,0:T(8,128)(2,1)} %get-tuple-element.45), channel_id=1, source_target_pairs={{0,16},{16,32},{32,48},{48,64},{64,80},{80,96},{96,112},{112,128},... | collective-permute-start | bytes 516104 | tf_op jit(solution)/shard_map/ppermute | solution.py:650
  8.8 1.9 %collective-permute-start.1 = (bf16[672,128]{1,0:T(8,128)(2,1)}, bf16[672,128]{1,0:T(8,128)(2,1)S(1)}, u32[]{:S(2)}, u32[]{:S(2)}) collective-permute-start(bf16[672,128]{1,0:T(8,128)(2,1)} %get-tuple-element.46), channel_id=1, source_target_pairs={{16,0},{32,16},{48,32},{64,48},{80,64},{96,80},{112,96},{128,112},... | collective-permute-start | bytes 516104 | tf_op jit(solution)/shard_map/ppermute | solution.py:650
  10.7 6.8 %all-to-all-start = ((f32[16,8,128]{2,1,0:T(8,128)}), f32[16,8,128]{2,1,0:T(8,128)S(1)}, u32[]{:S(2)}, u32[]{:S(2)}) async-start(f32[16,8,128]{2,1,0:T(8,128)} %get-tuple-element.49), calls=%async_computation | async-start | bytes 131072 | tf_op jit(solution)/shard_map/all_to_all | solution.py:687
  21.3 2.9 %collective-permute-start.2 = (bf16[160,128]{1,0:T(8,128)(2,1)S(1)}, bf16[160,128]{1,0:T(8,128)(2,1)S(1)}, u32[]{:S(2)}, u32[]{:S(2)}) collective-permute-start(bf16[160,128]{1,0:T(8,128)(2,1)S(1)} %get-tuple-element.48), channel_id=1, source_target_pairs={{0,1},{1,0},{2,3},{3,2},{4,5},{5,4},{6,7},{7,6},{8,9},{9,8},{10,11... | collective-permute-start | bytes 122888 | tf_op jit(solution)/shard_map/ppermute | solution.py:686
  24.3 1.5 %collective-permute-done.2.other_ref = bf16[160,128]{1,0:T(8,128)(2,1)S(1)} collective-permute-done((bf16[160,128]{1,0:T(8,128)(2,1)S(1)}, bf16[160,128]{1,0:T(8,128)(2,1)S(1)}, u32[]{:S(2)}, u32[]{:S(2)}) %collective-permute-start.2) | collective-permute-done | bytes 40992 | tf_op jit(solution)/shard_map/ppermute | solution.py:686
  25.9 3.3 %collective-permute-start.3 = (bf16[480,128]{1,0:T(8,128)(2,1)S(1)}, bf16[480,128]{1,0:T(8,128)(2,1)S(1)}, u32[]{:S(2)}, u32[]{:S(2)}) collective-permute-start(bf16[480,128]{1,0:T(8,128)(2,1)S(1)} %get-tuple-element.52), channel_id=1, source_target_pairs={{0,2},{2,4},{4,6},{6,8},{8,10},{10,12},{12,14},{1,3},{3,5},{5,7},{... | collective-permute-start | bytes 368648 | tf_op jit(solution)/shard_map/ppermute | solution.py:650
  29.1 1.3 collective-permute-start.4
  30.4 1.8 %compact.1 = (f32[18,8,128]{2,1,0:T(8,128)S(1)}, f32[8,128]{1,0:T(8,128)S(1)}, s32[17]{0:T(128)S(1)}) custom-call(s32[3]{0:T(128)S(1)} %pad_add_fusion.place_ref, f32[16,8,128]{2,1,0:T(8,128)S(1)} %all-to-all-done.target_ref.targets_ref), custom_call_target="tpu_custom_call" | custom-call | tf_op jit(solution)/shard_map/compact/pallas_call | solution.py:696
  32.3 4.0 %collective-permute-done.4.high_ref = bf16[480,128]{1,0:T(8,128)(2,1)S(1)} collective-permute-done((bf16[480,128]{1,0:T(8,128)(2,1)S(1)}, bf16[480,128]{1,0:T(8,128)(2,1)S(1)}, u32[]{:S(2)}, u32[]{:S(2)}) %collective-permute-start.4) | collective-permute-done | bytes 122912 | tf_op jit(solution)/shard_map/ppermute | solution.py:650
  36.2 3.2 %first.1 = (f32[4560,128]{1,0:T(8,128)S(1)}, bf16[384,128]{1,0:T(8,128)(2,1)S(1)}, bf16[384,128]{1,0:T(8,128)(2,1)S(1)}) custom-call(s32[3]{0:T(128)S(1)} %pad_add_fusion.place_ref, f32[4560,128]{1,0:T(8,128)S(1)} %get-tuple-element.47.kept_ref._, f32[240,128]{1,0:T(8,128)S(1)} %get-tuple-element.51.depth_ref, ...), custom_call_target="tpu_custom_call", output_to_operand_aliasing={{0}: (1, {})} | custom-call | tf_op jit(solution)/shard_map/first/pallas_call | solution.py:52
  39.4 1.4 density.1
  40.8 11.6 %all-to-all-start.1 = ((f32[16,16,128]{2,1,0:T(8,128)}), f32[16,16,128]{2,1,0:T(8,128)S(1)}, u32[]{:S(2)}, u32[]{:S(2)}) async-start(f32[16,16,128]{2,1,0:T(8,128)} %density.1), calls=%async_computation.1 | async-start | bytes 262144 | tf_op jit(solution)/shard_map/all_to_all | solution.py:717
  52.4 3.5 %collective-permute-start.5 = (bf16[384,128]{1,0:T(8,128)(2,1)S(1)}, bf16[384,128]{1,0:T(8,128)(2,1)S(1)}, u32[]{:S(2)}, u32[]{:S(2)}) collective-permute-start(bf16[384,128]{1,0:T(8,128)(2,1)S(1)} %get-tuple-element.61), channel_id=1, source_target_pairs={{0,16},{16,32},{32,48},{48,64},{64,80},{80,96},{96,112},{112,128},... | collective-permute-start | bytes 294920 | tf_op jit(solution)/shard_map/ppermute | solution.py:650
  55.9 1.9 %collective-permute-start.6 = (bf16[384,128]{1,0:T(8,128)(2,1)S(1)}, bf16[384,128]{1,0:T(8,128)(2,1)S(1)}, u32[]{:S(2)}, u32[]{:S(2)}) collective-permute-start(bf16[384,128]{1,0:T(8,128)(2,1)S(1)} %get-tuple-element.62), channel_id=1, source_target_pairs={{16,0},{32,16},{48,32},{64,48},{80,64},{96,80},{112,96},{128,112},... | collective-permute-start | bytes 294920 | tf_op jit(solution)/shard_map/ppermute | solution.py:650
  57.8 3.8 %all-to-all-done.1.source_ref = f32[16,16,128]{2,1,0:T(8,128)S(1)} async-done(((f32[16,16,128]{2,1,0:T(8,128)}), f32[16,16,128]{2,1,0:T(8,128)S(1)}, u32[]{:S(2)}, u32[]{:S(2)}) %all-to-all-start.1) | async-done | bytes 131104 | tf_op jit(solution)/shard_map/all_to_all | solution.py:717
  61.6 7.3 %tile.3 = (bf16[16384,2048]{1,0:T(8,128)(2,1)}, f32[18,8,128]{2,1,0:T(8,128)S(1)}) custom-call(s32[17]{0:T(128)S(1)} %get-tuple-element.63.table_ref, f32[16,16,128]{2,1,0:T(8,128)S(1)} %all-to-all-done.1.source_ref, f32[18,8,128]{2,1,0:T(8,128)S(1)} %get-tuple-element.64.target_ref), custom_call_target="tpu_custom_call" | custom-call | tf_op jit(solution)/shard_map/tile/pallas_call | solution.py:148
  69.6 2.8 %collective-permute-start.7 = (bf16[160,128]{1,0:T(8,128)(2,1)S(1)}, bf16[160,128]{1,0:T(8,128)(2,1)S(1)}, u32[]{:S(2)}, u32[]{:S(2)}) collective-permute-start(bf16[160,128]{1,0:T(8,128)(2,1)S(1)} %get-tuple-element.70), channel_id=1, source_target_pairs={{0,1},{1,0},{2,3},{3,2},{4,5},{5,4},{6,7},{7,6},{8,9},{9,8},{10,11... | collective-permute-start | bytes 122888 | tf_op jit(solution)/shard_map/ppermute | solution.py:725
  72.4 7.3 %tile.4 = (bf16[16384,2048]{1,0:T(8,128)(2,1)}, f32[18,8,128]{2,1,0:T(8,128)S(1)}) custom-call(s32[17]{0:T(128)S(1)} %get-tuple-element.63.table_ref, f32[16,16,128]{2,1,0:T(8,128)S(1)} %all-to-all-done.1.source_ref, f32[18,8,128]{2,1,0:T(8,128)S(1)} %get-tuple-element.64.target_ref, ...), custom_call_target="tpu_custom_call", output_to_operand_aliasing={{0}: (3, {}), {1}: (4, {})} | custom-call | tf_op jit(solution)/shard_map/tile/pallas_call | solution.py:148
  79.8 7.3 %tile.5 = (bf16[16384,2048]{1,0:T(8,128)(2,1)}, f32[18,8,128]{2,1,0:T(8,128)S(1)}) custom-call(s32[17]{0:T(128)S(1)} %get-tuple-element.63.table_ref, f32[16,16,128]{2,1,0:T(8,128)S(1)} %all-to-all-done.1.source_ref, f32[18,8,128]{2,1,0:T(8,128)S(1)} %get-tuple-element.64.target_ref, ...), custom_call_target="tpu_custom_call", output_to_operand_aliasing={{0}: (3, {}), {1}: (4, {})} | custom-call | tf_op jit(solution)/shard_map/tile/pallas_call | solution.py:148
  87.0 1.4 arrange.1
  88.5 5.9 %all-to-all-start.2 = ((f32[16,6,8,128]{3,2,1,0:T(8,128)}), f32[16,6,8,128]{3,2,1,0:T(8,128)S(1)}, u32[]{:S(2)}, u32[]{:S(2)}) async-start(f32[16,6,8,128]{3,2,1,0:T(8,128)} %arrange.1), calls=%async_computation.2 | async-start | bytes 786432 | tf_op jit(solution)/shard_map/all_to_all | solution.py:737
  94.3 1.3 collective-permute-start.9
  95.6 4.0 %collective-permute-start.8 = (bf16[288,128]{1,0:T(8,128)(2,1)S(1)}, bf16[288,128]{1,0:T(8,128)(2,1)S(1)}, u32[]{:S(2)}, u32[]{:S(2)}) collective-permute-start(bf16[288,128]{1,0:T(8,128)(2,1)S(1)} %get-tuple-element.78), channel_id=1, source_target_pairs={{0,2},{2,4},{4,6},{6,8},{8,10},{10,12},{12,14},{1,3},{3,5},{5,7},{... | collective-permute-start | bytes 221192 | tf_op jit(solution)/shard_map/ppermute | solution.py:650
  99.6 3.0 %all-to-all-done.2.parts_ref = f32[16,6,8,128]{3,2,1,0:T(8,128)S(1)} async-done(((f32[16,6,8,128]{3,2,1,0:T(8,128)}), f32[16,6,8,128]{3,2,1,0:T(8,128)S(1)}, u32[]{:S(2)}, u32[]{:S(2)}) %all-to-all-start.2) | async-done | bytes 393248 | tf_op jit(solution)/shard_map/all_to_all | solution.py:737
  102.6 1.2 near.1
  103.8 1.9 %collective-permute-start.11 = (f32[7,8,128]{2,1,0:T(8,128)S(1)}, f32[7,8,128]{2,1,0:T(8,128)S(1)}, u32[]{:S(2)}, u32[]{:S(2)}) collective-permute-start(f32[7,8,128]{2,1,0:T(8,128)S(1)} %get-tuple-element.84.near_own), channel_id=1, source_target_pairs={{16,0},{32,16},{48,32},{64,48},{80,64},{96,80},{112,96},{128,112},... | collective-permute-start | bytes 86024 | tf_op jit(solution)/shard_map/ppermute | solution.py:650
  105.7 3.8 %collective-permute-start.10 = (f32[7,8,128]{2,1,0:T(8,128)S(1)}, f32[7,8,128]{2,1,0:T(8,128)S(1)}, u32[]{:S(2)}, u32[]{:S(2)}) collective-permute-start(f32[7,8,128]{2,1,0:T(8,128)S(1)} %get-tuple-element.84.near_own), channel_id=1, source_target_pairs={{0,16},{16,32},{32,48},{48,64},{64,80},{80,96},{96,112},{112,128},... | collective-permute-start | bytes 86024 | tf_op jit(solution)/shard_map/ppermute | solution.py:650
  110.3 4.2 %second.1 = (f32[8,4,16,128]{3,2,1,0:T(8,128)}, bf16[16,8,128]{2,1,0:T(8,128)(2,1)S(1)}) custom-call(s32[3]{0:T(128)S(1)} %pad_add_fusion.place_ref, f32[4560,128]{1,0:T(8,128)S(1)} %get-tuple-element.69.kept_ref, f32[240,128]{1,0:T(8,128)S(1)} %get-tuple-element.77.depth_ref, bf16[288,128]{1,0:T(8,128)(2,1)S(1)} %collective-permute-done.8.low_ref, ...), custom_call_target="tpu_custom_call" | custom-call | tf_op jit(solution)/shard_map/second/pallas_call | solution.py:52
  114.5 15.5 %all_to_all.25.density_ref = bf16[16,8,128]{2,1,0:T(8,128)(2,1)S(1)} all-to-all(bf16[16,8,128]{2,1,0:T(8,128)(2,1)S(1)} %get-tuple-element.86), channel_id=1, replica_groups=mesh['row'=16,'col'=8,'gz'=2] {'row'}, dimensions={0} | all-to-all | bytes 65536 | tf_op jit(solution)/shard_map/all_to_all | solution.py:745
  130.0 5.2 %product.1 = f32[16,8,128]{2,1,0:T(8,128)S(1)} custom-call(s32[17]{0:T(128)S(1)} %get-tuple-element.63.table_ref, bf16[16,8,128]{2,1,0:T(8,128)(2,1)S(1)} %all_to_all.25.density_ref, bf16[16384,2048]{1,0:T(8,128)(2,1)} %get-tuple-element.87.tile_ref), custom_call_target="tpu_custom_call" | custom-call | tf_op jit(solution)/shard_map/product/pallas_call | solution.py:231
  135.2 11.7 %all_to_all.26.parts_ref = f32[16,8,128]{2,1,0:T(8,128)S(1)} all-to-all(f32[16,8,128]{2,1,0:T(8,128)S(1)} %product.1), channel_id=1, replica_groups=mesh['row'=16,'col'=8,'gz'=2] {'col','gz'}, dimensions={0} | all-to-all | bytes 131072 | tf_op jit(solution)/shard_map/all_to_all | solution.py:747
  (24 shorter events, 6.6 us)
Async XLA Ops:
  3.8 16.6 %collective-permute-start = (bf16[672,128]{1,0:T(8,128)(2,1)}, bf16[672,128]{1,0:T(8,128)(2,1)S(1)}, u32[]{:S(2)}, u32[]{:S(2)}) collective-permute-start(bf16[672,128]{1,0:T(8,128)(2,1)} %get-tuple-element.45), channel_id=1, source_target_pairs={{0,16},{16,32},{32,48},{48,64},{64,80},{80,96},{96,112},{112,128},... | collective-permute-start | bytes 516104 | tf_op jit(solution)/shard_map/ppermute | solution.py:650
  8.8 11.6 %collective-permute-start.1 = (bf16[672,128]{1,0:T(8,128)(2,1)}, bf16[672,128]{1,0:T(8,128)(2,1)S(1)}, u32[]{:S(2)}, u32[]{:S(2)}) collective-permute-start(bf16[672,128]{1,0:T(8,128)(2,1)} %get-tuple-element.46), channel_id=1, source_target_pairs={{16,0},{32,16},{48,32},{64,48},{80,64},{96,80},{112,96},{128,112},... | collective-permute-start | bytes 516104 | tf_op jit(solution)/shard_map/ppermute | solution.py:650
  10.7 13.6 %all-to-all-start = ((f32[16,8,128]{2,1,0:T(8,128)}), f32[16,8,128]{2,1,0:T(8,128)S(1)}, u32[]{:S(2)}, u32[]{:S(2)}) async-start(f32[16,8,128]{2,1,0:T(8,128)} %get-tuple-element.49), calls=%async_computation | async-start | bytes 131072 | tf_op jit(solution)/shard_map/all_to_all | solution.py:687
  17.6 1.0 copy-start
  18.5 0.9 copy-start.1
  19.5 0.8 copy-start.2
  21.3 4.4 %collective-permute-start.2 = (bf16[160,128]{1,0:T(8,128)(2,1)S(1)}, bf16[160,128]{1,0:T(8,128)(2,1)S(1)}, u32[]{:S(2)}, u32[]{:S(2)}) collective-permute-start(bf16[160,128]{1,0:T(8,128)(2,1)S(1)} %get-tuple-element.48), channel_id=1, source_target_pairs={{0,1},{1,0},{2,3},{3,2},{4,5},{5,4},{6,7},{7,6},{8,9},{9,8},{10,11... | collective-permute-start | bytes 122888 | tf_op jit(solution)/shard_map/ppermute | solution.py:686
  25.9 6.4 %collective-permute-start.3 = (bf16[480,128]{1,0:T(8,128)(2,1)S(1)}, bf16[480,128]{1,0:T(8,128)(2,1)S(1)}, u32[]{:S(2)}, u32[]{:S(2)}) collective-permute-start(bf16[480,128]{1,0:T(8,128)(2,1)S(1)} %get-tuple-element.52), channel_id=1, source_target_pairs={{0,2},{2,4},{4,6},{6,8},{8,10},{10,12},{12,14},{1,3},{3,5},{5,7},{... | collective-permute-start | bytes 368648 | tf_op jit(solution)/shard_map/ppermute | solution.py:650
  29.1 7.1 %collective-permute-start.4 = (bf16[480,128]{1,0:T(8,128)(2,1)S(1)}, bf16[480,128]{1,0:T(8,128)(2,1)S(1)}, u32[]{:S(2)}, u32[]{:S(2)}) collective-permute-start(bf16[480,128]{1,0:T(8,128)(2,1)S(1)} %get-tuple-element.53), channel_id=1, source_target_pairs={{2,0},{4,2},{6,4},{8,6},{10,8},{12,10},{14,12},{3,1},{5,3},{7,5},{... | collective-permute-start | bytes 368648 | tf_op jit(solution)/shard_map/ppermute | solution.py:650
  40.8 20.8 %all-to-all-start.1 = ((f32[16,16,128]{2,1,0:T(8,128)}), f32[16,16,128]{2,1,0:T(8,128)S(1)}, u32[]{:S(2)}, u32[]{:S(2)}) async-start(f32[16,16,128]{2,1,0:T(8,128)} %density.1), calls=%async_computation.1 | async-start | bytes 262144 | tf_op jit(solution)/shard_map/all_to_all | solution.py:717
  52.4 16.5 %collective-permute-start.5 = (bf16[384,128]{1,0:T(8,128)(2,1)S(1)}, bf16[384,128]{1,0:T(8,128)(2,1)S(1)}, u32[]{:S(2)}, u32[]{:S(2)}) collective-permute-start(bf16[384,128]{1,0:T(8,128)(2,1)S(1)} %get-tuple-element.61), channel_id=1, source_target_pairs={{0,16},{16,32},{32,48},{48,64},{64,80},{80,96},{96,112},{112,128},... | collective-permute-start | bytes 294920 | tf_op jit(solution)/shard_map/ppermute | solution.py:650
  55.9 13.0 %collective-permute-start.6 = (bf16[384,128]{1,0:T(8,128)(2,1)S(1)}, bf16[384,128]{1,0:T(8,128)(2,1)S(1)}, u32[]{:S(2)}, u32[]{:S(2)}) collective-permute-start(bf16[384,128]{1,0:T(8,128)(2,1)S(1)} %get-tuple-element.62), channel_id=1, source_target_pairs={{16,0},{32,16},{48,32},{64,48},{80,64},{96,80},{112,96},{128,112},... | collective-permute-start | bytes 294920 | tf_op jit(solution)/shard_map/ppermute | solution.py:650
  69.6 10.1 %collective-permute-start.7 = (bf16[160,128]{1,0:T(8,128)(2,1)S(1)}, bf16[160,128]{1,0:T(8,128)(2,1)S(1)}, u32[]{:S(2)}, u32[]{:S(2)}) collective-permute-start(bf16[160,128]{1,0:T(8,128)(2,1)S(1)} %get-tuple-element.70), channel_id=1, source_target_pairs={{0,1},{1,0},{2,3},{3,2},{4,5},{5,4},{6,7},{7,6},{8,9},{9,8},{10,11... | collective-permute-start | bytes 122888 | tf_op jit(solution)/shard_map/ppermute | solution.py:725
  88.5 14.2 %all-to-all-start.2 = ((f32[16,6,8,128]{3,2,1,0:T(8,128)}), f32[16,6,8,128]{3,2,1,0:T(8,128)S(1)}, u32[]{:S(2)}, u32[]{:S(2)}) async-start(f32[16,6,8,128]{3,2,1,0:T(8,128)} %arrange.1), calls=%async_computation.2 | async-start | bytes 786432 | tf_op jit(solution)/shard_map/all_to_all | solution.py:737
  94.3 15.2 %collective-permute-start.9 = (bf16[288,128]{1,0:T(8,128)(2,1)S(1)}, bf16[288,128]{1,0:T(8,128)(2,1)S(1)}, u32[]{:S(2)}, u32[]{:S(2)}) collective-permute-start(bf16[288,128]{1,0:T(8,128)(2,1)S(1)} %get-tuple-element.79), channel_id=1, source_target_pairs={{2,0},{4,2},{6,4},{8,6},{10,8},{12,10},{14,12},{3,1},{5,3},{7,5},{... | collective-permute-start | bytes 221192 | tf_op jit(solution)/shard_map/ppermute | solution.py:650
  95.6 13.9 %collective-permute-start.8 = (bf16[288,128]{1,0:T(8,128)(2,1)S(1)}, bf16[288,128]{1,0:T(8,128)(2,1)S(1)}, u32[]{:S(2)}, u32[]{:S(2)}) collective-permute-start(bf16[288,128]{1,0:T(8,128)(2,1)S(1)} %get-tuple-element.78), channel_id=1, source_target_pairs={{0,2},{2,4},{4,6},{6,8},{8,10},{10,12},{12,14},{1,3},{3,5},{5,7},{... | collective-permute-start | bytes 221192 | tf_op jit(solution)/shard_map/ppermute | solution.py:650
  103.8 5.8 %collective-permute-start.11 = (f32[7,8,128]{2,1,0:T(8,128)S(1)}, f32[7,8,128]{2,1,0:T(8,128)S(1)}, u32[]{:S(2)}, u32[]{:S(2)}) collective-permute-start(f32[7,8,128]{2,1,0:T(8,128)S(1)} %get-tuple-element.84.near_own), channel_id=1, source_target_pairs={{16,0},{32,16},{48,32},{64,48},{80,64},{96,80},{112,96},{128,112},... | collective-permute-start | bytes 86024 | tf_op jit(solution)/shard_map/ppermute | solution.py:650
  105.7 4.6 %collective-permute-start.10 = (f32[7,8,128]{2,1,0:T(8,128)S(1)}, f32[7,8,128]{2,1,0:T(8,128)S(1)}, u32[]{:S(2)}, u32[]{:S(2)}) collective-permute-start(f32[7,8,128]{2,1,0:T(8,128)S(1)} %get-tuple-element.84.near_own), channel_id=1, source_target_pairs={{0,16},{16,32},{32,48},{48,64},{64,80},{80,96},{96,112},{112,128},... | collective-permute-start | bytes 86024 | tf_op jit(solution)/shard_map/ppermute | solution.py:650

commit v6 on v5

--- a/solution.py
+++ b/solution.py
@@ -78,7 +78,7 @@
     return lax.dot_general(a, b, (((1,), (1,)), ((), ())), preferred_element_type=jnp.float32)
 
 
-def compact_kernel(place_ref, target_ref, target_out, note_ref, table_ref, counts, table, arrived):
+def compact_kernel(target_ref, target_out, note_ref, table_ref, counts, table, arrived):
     bricks, depth, slots = target_ref.shape
     lane = lanes((depth, slots))
     first = jnp.zeros((depth, slots), jnp.float32)
@@ -88,7 +88,7 @@
     copy = pltpu.make_async_copy(counts, table, arrived)
     copy.start()
     target_out[...] = jnp.zeros_like(target_out)
-    note_ref[...] = target_ref[place_ref[0] * 2 + place_ref[1]]
+    note_ref[...] = target_ref[lax.axis_index("col") * 2 + lax.axis_index("gz")]
     copy.wait()
     begin = jnp.int32(0)
     for brick in range(bricks):
@@ -281,22 +281,22 @@
 
 
 def planes_kernel(
-    factor, live_ref, shift_ref, state_hbm, source_hbm, class_hbm, geometry_hbm, cell_hbm,
-    up_ref, down_ref, message_ref, state_ref, source_ref, class_ref, geometry_ref, cell_ref, arrived,
+    factor, state_hbm, source_hbm, class_hbm, geometry_hbm, cell_hbm, live_hbm, shift_hbm,
+    up_ref, down_ref, message_ref, state_ref, source_ref, class_ref, geometry_ref, cell_ref, live_ref, shift_ref, arrived,
 ):
     pairs = (
-        (geometry_hbm, geometry_ref), (cell_hbm, cell_ref),
+        (live_hbm, live_ref), (shift_hbm, shift_ref), (geometry_hbm, geometry_ref), (cell_hbm, cell_ref),
         (state_hbm, state_ref), (source_hbm, source_ref), (class_hbm, class_ref),
     )
     copies = [pltpu.make_async_copy(a, b, arrived.at[n]) for n, (a, b) in enumerate(pairs)]
     for copy in copies:
         copy.start()
     slots = cell_ref.shape[1]
+    for copy in copies[:4]:
+        copy.wait()
     shifts = jnp.zeros((1, slots), jnp.float32)
     for index in range(CLASSES):
         shifts = jnp.where(lanes((1, slots)) == index, shift_ref[index], shifts)
-    copies[0].wait()
-    copies[1].wait()
     message = jnp.concatenate(
         [
             geometry_ref[:3] * TURNS,
@@ -310,7 +310,7 @@
     )
     for brick in range(message_ref.shape[0]):
         message_ref[brick] = message
-    for copy in copies[2:]:
+    for copy in copies[4:]:
         copy.wait()
     base = put_planes(up_ref, down_ref, 0, state_ref, 3)
     base = put_planes(up_ref, down_ref, base, source_ref, 2)
@@ -351,7 +351,7 @@
     return out
 
 
-def frame_kernel(full, channels, place_ref, _, low_ref, high_ref, kept_ref, depth_ref):
+def frame_kernel(full, channels, _, low_ref, high_ref, kept_ref, depth_ref):
     frame_ref, forcing_ref, code_ref, _, _ = parted(kept_ref)
     rows = SIZE_Y + 2 * YO
     planes = frame_ref.shape[0] // (channels * rows)
@@ -361,7 +361,7 @@
         base = beside(forcing_ref, channels, low_ref, high_ref, base, 2)
         beside(code_ref, 1, low_ref, high_ref, base, 2)
         frames = [frame_ref, forcing_ref, code_ref]
-    gz = place_ref[1]
+    gz = lax.axis_index("gz")
     for x in range(planes):
         out = depth_rows(frames, gz, x, SIZE_Y, rows, planes, channels)
         depth_ref[x * SIZE_Y : (x + 1) * SIZE_Y, :] = out.astype(jnp.bfloat16)
@@ -479,7 +479,7 @@
     pick = (lax.broadcasted_iota(jnp.int32, (size_z, slots), 0) == (cell & (size_z - 1))).astype(jnp.bfloat16)
     count = layers.shape[0] // channels
     lines = jnp.dot(layers.astype(jnp.bfloat16), pick, preferred_element_type=jnp.float32)
-    used = lanes((count, slots)) < live
+    used = lanes((count, slots)) < live.astype(jnp.int32)
     mask = used & (lax.broadcasted_iota(jnp.int32, (count, slots), 0) == (cell >> 7))
     found = [
         jnp.sum(jnp.where(mask, lines[e * count : (e + 1) * count, :], 0.0), axis=0, keepdims=True)
@@ -496,10 +496,10 @@
 
 
 def first_kernel(
-    place_ref, _, depth_ref, low_ref, high_ref, note_ref,
-    kept_ref, up_ref, down_ref, first, second, zfirst, zsecond, code, zcode,
+    _, depth_ref, low_ref, high_ref, note_ref,
+    kept_ref, density_ref, up_ref, down_ref, first, second, zfirst, zsecond, code, zcode, layers,
 ):
-    gz = place_ref[1]
+    gz = lax.axis_index("gz")
     rows = SIZE_Y + 2 * YO
     planes = depth_ref.shape[0] // rows
     state, forcing, coef, zforcing, zcoef = parted(kept_ref)
@@ -530,22 +530,13 @@
         coef[here, :] = jnp.where(own_level > 0.0, relax_weight / (6.0 + shift), 0.0)
 
     def finish(e, x, new):
-        state[pl.ds((e * planes + x) * rows + YO, SIZE_Y), :] = new[YO : YO + SIZE_Y, :]
+        own = new[YO : YO + SIZE_Y, :]
+        state[pl.ds((e * planes + x) * rows + YO, SIZE_Y), :] = own
+        layers[pl.ds((e * (planes - 2 * XO) + x - XO) * SIZE_Y, SIZE_Y), :] = own
 
     sweeps(first, second, zfirst, zsecond, forcing, coef, zforcing, zcoef, gz, channels, planes, finish)
     put_framed_planes(up_ref, down_ref, state, channels, 3)
-
-
-def density_kernel(channels, place_ref, kept_ref, note_ref, density_ref, layers):
-    state = parted(kept_ref)[0]
-    rows = SIZE_Y + 2 * YO
-    planes = state.shape[0] // (channels * rows)
-    inner = planes - 2 * XO
-    for e in range(channels):
-        for x in range(inner):
-            at = (e * planes + XO + x) * rows + YO
-            layers[(e * inner + x) * SIZE_Y : (e * inner + x + 1) * SIZE_Y, :] = state[at : at + SIZE_Y, :]
-    density = density_of(layers[...], note_ref[5:6, :].astype(jnp.int32), place_ref[2], channels)
+    density = density_of(layers[...], note_ref[5:6, :].astype(jnp.int32), note_ref[4:5, :], channels)
     message = jnp.concatenate([density.astype(jnp.float32), note_ref[...]], axis=0)
     for brick in range(density_ref.shape[0]):
         density_ref[brick] = message
@@ -590,10 +581,10 @@
 
 
 def second_kernel(
-    place_ref, kept_ref, depth_ref, low_ref, high_ref, near_low, near_own, near_high,
+    kept_ref, depth_ref, low_ref, high_ref, near_low, near_own, near_high,
     out_ref, density_ref, first, second, zfirst, zsecond, forcing, zforcing,
 ):
-    gz = place_ref[1]
+    gz = lax.axis_index("gz")
     rows = SIZE_Y + 2 * YO
     planes = depth_ref.shape[0] // rows
     channels = out_ref.shape[0]
@@ -612,13 +603,13 @@
 
     sweeps(first, second, zfirst, zsecond, forcing, coef, zforcing, zcoef, gz, channels, planes, finish)
     layers = out_ref[...].reshape(-1, out_ref.shape[3])
-    density = density_of(layers, near_own[6, 1:2, :].astype(jnp.int32), place_ref[2], channels)
+    density = density_of(layers, near_own[6, 1:2, :].astype(jnp.int32), near_own[6, 7:8, :], channels)
     for brick in range(density_ref.shape[0]):
         density_ref[brick] = density
 
 
-def near_kernel(place_ref, parts_ref, targets_ref, near_ref, own_ref):
-    col, gz = place_ref[0], place_ref[1]
+def near_kernel(parts_ref, targets_ref, near_ref):
+    col, gz = lax.axis_index("col"), lax.axis_index("gz")
     cols = targets_ref.shape[0] // 2
     slots = targets_ref.shape[2]
     lane = lanes((8, slots))
@@ -634,14 +625,14 @@
         near_ref[n] = total
         near_ref[6, n : n + 1, :] = about[5:6, :]
         if n == 1:
-            own_ref[...] = total
-
-
-def last_kernel(place_ref, parts_ref, own_ref):
+            near_ref[6, 7:8, :] = about[4:5, :]
+
+
+def last_kernel(parts_ref, own_ref):
     total = parts_ref[0]
     for sender in range(1, parts_ref.shape[0]):
         total = total + parts_ref[sender]
-    own_ref[...] = jnp.where(lanes(total.shape) < place_ref[2], total, 0.0)
+    own_ref[...] = total
 
 
 def both_ways(up, down, axis):
@@ -660,7 +651,6 @@
     factor = 1.0 / math.sqrt(panels)
     planes, rows = size_x + 2 * XO, size_y + 2 * YO
     frame, flat = (channels * planes * rows, 128), (planes * rows, 128)
-    place = jnp.stack([lax.axis_index("col"), lax.axis_index("gz"), live_count[0]]).astype(jnp.int32)
     cells = surface_cell[None]
     vm = lambda shape, dtype=jnp.float32: pltpu.VMEM(shape, dtype)
 
@@ -669,9 +659,10 @@
         functools.partial(planes_kernel, factor),
         (bf16(send_x, 128), bf16(send_x, 128), f32(bricks, 8, slots)),
         [vm(initial_field.shape), vm(initial_field.shape), vm((1, *cell_class.shape), jnp.int32),
-         vm(panel_geometry.shape), vm(cells.shape, jnp.int32), pltpu.SemaphoreType.DMA((5,))],
-        "planes", (live_count, class_shift), initial_field, source_term, cell_class[None], panel_geometry, cells,
-        away=(0, 1, 2, 3, 4), megabytes=62,
+         vm(panel_geometry.shape), vm(cells.shape, jnp.int32), pltpu.SMEM((1,), jnp.int32), pltpu.SMEM((CLASSES,), jnp.float32),
+         pltpu.SemaphoreType.DMA((7,))],
+        "planes", (), initial_field, source_term, cell_class[None], panel_geometry, cells, live_count, class_shift,
+        away=(0, 1, 2, 3, 4, 5, 6), megabytes=62,
     )
     kept = whole_call(
         own_kernel, f32(2 * frame[0] + 3 * flat[0], 128), [], "own", (),
@@ -680,7 +671,7 @@
     low, high = both_ways(up, down, "row")
     kept, depth = whole_call(
         functools.partial(frame_kernel, True, channels),
-        (f32(*kept.shape), bf16(planes * size_y, 128)), [], "frame", (place,),
+        (f32(*kept.shape), bf16(planes * size_y, 128)), [], "frame", (),
         kept, low, high, aliases={0: 0},
     )
     other = lax.ppermute(depth, "gz", [(0, 1), (1, 0)])
@@ -695,23 +686,21 @@
     vmem = pl.BlockSpec(memory_space=pltpu.VMEM)
     aims, note, table = pl.pallas_call(
         compact_kernel,
-        in_specs=[smem, vmem],
+        in_specs=[vmem],
         out_specs=(vmem, vmem, smem),
         out_shape=(f32(bricks + 2, 8, slots), f32(8, slots), jax.ShapeDtypeStruct((bricks + 1,), jnp.int32)),
         scratch_shapes=[vm((8, slots), jnp.int32), pltpu.SMEM((8, slots), jnp.int32), pltpu.SemaphoreType.DMA],
         compiler_params=params(4),
         name="compact",
-    )(place, targets)
+    )(targets)
     low, high, aims, table = lax.optimization_barrier((low, high, aims, table))
-    kept, up, down = whole_call(
+    kept, density, up, down = whole_call(
         first_kernel,
-        (f32(*kept.shape), bf16(channels * 3 * size_y, 128), bf16(channels * 3 * size_y, 128)),
-        [vm(frame), vm(frame), vm(flat), vm(flat), vm(flat), vm(flat)], "first", (place,),
+        (f32(*kept.shape), f32(bricks, 2 * channels, slots),
+         bf16(channels * 3 * size_y, 128), bf16(channels * 3 * size_y, 128)),
+        [vm(frame), vm(frame), vm(flat), vm(flat), vm(flat), vm(flat),
+         vm((channels * size_x * size_y, size_z))], "first", (),
         kept, zframe, low, high, note, aliases={0: 0}, megabytes=8,
-    )
-    density = whole_call(
-        functools.partial(density_kernel, channels), f32(bricks, 2 * channels, slots),
-        [vm((channels * size_x * size_y, size_z))], "density", (place,), kept, note,
     )
     low, high = both_ways(up, down, "row")
     densities = lax.all_to_all(density, "row", 0, 0, tiled=True)
@@ -719,7 +708,7 @@
     low, high, done = lax.optimization_barrier((low, high, done))
     kept, depth = whole_call(
         functools.partial(frame_kernel, False, channels),
-        (f32(*kept.shape), bf16(planes * size_y, 128)), [], "frame", (place,),
+        (f32(*kept.shape), bf16(planes * size_y, 128)), [], "frame", (),
         kept, low, high, aliases={0: 0},
     )
     other = lax.ppermute(depth, "gz", [(0, 1), (1, 0)])
@@ -735,17 +724,17 @@
     tile, shares = make_tile(2, table, densities, aims, channels, done)
     shares = whole_call(arrange_kernel, f32(bricks, 6, channels, slots), [], "arrange", (table,), shares)
     parts = lax.all_to_all(shares, ("col", "gz"), 0, 0, tiled=True)
-    near, _ = whole_call(near_kernel, (f32(7, channels, slots), f32(channels, slots)), [], "near", (place,), parts, targets)
+    near = whole_call(near_kernel, f32(7, channels, slots), [], "near", (), parts, targets)
     near_low, near_high = both_ways(near, near, "row")
     state, density = whole_call(
         second_kernel, (f32(*initial_field.shape), bf16(bricks, channels, slots)),
-        [vm(frame), vm(frame), vm(flat), vm(flat), vm(frame), vm(flat)], "second", (place,),
+        [vm(frame), vm(frame), vm(flat), vm(flat), vm(frame), vm(flat)], "second", (),
         kept, zframe, low, high, near_low, near, near_high, megabytes=8,
     )
     densities = lax.all_to_all(density, "row", 0, 0, tiled=True)
     shares = products(table, densities, tile, 512)
     parts = lax.all_to_all(shares, ("col", "gz"), 0, 0, tiled=True)
-    potential = whole_call(last_kernel, f32(channels, slots), [], "last", (place,), parts)
+    potential = whole_call(last_kernel, f32(channels, slots), [], "last", (), parts)
     return (state, potential)
 
 

time: 149 us -> 143 us (0.960)
  Pallas kernels: 45.9 us -> 40.1 us
  blocking collectives: 27.2 us -> 24.5 us
  waiting for transfers between devices: 13 us -> 15.2 us
    pallas_call x12 -> x11, Pallas kernels: 17 us -> 11.8 us  [whole_call(): pl.pallas_call(kernel, in_specs=[smem] * len(scalars) + [far if n in away...]
    all_to_all x1, blocking collectives: 15.5 us -> 13.1 us  [local(): densities = lax.all_to_all(density, 'row', 0, 0, tiled=True)]
    all_to_all x1, waiting for transfers between devices: 2.97 us -> 4.64 us  [local(): parts = lax.all_to_all(shares, ('col', 'gz'), 0, 0, tiled=True)]
  transfers between devices with their start and end apart: 15 -> 15, of which waited for: 5 -> 7; matrix products, arithmetic and copies ran while one was open for 0% -> 0% of each run, Pallas kernels for 13% -> 12%
where the time goes in v6:
time: 143 us; the launch traced here: 142 us
  starting transfers between devices  57.8 us (40%)
  Pallas kernels  40.1 us (28%)
  blocking collectives  24.5 us (17%)
  waiting for transfers between devices  15.2 us (11%)
  local copies, waits for them, and re-layouts  2.65 us (2%)
  between operations  1.48 us (1%)
    pallas_call x3, Pallas kernels, make_tile(): pl.pallas_call(functools.partial(tile_kernel, part), grid=(-(-bricks // T...  21.9 us
    ppermute x5, starting transfers between devices, both_ways(): lax.ppermute(up, axis, pairs)  19.4 us
    all_to_all x1, blocking collectives, local(): densities = lax.all_to_all(density, 'row', 0, 0, tiled=True)  13.1 us
    pallas_call x11, Pallas kernels, whole_call(): pl.pallas_call(kernel, in_specs=[smem] * len(scalars) + [far if n in away...  11.8 us
    all_to_all x1, starting transfers between devices, local(): densities = lax.all_to_all(density, 'row', 0, 0, tiled=True)  11.6 us
    all_to_all x1, blocking collectives, local(): parts = lax.all_to_all(shares, ('col', 'gz'), 0, 0, tiled=True)  11.3 us
    ppermute x5, starting transfers between devices, both_ways(): lax.ppermute(down, axis, [(b, a) for a, b in pairs])  8.53 us
    all_to_all x1, starting transfers between devices, local(): targets = lax.all_to_all(message, ('col', 'gz'), 0, 0, tiled=True)  6.77 us
  transfers between devices with their start and end apart: 15, of which 7 were waited for; matrix products, arithmetic and copies ran while one was open for 0% of the time, Pallas kernels for 12%

profile of v6, /device:TPU:1, one launch (start us, length us, event | category | flops | bytes accessed | tf_op | source)
XLA Modules:
  0.0 141.8 jit_solution(8444182970446318978)
XLA Ops:
  1.3 1.9 %planes.1 = (bf16[672,128]{1,0:T(8,128)(2,1)}, bf16[672,128]{1,0:T(8,128)(2,1)}, f32[16,8,128]{2,1,0:T(8,128)}) custom-call(f32[8,4,16,128]{3,2,1,0:T(8,128)} %state_hbm.1, f32[8,4,16,128]{3,2,1,0:T(8,128)} %source_hbm.1, s32[1,4,16,128]{3,2,1,0:T(8,128)} %bitcast.2, f32[4,128]{1,0:T(4,128)} %geometry_hbm.1, s32[1,128]{1,0:T(1,128)} %bitcast.4, ...), custom_call_target="tpu_custom_call" | custom-call | tf_op jit(solution)/shard_map/planes/pallas_call | solution.py:52
  3.2 4.9 %collective-permute-start = (bf16[672,128]{1,0:T(8,128)(2,1)}, bf16[672,128]{1,0:T(8,128)(2,1)S(1)}, u32[]{:S(2)}, u32[]{:S(2)}) collective-permute-start(bf16[672,128]{1,0:T(8,128)(2,1)} %get-tuple-element.45), channel_id=1, source_target_pairs={{0,16},{16,32},{32,48},{48,64},{64,80},{80,96},{96,112},{112,128},... | collective-permute-start | bytes 516104 | tf_op jit(solution)/shard_map/ppermute | solution.py:641
  8.1 1.9 %collective-permute-start.1 = (bf16[672,128]{1,0:T(8,128)(2,1)}, bf16[672,128]{1,0:T(8,128)(2,1)S(1)}, u32[]{:S(2)}, u32[]{:S(2)}) collective-permute-start(bf16[672,128]{1,0:T(8,128)(2,1)} %get-tuple-element.46), channel_id=1, source_target_pairs={{16,0},{32,16},{48,32},{64,48},{80,64},{96,80},{112,96},{128,112},... | collective-permute-start | bytes 516104 | tf_op jit(solution)/shard_map/ppermute | solution.py:641
  10.1 6.8 %all-to-all-start = ((f32[16,8,128]{2,1,0:T(8,128)}), f32[16,8,128]{2,1,0:T(8,128)S(1)}, u32[]{:S(2)}, u32[]{:S(2)}) async-start(f32[16,8,128]{2,1,0:T(8,128)} %get-tuple-element.49), calls=%async_computation | async-start | bytes 131072 | tf_op jit(solution)/shard_map/all_to_all | solution.py:678
  16.8 0.9 copy-done
  17.8 0.9 copy-done.1
  20.1 3.0 %collective-permute-start.2 = (bf16[160,128]{1,0:T(8,128)(2,1)S(1)}, bf16[160,128]{1,0:T(8,128)(2,1)S(1)}, u32[]{:S(2)}, u32[]{:S(2)}) collective-permute-start(bf16[160,128]{1,0:T(8,128)(2,1)S(1)} %get-tuple-element.48), channel_id=1, source_target_pairs={{0,1},{1,0},{2,3},{3,2},{4,5},{5,4},{6,7},{7,6},{8,9},{9,8},{10,11... | collective-permute-start | bytes 122888 | tf_op jit(solution)/shard_map/ppermute | solution.py:677
  23.6 0.9 collective-permute-done.2.other_ref
  24.6 3.3 %collective-permute-start.3 = (bf16[480,128]{1,0:T(8,128)(2,1)S(1)}, bf16[480,128]{1,0:T(8,128)(2,1)S(1)}, u32[]{:S(2)}, u32[]{:S(2)}) collective-permute-start(bf16[480,128]{1,0:T(8,128)(2,1)S(1)} %get-tuple-element.52), channel_id=1, source_target_pairs={{0,2},{2,4},{4,6},{6,8},{8,10},{10,12},{12,14},{1,3},{3,5},{5,7},{... | collective-permute-start | bytes 368648 | tf_op jit(solution)/shard_map/ppermute | solution.py:641
  27.9 1.3 collective-permute-start.4
  29.2 1.2 compact.1
  30.9 4.1 %collective-permute-done.4.high_ref = bf16[480,128]{1,0:T(8,128)(2,1)S(1)} collective-permute-done((bf16[480,128]{1,0:T(8,128)(2,1)S(1)}, bf16[480,128]{1,0:T(8,128)(2,1)S(1)}, u32[]{:S(2)}, u32[]{:S(2)}) %collective-permute-start.4) | collective-permute-done | bytes 122912 | tf_op jit(solution)/shard_map/ppermute | solution.py:641
  35.0 3.3 %first.1 = (f32[4560,128]{1,0:T(8,128)S(1)}, f32[16,16,128]{2,1,0:T(8,128)}, bf16[384,128]{1,0:T(8,128)(2,1)S(1)}, bf16[384,128]{1,0:T(8,128)(2,1)S(1)}) custom-call(f32[4560,128]{1,0:T(8,128)S(1)} %get-tuple-element.47.kept_ref._, f32[240,128]{1,0:T(8,128)S(1)} %get-tuple-element.51.depth_ref, ...), custom_call_target="tpu_custom_call", output_to_operand_aliasing={{0}: (0, {})} | custom-call | tf_op jit(solution)/shard_map/first/pallas_call | solution.py:52
  38.3 11.6 %all-to-all-start.1 = ((f32[16,16,128]{2,1,0:T(8,128)}), f32[16,16,128]{2,1,0:T(8,128)S(1)}, u32[]{:S(2)}, u32[]{:S(2)}) async-start(f32[16,16,128]{2,1,0:T(8,128)} %get-tuple-element.64), calls=%async_computation.1 | async-start | bytes 262144 | tf_op jit(solution)/shard_map/all_to_all | solution.py:706
  49.9 3.5 %collective-permute-start.5 = (bf16[384,128]{1,0:T(8,128)(2,1)S(1)}, bf16[384,128]{1,0:T(8,128)(2,1)S(1)}, u32[]{:S(2)}, u32[]{:S(2)}) collective-permute-start(bf16[384,128]{1,0:T(8,128)(2,1)S(1)} %get-tuple-element.61), channel_id=1, source_target_pairs={{0,16},{16,32},{32,48},{48,64},{64,80},{80,96},{96,112},{112,128},... | collective-permute-start | bytes 294920 | tf_op jit(solution)/shard_map/ppermute | solution.py:641
  53.4 1.9 %collective-permute-start.6 = (bf16[384,128]{1,0:T(8,128)(2,1)S(1)}, bf16[384,128]{1,0:T(8,128)(2,1)S(1)}, u32[]{:S(2)}, u32[]{:S(2)}) collective-permute-start(bf16[384,128]{1,0:T(8,128)(2,1)S(1)} %get-tuple-element.62), channel_id=1, source_target_pairs={{16,0},{32,16},{48,32},{64,48},{80,64},{96,80},{112,96},{128,112},... | collective-permute-start | bytes 294920 | tf_op jit(solution)/shard_map/ppermute | solution.py:641
  55.3 3.8 %all-to-all-done.1.source_ref = f32[16,16,128]{2,1,0:T(8,128)S(1)} async-done(((f32[16,16,128]{2,1,0:T(8,128)}), f32[16,16,128]{2,1,0:T(8,128)S(1)}, u32[]{:S(2)}, u32[]{:S(2)}) %all-to-all-start.1) | async-done | bytes 131104 | tf_op jit(solution)/shard_map/all_to_all | solution.py:706
  59.1 7.3 %tile.3 = (bf16[16384,2048]{1,0:T(8,128)(2,1)}, f32[18,8,128]{2,1,0:T(8,128)S(1)}) custom-call(s32[17]{0:T(128)S(1)} %get-tuple-element.63.table_ref, f32[16,16,128]{2,1,0:T(8,128)S(1)} %all-to-all-done.1.source_ref, f32[18,8,128]{2,1,0:T(8,128)S(1)} %get-tuple-element.65.target_ref), custom_call_target="tpu_custom_call" | custom-call | tf_op jit(solution)/shard_map/tile/pallas_call | solution.py:148
  66.6 2.8 %collective-permute-start.7 = (bf16[160,128]{1,0:T(8,128)(2,1)S(1)}, bf16[160,128]{1,0:T(8,128)(2,1)S(1)}, u32[]{:S(2)}, u32[]{:S(2)}) collective-permute-start(bf16[160,128]{1,0:T(8,128)(2,1)S(1)} %get-tuple-element.71), channel_id=1, source_target_pairs={{0,1},{1,0},{2,3},{3,2},{4,5},{5,4},{6,7},{7,6},{8,9},{9,8},{10,11... | collective-permute-start | bytes 122888 | tf_op jit(solution)/shard_map/ppermute | solution.py:714
  69.4 7.3 %tile.4 = (bf16[16384,2048]{1,0:T(8,128)(2,1)}, f32[18,8,128]{2,1,0:T(8,128)S(1)}) custom-call(s32[17]{0:T(128)S(1)} %get-tuple-element.63.table_ref, f32[16,16,128]{2,1,0:T(8,128)S(1)} %all-to-all-done.1.source_ref, f32[18,8,128]{2,1,0:T(8,128)S(1)} %get-tuple-element.65.target_ref, ...), custom_call_target="tpu_custom_call", output_to_operand_aliasing={{0}: (3, {}), {1}: (4, {})} | custom-call | tf_op jit(solution)/shard_map/tile/pallas_call | solution.py:148
  76.7 7.3 %tile.5 = (bf16[16384,2048]{1,0:T(8,128)(2,1)}, f32[18,8,128]{2,1,0:T(8,128)S(1)}) custom-call(s32[17]{0:T(128)S(1)} %get-tuple-element.63.table_ref, f32[16,16,128]{2,1,0:T(8,128)S(1)} %all-to-all-done.1.source_ref, f32[18,8,128]{2,1,0:T(8,128)S(1)} %get-tuple-element.65.target_ref, ...), custom_call_target="tpu_custom_call", output_to_operand_aliasing={{0}: (3, {}), {1}: (4, {})} | custom-call | tf_op jit(solution)/shard_map/tile/pallas_call | solution.py:148
  84.0 1.4 %arrange.1 = f32[16,6,8,128]{3,2,1,0:T(8,128)} custom-call(s32[17]{0:T(128)S(1)} %get-tuple-element.63.table_ref, f32[18,8,128]{2,1,0:T(8,128)S(1)} %get-tuple-element.84.share_ref), custom_call_target="tpu_custom_call" | custom-call | tf_op jit(solution)/shard_map/arrange/pallas_call | solution.py:52
  85.5 5.9 %all-to-all-start.2 = ((f32[16,6,8,128]{3,2,1,0:T(8,128)}), f32[16,6,8,128]{3,2,1,0:T(8,128)S(1)}, u32[]{:S(2)}, u32[]{:S(2)}) async-start(f32[16,6,8,128]{3,2,1,0:T(8,128)} %arrange.1), calls=%async_computation.2 | async-start | bytes 786432 | tf_op jit(solution)/shard_map/all_to_all | solution.py:726
  91.3 1.3 collective-permute-start.9
  92.6 4.0 %collective-permute-start.8 = (bf16[288,128]{1,0:T(8,128)(2,1)S(1)}, bf16[288,128]{1,0:T(8,128)(2,1)S(1)}, u32[]{:S(2)}, u32[]{:S(2)}) collective-permute-start(bf16[288,128]{1,0:T(8,128)(2,1)S(1)} %get-tuple-element.79), channel_id=1, source_target_pairs={{0,2},{2,4},{4,6},{6,8},{8,10},{10,12},{12,14},{1,3},{3,5},{5,7},{... | collective-permute-start | bytes 221192 | tf_op jit(solution)/shard_map/ppermute | solution.py:641
  96.6 4.6 %all-to-all-done.2.parts_ref = f32[16,6,8,128]{3,2,1,0:T(8,128)S(1)} async-done(((f32[16,6,8,128]{3,2,1,0:T(8,128)}), f32[16,6,8,128]{3,2,1,0:T(8,128)S(1)}, u32[]{:S(2)}, u32[]{:S(2)}) %all-to-all-start.2) | async-done | bytes 393248 | tf_op jit(solution)/shard_map/all_to_all | solution.py:726
  101.3 2.1 %collective-permute-start.11 = (f32[7,8,128]{2,1,0:T(8,128)S(1)}, f32[7,8,128]{2,1,0:T(8,128)S(1)}, u32[]{:S(2)}, u32[]{:S(2)}) collective-permute-start(f32[7,8,128]{2,1,0:T(8,128)S(1)} %near.1.near_own), channel_id=1, source_target_pairs={{16,0},{32,16},{48,32},{64,48},{80,64},{96,80},{112,96},{128,112},... | collective-permute-start | bytes 86024 | tf_op jit(solution)/shard_map/ppermute | solution.py:641
  103.4 3.6 %collective-permute-start.10 = (f32[7,8,128]{2,1,0:T(8,128)S(1)}, f32[7,8,128]{2,1,0:T(8,128)S(1)}, u32[]{:S(2)}, u32[]{:S(2)}) collective-permute-start(f32[7,8,128]{2,1,0:T(8,128)S(1)} %near.1.near_own), channel_id=1, source_target_pairs={{0,16},{16,32},{32,48},{48,64},{64,80},{80,96},{96,112},{112,128},... | collective-permute-start | bytes 86024 | tf_op jit(solution)/shard_map/ppermute | solution.py:641
  107.9 3.7 %second.1 = (f32[8,4,16,128]{3,2,1,0:T(8,128)}, bf16[16,8,128]{2,1,0:T(8,128)(2,1)S(1)}) custom-call(f32[4560,128]{1,0:T(8,128)S(1)} %get-tuple-element.70.kept_ref, f32[240,128]{1,0:T(8,128)S(1)} %get-tuple-element.78.depth_ref, bf16[288,128]{1,0:T(8,128)(2,1)S(1)} %collective-permute-done.8.low_ref, bf16[288,128]{1,0:T(8,128)(2,1)S(1)} %collective-permute-done.9.high_ref, ...), custom_call_target="tpu_custom_call" | custom-call | tf_op jit(solution)/shard_map/second/pallas_call | solution.py:52
  111.5 13.1 %all_to_all.25.density_ref = bf16[16,8,128]{2,1,0:T(8,128)(2,1)S(1)} all-to-all(bf16[16,8,128]{2,1,0:T(8,128)(2,1)S(1)} %get-tuple-element.86), channel_id=1, replica_groups=mesh['row'=16,'col'=8,'gz'=2] {'row'}, dimensions={0} | all-to-all | bytes 65536 | tf_op jit(solution)/shard_map/all_to_all | solution.py:734
  124.6 5.2 %product.1 = f32[16,8,128]{2,1,0:T(8,128)S(1)} custom-call(s32[17]{0:T(128)S(1)} %get-tuple-element.63.table_ref, bf16[16,8,128]{2,1,0:T(8,128)(2,1)S(1)} %all_to_all.25.density_ref, bf16[16384,2048]{1,0:T(8,128)(2,1)} %get-tuple-element.87.tile_ref), custom_call_target="tpu_custom_call" | custom-call | tf_op jit(solution)/shard_map/product/pallas_call | solution.py:231
  129.9 11.3 %all_to_all.26.parts_ref = f32[16,8,128]{2,1,0:T(8,128)S(1)} all-to-all(f32[16,8,128]{2,1,0:T(8,128)S(1)} %product.1), channel_id=1, replica_groups=mesh['row'=16,'col'=8,'gz'=2] {'col','gz'}, dimensions={0} | all-to-all | bytes 131072 | tf_op jit(solution)/shard_map/all_to_all | solution.py:736
  (22 shorter events, 4.0 us)
Async XLA Ops:
  3.2 16.5 %collective-permute-start = (bf16[672,128]{1,0:T(8,128)(2,1)}, bf16[672,128]{1,0:T(8,128)(2,1)S(1)}, u32[]{:S(2)}, u32[]{:S(2)}) collective-permute-start(bf16[672,128]{1,0:T(8,128)(2,1)} %get-tuple-element.45), channel_id=1, source_target_pairs={{0,16},{16,32},{32,48},{48,64},{64,80},{80,96},{96,112},{112,128},... | collective-permute-start | bytes 516104 | tf_op jit(solution)/shard_map/ppermute | solution.py:641
  8.1 11.6 %collective-permute-start.1 = (bf16[672,128]{1,0:T(8,128)(2,1)}, bf16[672,128]{1,0:T(8,128)(2,1)S(1)}, u32[]{:S(2)}, u32[]{:S(2)}) collective-permute-start(bf16[672,128]{1,0:T(8,128)(2,1)} %get-tuple-element.46), channel_id=1, source_target_pairs={{16,0},{32,16},{48,32},{64,48},{80,64},{96,80},{112,96},{128,112},... | collective-permute-start | bytes 516104 | tf_op jit(solution)/shard_map/ppermute | solution.py:641
  10.1 13.5 %all-to-all-start = ((f32[16,8,128]{2,1,0:T(8,128)}), f32[16,8,128]{2,1,0:T(8,128)S(1)}, u32[]{:S(2)}, u32[]{:S(2)}) async-start(f32[16,8,128]{2,1,0:T(8,128)} %get-tuple-element.49), calls=%async_computation | async-start | bytes 131072 | tf_op jit(solution)/shard_map/all_to_all | solution.py:678
  16.8 1.0 copy-start
  17.8 0.9 copy-start.1
  18.7 0.8 copy-start.2
  20.1 4.4 %collective-permute-start.2 = (bf16[160,128]{1,0:T(8,128)(2,1)S(1)}, bf16[160,128]{1,0:T(8,128)(2,1)S(1)}, u32[]{:S(2)}, u32[]{:S(2)}) collective-permute-start(bf16[160,128]{1,0:T(8,128)(2,1)S(1)} %get-tuple-element.48), channel_id=1, source_target_pairs={{0,1},{1,0},{2,3},{3,2},{4,5},{5,4},{6,7},{7,6},{8,9},{9,8},{10,11... | collective-permute-start | bytes 122888 | tf_op jit(solution)/shard_map/ppermute | solution.py:677
  24.6 6.3 %collective-permute-start.3 = (bf16[480,128]{1,0:T(8,128)(2,1)S(1)}, bf16[480,128]{1,0:T(8,128)(2,1)S(1)}, u32[]{:S(2)}, u32[]{:S(2)}) collective-permute-start(bf16[480,128]{1,0:T(8,128)(2,1)S(1)} %get-tuple-element.52), channel_id=1, source_target_pairs={{0,2},{2,4},{4,6},{6,8},{8,10},{10,12},{12,14},{1,3},{3,5},{5,7},{... | collective-permute-start | bytes 368648 | tf_op jit(solution)/shard_map/ppermute | solution.py:641
  27.9 7.1 %collective-permute-start.4 = (bf16[480,128]{1,0:T(8,128)(2,1)S(1)}, bf16[480,128]{1,0:T(8,128)(2,1)S(1)}, u32[]{:S(2)}, u32[]{:S(2)}) collective-permute-start(bf16[480,128]{1,0:T(8,128)(2,1)S(1)} %get-tuple-element.53), channel_id=1, source_target_pairs={{2,0},{4,2},{6,4},{8,6},{10,8},{12,10},{14,12},{3,1},{5,3},{7,5},{... | collective-permute-start | bytes 368648 | tf_op jit(solution)/shard_map/ppermute | solution.py:641
  38.3 20.8 %all-to-all-start.1 = ((f32[16,16,128]{2,1,0:T(8,128)}), f32[16,16,128]{2,1,0:T(8,128)S(1)}, u32[]{:S(2)}, u32[]{:S(2)}) async-start(f32[16,16,128]{2,1,0:T(8,128)} %get-tuple-element.64), calls=%async_computation.1 | async-start | bytes 262144 | tf_op jit(solution)/shard_map/all_to_all | solution.py:706
  49.9 16.5 %collective-permute-start.5 = (bf16[384,128]{1,0:T(8,128)(2,1)S(1)}, bf16[384,128]{1,0:T(8,128)(2,1)S(1)}, u32[]{:S(2)}, u32[]{:S(2)}) collective-permute-start(bf16[384,128]{1,0:T(8,128)(2,1)S(1)} %get-tuple-element.61), channel_id=1, source_target_pairs={{0,16},{16,32},{32,48},{48,64},{64,80},{80,96},{96,112},{112,128},... | collective-permute-start | bytes 294920 | tf_op jit(solution)/shard_map/ppermute | solution.py:641
  53.4 13.0 %collective-permute-start.6 = (bf16[384,128]{1,0:T(8,128)(2,1)S(1)}, bf16[384,128]{1,0:T(8,128)(2,1)S(1)}, u32[]{:S(2)}, u32[]{:S(2)}) collective-permute-start(bf16[384,128]{1,0:T(8,128)(2,1)S(1)} %get-tuple-element.62), channel_id=1, source_target_pairs={{16,0},{32,16},{48,32},{64,48},{80,64},{96,80},{112,96},{128,112},... | collective-permute-start | bytes 294920 | tf_op jit(solution)/shard_map/ppermute | solution.py:641
  66.6 10.1 %collective-permute-start.7 = (bf16[160,128]{1,0:T(8,128)(2,1)S(1)}, bf16[160,128]{1,0:T(8,128)(2,1)S(1)}, u32[]{:S(2)}, u32[]{:S(2)}) collective-permute-start(bf16[160,128]{1,0:T(8,128)(2,1)S(1)} %get-tuple-element.71), channel_id=1, source_target_pairs={{0,1},{1,0},{2,3},{3,2},{4,5},{5,4},{6,7},{7,6},{8,9},{9,8},{10,11... | collective-permute-start | bytes 122888 | tf_op jit(solution)/shard_map/ppermute | solution.py:714
  85.5 15.8 %all-to-all-start.2 = ((f32[16,6,8,128]{3,2,1,0:T(8,128)}), f32[16,6,8,128]{3,2,1,0:T(8,128)S(1)}, u32[]{:S(2)}, u32[]{:S(2)}) async-start(f32[16,6,8,128]{3,2,1,0:T(8,128)} %arrange.1), calls=%async_computation.2 | async-start | bytes 786432 | tf_op jit(solution)/shard_map/all_to_all | solution.py:726
  91.3 15.7 %collective-permute-start.9 = (bf16[288,128]{1,0:T(8,128)(2,1)S(1)}, bf16[288,128]{1,0:T(8,128)(2,1)S(1)}, u32[]{:S(2)}, u32[]{:S(2)}) collective-permute-start(bf16[288,128]{1,0:T(8,128)(2,1)S(1)} %get-tuple-element.80), channel_id=1, source_target_pairs={{2,0},{4,2},{6,4},{8,6},{10,8},{12,10},{14,12},{3,1},{5,3},{7,5},{... | collective-permute-start | bytes 221192 | tf_op jit(solution)/shard_map/ppermute | solution.py:641
  92.6 14.4 %collective-permute-start.8 = (bf16[288,128]{1,0:T(8,128)(2,1)S(1)}, bf16[288,128]{1,0:T(8,128)(2,1)S(1)}, u32[]{:S(2)}, u32[]{:S(2)}) collective-permute-start(bf16[288,128]{1,0:T(8,128)(2,1)S(1)} %get-tuple-element.79), channel_id=1, source_target_pairs={{0,2},{2,4},{4,6},{6,8},{8,10},{10,12},{12,14},{1,3},{3,5},{5,7},{... | collective-permute-start | bytes 221192 | tf_op jit(solution)/shard_map/ppermute | solution.py:641
  101.3 5.8 %collective-permute-start.11 = (f32[7,8,128]{2,1,0:T(8,128)S(1)}, f32[7,8,128]{2,1,0:T(8,128)S(1)}, u32[]{:S(2)}, u32[]{:S(2)}) collective-permute-start(f32[7,8,128]{2,1,0:T(8,128)S(1)} %near.1.near_own), channel_id=1, source_target_pairs={{16,0},{32,16},{48,32},{64,48},{80,64},{96,80},{112,96},{128,112},... | collective-permute-start | bytes 86024 | tf_op jit(solution)/shard_map/ppermute | solution.py:641
  103.4 4.4 %collective-permute-start.10 = (f32[7,8,128]{2,1,0:T(8,128)S(1)}, f32[7,8,128]{2,1,0:T(8,128)S(1)}, u32[]{:S(2)}, u32[]{:S(2)}) collective-permute-start(f32[7,8,128]{2,1,0:T(8,128)S(1)} %near.1.near_own), channel_id=1, source_target_pairs={{0,16},{16,32},{32,48},{48,64},{64,80},{80,96},{96,112},{112,128},... | collective-permute-start | bytes 86024 | tf_op jit(solution)/shard_map/ppermute | solution.py:641

commit v7 on v6

--- a/solution.py
+++ b/solution.py
@@ -106,7 +106,7 @@
     out[group + 1] = jnp.where(lane < shift + count - rows.shape[1], moved, out[group + 1])
 
 
-def tile_kernel(part, table_ref, source_ref, target_ref, *refs):
+def tile_kernel(source_ref, target_ref, *refs):
     tile_ref, share_ref, columns, density = refs[-4:]
     bricks, slots = source_ref.shape[0], source_ref.shape[2]
     channels = share_ref.shape[1]
@@ -117,7 +117,7 @@
         for brick in range(bricks):
             density[:, brick * slots : (brick + 1) * slots] = source_ref[brick, :channels].astype(jnp.bfloat16)
 
-    @pl.when((TILES * step + part) * slots < table_ref[bricks])
+    @pl.when(jnp.max(target_ref[0, 4:5, :]) > 0.0)
     def _():
         columns[...] = jnp.transpose(target_ref[0])
         spread = [jnp.broadcast_to(columns[:, d : d + 1], (slots, slots)) for d in range(3)]
@@ -142,14 +142,13 @@
         share_ref[0] = total
 
 
-def make_tile(part, table, sources, targets, channels, before=()):
+def make_tile(part, sources, targets, channels, before=()):
     bricks, slots = sources.shape[0], sources.shape[2]
     far = pl.BlockSpec(memory_space=pl.ANY)
     return pl.pallas_call(
-        functools.partial(tile_kernel, part),
+        tile_kernel,
         grid=(-(-bricks // TILES),),
         in_specs=[
-            pl.BlockSpec(memory_space=pltpu.SMEM),
             pl.BlockSpec(sources.shape, lambda b: (0, 0, 0)),
             pl.BlockSpec((1, targets.shape[1], slots), lambda b: (TILES * b + part, 0, 0)),
         ]
@@ -166,10 +165,10 @@
             pltpu.VMEM((slots, targets.shape[1]), jnp.float32),
             pltpu.VMEM((channels, bricks * slots), jnp.bfloat16),
         ],
-        input_output_aliases={3 + n: n for n in range(len(before))},
+        input_output_aliases={2 + n: n for n in range(len(before))},
         compiler_params=params(8),
         name="tile",
-    )(table, sources, targets, *before)
+    )(sources, targets, *before)
 
 
 def taken(share_ref, table_ref, brick, bricks):
@@ -704,7 +703,7 @@
     )
     low, high = both_ways(up, down, "row")
     densities = lax.all_to_all(density, "row", 0, 0, tiled=True)
-    done = make_tile(0, table, densities, aims, channels)
+    done = make_tile(0, densities, aims, channels)
     low, high, done = lax.optimization_barrier((low, high, done))
     kept, depth = whole_call(
         functools.partial(frame_kernel, False, channels),
@@ -713,7 +712,7 @@
     )
     other = lax.ppermute(depth, "gz", [(0, 1), (1, 0)])
     densities, depth = lax.optimization_barrier((densities, depth))
-    done = make_tile(1, table, densities, aims, channels, done)
+    done = make_tile(1, densities, aims, channels, done)
     other, done = lax.optimization_barrier((other, done))
     zframe, up, down = whole_call(
         functools.partial(edge_kernel, False), (f32(*flat), bf16(288, 128), bf16(288, 128)), [], "edges", (),
@@ -721,7 +720,7 @@
     )
     low, high = both_ways(up, down, "col")
     densities, up = lax.optimization_barrier((densities, up))
-    tile, shares = make_tile(2, table, densities, aims, channels, done)
+    tile, shares = make_tile(2, densities, aims, channels, done)
     shares = whole_call(arrange_kernel, f32(bricks, 6, channels, slots), [], "arrange", (table,), shares)
     parts = lax.all_to_all(shares, ("col", "gz"), 0, 0, tiled=True)
     near = whole_call(near_kernel, f32(7, channels, slots), [], "near", (), parts, targets)

time: 143 us -> 143 us (level)
  starting transfers between devices: 57.8 us -> 61.7 us
  Pallas kernels: 40.1 us -> 36.5 us
    ppermute x5, starting transfers between devices: 8.53 us -> 13.9 us  [both_ways(): lax.ppermute(down, axis, [(b, a) for a, b in pairs])]
    pallas_call x3, Pallas kernels: 21.9 us -> 18.3 us  [make_tile(): pl.pallas_call(tile_kernel, grid=(-(-bricks // TILES),), in_specs=[pl.Blo...]
    all_to_all x1, waiting for transfers between devices: 4.64 us -> 3.08 us  [local(): parts = lax.all_to_all(shares, ('col', 'gz'), 0, 0, tiled=True)]
    ppermute x5, starting transfers between devices: 19.4 us -> 17.8 us  [both_ways(): lax.ppermute(up, axis, pairs)]
  transfers between devices with their start and end apart: 15 -> 15, of which waited for: 7 -> 7; matrix products, arithmetic and copies ran while one was open for 0% -> 0% of each run, Pallas kernels for 12% -> 10%
where the time goes in v7:
time: 143 us; the launch traced here: 142 us
  starting transfers between devices  61.7 us (43%)
  Pallas kernels  36.5 us (26%)
  blocking collectives  25.4 us (18%)
  waiting for transfers between devices  13.8 us (10%)
  local copies, waits for them, and re-layouts  2.65 us (2%)
  between operations  1.48 us (1%)
    pallas_call x3, Pallas kernels, make_tile(): pl.pallas_call(tile_kernel, grid=(-(-bricks // TILES),), in_specs=[pl.Blo...  18.3 us
    ppermute x5, starting transfers between devices, both_ways(): lax.ppermute(up, axis, pairs)  17.8 us
    ppermute x5, starting transfers between devices, both_ways(): lax.ppermute(down, axis, [(b, a) for a, b in pairs])  13.9 us
    all_to_all x1, blocking collectives, local(): densities = lax.all_to_all(density, 'row', 0, 0, tiled=True)  13.7 us
    pallas_call x11, Pallas kernels, whole_call(): pl.pallas_call(kernel, in_specs=[smem] * len(scalars) + [far if n in away...  11.8 us
    all_to_all x1, blocking collectives, local(): parts = lax.all_to_all(shares, ('col', 'gz'), 0, 0, tiled=True)  11.7 us
    all_to_all x1, starting transfers between devices, local(): densities = lax.all_to_all(density, 'row', 0, 0, tiled=True)  11.6 us
    all_to_all x1, starting transfers between devices, local(): targets = lax.all_to_all(message, ('col', 'gz'), 0, 0, tiled=True)  6.77 us
  transfers between devices with their start and end apart: 15, of which 7 were waited for; matrix products, arithmetic and copies ran while one was open for 0% of the time, Pallas kernels for 10%

profile of v7, /device:TPU:1, one launch (start us, length us, event | category | flops | bytes accessed | tf_op | source)
XLA Modules:
  0.0 141.6 jit_solution(2893897711134321927)
XLA Ops:
  1.3 1.9 %planes.1 = (bf16[672,128]{1,0:T(8,128)(2,1)}, bf16[672,128]{1,0:T(8,128)(2,1)}, f32[16,8,128]{2,1,0:T(8,128)}) custom-call(f32[8,4,16,128]{3,2,1,0:T(8,128)} %state_hbm.1, f32[8,4,16,128]{3,2,1,0:T(8,128)} %source_hbm.1, s32[1,4,16,128]{3,2,1,0:T(8,128)} %bitcast.2, f32[4,128]{1,0:T(4,128)} %geometry_hbm.1, s32[1,128]{1,0:T(1,128)} %bitcast.4, ...), custom_call_target="tpu_custom_call" | custom-call | tf_op jit(solution)/shard_map/planes/pallas_call | solution.py:52
  3.2 4.9 %collective-permute-start = (bf16[672,128]{1,0:T(8,128)(2,1)}, bf16[672,128]{1,0:T(8,128)(2,1)S(1)}, u32[]{:S(2)}, u32[]{:S(2)}) collective-permute-start(bf16[672,128]{1,0:T(8,128)(2,1)} %get-tuple-element.45), channel_id=1, source_target_pairs={{0,16},{16,32},{32,48},{48,64},{64,80},{80,96},{96,112},{112,128},... | collective-permute-start | bytes 516104 | tf_op jit(solution)/shard_map/ppermute | solution.py:640
  8.1 1.9 %collective-permute-start.1 = (bf16[672,128]{1,0:T(8,128)(2,1)}, bf16[672,128]{1,0:T(8,128)(2,1)S(1)}, u32[]{:S(2)}, u32[]{:S(2)}) collective-permute-start(bf16[672,128]{1,0:T(8,128)(2,1)} %get-tuple-element.46), channel_id=1, source_target_pairs={{16,0},{32,16},{48,32},{64,48},{80,64},{96,80},{112,96},{128,112},... | collective-permute-start | bytes 516104 | tf_op jit(solution)/shard_map/ppermute | solution.py:640
  10.1 6.8 %all-to-all-start = ((f32[16,8,128]{2,1,0:T(8,128)}), f32[16,8,128]{2,1,0:T(8,128)S(1)}, u32[]{:S(2)}, u32[]{:S(2)}) async-start(f32[16,8,128]{2,1,0:T(8,128)} %get-tuple-element.49), calls=%async_computation | async-start | bytes 131072 | tf_op jit(solution)/shard_map/all_to_all | solution.py:677
  16.8 0.9 copy-done
  17.8 0.9 copy-done.1
  20.1 3.0 %collective-permute-start.2 = (bf16[160,128]{1,0:T(8,128)(2,1)S(1)}, bf16[160,128]{1,0:T(8,128)(2,1)S(1)}, u32[]{:S(2)}, u32[]{:S(2)}) collective-permute-start(bf16[160,128]{1,0:T(8,128)(2,1)S(1)} %get-tuple-element.48), channel_id=1, source_target_pairs={{0,1},{1,0},{2,3},{3,2},{4,5},{5,4},{6,7},{7,6},{8,9},{9,8},{10,11... | collective-permute-start | bytes 122888 | tf_op jit(solution)/shard_map/ppermute | solution.py:676
  24.6 3.3 %collective-permute-start.3 = (bf16[480,128]{1,0:T(8,128)(2,1)S(1)}, bf16[480,128]{1,0:T(8,128)(2,1)S(1)}, u32[]{:S(2)}, u32[]{:S(2)}) collective-permute-start(bf16[480,128]{1,0:T(8,128)(2,1)S(1)} %get-tuple-element.52), channel_id=1, source_target_pairs={{0,2},{2,4},{4,6},{6,8},{8,10},{10,12},{12,14},{1,3},{3,5},{5,7},{... | collective-permute-start | bytes 368648 | tf_op jit(solution)/shard_map/ppermute | solution.py:640
  27.9 1.3 collective-permute-start.4
  29.2 1.2 compact.1
  30.9 4.1 %collective-permute-done.4.high_ref = bf16[480,128]{1,0:T(8,128)(2,1)S(1)} collective-permute-done((bf16[480,128]{1,0:T(8,128)(2,1)S(1)}, bf16[480,128]{1,0:T(8,128)(2,1)S(1)}, u32[]{:S(2)}, u32[]{:S(2)}) %collective-permute-start.4) | collective-permute-done | bytes 122912 | tf_op jit(solution)/shard_map/ppermute | solution.py:640
  35.0 3.3 %first.1 = (f32[4560,128]{1,0:T(8,128)S(1)}, f32[16,16,128]{2,1,0:T(8,128)}, bf16[384,128]{1,0:T(8,128)(2,1)S(1)}, bf16[384,128]{1,0:T(8,128)(2,1)S(1)}) custom-call(f32[4560,128]{1,0:T(8,128)S(1)} %get-tuple-element.47.kept_ref._, f32[240,128]{1,0:T(8,128)S(1)} %get-tuple-element.51.depth_ref, ...), custom_call_target="tpu_custom_call", output_to_operand_aliasing={{0}: (0, {})} | custom-call | tf_op jit(solution)/shard_map/first/pallas_call | solution.py:52
  38.3 11.6 %all-to-all-start.1 = ((f32[16,16,128]{2,1,0:T(8,128)}), f32[16,16,128]{2,1,0:T(8,128)S(1)}, u32[]{:S(2)}, u32[]{:S(2)}) async-start(f32[16,16,128]{2,1,0:T(8,128)} %get-tuple-element.63), calls=%async_computation.1 | async-start | bytes 262144 | tf_op jit(solution)/shard_map/all_to_all | solution.py:705
  49.9 3.5 %collective-permute-start.5 = (bf16[384,128]{1,0:T(8,128)(2,1)S(1)}, bf16[384,128]{1,0:T(8,128)(2,1)S(1)}, u32[]{:S(2)}, u32[]{:S(2)}) collective-permute-start(bf16[384,128]{1,0:T(8,128)(2,1)S(1)} %get-tuple-element.61), channel_id=1, source_target_pairs={{0,16},{16,32},{32,48},{48,64},{64,80},{80,96},{96,112},{112,128},... | collective-permute-start | bytes 294920 | tf_op jit(solution)/shard_map/ppermute | solution.py:640
  53.4 1.9 %collective-permute-start.6 = (bf16[384,128]{1,0:T(8,128)(2,1)S(1)}, bf16[384,128]{1,0:T(8,128)(2,1)S(1)}, u32[]{:S(2)}, u32[]{:S(2)}) collective-permute-start(bf16[384,128]{1,0:T(8,128)(2,1)S(1)} %get-tuple-element.62), channel_id=1, source_target_pairs={{16,0},{32,16},{48,32},{64,48},{80,64},{96,80},{112,96},{128,112},... | collective-permute-start | bytes 294920 | tf_op jit(solution)/shard_map/ppermute | solution.py:640
  55.3 3.8 %all-to-all-done.1.source_ref = f32[16,16,128]{2,1,0:T(8,128)S(1)} async-done(((f32[16,16,128]{2,1,0:T(8,128)}), f32[16,16,128]{2,1,0:T(8,128)S(1)}, u32[]{:S(2)}, u32[]{:S(2)}) %all-to-all-start.1) | async-done | bytes 131104 | tf_op jit(solution)/shard_map/all_to_all | solution.py:705
  59.1 6.1 %tile.3 = (bf16[16384,2048]{1,0:T(8,128)(2,1)}, f32[18,8,128]{2,1,0:T(8,128)S(1)}) custom-call(f32[16,16,128]{2,1,0:T(8,128)S(1)} %all-to-all-done.1.source_ref, f32[18,8,128]{2,1,0:T(8,128)S(1)} %get-tuple-element.64.target_ref), custom_call_target="tpu_custom_call" | custom-call | tf_op jit(solution)/shard_map/tile/pallas_call | solution.py:148
  65.4 2.8 %collective-permute-start.7 = (bf16[160,128]{1,0:T(8,128)(2,1)S(1)}, bf16[160,128]{1,0:T(8,128)(2,1)S(1)}, u32[]{:S(2)}, u32[]{:S(2)}) collective-permute-start(bf16[160,128]{1,0:T(8,128)(2,1)S(1)} %get-tuple-element.70), channel_id=1, source_target_pairs={{0,1},{1,0},{2,3},{3,2},{4,5},{5,4},{6,7},{7,6},{8,9},{9,8},{10,11... | collective-permute-start | bytes 122888 | tf_op jit(solution)/shard_map/ppermute | solution.py:713
  68.1 6.1 %tile.4 = (bf16[16384,2048]{1,0:T(8,128)(2,1)}, f32[18,8,128]{2,1,0:T(8,128)S(1)}) custom-call(f32[16,16,128]{2,1,0:T(8,128)S(1)} %all-to-all-done.1.source_ref, f32[18,8,128]{2,1,0:T(8,128)S(1)} %get-tuple-element.64.target_ref, bf16[16384,2048]{1,0:T(8,128)(2,1)} %get-tuple-element.72.refs_0_, ...), custom_call_target="tpu_custom_call", output_to_operand_aliasing={{0}: (2, {}), {1}: (3, {})} | custom-call | tf_op jit(solution)/shard_map/tile/pallas_call | solution.py:148
  74.3 6.1 %tile.5 = (bf16[16384,2048]{1,0:T(8,128)(2,1)}, f32[18,8,128]{2,1,0:T(8,128)S(1)}) custom-call(f32[16,16,128]{2,1,0:T(8,128)S(1)} %all-to-all-done.1.source_ref, f32[18,8,128]{2,1,0:T(8,128)S(1)} %get-tuple-element.64.target_ref, bf16[16384,2048]{1,0:T(8,128)(2,1)} %get-tuple-element.82.refs_0_, ...), custom_call_target="tpu_custom_call", output_to_operand_aliasing={{0}: (2, {}), {1}: (3, {})} | custom-call | tf_op jit(solution)/shard_map/tile/pallas_call | solution.py:148
  80.4 1.4 %arrange.1 = f32[16,6,8,128]{3,2,1,0:T(8,128)} custom-call(s32[17]{0:T(128)S(1)} %get-tuple-element.80.table_ref, f32[18,8,128]{2,1,0:T(8,128)S(1)} %get-tuple-element.84.share_ref), custom_call_target="tpu_custom_call" | custom-call | tf_op jit(solution)/shard_map/arrange/pallas_call | solution.py:52
  81.8 5.9 %all-to-all-start.2 = ((f32[16,6,8,128]{3,2,1,0:T(8,128)}), f32[16,6,8,128]{3,2,1,0:T(8,128)S(1)}, u32[]{:S(2)}, u32[]{:S(2)}) async-start(f32[16,6,8,128]{3,2,1,0:T(8,128)} %arrange.1), calls=%async_computation.2 | async-start | bytes 786432 | tf_op jit(solution)/shard_map/all_to_all | solution.py:725
  87.7 1.3 collective-permute-start.9
  89.0 4.0 %collective-permute-start.8 = (bf16[288,128]{1,0:T(8,128)(2,1)S(1)}, bf16[288,128]{1,0:T(8,128)(2,1)S(1)}, u32[]{:S(2)}, u32[]{:S(2)}) collective-permute-start(bf16[288,128]{1,0:T(8,128)(2,1)S(1)} %get-tuple-element.78), channel_id=1, source_target_pairs={{0,2},{2,4},{4,6},{6,8},{8,10},{10,12},{12,14},{1,3},{3,5},{5,7},{... | collective-permute-start | bytes 221192 | tf_op jit(solution)/shard_map/ppermute | solution.py:640
  93.0 3.1 %all-to-all-done.2.parts_ref = f32[16,6,8,128]{3,2,1,0:T(8,128)S(1)} async-done(((f32[16,6,8,128]{3,2,1,0:T(8,128)}), f32[16,6,8,128]{3,2,1,0:T(8,128)S(1)}, u32[]{:S(2)}, u32[]{:S(2)}) %all-to-all-start.2) | async-done | bytes 393248 | tf_op jit(solution)/shard_map/all_to_all | solution.py:725
  96.1 7.5 %collective-permute-start.11 = (f32[7,8,128]{2,1,0:T(8,128)S(1)}, f32[7,8,128]{2,1,0:T(8,128)S(1)}, u32[]{:S(2)}, u32[]{:S(2)}) collective-permute-start(f32[7,8,128]{2,1,0:T(8,128)S(1)} %near.1.near_own), channel_id=1, source_target_pairs={{16,0},{32,16},{48,32},{64,48},{80,64},{96,80},{112,96},{128,112},... | collective-permute-start | bytes 86024 | tf_op jit(solution)/shard_map/ppermute | solution.py:640
  103.6 2.1 %collective-permute-start.10 = (f32[7,8,128]{2,1,0:T(8,128)S(1)}, f32[7,8,128]{2,1,0:T(8,128)S(1)}, u32[]{:S(2)}, u32[]{:S(2)}) collective-permute-start(f32[7,8,128]{2,1,0:T(8,128)S(1)} %near.1.near_own), channel_id=1, source_target_pairs={{0,16},{16,32},{32,48},{48,64},{64,80},{80,96},{96,112},{112,128},... | collective-permute-start | bytes 86024 | tf_op jit(solution)/shard_map/ppermute | solution.py:640
  105.8 1.0 collective-permute-done.10.near_low
  106.7 3.7 %second.1 = (f32[8,4,16,128]{3,2,1,0:T(8,128)}, bf16[16,8,128]{2,1,0:T(8,128)(2,1)S(1)}) custom-call(f32[4560,128]{1,0:T(8,128)S(1)} %get-tuple-element.69.kept_ref, f32[240,128]{1,0:T(8,128)S(1)} %get-tuple-element.77.depth_ref, bf16[288,128]{1,0:T(8,128)(2,1)S(1)} %collective-permute-done.8.low_ref, bf16[288,128]{1,0:T(8,128)(2,1)S(1)} %collective-permute-done.9.high_ref, ...), custom_call_target="tpu_custom_call" | custom-call | tf_op jit(solution)/shard_map/second/pallas_call | solution.py:52
  110.4 13.7 %all_to_all.25.density_ref = bf16[16,8,128]{2,1,0:T(8,128)(2,1)S(1)} all-to-all(bf16[16,8,128]{2,1,0:T(8,128)(2,1)S(1)} %get-tuple-element.86), channel_id=1, replica_groups=mesh['row'=16,'col'=8,'gz'=2] {'row'}, dimensions={0} | all-to-all | bytes 65536 | tf_op jit(solution)/shard_map/all_to_all | solution.py:733
  124.1 5.2 %product.1 = f32[16,8,128]{2,1,0:T(8,128)S(1)} custom-call(s32[17]{0:T(128)S(1)} %get-tuple-element.80.table_ref, bf16[16,8,128]{2,1,0:T(8,128)(2,1)S(1)} %all_to_all.25.density_ref, bf16[16384,2048]{1,0:T(8,128)(2,1)} %get-tuple-element.87.tile_ref), custom_call_target="tpu_custom_call" | custom-call | tf_op jit(solution)/shard_map/product/pallas_call | solution.py:230
  129.3 11.7 %all_to_all.26.parts_ref = f32[16,8,128]{2,1,0:T(8,128)S(1)} all-to-all(f32[16,8,128]{2,1,0:T(8,128)S(1)} %product.1), channel_id=1, replica_groups=mesh['row'=16,'col'=8,'gz'=2] {'col','gz'}, dimensions={0} | all-to-all | bytes 131072 | tf_op jit(solution)/shard_map/all_to_all | solution.py:735
  (22 shorter events, 4.2 us)
Async XLA Ops:
  3.2 16.5 %collective-permute-start = (bf16[672,128]{1,0:T(8,128)(2,1)}, bf16[672,128]{1,0:T(8,128)(2,1)S(1)}, u32[]{:S(2)}, u32[]{:S(2)}) collective-permute-start(bf16[672,128]{1,0:T(8,128)(2,1)} %get-tuple-element.45), channel_id=1, source_target_pairs={{0,16},{16,32},{32,48},{48,64},{64,80},{80,96},{96,112},{112,128},... | collective-permute-start | bytes 516104 | tf_op jit(solution)/shard_map/ppermute | solution.py:640
  8.1 11.6 %collective-permute-start.1 = (bf16[672,128]{1,0:T(8,128)(2,1)}, bf16[672,128]{1,0:T(8,128)(2,1)S(1)}, u32[]{:S(2)}, u32[]{:S(2)}) collective-permute-start(bf16[672,128]{1,0:T(8,128)(2,1)} %get-tuple-element.46), channel_id=1, source_target_pairs={{16,0},{32,16},{48,32},{64,48},{80,64},{96,80},{112,96},{128,112},... | collective-permute-start | bytes 516104 | tf_op jit(solution)/shard_map/ppermute | solution.py:640
  10.1 13.5 %all-to-all-start = ((f32[16,8,128]{2,1,0:T(8,128)}), f32[16,8,128]{2,1,0:T(8,128)S(1)}, u32[]{:S(2)}, u32[]{:S(2)}) async-start(f32[16,8,128]{2,1,0:T(8,128)} %get-tuple-element.49), calls=%async_computation | async-start | bytes 131072 | tf_op jit(solution)/shard_map/all_to_all | solution.py:677
  16.8 1.0 copy-start
  17.8 0.9 copy-start.1
  18.7 0.8 copy-start.2
  20.1 4.4 %collective-permute-start.2 = (bf16[160,128]{1,0:T(8,128)(2,1)S(1)}, bf16[160,128]{1,0:T(8,128)(2,1)S(1)}, u32[]{:S(2)}, u32[]{:S(2)}) collective-permute-start(bf16[160,128]{1,0:T(8,128)(2,1)S(1)} %get-tuple-element.48), channel_id=1, source_target_pairs={{0,1},{1,0},{2,3},{3,2},{4,5},{5,4},{6,7},{7,6},{8,9},{9,8},{10,11... | collective-permute-start | bytes 122888 | tf_op jit(solution)/shard_map/ppermute | solution.py:676
  24.6 6.3 %collective-permute-start.3 = (bf16[480,128]{1,0:T(8,128)(2,1)S(1)}, bf16[480,128]{1,0:T(8,128)(2,1)S(1)}, u32[]{:S(2)}, u32[]{:S(2)}) collective-permute-start(bf16[480,128]{1,0:T(8,128)(2,1)S(1)} %get-tuple-element.52), channel_id=1, source_target_pairs={{0,2},{2,4},{4,6},{6,8},{8,10},{10,12},{12,14},{1,3},{3,5},{5,7},{... | collective-permute-start | bytes 368648 | tf_op jit(solution)/shard_map/ppermute | solution.py:640
  27.9 7.1 %collective-permute-start.4 = (bf16[480,128]{1,0:T(8,128)(2,1)S(1)}, bf16[480,128]{1,0:T(8,128)(2,1)S(1)}, u32[]{:S(2)}, u32[]{:S(2)}) collective-permute-start(bf16[480,128]{1,0:T(8,128)(2,1)S(1)} %get-tuple-element.53), channel_id=1, source_target_pairs={{2,0},{4,2},{6,4},{8,6},{10,8},{12,10},{14,12},{3,1},{5,3},{7,5},{... | collective-permute-start | bytes 368648 | tf_op jit(solution)/shard_map/ppermute | solution.py:640
  38.3 20.8 %all-to-all-start.1 = ((f32[16,16,128]{2,1,0:T(8,128)}), f32[16,16,128]{2,1,0:T(8,128)S(1)}, u32[]{:S(2)}, u32[]{:S(2)}) async-start(f32[16,16,128]{2,1,0:T(8,128)} %get-tuple-element.63), calls=%async_computation.1 | async-start | bytes 262144 | tf_op jit(solution)/shard_map/all_to_all | solution.py:705
  49.9 15.3 %collective-permute-start.5 = (bf16[384,128]{1,0:T(8,128)(2,1)S(1)}, bf16[384,128]{1,0:T(8,128)(2,1)S(1)}, u32[]{:S(2)}, u32[]{:S(2)}) collective-permute-start(bf16[384,128]{1,0:T(8,128)(2,1)S(1)} %get-tuple-element.61), channel_id=1, source_target_pairs={{0,16},{16,32},{32,48},{48,64},{64,80},{80,96},{96,112},{112,128},... | collective-permute-start | bytes 294920 | tf_op jit(solution)/shard_map/ppermute | solution.py:640
  53.4 11.8 %collective-permute-start.6 = (bf16[384,128]{1,0:T(8,128)(2,1)S(1)}, bf16[384,128]{1,0:T(8,128)(2,1)S(1)}, u32[]{:S(2)}, u32[]{:S(2)}) collective-permute-start(bf16[384,128]{1,0:T(8,128)(2,1)S(1)} %get-tuple-element.62), channel_id=1, source_target_pairs={{16,0},{32,16},{48,32},{64,48},{80,64},{96,80},{112,96},{128,112},... | collective-permute-start | bytes 294920 | tf_op jit(solution)/shard_map/ppermute | solution.py:640
  65.4 8.9 %collective-permute-start.7 = (bf16[160,128]{1,0:T(8,128)(2,1)S(1)}, bf16[160,128]{1,0:T(8,128)(2,1)S(1)}, u32[]{:S(2)}, u32[]{:S(2)}) collective-permute-start(bf16[160,128]{1,0:T(8,128)(2,1)S(1)} %get-tuple-element.70), channel_id=1, source_target_pairs={{0,1},{1,0},{2,3},{3,2},{4,5},{5,4},{6,7},{7,6},{8,9},{9,8},{10,11... | collective-permute-start | bytes 122888 | tf_op jit(solution)/shard_map/ppermute | solution.py:713
  81.8 14.3 %all-to-all-start.2 = ((f32[16,6,8,128]{3,2,1,0:T(8,128)}), f32[16,6,8,128]{3,2,1,0:T(8,128)S(1)}, u32[]{:S(2)}, u32[]{:S(2)}) async-start(f32[16,6,8,128]{3,2,1,0:T(8,128)} %arrange.1), calls=%async_computation.2 | async-start | bytes 786432 | tf_op jit(solution)/shard_map/all_to_all | solution.py:725
  87.7 18.0 %collective-permute-start.9 = (bf16[288,128]{1,0:T(8,128)(2,1)S(1)}, bf16[288,128]{1,0:T(8,128)(2,1)S(1)}, u32[]{:S(2)}, u32[]{:S(2)}) collective-permute-start(bf16[288,128]{1,0:T(8,128)(2,1)S(1)} %get-tuple-element.79), channel_id=1, source_target_pairs={{2,0},{4,2},{6,4},{8,6},{10,8},{12,10},{14,12},{3,1},{5,3},{7,5},{... | collective-permute-start | bytes 221192 | tf_op jit(solution)/shard_map/ppermute | solution.py:640
  89.0 16.7 %collective-permute-start.8 = (bf16[288,128]{1,0:T(8,128)(2,1)S(1)}, bf16[288,128]{1,0:T(8,128)(2,1)S(1)}, u32[]{:S(2)}, u32[]{:S(2)}) collective-permute-start(bf16[288,128]{1,0:T(8,128)(2,1)S(1)} %get-tuple-element.78), channel_id=1, source_target_pairs={{0,2},{2,4},{4,6},{6,8},{8,10},{10,12},{12,14},{1,3},{3,5},{5,7},{... | collective-permute-start | bytes 221192 | tf_op jit(solution)/shard_map/ppermute | solution.py:640
  96.1 9.6 %collective-permute-start.11 = (f32[7,8,128]{2,1,0:T(8,128)S(1)}, f32[7,8,128]{2,1,0:T(8,128)S(1)}, u32[]{:S(2)}, u32[]{:S(2)}) collective-permute-start(f32[7,8,128]{2,1,0:T(8,128)S(1)} %near.1.near_own), channel_id=1, source_target_pairs={{16,0},{32,16},{48,32},{64,48},{80,64},{96,80},{112,96},{128,112},... | collective-permute-start | bytes 86024 | tf_op jit(solution)/shard_map/ppermute | solution.py:640
  103.6 3.1 %collective-permute-start.10 = (f32[7,8,128]{2,1,0:T(8,128)S(1)}, f32[7,8,128]{2,1,0:T(8,128)S(1)}, u32[]{:S(2)}, u32[]{:S(2)}) collective-permute-start(f32[7,8,128]{2,1,0:T(8,128)S(1)} %near.1.near_own), channel_id=1, source_target_pairs={{0,16},{16,32},{32,48},{48,64},{64,80},{80,96},{96,112},{112,128},... | collective-permute-start | bytes 86024 | tf_op jit(solution)/shard_map/ppermute | solution.py:640

commit v8 on v7

--- a/solution.py
+++ b/solution.py
@@ -579,22 +579,23 @@
         zforcing[row : row + rows, :] += across(mask, high) + across(mask, low)
 
 
+def ready_kernel(channels, _, unused, low_ref, high_ref, near_own, kept_ref, depth_ref):
+    gz = lax.axis_index("gz")
+    planes = depth_ref.shape[0] // (SIZE_Y + 2 * YO)
+    state, forcing, _, zforcing, _ = parted(kept_ref)
+    base = take_edges(state, low_ref, high_ref, 0, 3, 80)
+    take_edges(depth_ref, low_ref, high_ref, base, 3, 16)
+    add_load(forcing, zforcing, near_own, 0, gz, channels, planes)
+
+
 def second_kernel(
-    kept_ref, depth_ref, low_ref, high_ref, near_low, near_own, near_high,
-    out_ref, density_ref, first, second, zfirst, zsecond, forcing, zforcing,
+    _, unused, near_low, near_own, near_high, out_ref, density_ref, kept_ref, zfirst, second, zsecond,
 ):
     gz = lax.axis_index("gz")
-    rows = SIZE_Y + 2 * YO
-    planes = depth_ref.shape[0] // rows
+    planes = zfirst.shape[0] // (SIZE_Y + 2 * YO)
     channels = out_ref.shape[0]
-    state, old, coef, zold, zcoef = parted(kept_ref)
-    first[...] = state[...]
-    zfirst[...] = depth_ref[...]
-    forcing[...] = old[...]
-    zforcing[...] = zold[...]
-    base = take_edges(first, low_ref, high_ref, 0, 3, 80)
-    take_edges(zfirst, low_ref, high_ref, base, 3, 16)
-    for side, near in ((-1, near_low), (0, near_own), (1, near_high)):
+    first, forcing, coef, zforcing, zcoef = parted(kept_ref)
+    for side, near in ((-1, near_low), (1, near_high)):
         add_load(forcing, zforcing, near, side, gz, channels, planes)
 
     def finish(e, x, new):
@@ -725,10 +726,15 @@
     parts = lax.all_to_all(shares, ("col", "gz"), 0, 0, tiled=True)
     near = whole_call(near_kernel, f32(7, channels, slots), [], "near", (), parts, targets)
     near_low, near_high = both_ways(near, near, "row")
-    state, density = whole_call(
-        second_kernel, (f32(*initial_field.shape), bf16(bricks, channels, slots)),
-        [vm(frame), vm(frame), vm(flat), vm(flat), vm(frame), vm(flat)], "second", (),
-        kept, zframe, low, high, near_low, near, near_high, megabytes=8,
+    kept, zframe = whole_call(
+        functools.partial(ready_kernel, channels), (f32(*kept.shape), f32(*flat)), [], "ready", (),
+        kept, zframe, low, high, near, aliases={0: 0, 1: 1},
+    )
+    state, density, _, _ = whole_call(
+        second_kernel,
+        (f32(*initial_field.shape), bf16(bricks, channels, slots), f32(*kept.shape), f32(*flat)),
+        [vm(frame), vm(flat)], "second", (),
+        kept, zframe, near_low, near, near_high, aliases={0: 2, 1: 3}, megabytes=8,
     )
     densities = lax.all_to_all(density, "row", 0, 0, tiled=True)
     shares = products(table, densities, tile, 512)

time: 143 us -> 141 us (0.986)
  starting transfers between devices: 61.7 us -> 58.6 us
  Pallas kernels: 36.5 us -> 38.4 us
    ppermute x5, starting transfers between devices: 13.9 us -> 9.72 us  [both_ways(): lax.ppermute(down, axis, [(b, a) for a, b in pairs])]
    pallas_call x11 -> x12, Pallas kernels: 11.8 us -> 12.6 us  [whole_call(): pl.pallas_call(kernel, in_specs=[smem] * len(scalars) + [far if n in away...]
  transfers between devices with their start and end apart: 15 -> 15, of which waited for: 7 -> 6; matrix products, arithmetic and copies ran while one was open for 0% -> 0% of each run, Pallas kernels for 10% -> 11%
where the time goes in v8:
time: 141 us; the launch traced here: 140 us
  starting transfers between devices  58.6 us (42%)
  Pallas kernels  38.4 us (27%)
  blocking collectives  24.9 us (18%)
  waiting for transfers between devices  14.2 us (10%)
  local copies, waits for them, and re-layouts  2.65 us (2%)
  between operations  1.49 us (1%)
    pallas_call x3, Pallas kernels, make_tile(): pl.pallas_call(tile_kernel, grid=(-(-bricks // TILES),), in_specs=[pl.Blo...  19.4 us
    ppermute x5, starting transfers between devices, both_ways(): lax.ppermute(up, axis, pairs)  19 us
    all_to_all x1, blocking collectives, local(): densities = lax.all_to_all(density, 'row', 0, 0, tiled=True)  13.1 us
    pallas_call x12, Pallas kernels, whole_call(): pl.pallas_call(kernel, in_specs=[smem] * len(scalars) + [far if n in away...  12.6 us
    all_to_all x1, blocking collectives, local(): parts = lax.all_to_all(shares, ('col', 'gz'), 0, 0, tiled=True)  11.7 us
    all_to_all x1, starting transfers between devices, local(): densities = lax.all_to_all(density, 'row', 0, 0, tiled=True)  11.6 us
    ppermute x5, starting transfers between devices, both_ways(): lax.ppermute(down, axis, [(b, a) for a, b in pairs])  9.72 us
    all_to_all x1, starting transfers between devices, local(): targets = lax.all_to_all(message, ('col', 'gz'), 0, 0, tiled=True)  6.77 us
  transfers between devices with their start and end apart: 15, of which 6 were waited for; matrix products, arithmetic and copies ran while one was open for 0% of the time, Pallas kernels for 11%

profile of v8, /device:TPU:1, one launch (start us, length us, event | category | flops | bytes accessed | tf_op | source)
XLA Modules:
  0.0 140.3 jit_solution(4225354966396162205)
XLA Ops:
  1.3 1.9 %planes.1 = (bf16[672,128]{1,0:T(8,128)(2,1)}, bf16[672,128]{1,0:T(8,128)(2,1)}, f32[16,8,128]{2,1,0:T(8,128)}) custom-call(f32[8,4,16,128]{3,2,1,0:T(8,128)} %state_hbm.1, f32[8,4,16,128]{3,2,1,0:T(8,128)} %source_hbm.1, s32[1,4,16,128]{3,2,1,0:T(8,128)} %bitcast.2, f32[4,128]{1,0:T(4,128)} %geometry_hbm.1, s32[1,128]{1,0:T(1,128)} %bitcast.4, ...), custom_call_target="tpu_custom_call" | custom-call | tf_op jit(solution)/shard_map/planes/pallas_call | solution.py:52
  3.2 4.9 %collective-permute-start = (bf16[672,128]{1,0:T(8,128)(2,1)}, bf16[672,128]{1,0:T(8,128)(2,1)S(1)}, u32[]{:S(2)}, u32[]{:S(2)}) collective-permute-start(bf16[672,128]{1,0:T(8,128)(2,1)} %get-tuple-element.47), channel_id=1, source_target_pairs={{0,16},{16,32},{32,48},{48,64},{64,80},{80,96},{96,112},{112,128},... | collective-permute-start | bytes 516104 | tf_op jit(solution)/shard_map/ppermute | solution.py:641
  8.1 1.9 %collective-permute-start.1 = (bf16[672,128]{1,0:T(8,128)(2,1)}, bf16[672,128]{1,0:T(8,128)(2,1)S(1)}, u32[]{:S(2)}, u32[]{:S(2)}) collective-permute-start(bf16[672,128]{1,0:T(8,128)(2,1)} %get-tuple-element.48), channel_id=1, source_target_pairs={{16,0},{32,16},{48,32},{64,48},{80,64},{96,80},{112,96},{128,112},... | collective-permute-start | bytes 516104 | tf_op jit(solution)/shard_map/ppermute | solution.py:641
  10.1 6.8 %all-to-all-start = ((f32[16,8,128]{2,1,0:T(8,128)}), f32[16,8,128]{2,1,0:T(8,128)S(1)}, u32[]{:S(2)}, u32[]{:S(2)}) async-start(f32[16,8,128]{2,1,0:T(8,128)} %get-tuple-element.51), calls=%async_computation | async-start | bytes 131072 | tf_op jit(solution)/shard_map/all_to_all | solution.py:678
  16.8 0.9 copy-done
  17.8 0.9 copy-done.1
  20.1 3.0 %collective-permute-start.2 = (bf16[160,128]{1,0:T(8,128)(2,1)S(1)}, bf16[160,128]{1,0:T(8,128)(2,1)S(1)}, u32[]{:S(2)}, u32[]{:S(2)}) collective-permute-start(bf16[160,128]{1,0:T(8,128)(2,1)S(1)} %get-tuple-element.50), channel_id=1, source_target_pairs={{0,1},{1,0},{2,3},{3,2},{4,5},{5,4},{6,7},{7,6},{8,9},{9,8},{10,11... | collective-permute-start | bytes 122888 | tf_op jit(solution)/shard_map/ppermute | solution.py:677
  23.6 0.9 collective-permute-done.2.other_ref
  24.6 3.3 %collective-permute-start.3 = (bf16[480,128]{1,0:T(8,128)(2,1)S(1)}, bf16[480,128]{1,0:T(8,128)(2,1)S(1)}, u32[]{:S(2)}, u32[]{:S(2)}) collective-permute-start(bf16[480,128]{1,0:T(8,128)(2,1)S(1)} %get-tuple-element.54), channel_id=1, source_target_pairs={{0,2},{2,4},{4,6},{6,8},{8,10},{10,12},{12,14},{1,3},{3,5},{5,7},{... | collective-permute-start | bytes 368648 | tf_op jit(solution)/shard_map/ppermute | solution.py:641
  27.9 1.3 collective-permute-start.4
  29.2 1.2 compact.1
  30.9 4.1 %collective-permute-done.4.high_ref = bf16[480,128]{1,0:T(8,128)(2,1)S(1)} collective-permute-done((bf16[480,128]{1,0:T(8,128)(2,1)S(1)}, bf16[480,128]{1,0:T(8,128)(2,1)S(1)}, u32[]{:S(2)}, u32[]{:S(2)}) %collective-permute-start.4) | collective-permute-done | bytes 122912 | tf_op jit(solution)/shard_map/ppermute | solution.py:641
  35.0 3.3 %first.1 = (f32[4560,128]{1,0:T(8,128)S(1)}, f32[16,16,128]{2,1,0:T(8,128)}, bf16[384,128]{1,0:T(8,128)(2,1)S(1)}, bf16[384,128]{1,0:T(8,128)(2,1)S(1)}) custom-call(f32[4560,128]{1,0:T(8,128)S(1)} %get-tuple-element.49.kept_ref._, f32[240,128]{1,0:T(8,128)S(1)} %get-tuple-element.53.depth_ref, ...), custom_call_target="tpu_custom_call", output_to_operand_aliasing={{0}: (0, {})} | custom-call | tf_op jit(solution)/shard_map/first/pallas_call | solution.py:52
  38.3 11.6 %all-to-all-start.1 = ((f32[16,16,128]{2,1,0:T(8,128)}), f32[16,16,128]{2,1,0:T(8,128)S(1)}, u32[]{:S(2)}, u32[]{:S(2)}) async-start(f32[16,16,128]{2,1,0:T(8,128)} %get-tuple-element.65), calls=%async_computation.1 | async-start | bytes 262144 | tf_op jit(solution)/shard_map/all_to_all | solution.py:706
  49.9 3.5 %collective-permute-start.5 = (bf16[384,128]{1,0:T(8,128)(2,1)S(1)}, bf16[384,128]{1,0:T(8,128)(2,1)S(1)}, u32[]{:S(2)}, u32[]{:S(2)}) collective-permute-start(bf16[384,128]{1,0:T(8,128)(2,1)S(1)} %get-tuple-element.63), channel_id=1, source_target_pairs={{0,16},{16,32},{32,48},{48,64},{64,80},{80,96},{96,112},{112,128},... | collective-permute-start | bytes 294920 | tf_op jit(solution)/shard_map/ppermute | solution.py:641
  53.4 1.9 %collective-permute-start.6 = (bf16[384,128]{1,0:T(8,128)(2,1)S(1)}, bf16[384,128]{1,0:T(8,128)(2,1)S(1)}, u32[]{:S(2)}, u32[]{:S(2)}) collective-permute-start(bf16[384,128]{1,0:T(8,128)(2,1)S(1)} %get-tuple-element.64), channel_id=1, source_target_pairs={{16,0},{32,16},{48,32},{64,48},{80,64},{96,80},{112,96},{128,112},... | collective-permute-start | bytes 294920 | tf_op jit(solution)/shard_map/ppermute | solution.py:641
  55.3 3.8 %all-to-all-done.1.source_ref = f32[16,16,128]{2,1,0:T(8,128)S(1)} async-done(((f32[16,16,128]{2,1,0:T(8,128)}), f32[16,16,128]{2,1,0:T(8,128)S(1)}, u32[]{:S(2)}, u32[]{:S(2)}) %all-to-all-start.1) | async-done | bytes 131104 | tf_op jit(solution)/shard_map/all_to_all | solution.py:706
  59.1 7.3 %tile.3 = (bf16[16384,2048]{1,0:T(8,128)(2,1)}, f32[18,8,128]{2,1,0:T(8,128)S(1)}) custom-call(f32[16,16,128]{2,1,0:T(8,128)S(1)} %all-to-all-done.1.source_ref, f32[18,8,128]{2,1,0:T(8,128)S(1)} %get-tuple-element.66.target_ref), custom_call_target="tpu_custom_call" | custom-call | tf_op jit(solution)/shard_map/tile/pallas_call | solution.py:148
  66.6 2.8 %collective-permute-start.7 = (bf16[160,128]{1,0:T(8,128)(2,1)S(1)}, bf16[160,128]{1,0:T(8,128)(2,1)S(1)}, u32[]{:S(2)}, u32[]{:S(2)}) collective-permute-start(bf16[160,128]{1,0:T(8,128)(2,1)S(1)} %get-tuple-element.72), channel_id=1, source_target_pairs={{0,1},{1,0},{2,3},{3,2},{4,5},{5,4},{6,7},{7,6},{8,9},{9,8},{10,11... | collective-permute-start | bytes 122888 | tf_op jit(solution)/shard_map/ppermute | solution.py:714
  69.3 6.1 %tile.4 = (bf16[16384,2048]{1,0:T(8,128)(2,1)}, f32[18,8,128]{2,1,0:T(8,128)S(1)}) custom-call(f32[16,16,128]{2,1,0:T(8,128)S(1)} %all-to-all-done.1.source_ref, f32[18,8,128]{2,1,0:T(8,128)S(1)} %get-tuple-element.66.target_ref, bf16[16384,2048]{1,0:T(8,128)(2,1)} %get-tuple-element.74.refs_0_, ...), custom_call_target="tpu_custom_call", output_to_operand_aliasing={{0}: (2, {}), {1}: (3, {})} | custom-call | tf_op jit(solution)/shard_map/tile/pallas_call | solution.py:148
  75.5 6.1 %tile.5 = (bf16[16384,2048]{1,0:T(8,128)(2,1)}, f32[18,8,128]{2,1,0:T(8,128)S(1)}) custom-call(f32[16,16,128]{2,1,0:T(8,128)S(1)} %all-to-all-done.1.source_ref, f32[18,8,128]{2,1,0:T(8,128)S(1)} %get-tuple-element.66.target_ref, bf16[16384,2048]{1,0:T(8,128)(2,1)} %get-tuple-element.84.refs_0_, ...), custom_call_target="tpu_custom_call", output_to_operand_aliasing={{0}: (2, {}), {1}: (3, {})} | custom-call | tf_op jit(solution)/shard_map/tile/pallas_call | solution.py:148
  81.6 1.4 %arrange.1 = f32[16,6,8,128]{3,2,1,0:T(8,128)} custom-call(s32[17]{0:T(128)S(1)} %get-tuple-element.82.table_ref, f32[18,8,128]{2,1,0:T(8,128)S(1)} %get-tuple-element.86.share_ref), custom_call_target="tpu_custom_call" | custom-call | tf_op jit(solution)/shard_map/arrange/pallas_call | solution.py:52
  83.0 5.9 %all-to-all-start.2 = ((f32[16,6,8,128]{3,2,1,0:T(8,128)}), f32[16,6,8,128]{3,2,1,0:T(8,128)S(1)}, u32[]{:S(2)}, u32[]{:S(2)}) async-start(f32[16,6,8,128]{3,2,1,0:T(8,128)} %arrange.1), calls=%async_computation.2 | async-start | bytes 786432 | tf_op jit(solution)/shard_map/all_to_all | solution.py:726
  88.9 1.3 collective-permute-start.9
  90.2 4.0 %collective-permute-start.8 = (bf16[288,128]{1,0:T(8,128)(2,1)S(1)}, bf16[288,128]{1,0:T(8,128)(2,1)S(1)}, u32[]{:S(2)}, u32[]{:S(2)}) collective-permute-start(bf16[288,128]{1,0:T(8,128)(2,1)S(1)} %get-tuple-element.80), channel_id=1, source_target_pairs={{0,2},{2,4},{4,6},{6,8},{8,10},{10,12},{12,14},{1,3},{3,5},{5,7},{... | collective-permute-start | bytes 221192 | tf_op jit(solution)/shard_map/ppermute | solution.py:641
  94.2 4.4 %all-to-all-done.2.parts_ref = f32[16,6,8,128]{3,2,1,0:T(8,128)S(1)} async-done(((f32[16,6,8,128]{3,2,1,0:T(8,128)}), f32[16,6,8,128]{3,2,1,0:T(8,128)S(1)}, u32[]{:S(2)}, u32[]{:S(2)}) %all-to-all-start.2) | async-done | bytes 393248 | tf_op jit(solution)/shard_map/all_to_all | solution.py:726
  98.6 3.3 %collective-permute-start.11 = (f32[7,8,128]{2,1,0:T(8,128)S(1)}, f32[7,8,128]{2,1,0:T(8,128)S(1)}, u32[]{:S(2)}, u32[]{:S(2)}) collective-permute-start(f32[7,8,128]{2,1,0:T(8,128)S(1)} %near.1.near_own), channel_id=1, source_target_pairs={{16,0},{32,16},{48,32},{64,48},{80,64},{96,80},{112,96},{128,112},... | collective-permute-start | bytes 86024 | tf_op jit(solution)/shard_map/ppermute | solution.py:641
  101.9 3.3 %collective-permute-start.10 = (f32[7,8,128]{2,1,0:T(8,128)S(1)}, f32[7,8,128]{2,1,0:T(8,128)S(1)}, u32[]{:S(2)}, u32[]{:S(2)}) collective-permute-start(f32[7,8,128]{2,1,0:T(8,128)S(1)} %near.1.near_own), channel_id=1, source_target_pairs={{0,16},{16,32},{32,48},{48,64},{64,80},{80,96},{96,112},{112,128},... | collective-permute-start | bytes 86024 | tf_op jit(solution)/shard_map/ppermute | solution.py:641
  106.1 3.6 %second.1 = (f32[8,4,16,128]{3,2,1,0:T(8,128)}, bf16[16,8,128]{2,1,0:T(8,128)(2,1)S(1)}, f32[4560,128]{1,0:T(8,128)S(1)}, f32[240,128]{1,0:T(8,128)S(1)}) custom-call(f32[4560,128]{1,0:T(8,128)S(1)} %get-tuple-element.87._, f32[240,128]{1,0:T(8,128)S(1)} %get-tuple-element.88.unused, ...), custom_call_target="tpu_custom_call", output_to_operand_aliasing={{2}: (0, {}), {3}: (1, {})} | custom-call | tf_op jit(solution)/shard_map/second/pallas_call | solution.py:52
  109.6 13.1 %all_to_all.25.density_ref = bf16[16,8,128]{2,1,0:T(8,128)(2,1)S(1)} all-to-all(bf16[16,8,128]{2,1,0:T(8,128)(2,1)S(1)} %get-tuple-element.90), channel_id=1, replica_groups=mesh['row'=16,'col'=8,'gz'=2] {'row'}, dimensions={0} | all-to-all | bytes 65536 | tf_op jit(solution)/shard_map/all_to_all | solution.py:739
  122.8 5.2 %product.1 = f32[16,8,128]{2,1,0:T(8,128)S(1)} custom-call(s32[17]{0:T(128)S(1)} %get-tuple-element.82.table_ref, bf16[16,8,128]{2,1,0:T(8,128)(2,1)S(1)} %all_to_all.25.density_ref, bf16[16384,2048]{1,0:T(8,128)(2,1)} %get-tuple-element.91.tile_ref), custom_call_target="tpu_custom_call" | custom-call | tf_op jit(solution)/shard_map/product/pallas_call | solution.py:230
  128.0 11.7 %all_to_all.26.parts_ref = f32[16,8,128]{2,1,0:T(8,128)S(1)} all-to-all(f32[16,8,128]{2,1,0:T(8,128)S(1)} %product.1), channel_id=1, replica_groups=mesh['row'=16,'col'=8,'gz'=2] {'col','gz'}, dimensions={0} | all-to-all | bytes 131072 | tf_op jit(solution)/shard_map/all_to_all | solution.py:741
  (23 shorter events, 4.1 us)
Async XLA Ops:
  3.2 16.5 %collective-permute-start = (bf16[672,128]{1,0:T(8,128)(2,1)}, bf16[672,128]{1,0:T(8,128)(2,1)S(1)}, u32[]{:S(2)}, u32[]{:S(2)}) collective-permute-start(bf16[672,128]{1,0:T(8,128)(2,1)} %get-tuple-element.47), channel_id=1, source_target_pairs={{0,16},{16,32},{32,48},{48,64},{64,80},{80,96},{96,112},{112,128},... | collective-permute-start | bytes 516104 | tf_op jit(solution)/shard_map/ppermute | solution.py:641
  8.1 11.6 %collective-permute-start.1 = (bf16[672,128]{1,0:T(8,128)(2,1)}, bf16[672,128]{1,0:T(8,128)(2,1)S(1)}, u32[]{:S(2)}, u32[]{:S(2)}) collective-permute-start(bf16[672,128]{1,0:T(8,128)(2,1)} %get-tuple-element.48), channel_id=1, source_target_pairs={{16,0},{32,16},{48,32},{64,48},{80,64},{96,80},{112,96},{128,112},... | collective-permute-start | bytes 516104 | tf_op jit(solution)/shard_map/ppermute | solution.py:641
  10.1 13.5 %all-to-all-start = ((f32[16,8,128]{2,1,0:T(8,128)}), f32[16,8,128]{2,1,0:T(8,128)S(1)}, u32[]{:S(2)}, u32[]{:S(2)}) async-start(f32[16,8,128]{2,1,0:T(8,128)} %get-tuple-element.51), calls=%async_computation | async-start | bytes 131072 | tf_op jit(solution)/shard_map/all_to_all | solution.py:678
  16.8 1.0 copy-start
  17.8 0.9 copy-start.1
  18.7 0.8 copy-start.2
  20.1 4.4 %collective-permute-start.2 = (bf16[160,128]{1,0:T(8,128)(2,1)S(1)}, bf16[160,128]{1,0:T(8,128)(2,1)S(1)}, u32[]{:S(2)}, u32[]{:S(2)}) collective-permute-start(bf16[160,128]{1,0:T(8,128)(2,1)S(1)} %get-tuple-element.50), channel_id=1, source_target_pairs={{0,1},{1,0},{2,3},{3,2},{4,5},{5,4},{6,7},{7,6},{8,9},{9,8},{10,11... | collective-permute-start | bytes 122888 | tf_op jit(solution)/shard_map/ppermute | solution.py:677
  24.6 6.3 %collective-permute-start.3 = (bf16[480,128]{1,0:T(8,128)(2,1)S(1)}, bf16[480,128]{1,0:T(8,128)(2,1)S(1)}, u32[]{:S(2)}, u32[]{:S(2)}) collective-permute-start(bf16[480,128]{1,0:T(8,128)(2,1)S(1)} %get-tuple-element.54), channel_id=1, source_target_pairs={{0,2},{2,4},{4,6},{6,8},{8,10},{10,12},{12,14},{1,3},{3,5},{5,7},{... | collective-permute-start | bytes 368648 | tf_op jit(solution)/shard_map/ppermute | solution.py:641
  27.9 7.1 %collective-permute-start.4 = (bf16[480,128]{1,0:T(8,128)(2,1)S(1)}, bf16[480,128]{1,0:T(8,128)(2,1)S(1)}, u32[]{:S(2)}, u32[]{:S(2)}) collective-permute-start(bf16[480,128]{1,0:T(8,128)(2,1)S(1)} %get-tuple-element.55), channel_id=1, source_target_pairs={{2,0},{4,2},{6,4},{8,6},{10,8},{12,10},{14,12},{3,1},{5,3},{7,5},{... | collective-permute-start | bytes 368648 | tf_op jit(solution)/shard_map/ppermute | solution.py:641
  38.3 20.8 %all-to-all-start.1 = ((f32[16,16,128]{2,1,0:T(8,128)}), f32[16,16,128]{2,1,0:T(8,128)S(1)}, u32[]{:S(2)}, u32[]{:S(2)}) async-start(f32[16,16,128]{2,1,0:T(8,128)} %get-tuple-element.65), calls=%async_computation.1 | async-start | bytes 262144 | tf_op jit(solution)/shard_map/all_to_all | solution.py:706
  49.9 16.5 %collective-permute-start.5 = (bf16[384,128]{1,0:T(8,128)(2,1)S(1)}, bf16[384,128]{1,0:T(8,128)(2,1)S(1)}, u32[]{:S(2)}, u32[]{:S(2)}) collective-permute-start(bf16[384,128]{1,0:T(8,128)(2,1)S(1)} %get-tuple-element.63), channel_id=1, source_target_pairs={{0,16},{16,32},{32,48},{48,64},{64,80},{80,96},{96,112},{112,128},... | collective-permute-start | bytes 294920 | tf_op jit(solution)/shard_map/ppermute | solution.py:641
  53.4 13.0 %collective-permute-start.6 = (bf16[384,128]{1,0:T(8,128)(2,1)S(1)}, bf16[384,128]{1,0:T(8,128)(2,1)S(1)}, u32[]{:S(2)}, u32[]{:S(2)}) collective-permute-start(bf16[384,128]{1,0:T(8,128)(2,1)S(1)} %get-tuple-element.64), channel_id=1, source_target_pairs={{16,0},{32,16},{48,32},{64,48},{80,64},{96,80},{112,96},{128,112},... | collective-permute-start | bytes 294920 | tf_op jit(solution)/shard_map/ppermute | solution.py:641
  66.6 8.9 %collective-permute-start.7 = (bf16[160,128]{1,0:T(8,128)(2,1)S(1)}, bf16[160,128]{1,0:T(8,128)(2,1)S(1)}, u32[]{:S(2)}, u32[]{:S(2)}) collective-permute-start(bf16[160,128]{1,0:T(8,128)(2,1)S(1)} %get-tuple-element.72), channel_id=1, source_target_pairs={{0,1},{1,0},{2,3},{3,2},{4,5},{5,4},{6,7},{7,6},{8,9},{9,8},{10,11... | collective-permute-start | bytes 122888 | tf_op jit(solution)/shard_map/ppermute | solution.py:714
  83.0 15.6 %all-to-all-start.2 = ((f32[16,6,8,128]{3,2,1,0:T(8,128)}), f32[16,6,8,128]{3,2,1,0:T(8,128)S(1)}, u32[]{:S(2)}, u32[]{:S(2)}) async-start(f32[16,6,8,128]{3,2,1,0:T(8,128)} %arrange.1), calls=%async_computation.2 | async-start | bytes 786432 | tf_op jit(solution)/shard_map/all_to_all | solution.py:726
  88.9 16.3 %collective-permute-start.9 = (bf16[288,128]{1,0:T(8,128)(2,1)S(1)}, bf16[288,128]{1,0:T(8,128)(2,1)S(1)}, u32[]{:S(2)}, u32[]{:S(2)}) collective-permute-start(bf16[288,128]{1,0:T(8,128)(2,1)S(1)} %get-tuple-element.81), channel_id=1, source_target_pairs={{2,0},{4,2},{6,4},{8,6},{10,8},{12,10},{14,12},{3,1},{5,3},{7,5},{... | collective-permute-start | bytes 221192 | tf_op jit(solution)/shard_map/ppermute | solution.py:641
  90.2 15.0 %collective-permute-start.8 = (bf16[288,128]{1,0:T(8,128)(2,1)S(1)}, bf16[288,128]{1,0:T(8,128)(2,1)S(1)}, u32[]{:S(2)}, u32[]{:S(2)}) collective-permute-start(bf16[288,128]{1,0:T(8,128)(2,1)S(1)} %get-tuple-element.80), channel_id=1, source_target_pairs={{0,2},{2,4},{4,6},{6,8},{8,10},{10,12},{12,14},{1,3},{3,5},{5,7},{... | collective-permute-start | bytes 221192 | tf_op jit(solution)/shard_map/ppermute | solution.py:641
  98.6 7.5 %collective-permute-start.11 = (f32[7,8,128]{2,1,0:T(8,128)S(1)}, f32[7,8,128]{2,1,0:T(8,128)S(1)}, u32[]{:S(2)}, u32[]{:S(2)}) collective-permute-start(f32[7,8,128]{2,1,0:T(8,128)S(1)} %near.1.near_own), channel_id=1, source_target_pairs={{16,0},{32,16},{48,32},{64,48},{80,64},{96,80},{112,96},{128,112},... | collective-permute-start | bytes 86024 | tf_op jit(solution)/shard_map/ppermute | solution.py:641
  101.9 4.2 %collective-permute-start.10 = (f32[7,8,128]{2,1,0:T(8,128)S(1)}, f32[7,8,128]{2,1,0:T(8,128)S(1)}, u32[]{:S(2)}, u32[]{:S(2)}) collective-permute-start(f32[7,8,128]{2,1,0:T(8,128)S(1)} %near.1.near_own), channel_id=1, source_target_pairs={{0,16},{16,32},{32,48},{48,64},{64,80},{80,96},{96,112},{112,128},... | collective-permute-start | bytes 86024 | tf_op jit(solution)/shard_map/ppermute | solution.py:641

commit v9 on v8

--- a/solution.py
+++ b/solution.py
@@ -78,7 +78,7 @@
     return lax.dot_general(a, b, (((1,), (1,)), ((), ())), preferred_element_type=jnp.float32)
 
 
-def compact_kernel(target_ref, target_out, note_ref, table_ref, counts, table, arrived):
+def compact_kernel(target_ref, target_out, note_ref, counts, table_ref, table, arrived):
     bricks, depth, slots = target_ref.shape
     lane = lanes((depth, slots))
     first = jnp.zeros((depth, slots), jnp.float32)
@@ -171,9 +171,7 @@
     )(sources, targets, *before)
 
 
-def taken(share_ref, table_ref, brick, bricks):
-    begin = table_ref[brick]
-    count = table_ref[brick + 1] - begin
+def taken(share_ref, begin, count, bricks):
     group, shift = begin >> 7, begin & 127
     lane = lanes(share_ref.shape[1:])
     slots = share_ref.shape[2]
@@ -182,18 +180,23 @@
     return jnp.where(lane < count, jnp.where(lane < slots - shift, this, following), 0.0)
 
 
-def arrange_kernel(table_ref, share_ref, out_ref):
+def arrange_kernel(counts, share_ref, out_ref, table, arrived):
+    copy = pltpu.make_async_copy(counts, table, arrived)
+    copy.start()
     bricks = out_ref.shape[0]
+    for brick in range(bricks):
+        for n in range(6):
+            if not 0 <= brick // 2 + n % 3 - 1 < bricks // 2:
+                out_ref[brick, n] = jnp.zeros(out_ref.shape[2:], jnp.float32)
+    copy.wait()
+    begin = jnp.int32(0)
     for index in range(bricks):
-        value = taken(share_ref, table_ref, index, bricks)
+        value = taken(share_ref, begin, table[0, index], bricks)
+        begin = begin + table[0, index]
         for n in range(6):
             side, other = index // 2 - (n % 3 - 1), (index + n // 3) % 2
             if 0 <= side < bricks // 2:
                 out_ref[side * 2 + other, n] = value
-    for brick in range(bricks):
-        for n in range(6):
-            if not 0 <= brick // 2 + n % 3 - 1 < bricks // 2:
-                out_ref[brick, n] = jnp.zeros(out_ref.shape[2:], jnp.float32)
 
 
 def product_kernel(table_ref, density_ref, tile_ref, out_ref, density, shares):
@@ -215,7 +218,8 @@
     @pl.when(step == pl.num_programs(0) - 1)
     def _():
         for brick in range(bricks):
-            out_ref[brick] = taken(shares, table_ref, brick, bricks)
+            begin = table_ref[brick]
+            out_ref[brick] = taken(shares, begin, table_ref[brick + 1] - begin, bricks)
 
 
 def products(table, density, tile, rows):
@@ -684,12 +688,12 @@
     low, high = both_ways(up, down, "col")
     smem = pl.BlockSpec(memory_space=pltpu.SMEM)
     vmem = pl.BlockSpec(memory_space=pltpu.VMEM)
-    aims, note, table = pl.pallas_call(
+    aims, note, counts, table = pl.pallas_call(
         compact_kernel,
         in_specs=[vmem],
-        out_specs=(vmem, vmem, smem),
-        out_shape=(f32(bricks + 2, 8, slots), f32(8, slots), jax.ShapeDtypeStruct((bricks + 1,), jnp.int32)),
-        scratch_shapes=[vm((8, slots), jnp.int32), pltpu.SMEM((8, slots), jnp.int32), pltpu.SemaphoreType.DMA],
+        out_specs=(vmem, vmem, vmem, smem),
+        out_shape=(f32(bricks + 2, 8, slots), f32(8, slots), jax.ShapeDtypeStruct((8, slots), jnp.int32), jax.ShapeDtypeStruct((bricks + 1,), jnp.int32)),
+        scratch_shapes=[pltpu.SMEM((8, slots), jnp.int32), pltpu.SemaphoreType.DMA],
         compiler_params=params(4),
         name="compact",
     )(targets)
@@ -722,7 +726,10 @@
     low, high = both_ways(up, down, "col")
     densities, up = lax.optimization_barrier((densities, up))
     tile, shares = make_tile(2, densities, aims, channels, done)
-    shares = whole_call(arrange_kernel, f32(bricks, 6, channels, slots), [], "arrange", (table,), shares)
+    shares = whole_call(
+        arrange_kernel, f32(bricks, 6, channels, slots),
+        [pltpu.SMEM((8, slots), jnp.int32), pltpu.SemaphoreType.DMA], "arrange", (), counts, shares,
+    )
     parts = lax.all_to_all(shares, ("col", "gz"), 0, 0, tiled=True)
     near = whole_call(near_kernel, f32(7, channels, slots), [], "near", (), parts, targets)
     near_low, near_high = both_ways(near, near, "row")

time: 141 us -> 142 us (level)
  no operation moved by 1% of the time
where the time goes in v9:
time: 142 us; the launch traced here: 140 us
  starting transfers between devices  57.9 us (41%)
  Pallas kernels  38.5 us (27%)
  blocking collectives  25.7 us (18%)
  waiting for transfers between devices  14.2 us (10%)
  local copies, waits for them, and re-layouts  2.65 us (2%)
  between operations  1.5 us (1%)
    pallas_call x3, Pallas kernels, make_tile(): pl.pallas_call(tile_kernel, grid=(-(-bricks // TILES),), in_specs=[pl.Blo...  19.4 us
    ppermute x5, starting transfers between devices, both_ways(): lax.ppermute(up, axis, pairs)  18.2 us
    all_to_all x1, blocking collectives, local(): densities = lax.all_to_all(density, 'row', 0, 0, tiled=True)  14.4 us
    pallas_call x12, Pallas kernels, whole_call(): pl.pallas_call(kernel, in_specs=[smem] * len(scalars) + [far if n in away...  12.6 us
    all_to_all x1, starting transfers between devices, local(): densities = lax.all_to_all(density, 'row', 0, 0, tiled=True)  11.6 us
    all_to_all x1, blocking collectives, local(): parts = lax.all_to_all(shares, ('col', 'gz'), 0, 0, tiled=True)  11.3 us
    ppermute x5, starting transfers between devices, both_ways(): lax.ppermute(down, axis, [(b, a) for a, b in pairs])  9.72 us
    all_to_all x1, starting transfers between devices, local(): targets = lax.all_to_all(message, ('col', 'gz'), 0, 0, tiled=True)  6.77 us
  transfers between devices with their start and end apart: 15, of which 6 were waited for; matrix products, arithmetic and copies ran while one was open for 0% of the time, Pallas kernels for 11%

profile of v9, /device:TPU:1, one launch (start us, length us, event | category | flops | bytes accessed | tf_op | source)
XLA Modules:
  0.0 140.4 jit_solution(765262153769048078)
XLA Ops:
  1.3 1.9 %planes.1 = (bf16[672,128]{1,0:T(8,128)(2,1)}, bf16[672,128]{1,0:T(8,128)(2,1)}, f32[16,8,128]{2,1,0:T(8,128)}) custom-call(f32[8,4,16,128]{3,2,1,0:T(8,128)} %state_hbm.1, f32[8,4,16,128]{3,2,1,0:T(8,128)} %source_hbm.1, s32[1,4,16,128]{3,2,1,0:T(8,128)} %bitcast.2, f32[4,128]{1,0:T(4,128)} %geometry_hbm.1, s32[1,128]{1,0:T(1,128)} %bitcast.4, ...), custom_call_target="tpu_custom_call" | custom-call | tf_op jit(solution)/shard_map/planes/pallas_call | solution.py:52
  3.2 4.9 %collective-permute-start = (bf16[672,128]{1,0:T(8,128)(2,1)}, bf16[672,128]{1,0:T(8,128)(2,1)S(1)}, u32[]{:S(2)}, u32[]{:S(2)}) collective-permute-start(bf16[672,128]{1,0:T(8,128)(2,1)} %get-tuple-element.48), channel_id=1, source_target_pairs={{0,16},{16,32},{32,48},{48,64},{64,80},{80,96},{96,112},{112,128},... | collective-permute-start | bytes 516104 | tf_op jit(solution)/shard_map/ppermute | solution.py:645
  8.1 1.9 %collective-permute-start.1 = (bf16[672,128]{1,0:T(8,128)(2,1)}, bf16[672,128]{1,0:T(8,128)(2,1)S(1)}, u32[]{:S(2)}, u32[]{:S(2)}) collective-permute-start(bf16[672,128]{1,0:T(8,128)(2,1)} %get-tuple-element.49), channel_id=1, source_target_pairs={{16,0},{32,16},{48,32},{64,48},{80,64},{96,80},{112,96},{128,112},... | collective-permute-start | bytes 516104 | tf_op jit(solution)/shard_map/ppermute | solution.py:645
  10.1 6.8 %all-to-all-start = ((f32[16,8,128]{2,1,0:T(8,128)}), f32[16,8,128]{2,1,0:T(8,128)S(1)}, u32[]{:S(2)}, u32[]{:S(2)}) async-start(f32[16,8,128]{2,1,0:T(8,128)} %get-tuple-element.52), calls=%async_computation | async-start | bytes 131072 | tf_op jit(solution)/shard_map/all_to_all | solution.py:682
  16.8 0.9 copy-done
  17.8 0.9 copy-done.1
  20.1 3.0 %collective-permute-start.2 = (bf16[160,128]{1,0:T(8,128)(2,1)S(1)}, bf16[160,128]{1,0:T(8,128)(2,1)S(1)}, u32[]{:S(2)}, u32[]{:S(2)}) collective-permute-start(bf16[160,128]{1,0:T(8,128)(2,1)S(1)} %get-tuple-element.51), channel_id=1, source_target_pairs={{0,1},{1,0},{2,3},{3,2},{4,5},{5,4},{6,7},{7,6},{8,9},{9,8},{10,11... | collective-permute-start | bytes 122888 | tf_op jit(solution)/shard_map/ppermute | solution.py:681
  23.6 0.9 collective-permute-done.2.other_ref
  24.6 3.3 %collective-permute-start.3 = (bf16[480,128]{1,0:T(8,128)(2,1)S(1)}, bf16[480,128]{1,0:T(8,128)(2,1)S(1)}, u32[]{:S(2)}, u32[]{:S(2)}) collective-permute-start(bf16[480,128]{1,0:T(8,128)(2,1)S(1)} %get-tuple-element.55), channel_id=1, source_target_pairs={{0,2},{2,4},{4,6},{6,8},{8,10},{10,12},{12,14},{1,3},{3,5},{5,7},{... | collective-permute-start | bytes 368648 | tf_op jit(solution)/shard_map/ppermute | solution.py:645
  27.9 1.3 collective-permute-start.4
  29.2 1.2 compact.1
  30.9 4.1 %collective-permute-done.4.high_ref = bf16[480,128]{1,0:T(8,128)(2,1)S(1)} collective-permute-done((bf16[480,128]{1,0:T(8,128)(2,1)S(1)}, bf16[480,128]{1,0:T(8,128)(2,1)S(1)}, u32[]{:S(2)}, u32[]{:S(2)}) %collective-permute-start.4) | collective-permute-done | bytes 122912 | tf_op jit(solution)/shard_map/ppermute | solution.py:645
  35.0 3.3 %first.1 = (f32[4560,128]{1,0:T(8,128)S(1)}, f32[16,16,128]{2,1,0:T(8,128)}, bf16[384,128]{1,0:T(8,128)(2,1)S(1)}, bf16[384,128]{1,0:T(8,128)(2,1)S(1)}) custom-call(f32[4560,128]{1,0:T(8,128)S(1)} %get-tuple-element.50.kept_ref._, f32[240,128]{1,0:T(8,128)S(1)} %get-tuple-element.54.depth_ref, ...), custom_call_target="tpu_custom_call", output_to_operand_aliasing={{0}: (0, {})} | custom-call | tf_op jit(solution)/shard_map/first/pallas_call | solution.py:52
  38.3 11.6 %all-to-all-start.1 = ((f32[16,16,128]{2,1,0:T(8,128)}), f32[16,16,128]{2,1,0:T(8,128)S(1)}, u32[]{:S(2)}, u32[]{:S(2)}) async-start(f32[16,16,128]{2,1,0:T(8,128)} %get-tuple-element.66), calls=%async_computation.1 | async-start | bytes 262144 | tf_op jit(solution)/shard_map/all_to_all | solution.py:710
  49.9 3.5 %collective-permute-start.5 = (bf16[384,128]{1,0:T(8,128)(2,1)S(1)}, bf16[384,128]{1,0:T(8,128)(2,1)S(1)}, u32[]{:S(2)}, u32[]{:S(2)}) collective-permute-start(bf16[384,128]{1,0:T(8,128)(2,1)S(1)} %get-tuple-element.64), channel_id=1, source_target_pairs={{0,16},{16,32},{32,48},{48,64},{64,80},{80,96},{96,112},{112,128},... | collective-permute-start | bytes 294920 | tf_op jit(solution)/shard_map/ppermute | solution.py:645
  53.4 1.9 %collective-permute-start.6 = (bf16[384,128]{1,0:T(8,128)(2,1)S(1)}, bf16[384,128]{1,0:T(8,128)(2,1)S(1)}, u32[]{:S(2)}, u32[]{:S(2)}) collective-permute-start(bf16[384,128]{1,0:T(8,128)(2,1)S(1)} %get-tuple-element.65), channel_id=1, source_target_pairs={{16,0},{32,16},{48,32},{64,48},{80,64},{96,80},{112,96},{128,112},... | collective-permute-start | bytes 294920 | tf_op jit(solution)/shard_map/ppermute | solution.py:645
  55.3 3.8 %all-to-all-done.1.source_ref = f32[16,16,128]{2,1,0:T(8,128)S(1)} async-done(((f32[16,16,128]{2,1,0:T(8,128)}), f32[16,16,128]{2,1,0:T(8,128)S(1)}, u32[]{:S(2)}, u32[]{:S(2)}) %all-to-all-start.1) | async-done | bytes 131104 | tf_op jit(solution)/shard_map/all_to_all | solution.py:710
  59.1 7.3 %tile.3 = (bf16[16384,2048]{1,0:T(8,128)(2,1)}, f32[18,8,128]{2,1,0:T(8,128)S(1)}) custom-call(f32[16,16,128]{2,1,0:T(8,128)S(1)} %all-to-all-done.1.source_ref, f32[18,8,128]{2,1,0:T(8,128)S(1)} %get-tuple-element.67.target_ref), custom_call_target="tpu_custom_call" | custom-call | tf_op jit(solution)/shard_map/tile/pallas_call | solution.py:148
  66.6 2.8 %collective-permute-start.7 = (bf16[160,128]{1,0:T(8,128)(2,1)S(1)}, bf16[160,128]{1,0:T(8,128)(2,1)S(1)}, u32[]{:S(2)}, u32[]{:S(2)}) collective-permute-start(bf16[160,128]{1,0:T(8,128)(2,1)S(1)} %get-tuple-element.73), channel_id=1, source_target_pairs={{0,1},{1,0},{2,3},{3,2},{4,5},{5,4},{6,7},{7,6},{8,9},{9,8},{10,11... | collective-permute-start | bytes 122888 | tf_op jit(solution)/shard_map/ppermute | solution.py:718
  69.3 6.1 %tile.4 = (bf16[16384,2048]{1,0:T(8,128)(2,1)}, f32[18,8,128]{2,1,0:T(8,128)S(1)}) custom-call(f32[16,16,128]{2,1,0:T(8,128)S(1)} %all-to-all-done.1.source_ref, f32[18,8,128]{2,1,0:T(8,128)S(1)} %get-tuple-element.67.target_ref, bf16[16384,2048]{1,0:T(8,128)(2,1)} %get-tuple-element.75.refs_0_, ...), custom_call_target="tpu_custom_call", output_to_operand_aliasing={{0}: (2, {}), {1}: (3, {})} | custom-call | tf_op jit(solution)/shard_map/tile/pallas_call | solution.py:148
  75.5 6.1 %tile.5 = (bf16[16384,2048]{1,0:T(8,128)(2,1)}, f32[18,8,128]{2,1,0:T(8,128)S(1)}) custom-call(f32[16,16,128]{2,1,0:T(8,128)S(1)} %all-to-all-done.1.source_ref, f32[18,8,128]{2,1,0:T(8,128)S(1)} %get-tuple-element.67.target_ref, bf16[16384,2048]{1,0:T(8,128)(2,1)} %get-tuple-element.85.refs_0_, ...), custom_call_target="tpu_custom_call", output_to_operand_aliasing={{0}: (2, {}), {1}: (3, {})} | custom-call | tf_op jit(solution)/shard_map/tile/pallas_call | solution.py:148
  81.6 1.5 %arrange.1 = f32[16,6,8,128]{3,2,1,0:T(8,128)} custom-call(s32[8,128]{1,0:T(8,128)S(1)} %get-tuple-element.83.counts, f32[18,8,128]{2,1,0:T(8,128)S(1)} %get-tuple-element.87.share_ref), custom_call_target="tpu_custom_call" | custom-call | tf_op jit(solution)/shard_map/arrange/pallas_call | solution.py:52
  83.1 5.9 %all-to-all-start.2 = ((f32[16,6,8,128]{3,2,1,0:T(8,128)}), f32[16,6,8,128]{3,2,1,0:T(8,128)S(1)}, u32[]{:S(2)}, u32[]{:S(2)}) async-start(f32[16,6,8,128]{3,2,1,0:T(8,128)} %arrange.1), calls=%async_computation.2 | async-start | bytes 786432 | tf_op jit(solution)/shard_map/all_to_all | solution.py:733
  89.0 1.3 collective-permute-start.9
  90.3 4.0 %collective-permute-start.8 = (bf16[288,128]{1,0:T(8,128)(2,1)S(1)}, bf16[288,128]{1,0:T(8,128)(2,1)S(1)}, u32[]{:S(2)}, u32[]{:S(2)}) collective-permute-start(bf16[288,128]{1,0:T(8,128)(2,1)S(1)} %get-tuple-element.81), channel_id=1, source_target_pairs={{0,2},{2,4},{4,6},{6,8},{8,10},{10,12},{12,14},{1,3},{3,5},{5,7},{... | collective-permute-start | bytes 221192 | tf_op jit(solution)/shard_map/ppermute | solution.py:645
  94.3 4.4 %all-to-all-done.2.parts_ref = f32[16,6,8,128]{3,2,1,0:T(8,128)S(1)} async-done(((f32[16,6,8,128]{3,2,1,0:T(8,128)}), f32[16,6,8,128]{3,2,1,0:T(8,128)S(1)}, u32[]{:S(2)}, u32[]{:S(2)}) %all-to-all-start.2) | async-done | bytes 393248 | tf_op jit(solution)/shard_map/all_to_all | solution.py:733
  98.7 3.3 %collective-permute-start.11 = (f32[7,8,128]{2,1,0:T(8,128)S(1)}, f32[7,8,128]{2,1,0:T(8,128)S(1)}, u32[]{:S(2)}, u32[]{:S(2)}) collective-permute-start(f32[7,8,128]{2,1,0:T(8,128)S(1)} %near.1.near_own), channel_id=1, source_target_pairs={{16,0},{32,16},{48,32},{64,48},{80,64},{96,80},{112,96},{128,112},... | collective-permute-start | bytes 86024 | tf_op jit(solution)/shard_map/ppermute | solution.py:645
  102.0 2.5 %collective-permute-start.10 = (f32[7,8,128]{2,1,0:T(8,128)S(1)}, f32[7,8,128]{2,1,0:T(8,128)S(1)}, u32[]{:S(2)}, u32[]{:S(2)}) collective-permute-start(f32[7,8,128]{2,1,0:T(8,128)S(1)} %near.1.near_own), channel_id=1, source_target_pairs={{0,16},{16,32},{32,48},{48,64},{64,80},{80,96},{96,112},{112,128},... | collective-permute-start | bytes 86024 | tf_op jit(solution)/shard_map/ppermute | solution.py:645
  105.4 3.6 %second.1 = (f32[8,4,16,128]{3,2,1,0:T(8,128)}, bf16[16,8,128]{2,1,0:T(8,128)(2,1)S(1)}, f32[4560,128]{1,0:T(8,128)S(1)}, f32[240,128]{1,0:T(8,128)S(1)}) custom-call(f32[4560,128]{1,0:T(8,128)S(1)} %get-tuple-element.88._, f32[240,128]{1,0:T(8,128)S(1)} %get-tuple-element.89.unused, ...), custom_call_target="tpu_custom_call", output_to_operand_aliasing={{2}: (0, {}), {3}: (1, {})} | custom-call | tf_op jit(solution)/shard_map/second/pallas_call | solution.py:52
  108.9 14.4 %all_to_all.25.density_ref = bf16[16,8,128]{2,1,0:T(8,128)(2,1)S(1)} all-to-all(bf16[16,8,128]{2,1,0:T(8,128)(2,1)S(1)} %get-tuple-element.92), channel_id=1, replica_groups=mesh['row'=16,'col'=8,'gz'=2] {'row'}, dimensions={0} | all-to-all | bytes 65536 | tf_op jit(solution)/shard_map/all_to_all | solution.py:746
  123.3 5.2 %product.1 = f32[16,8,128]{2,1,0:T(8,128)S(1)} custom-call(s32[17]{0:T(128)S(1)} %get-tuple-element.91.table_ref, bf16[16,8,128]{2,1,0:T(8,128)(2,1)S(1)} %all_to_all.25.density_ref, bf16[16384,2048]{1,0:T(8,128)(2,1)} %get-tuple-element.93.tile_ref), custom_call_target="tpu_custom_call" | custom-call | tf_op jit(solution)/shard_map/product/pallas_call | solution.py:234
  128.5 11.3 %all_to_all.26.parts_ref = f32[16,8,128]{2,1,0:T(8,128)S(1)} all-to-all(f32[16,8,128]{2,1,0:T(8,128)S(1)} %product.1), channel_id=1, replica_groups=mesh['row'=16,'col'=8,'gz'=2] {'col','gz'}, dimensions={0} | all-to-all | bytes 131072 | tf_op jit(solution)/shard_map/all_to_all | solution.py:748
  (23 shorter events, 4.1 us)
Async XLA Ops:
  3.2 16.5 %collective-permute-start = (bf16[672,128]{1,0:T(8,128)(2,1)}, bf16[672,128]{1,0:T(8,128)(2,1)S(1)}, u32[]{:S(2)}, u32[]{:S(2)}) collective-permute-start(bf16[672,128]{1,0:T(8,128)(2,1)} %get-tuple-element.48), channel_id=1, source_target_pairs={{0,16},{16,32},{32,48},{48,64},{64,80},{80,96},{96,112},{112,128},... | collective-permute-start | bytes 516104 | tf_op jit(solution)/shard_map/ppermute | solution.py:645
  8.1 11.6 %collective-permute-start.1 = (bf16[672,128]{1,0:T(8,128)(2,1)}, bf16[672,128]{1,0:T(8,128)(2,1)S(1)}, u32[]{:S(2)}, u32[]{:S(2)}) collective-permute-start(bf16[672,128]{1,0:T(8,128)(2,1)} %get-tuple-element.49), channel_id=1, source_target_pairs={{16,0},{32,16},{48,32},{64,48},{80,64},{96,80},{112,96},{128,112},... | collective-permute-start | bytes 516104 | tf_op jit(solution)/shard_map/ppermute | solution.py:645
  10.1 13.5 %all-to-all-start = ((f32[16,8,128]{2,1,0:T(8,128)}), f32[16,8,128]{2,1,0:T(8,128)S(1)}, u32[]{:S(2)}, u32[]{:S(2)}) async-start(f32[16,8,128]{2,1,0:T(8,128)} %get-tuple-element.52), calls=%async_computation | async-start | bytes 131072 | tf_op jit(solution)/shard_map/all_to_all | solution.py:682
  16.8 1.0 copy-start
  17.8 0.9 copy-start.1
  18.7 0.8 copy-start.2
  20.1 4.4 %collective-permute-start.2 = (bf16[160,128]{1,0:T(8,128)(2,1)S(1)}, bf16[160,128]{1,0:T(8,128)(2,1)S(1)}, u32[]{:S(2)}, u32[]{:S(2)}) collective-permute-start(bf16[160,128]{1,0:T(8,128)(2,1)S(1)} %get-tuple-element.51), channel_id=1, source_target_pairs={{0,1},{1,0},{2,3},{3,2},{4,5},{5,4},{6,7},{7,6},{8,9},{9,8},{10,11... | collective-permute-start | bytes 122888 | tf_op jit(solution)/shard_map/ppermute | solution.py:681
  24.6 6.3 %collective-permute-start.3 = (bf16[480,128]{1,0:T(8,128)(2,1)S(1)}, bf16[480,128]{1,0:T(8,128)(2,1)S(1)}, u32[]{:S(2)}, u32[]{:S(2)}) collective-permute-start(bf16[480,128]{1,0:T(8,128)(2,1)S(1)} %get-tuple-element.55), channel_id=1, source_target_pairs={{0,2},{2,4},{4,6},{6,8},{8,10},{10,12},{12,14},{1,3},{3,5},{5,7},{... | collective-permute-start | bytes 368648 | tf_op jit(solution)/shard_map/ppermute | solution.py:645
  27.9 7.1 %collective-permute-start.4 = (bf16[480,128]{1,0:T(8,128)(2,1)S(1)}, bf16[480,128]{1,0:T(8,128)(2,1)S(1)}, u32[]{:S(2)}, u32[]{:S(2)}) collective-permute-start(bf16[480,128]{1,0:T(8,128)(2,1)S(1)} %get-tuple-element.56), channel_id=1, source_target_pairs={{2,0},{4,2},{6,4},{8,6},{10,8},{12,10},{14,12},{3,1},{5,3},{7,5},{... | collective-permute-start | bytes 368648 | tf_op jit(solution)/shard_map/ppermute | solution.py:645
  38.3 20.8 %all-to-all-start.1 = ((f32[16,16,128]{2,1,0:T(8,128)}), f32[16,16,128]{2,1,0:T(8,128)S(1)}, u32[]{:S(2)}, u32[]{:S(2)}) async-start(f32[16,16,128]{2,1,0:T(8,128)} %get-tuple-element.66), calls=%async_computation.1 | async-start | bytes 262144 | tf_op jit(solution)/shard_map/all_to_all | solution.py:710
  49.9 16.5 %collective-permute-start.5 = (bf16[384,128]{1,0:T(8,128)(2,1)S(1)}, bf16[384,128]{1,0:T(8,128)(2,1)S(1)}, u32[]{:S(2)}, u32[]{:S(2)}) collective-permute-start(bf16[384,128]{1,0:T(8,128)(2,1)S(1)} %get-tuple-element.64), channel_id=1, source_target_pairs={{0,16},{16,32},{32,48},{48,64},{64,80},{80,96},{96,112},{112,128},... | collective-permute-start | bytes 294920 | tf_op jit(solution)/shard_map/ppermute | solution.py:645
  53.4 13.0 %collective-permute-start.6 = (bf16[384,128]{1,0:T(8,128)(2,1)S(1)}, bf16[384,128]{1,0:T(8,128)(2,1)S(1)}, u32[]{:S(2)}, u32[]{:S(2)}) collective-permute-start(bf16[384,128]{1,0:T(8,128)(2,1)S(1)} %get-tuple-element.65), channel_id=1, source_target_pairs={{16,0},{32,16},{48,32},{64,48},{80,64},{96,80},{112,96},{128,112},... | collective-permute-start | bytes 294920 | tf_op jit(solution)/shard_map/ppermute | solution.py:645
  66.6 8.9 %collective-permute-start.7 = (bf16[160,128]{1,0:T(8,128)(2,1)S(1)}, bf16[160,128]{1,0:T(8,128)(2,1)S(1)}, u32[]{:S(2)}, u32[]{:S(2)}) collective-permute-start(bf16[160,128]{1,0:T(8,128)(2,1)S(1)} %get-tuple-element.73), channel_id=1, source_target_pairs={{0,1},{1,0},{2,3},{3,2},{4,5},{5,4},{6,7},{7,6},{8,9},{9,8},{10,11... | collective-permute-start | bytes 122888 | tf_op jit(solution)/shard_map/ppermute | solution.py:718
  83.1 15.6 %all-to-all-start.2 = ((f32[16,6,8,128]{3,2,1,0:T(8,128)}), f32[16,6,8,128]{3,2,1,0:T(8,128)S(1)}, u32[]{:S(2)}, u32[]{:S(2)}) async-start(f32[16,6,8,128]{3,2,1,0:T(8,128)} %arrange.1), calls=%async_computation.2 | async-start | bytes 786432 | tf_op jit(solution)/shard_map/all_to_all | solution.py:733
  89.0 15.5 %collective-permute-start.9 = (bf16[288,128]{1,0:T(8,128)(2,1)S(1)}, bf16[288,128]{1,0:T(8,128)(2,1)S(1)}, u32[]{:S(2)}, u32[]{:S(2)}) collective-permute-start(bf16[288,128]{1,0:T(8,128)(2,1)S(1)} %get-tuple-element.82), channel_id=1, source_target_pairs={{2,0},{4,2},{6,4},{8,6},{10,8},{12,10},{14,12},{3,1},{5,3},{7,5},{... | collective-permute-start | bytes 221192 | tf_op jit(solution)/shard_map/ppermute | solution.py:645
  90.3 14.2 %collective-permute-start.8 = (bf16[288,128]{1,0:T(8,128)(2,1)S(1)}, bf16[288,128]{1,0:T(8,128)(2,1)S(1)}, u32[]{:S(2)}, u32[]{:S(2)}) collective-permute-start(bf16[288,128]{1,0:T(8,128)(2,1)S(1)} %get-tuple-element.81), channel_id=1, source_target_pairs={{0,2},{2,4},{4,6},{6,8},{8,10},{10,12},{12,14},{1,3},{3,5},{5,7},{... | collective-permute-start | bytes 221192 | tf_op jit(solution)/shard_map/ppermute | solution.py:645
  98.7 6.6 %collective-permute-start.11 = (f32[7,8,128]{2,1,0:T(8,128)S(1)}, f32[7,8,128]{2,1,0:T(8,128)S(1)}, u32[]{:S(2)}, u32[]{:S(2)}) collective-permute-start(f32[7,8,128]{2,1,0:T(8,128)S(1)} %near.1.near_own), channel_id=1, source_target_pairs={{16,0},{32,16},{48,32},{64,48},{80,64},{96,80},{112,96},{128,112},... | collective-permute-start | bytes 86024 | tf_op jit(solution)/shard_map/ppermute | solution.py:645
  102.0 3.4 %collective-permute-start.10 = (f32[7,8,128]{2,1,0:T(8,128)S(1)}, f32[7,8,128]{2,1,0:T(8,128)S(1)}, u32[]{:S(2)}, u32[]{:S(2)}) collective-permute-start(f32[7,8,128]{2,1,0:T(8,128)S(1)} %near.1.near_own), channel_id=1, source_target_pairs={{0,16},{16,32},{32,48},{48,64},{64,80},{80,96},{96,112},{112,128},... | collective-permute-start | bytes 86024 | tf_op jit(solution)/shard_map/ppermute | solution.py:645
